TPU v7x, 32 devices: a whole 2x2x4 slice. The times are simulated.
32 devices in a mesh: batch: 16 (over z, x, core), mlp: 2 (over y).
Axes of the slice: x: 2, y: 2, z: 4, core: 2. Of those that a mesh axis runs over, the one named last changes fastest.
Arguments:
- inputs: bfloat16 [16384, 768], P(('batch', 'mlp')), may hold values from -6 to 6
- doc_lengths: int32 [32, 3], P(('batch', 'mlp')), may hold values from 1 to 256, 512 in all within a row
- ln1_gain: bfloat16 [768], replicated, may hold values from 0.5 to 1.5
- ln1_bias: bfloat16 [768], replicated, may hold values from -1.75 to 1.75
- attn_in: bfloat16 [768, 2304], replicated, may hold values from -0.21875 to 0.21875
- qv_bias: bfloat16 [2, 768], replicated, may hold values from -3 to 3
- attn_out: bfloat16 [768, 768], replicated, may hold values from -0.875 to 0.875
- attn_out_bias: bfloat16 [768], replicated, may hold values from -1.75 to 1.75
- ln2_gain: bfloat16 [768], replicated, may hold values from 0.5 to 1.5
- second_norm_bias: bfloat16 [768], replicated, may hold values from -1.75 to 1.75
- mlp_in: bfloat16 [768, 3072], P(None, 'mlp'), may hold values from -0.21875 to 0.21875
- mlp_in_bias: bfloat16 [3072], P('mlp'), may hold values from -3 to 3
- mlp_out: bfloat16 [3072, 768], P('mlp'), may hold values from -0.109375 to 0.109375
- mlp_out_bias: bfloat16 [768], replicated, may hold values from -1.75 to 1.75
- cotangent: bfloat16 [16384, 768], P(('batch', 'mlp')), may hold values from -6 to 6
Outputs:
- layer_output: bfloat16 [16384, 768], P(('batch', 'mlp'))
- input_grad: bfloat16 [16384, 768], P(('batch', 'mlp'))
- ln1_gain_grad: float32 [768], replicated
- ln1_bias_grad: float32 [768], replicated
- attn_in_grad: float32 [768, 2304], replicated
- qv_bias_grad: float32 [2, 768], replicated
- attn_out_grad: float32 [768, 768], replicated
- attn_out_bias_grad: float32 [768], replicated
- ln2_gain_grad: float32 [768], replicated
- ln2_bias_grad: float32 [768], replicated
- mlp_in_grad: float32 [768, 3072], P(None, 'mlp')
- perceptron_input_bias_gradient: float32 [3072], P('mlp')
- mlp_out_grad: float32 [3072, 768], P('mlp')
- mlp_out_bias_grad: float32 [768], replicated
Inputs may be any that keep to these rules, and one draw needn't show every extreme that they name: `doc_lengths`: row s holds the lengths of the 3 documents packed in segment s, in order; they sum to 512. A segment's first document continues the last document of the segment before it in its stream.
All inputs are finite; a program needn't handle non-finite values.
Results may differ from a plain program's by a relative error of at most 0.019.
Values may be sent and summed in bfloat16 or wider, within the bound.
No kernel may reach another device: no remote copies, remote signals or barrier semaphores. Data moves between devices by JAX's collectives and lax.ppermute only.
A program may use at most 192 MiB of HBM per device.

v0:
```python
import jax
import jax.numpy as jnp
from jax import lax
from jax.experimental import pallas as pl
from jax.experimental.pallas import tpu as pltpu
from jax.sharding import PartitionSpec as P

D = 768
H = 12
HD = 64
NB = 512
L = 512
NDOC = 3
HALF = L // 2
PAIRS = H // 2
LANES = 2 * HD

LOG2E = 1.4426950408889634
SCORE_LOG2 = LOG2E * HD**-0.5
MASKED = -1e30

bf16 = jnp.bfloat16
f32 = jnp.float32


def dot(a, b):
    return jnp.dot(a, b, preferred_element_type=f32)


def dot_nt(a, b):
    return lax.dot_general(a, b, (((1,), (1,)), ((), ())), preferred_element_type=f32)


def layer_norm(matrix, gain_row, shift_row):
    center = jnp.mean(matrix, axis=-1, keepdims=True)
    centered = matrix - center
    spread = jnp.mean(centered * centered, axis=-1, keepdims=True)
    return centered * lax.rsqrt(spread + 1e-05) * gain_row + shift_row


def norm_backward(matrix, gain_row, shift_row, upstream):
    unused, pullback = jax.vjp(layer_norm, matrix, gain_row, shift_row)
    return pullback(upstream)


def head_lanes(matrix, head):
    lane = lax.broadcasted_iota(jnp.int32, (1, LANES), 1)
    return jnp.where(lane // HD == head, matrix, jnp.zeros_like(matrix))


def fill_mask(lens, mask):
    key = lax.broadcasted_iota(jnp.int32, (L, L), 0)
    query = lax.broadcasted_iota(jnp.int32, (L, L), 1)
    one = lens[0, 0]
    two = one + lens[0, 1]
    start = jnp.where(query >= two, two, jnp.where(query >= one, one, 0))
    mask[...] = jnp.where((key <= query) & (key >= start), 0.0, MASKED)


def local_kernel(
    lens,
    q_ref,
    k_ref,
    v_ref,
    wo_ref,
    x_ref,
    rows_ref,
    out_ref,
    lse_ref,
    mix_ref,
    middle_ref,
    normed_ref,
    mask,
    turned,
    acc,
):
    step = pl.program_id(0)

    @pl.when(step == 0)
    def _():
        fill_mask(lens, mask)
        acc[...] = jnp.zeros_like(acc)

    q, k = q_ref[...], k_ref[...]
    v_t = v_ref[...].T
    for head in range(2):
        q_head = head_lanes(q, head)
        rows = slice(head * HD, (head + 1) * HD)
        for part in range(2):
            keys = HALF * (part + 1)
            cols = slice(part * HALF, (part + 1) * HALF)
            s = dot_nt(k[:keys], q_head[cols]) * SCORE_LOG2 + mask[:keys, cols]
            top = jnp.max(s, axis=0, keepdims=True)
            e = jnp.exp2(s - top)
            total = jnp.sum(e, axis=0, keepdims=True)
            out = dot(v_t[rows, :keys], e.astype(bf16))
            turned[rows, cols] = out / total
            lse_ref[0, head : head + 1, cols] = top + jnp.log2(total)
    out_ref[...] = turned[:, :HALF].T
    mixed = turned[:, HALF:].T.astype(bf16)
    mix_ref[...] = mixed
    acc[...] += dot(mixed, wo_ref[...])

    @pl.when(step == PAIRS - 1)
    def _():
        finish_middle(x_ref, acc, rows_ref, middle_ref, normed_ref)


def finish_middle(x_ref, acc, rows_ref, middle_ref, normed_ref):
    middle = x_ref[...].astype(f32) + (acc[...] + rows_ref[0:1])
    middle_ref[...] = middle
    normed_ref[...] = layer_norm(middle, rows_ref[1:2], rows_ref[2:3]).astype(bf16)


def local_attention(lens, qkv, attn_out, inputs, rows):
    column = lambda k: pl.BlockSpec((L, LANES), lambda i: (0, k * PAIRS + i))
    upper = pl.BlockSpec((HALF, D), lambda i: (1, 0))
    return pl.pallas_call(
        local_kernel,
        grid=(PAIRS,),
        in_specs=[
            pl.BlockSpec(memory_space=pltpu.SMEM),
            column(0),
            column(1),
            column(2),
            pl.BlockSpec((LANES, D), lambda i: (i, 0)),
            upper,
            pl.BlockSpec((8, D), lambda i: (0, 0)),
        ],
        out_specs=[
            pl.BlockSpec((HALF, LANES), lambda i: (0, i)),
            pl.BlockSpec((1, 8, L), lambda i: (i, 0, 0)),
            pl.BlockSpec((HALF, LANES), lambda i: (1, i)),
            upper,
            upper,
        ],
        out_shape=[
            jax.ShapeDtypeStruct((HALF, D), f32),
            jax.ShapeDtypeStruct((PAIRS, 8, L), f32),
            jax.ShapeDtypeStruct((L, D), bf16),
            jax.ShapeDtypeStruct((L, D), f32),
            jax.ShapeDtypeStruct((L, D), bf16),
        ],
        scratch_shapes=[
            pltpu.VMEM((L, L), f32),
            pltpu.VMEM((LANES, L), f32),
            pltpu.VMEM((HALF, D), f32),
        ],
        cost_estimate=pl.CostEstimate(
            flops=H * 12 * HALF * HALF * 256, bytes_accessed=8 * L * D, transcendentals=H * L * L
        ),
        name="local_attention",
    )(lens, qkv, qkv, qkv, attn_out, inputs, rows)


def basis_rows(last_len, transposed):
    shape = (HALF, NB) if transposed else (NB, HALF)
    slot_dim, place_dim = (1, 0) if transposed else (0, 1)
    slot = lax.broadcasted_iota(jnp.int32, shape, slot_dim).astype(f32)
    place = lax.broadcasted_iota(jnp.int32, shape, place_dim).astype(f32)
    offsets = place - HALF + last_len + 0.5
    distances = (slot + 0.5) / NB * last_len - offsets
    weights = jnp.where(offsets > 0.0, jnp.exp(-0.5 * distances * distances), 0.0)
    return weights / jnp.sum(weights, axis=place_dim, keepdims=True)


def memory_kernel(
    reads,
    last_ref,
    q_ref,
    kt_ref,
    vt_ref,
    vb_ref,
    local_ref,
    wo_ref,
    x_ref,
    rows_ref,
    mix_whole,
    middle_whole,
    normed_whole,
    mix_ref,
    mk_ref,
    mv_ref,
    lse_ref,
    middle_ref,
    normed_ref,
    basis_t_ref,
    basis,
    turned,
    acc,
):
    step = pl.program_id(0)

    @pl.when(step == 0)
    def _():
        last_len = last_ref[0:1, 0:1]
        basis[...] = basis_rows(last_len, False).astype(bf16)
        basis_t_ref[...] = basis_rows(last_len, True).astype(bf16)
        acc[...] = jnp.zeros_like(acc)

    mem_k = dot(basis[...], kt_ref[...]).astype(bf16)
    mem_v = (dot(basis[...], vt_ref[...]) + vb_ref[0:1]).astype(bf16)
    mk_ref[...] = mem_k
    mv_ref[...] = mem_v
    v_t = mem_v.T
    query = lax.broadcasted_iota(jnp.int32, (1, HALF), 1)
    reading = query < reads[0, 0]
    q = q_ref[...]
    for head in range(2):
        rows = slice(head * HD, (head + 1) * HD)
        s = dot_nt(mem_k, head_lanes(q, head)) * SCORE_LOG2
        top = jnp.max(s, axis=0, keepdims=True)
        e = jnp.exp2(s - top)
        total = jnp.sum(e, axis=0, keepdims=True)
        out = dot(v_t[rows], e.astype(bf16))
        turned[rows, :] = jnp.where(reading, out / total, 0.0)
        lse_ref[0, head : head + 1, :] = jnp.where(reading, top + jnp.log2(total), -MASKED)
    mixed = (local_ref[...] + turned[...].T).astype(bf16)
    mix_ref[...] = mixed
    acc[...] += dot(mixed, wo_ref[...])

    @pl.when(step == PAIRS - 1)
    def _():
        finish_middle(x_ref, acc, rows_ref, middle_ref, normed_ref)


def memory_attention(
    reads, last_rows, qkv, tail_kv, value_bias, local, attn_out, inputs, rows, mixture, middle, normed
):
    whole = lambda shape: pl.BlockSpec(shape, lambda i: (0,) * len(shape))
    untouched = pl.BlockSpec(memory_space=pl.ANY)
    return pl.pallas_call(
        memory_kernel,
        grid=(PAIRS,),
        in_specs=[
            pl.BlockSpec(memory_space=pltpu.SMEM),
            whole((16, D)),
            pl.BlockSpec((HALF, LANES), lambda i: (0, i)),
            pl.BlockSpec((HALF, LANES), lambda i: (0, i)),
            pl.BlockSpec((HALF, LANES), lambda i: (0, PAIRS + i)),
            pl.BlockSpec((8, LANES), lambda i: (0, i)),
            pl.BlockSpec((HALF, LANES), lambda i: (0, i)),
            pl.BlockSpec((LANES, D), lambda i: (i, 0)),
            whole((HALF, D)),
            whole((8, D)),
            untouched,
            untouched,
            untouched,
        ],
        out_specs=[
            pl.BlockSpec((HALF, LANES), lambda i: (0, i)),
            pl.BlockSpec((NB, LANES), lambda i: (0, i)),
            pl.BlockSpec((NB, LANES), lambda i: (0, i)),
            pl.BlockSpec((1, 8, HALF), lambda i: (i, 0, 0)),
            whole((HALF, D)),
            whole((HALF, D)),
            whole((HALF, NB)),
        ],
        out_shape=[
            jax.ShapeDtypeStruct((L, D), bf16),
            jax.ShapeDtypeStruct((NB, D), bf16),
            jax.ShapeDtypeStruct((NB, D), bf16),
            jax.ShapeDtypeStruct((PAIRS, 8, HALF), f32),
            jax.ShapeDtypeStruct((L, D), f32),
            jax.ShapeDtypeStruct((L, D), bf16),
            jax.ShapeDtypeStruct((HALF, NB), bf16),
        ],
        scratch_shapes=[
            pltpu.VMEM((NB, HALF), bf16),
            pltpu.VMEM((LANES, HALF), f32),
            pltpu.VMEM((HALF, D), f32),
        ],
        input_output_aliases={10: 0, 11: 4, 12: 5},
        cost_estimate=pl.CostEstimate(
            flops=H * 16 * HALF * HALF * 256, bytes_accessed=16 * L * D, transcendentals=H * L * HALF
        ),
        name="memory_attention",
    )(
        reads,
        last_rows,
        qkv,
        tail_kv,
        tail_kv,
        value_bias,
        local,
        attn_out,
        inputs,
        rows,
        mixture,
        middle,
        normed,
    )


def mlp_kernel(x_ref, ct_ref, wi_ref, bi_ref, wo_ref, *refs):
    hid_ref, dpre_ref, bias_ref, y_ref, dx_ref, y_acc, dx_acc = refs[-7:]
    step = pl.program_id(0)
    pre = dot(x_ref[...], wi_ref[...]) + bi_ref[0:1]
    squared = pre * pre
    tanh = jnp.tanh(pre * (0.7978845608028654 + 0.7978845608028654 * 0.044715 * squared))
    half = 0.5 * pre
    hidden = (half + half * tanh).astype(bf16)
    slope = (
        0.5
        + 0.5 * tanh
        + half
        * (1.0 - tanh * tanh)
        * (0.7978845608028654 + 3 * 0.7978845608028654 * 0.044715 * squared)
    )
    d_pre = (slope * dot_nt(ct_ref[...], wo_ref[...])).astype(bf16)
    hid_ref[...] = hidden
    dpre_ref[...] = d_pre
    bias_ref[...] = jnp.broadcast_to(
        jnp.sum(d_pre.astype(f32), axis=0, keepdims=True), bias_ref.shape
    )
    y = dot(hidden, wo_ref[...])
    dx = dot_nt(d_pre, wi_ref[...])

    @pl.when(step == 0)
    def _():
        y_acc[...] = y
        dx_acc[...] = dx

    @pl.when(step > 0)
    def _():
        y_acc[...] += y
        dx_acc[...] += dx

    @pl.when(step == pl.num_programs(0) - 1)
    def _():
        y_ref[...] = y_acc[...].astype(bf16)
        dx_ref[...] = dx_acc[...].astype(bf16)


def mlp_block(rows, cotangent, part, mlp_in, bias_rows, mlp_out, total, place, kept):
    count, hidden = rows.shape[0], mlp_in.shape[1]
    tile = 256 if hidden % 256 == 0 else 128
    fixed = pl.BlockSpec((count, D), lambda i: (0, 0))
    across = pl.BlockSpec((count, tile), lambda i: (place, i))
    return pl.pallas_call(
        mlp_kernel,
        grid=(hidden // tile,),
        in_specs=[
            fixed,
            pl.BlockSpec((count, D), lambda i: (part, 0)),
            pl.BlockSpec((D, tile), lambda i: (0, i)),
            pl.BlockSpec((8, tile), lambda i: (0, i)),
            pl.BlockSpec((tile, D), lambda i: (i, 0)),
        ]
        + [pl.BlockSpec(memory_space=pl.ANY)] * len(kept),
        out_specs=[across, across, pl.BlockSpec((8, tile), lambda i: (0, i)), fixed, fixed],
        out_shape=[
            jax.ShapeDtypeStruct((total, hidden), bf16),
            jax.ShapeDtypeStruct((total, hidden), bf16),
            jax.ShapeDtypeStruct((8, hidden), f32),
            jax.ShapeDtypeStruct((count, D), bf16),
            jax.ShapeDtypeStruct((count, D), bf16),
        ],
        scratch_shapes=[pltpu.VMEM((count, D), f32), pltpu.VMEM((count, D), f32)],
        input_output_aliases={5 + i: i for i in range(len(kept))},
        cost_estimate=pl.CostEstimate(
            flops=8 * count * D * hidden,
            bytes_accessed=4 * D * hidden + 4 * count * hidden + 8 * count * D,
            transcendentals=count * hidden,
        ),
        name="mlp_block",
    )(rows, cotangent, mlp_in, bias_rows, mlp_out, *kept)


def backward_kernel(
    lens,
    q_ref,
    k_ref,
    v_ref,
    mk_ref,
    mv_ref,
    db_ref,
    wo_ref,
    ll_ref,
    lm_ref,
    bt_ref,
    dqkv_ref,
    dtail_ref,
    sums_ref,
    mask,
    turned,
    dk_acc,
    dv_acc,
):
    @pl.when(pl.program_id(0) == 0)
    def _():
        fill_mask(lens, mask)

    q, k, v = q_ref[...], k_ref[...], v_ref[...]
    mem_k, mem_v = mk_ref[...], mv_ref[...]
    d_mix = dot_nt(db_ref[...], wo_ref[...]).astype(bf16)
    k_t, mk_t = k.T, mem_k.T
    d_mem_k = d_mem_v = None

    def one(keys, values, q_part, d_part, lse, extra):
        s = dot_nt(keys, q_part) * SCORE_LOG2
        if extra is not None:
            s = s + extra
        weights = jnp.exp2(s - lse)
        d_weights = dot_nt(values, d_part)
        inner = jnp.sum(weights * d_weights, axis=0, keepdims=True)
        d_scores = (weights * (d_weights - inner)).astype(bf16)
        return d_scores, dot(d_scores, q_part), dot(weights.astype(bf16), d_part)

    for head in range(2):
        rows = slice(head * HD, (head + 1) * HD)
        q_head, d_head = head_lanes(q, head), head_lanes(d_mix, head)
        for part in range(2):
            keys = HALF * (part + 1)
            cols = slice(part * HALF, (part + 1) * HALF)
            ds, dk, dv = one(
                k[:keys],
                v[:keys],
                q_head[cols],
                d_head[cols],
                ll_ref[0, head : head + 1, cols],
                mask[:keys, cols],
            )
            dq = dot(k_t[rows, :keys], ds)
            if part == 0:
                ds, d_key, d_value = one(
                    mem_k, mem_v, q_head[cols], d_head[cols], lm_ref[0, head : head + 1, :], None
                )
                dq = dq + dot(mk_t[rows], ds)
                d_mem_k = d_key if d_mem_k is None else d_mem_k + d_key
                d_mem_v = d_value if d_mem_v is None else d_mem_v + d_value
            turned[rows, cols] = dq
            if head == 0 and part == 0:
                dk_acc[:HALF] = dk
                dv_acc[:HALF] = dv
            elif head == 0:
                dk_acc[:HALF] += dk[:HALF]
                dv_acc[:HALF] += dv[:HALF]
                dk_acc[HALF:] = dk[HALF:]
                dv_acc[HALF:] = dv[HALF:]
            else:
                dk_acc[:keys] += dk
                dv_acc[:keys] += dv
    scale = HD**-0.5
    d_q = (turned[...].T * scale).astype(bf16)
    d_v = dv_acc[...].astype(bf16)
    dqkv_ref[0] = d_q
    dqkv_ref[1] = (dk_acc[...] * scale).astype(bf16)
    dqkv_ref[2] = d_v
    d_mem_k = (d_mem_k * scale).astype(bf16)
    d_mem_v = d_mem_v.astype(bf16)
    dtail_ref[0] = dot(bt_ref[...], d_mem_k).astype(bf16)
    dtail_ref[1] = dot(bt_ref[...], d_mem_v).astype(bf16)
    sums_ref[0:1] = jnp.sum(d_q.astype(f32), axis=0, keepdims=True)
    sums_ref[1:2] = jnp.sum(d_v.astype(f32), axis=0, keepdims=True) + jnp.sum(
        d_mem_v.astype(f32), axis=0, keepdims=True
    )


HIDDEN = pl.CostEstimate(flops=1000, bytes_accessed=1000, transcendentals=0)


def attention_backward(
    first, pairs, lens, qkv, mem_k, mem_v, d_branch, attn_out, lse_local, lse_mem, basis_t
):
    column = lambda k: pl.BlockSpec((L, LANES), lambda i: (0, k * PAIRS + first + i))
    whole = lambda shape: pl.BlockSpec(shape, lambda i: (0,) * len(shape))
    width = pairs * LANES
    return pl.pallas_call(
        backward_kernel,
        grid=(pairs,),
        in_specs=[
            pl.BlockSpec(memory_space=pltpu.SMEM),
            column(0),
            column(1),
            column(2),
            column(0),
            column(0),
            whole((L, D)),
            pl.BlockSpec((LANES, D), lambda i: (first + i, 0)),
            pl.BlockSpec((1, 8, L), lambda i: (first + i, 0, 0)),
            pl.BlockSpec((1, 8, HALF), lambda i: (first + i, 0, 0)),
            whole((HALF, NB)),
        ],
        out_specs=[
            pl.BlockSpec((3, L, LANES), lambda i: (0, 0, i)),
            pl.BlockSpec((2, HALF, LANES), lambda i: (0, 0, i)),
            pl.BlockSpec((8, LANES), lambda i: (0, i)),
        ],
        out_shape=[
            jax.ShapeDtypeStruct((3, L, width), bf16),
            jax.ShapeDtypeStruct((2, HALF, width), bf16),
            jax.ShapeDtypeStruct((8, width), f32),
        ],
        scratch_shapes=[
            pltpu.VMEM((L, L), f32),
            pltpu.VMEM((LANES, L), f32),
            pltpu.VMEM((L, LANES), f32),
            pltpu.VMEM((L, LANES), f32),
        ],
        cost_estimate=pl.CostEstimate(
            flops=2 * pairs * 56 * HALF * HALF * 256,
            bytes_accessed=20 * L * width,
            transcendentals=2 * pairs * L * L,
        ),
        name="attention_backward",
    )(lens, qkv, qkv, qkv, mem_k, mem_v, d_branch, attn_out, lse_local, lse_mem, basis_t)


def rotated(value, axis, by):
    count = lax.axis_size(axis)
    return lax.ppermute(value, axis, [(i, (i + by) % count) for i in range(count)])


fence = lax.optimization_barrier
GRID = ("batch", "mlp")


def flipped(value, mask):
    count = lax.axis_size("batch") * lax.axis_size("mlp")
    return lax.ppermute(value, GRID, [(i, i ^ mask) for i in range(count)])


def place_in(bits):
    number = lax.axis_index(GRID)
    return sum(((number >> bit) & 1) << i for i, bit in enumerate(bits))


def peers(bits):
    return [sum(((q >> i) & 1) << bit for i, bit in enumerate(bits)) for q in range(1, 1 << len(bits))]


def grouped(bits):
    odd = len(bits) % 2
    return ([bits[:1]] if odd else []) + [bits[i : i + 2] for i in range(odd, len(bits), 2)]


class Chain:
    def __init__(self, kept, given, groups):
        self.stages = [(True, bits) for bits in groups] + [(False, bits) for bits in groups[::-1]]
        self.turn()
        self.kept, self.given = kept, [given]

    def turn(self):
        self.scatters, self.bits = self.stages.pop(0)
        self.place = place_in(self.bits)

    def prepare(self):
        self.turn()
        count = 1 << len(self.bits)
        if self.scatters:
            size = self.value.shape[0] // count
            piece = lambda i: lax.dynamic_slice_in_dim(self.value, i * size, size, 0)
            self.kept = piece(self.place)
            self.given = [piece(self.place ^ q) for q in range(1, count)]
        else:
            self.kept = self.value
            self.given = [self.value]

    def fly(self):
        masks = peers(self.bits)
        given = self.given if self.scatters else self.given * len(masks)
        self.got = [flipped(piece, mask) for piece, mask in zip(given, masks)]

    def land(self):
        if self.scatters:
            total = self.kept.astype(f32)
            for piece in self.got:
                total = total + piece.astype(f32)
            self.value = total.astype(self.kept.dtype)
        else:
            pieces = [self.kept] + self.got
            order = [
                lax.select_n(self.place ^ i, *pieces)
                if len(pieces) > 2
                else jnp.where(self.place == i, *pieces)
                for i in range(len(pieces))
            ]
            self.value = jnp.concatenate(order, axis=0)
        if self.stages:
            self.prepare()
            return True
        return False


def sum_small(value, groups):
    for bits in groups:
        value = value + sum(flipped(value, mask) for mask in peers(bits))
    return value


def weight_grads(normed, normed_tail, d, d_tail, ready, side):
    width = d.shape[2]
    tile = 256
    each = width // tile
    extra = 0 if ready is None else ready.shape[1] // tile
    half = D // 2

    def kernel(side_ref, n_ref, nt_ref, d_ref, dt_ref, *refs):
        kept_ref, given_ref, turned, tail_turned = refs[-4:]
        step = pl.program_id(0)

        @pl.when(step == 0)
        def _():
            turned[...] = n_ref[...].T
            tail_turned[...] = nt_ref[...].T

        def rows(which, ref):
            return ref[pl.ds(pl.multiple_of(which * half, half), half), :]

        for which, out_ref in ((side_ref[0], kept_ref), (1 - side_ref[0], given_ref)):

            @pl.when(step < each)
            def _():
                out_ref[...] = dot(rows(which, turned), d_ref[0]).astype(bf16)

            @pl.when((step >= each) & (step < 3 * each))
            def _():
                out_ref[...] = (
                    dot(rows(which, turned), d_ref[0]) + dot(rows(which, tail_turned), dt_ref[0])
                ).astype(bf16)

            if extra:

                @pl.when(step >= 3 * each)
                def _():
                    out_ref[...] = rows(which, refs[0])

    column = lambda i: jnp.where(i < 3 * each, i % each, each - 1)
    in_specs = [
        pl.BlockSpec(memory_space=pltpu.SMEM),
        pl.BlockSpec((L, D), lambda i: (0, 0)),
        pl.BlockSpec((HALF, D), lambda i: (0, 0)),
        pl.BlockSpec((1, L, tile), lambda i: (jnp.minimum(i // each, 2), 0, column(i))),
        pl.BlockSpec((1, HALF, tile), lambda i: (jnp.clip(i // each - 1, 0, 1), 0, column(i))),
    ]
    operands = [side, normed, normed_tail, d, d_tail]
    if extra:
        in_specs.append(pl.BlockSpec((D, tile), lambda i: (0, jnp.maximum(i - 3 * each, 0))))
        operands.append(ready)
    steps = 3 * each + extra
    return pl.pallas_call(
        kernel,
        grid=(steps,),
        in_specs=in_specs,
        out_specs=[pl.BlockSpec((half, tile), lambda i: (0, i))] * 2,
        out_shape=[jax.ShapeDtypeStruct((half, steps * tile), bf16)] * 2,
        scratch_shapes=[pltpu.VMEM((D, L), bf16), pltpu.VMEM((D, HALF), bf16)],
        cost_estimate=HIDDEN,
        name="weight_grads",
    )(*operands)


def shards(
    inputs,
    doc_lengths,
    ln1_gain,
    ln1_bias,
    attn_in,
    qv_bias,
    attn_out,
    attn_out_bias,
    ln2_gain,
    second_norm_bias,
    mlp_in,
    mlp_in_bias,
    mlp_out,
    mlp_out_bias,
    cotangent,
):
    n_mlp = lax.axis_size("mlp")
    place = lax.axis_index("mlp")
    gain_one = ln1_gain.astype(f32)
    bias_one = ln1_bias.astype(f32)
    gain_two = ln2_gain.astype(f32)
    bias_two = second_norm_bias.astype(f32)

    own_tail = jnp.concatenate(
        [
            inputs[HALF:],
            jnp.broadcast_to(doc_lengths[:, NDOC - 1 :].astype(bf16), (16, D)),
        ],
        axis=0,
    )
    tail = rotated(own_tail, "mlp", 1)
    cotangents = [cotangent] + [rotated(cotangent, "mlp", by) for by in range(1, n_mlp)]

    activations = inputs.astype(f32)
    normed = layer_norm(activations, gain_one, bias_one).astype(bf16)
    zeros = jnp.zeros((D,), f32)
    qkv_bias = jnp.concatenate([qv_bias[0].astype(f32), zeros, qv_bias[1].astype(f32)])
    qkv = (dot(normed, attn_in) + qkv_bias).astype(bf16)
    rows = jnp.concatenate(
        [
            jnp.stack([attn_out_bias.astype(f32), gain_two, bias_two]),
            jnp.zeros((5, D), f32),
        ]
    )
    local, lse_local, mixture, middle, normed_two = local_attention(
        doc_lengths, qkv, attn_out, inputs, rows
    )
    steps = range(1, n_mlp)
    arrived_hi = [rotated(normed_two[HALF:], "mlp", by) for by in steps]

    tail_rows = tail[:HALF].astype(f32)
    normed_tail = layer_norm(tail_rows, gain_one, bias_one).astype(bf16)
    tail_kv = dot(normed_tail, attn_in[:, D:]).astype(bf16)
    reads = jnp.where(place == 0, 0, doc_lengths[:, :1])
    value_bias = jnp.broadcast_to(qv_bias[1].astype(f32), (8, D))
    tail_kv, *cotangents[1:] = fence((tail_kv, *cotangents[1:]))
    mixture, mem_k, mem_v, lse_mem, middle, normed_two, basis_t = memory_attention(
        reads,
        tail[HALF:],
        qkv,
        tail_kv,
        value_bias,
        local,
        attn_out,
        inputs,
        rows,
        mixture,
        middle,
        normed_two,
    )
    arrived_lo = [rotated(normed_two[:HALF], "mlp", by) for by in steps]
    mem_k, arrived_hi = fence((mem_k, arrived_hi))

    bias_rows = jnp.broadcast_to(mlp_in_bias.astype(f32), (8, mlp_in.shape[1]))
    kept = ()
    d_mlp_in_bias = 0.0
    returned_y, returned_dx = [], []
    calls = [(by, part) for by in steps for part in (1, 0)]
    for by, part in calls:
        block = (arrived_lo, arrived_hi)[part][by - 1]
        hidden, d_pre, d_bias, y, dx = mlp_block(
            block, cotangents[by], part, mlp_in, bias_rows, mlp_out, n_mlp * L, 2 * by + part, kept
        )
        kept = (hidden, d_pre)
        d_mlp_in_bias = d_mlp_in_bias + d_bias[0]
        returned_dx.append(rotated(dx, "mlp", -by))
        returned_y.append(y)
    hidden, d_pre, d_bias, y_own, dx_own = mlp_block(
        normed_two, cotangent, 0, mlp_in, bias_rows, mlp_out, n_mlp * L, 0, kept
    )
    d_mlp_in_bias = d_mlp_in_bias + d_bias[0]
    hidden, d_pre, returned_dx = fence((hidden, d_pre, returned_dx))
    over_rows = lambda a, b: lax.dot_general(
        a, b, (((0,), (0,)), ((), ())), preferred_element_type=f32
    )
    all_rows = jnp.concatenate(
        [normed_two] + [piece for pair in zip(arrived_lo, arrived_hi) for piece in pair], axis=0
    )
    d_mlp_in = over_rows(all_rows, d_pre).astype(bf16)
    d_mlp_out = over_rows(hidden, jnp.concatenate(cotangents, axis=0)).astype(bf16)

    hidden_count = mlp_in.shape[1]
    mlp_count = n_mlp.bit_length() - 1
    batch_count = lax.axis_size("batch").bit_length() - 1
    mlp_bits = list(range(mlp_count))
    core = [[mlp_count]]
    rest = list(range(mlp_count + 1, mlp_count + batch_count))
    groups = core + [mlp_bits[:1] + rest[:1]] + [[bit] for bit in mlp_bits[1:] + rest[1:]]

    d_mlp_in, d_mlp_out = lax.psum((d_mlp_in, d_mlp_out), "batch")

    def finish():
        halves = [dx_own[:HALF].astype(f32), dx_own[HALF:].astype(f32)]
        for (by, part), dx in zip(calls, returned_dx):
            halves[part] = halves[part] + dx.astype(f32)
        d_normed_two = jnp.concatenate(halves, axis=0)
        upstream = cotangent.astype(f32)
        d_out_bias = jnp.sum(upstream, axis=0)
        d_middle_norm, d_ln2_gain, d_ln2_bias = norm_backward(middle, gain_two, bias_two, d_normed_two)
        d_middle = upstream + d_middle_norm
        d_branch = d_middle.astype(bf16)
        d_attn_out_bias = jnp.sum(d_branch, axis=0, dtype=f32)

        backward = lambda first, pairs, d: attention_backward(
            first, pairs, doc_lengths, qkv, mem_k, mem_v, d, attn_out, lse_local, lse_mem, basis_t
        )
        early = PAIRS // 3
        side = place_in(core[0]).reshape(1)
        d_one, d_tail_one, sums_one = backward(0, early, d_branch)
        d_attn_out = over_rows(mixture, d_branch).astype(bf16)
        chain_one = Chain(
            *weight_grads(normed, normed_tail, d_one, d_tail_one, d_attn_out, side), groups
        )
        chain_one.fly()
        chain_one.land()
        d_branch, chain_one.given = fence((d_branch, chain_one.given))
        chain_one.fly()
        d_two, d_tail_two, sums_two = backward(early, PAIRS - early, d_branch)
        d_two, d_tail_two, chain_one.got = fence((d_two, d_tail_two, chain_one.got))
        chain_one.land()
        d_two, d_tail_two, chain_one.given = fence((d_two, d_tail_two, chain_one.given))
        chain_one.fly()
        chain_two = Chain(*weight_grads(normed, normed_tail, d_two, d_tail_two, None, side), groups)
        chain_two.fly()
        chain_two.land()
        d_qkv, d_tail, sums, later, chain_two.given = fence(
            (
                (d_one, d_two),
                (d_tail_one, d_tail_two),
                (sums_one, sums_two),
                (d_mlp_in_bias, returned_y, y_own),
                chain_two.given,
            )
        )
        bias_grad, y_given, y_mine = later
        chain_two.fly()

        token = chain_two.given
        flying = [chain_one, chain_two]
        events = 0
        while flying:
            for chain in list(flying):
                chain.got, token = fence((chain.got, token))
                events += 1
                if events == 2:
                    chain.got, y_given = fence((chain.got, y_given))
                    returned = [rotated(y, "mlp", -by) for (by, part), y in zip(calls, y_given)]
                if events == 6:
                    chain.got, returned = fence((chain.got, returned))
                if chain.land():
                    token = chain.given
                    chain.fly()
                else:
                    flying.remove(chain)

        d_qkv = jnp.concatenate(d_qkv, axis=2)
        d_tail = jnp.concatenate(d_tail, axis=2)
        sums = jnp.concatenate(sums, axis=1)
        columns = [attn_in[:, i * D : (i + 1) * D] for i in range(3)]
        d_tail_rows = dot_nt(d_tail[0], columns[1]) + dot_nt(d_tail[1], columns[2])
        from_next = rotated(d_tail_rows.astype(bf16), "mlp", -1)
        d_normed = (
            dot_nt(d_qkv[0], columns[0]) + dot_nt(d_qkv[1], columns[1]) + dot_nt(d_qkv[2], columns[2])
        )
        unused, d_ln1_gain, d_ln1_bias = norm_backward(activations, gain_one, bias_one, d_normed)
        unused, d_tail_gain, d_tail_bias = norm_backward(tail_rows, gain_one, bias_one, d_tail_rows)
        d_ln1_gain, d_ln1_bias = d_ln1_gain + d_tail_gain, d_ln1_bias + d_tail_bias

        placed_bias = lax.dynamic_update_slice(
            jnp.zeros((n_mlp * hidden_count,), f32), bias_grad, (place * hidden_count,)
        )
        vectors = jnp.concatenate(
            [
                jnp.stack(
                    [d_ln1_gain, d_ln1_bias, d_attn_out_bias, d_ln2_gain, d_ln2_bias, d_out_bias]
                ),
                sums[:2],
                placed_bias.reshape(-1, D),
            ],
            axis=0,
        )
        vectors = sum_small(vectors, groups)

        d_normed = jnp.concatenate(
            [d_normed[:HALF], d_normed[HALF:] + from_next.astype(f32)], axis=0
        )
        d_in_norm, unused, unused = norm_backward(activations, gain_one, bias_one, d_normed)
        input_grad = (d_middle + d_in_norm).astype(bf16)

        halves = [y_mine[:HALF].astype(f32), y_mine[HALF:].astype(f32)]
        for (by, part), y in zip(calls, returned):
            halves[part] = halves[part] + y.astype(f32)
        result = jnp.concatenate(halves, axis=0)
        layer_output = (middle + (result + mlp_out_bias)).astype(bf16)

        width = early * LANES
        rest = D - width
        d_attn_in = jnp.concatenate(
            [
                piece
                for i in range(3)
                for piece in (
                    chain_one.value[:, i * width : (i + 1) * width],
                    chain_two.value[:, i * rest : (i + 1) * rest],
                )
            ],
            axis=1,
        )
        return (
            layer_output,
            input_grad,
            vectors[0],
            vectors[1],
            d_attn_in.astype(f32),
            vectors[6:8],
            chain_one.value[:, 3 * width :].astype(f32),
            vectors[2],
            vectors[3],
            vectors[4],
            lax.dynamic_slice(vectors[8:].reshape(-1), (place * hidden_count,), (hidden_count,)),
            vectors[5],
        )

    shapes = jax.eval_shape(finish)
    done = lax.cond(
        doc_lengths[0, 0] > 0,
        finish,
        lambda: jax.tree.map(lambda leaf: jnp.zeros(leaf.shape, leaf.dtype), shapes),
    )
    return (*done[:10], d_mlp_in.astype(f32), done[10], d_mlp_out.astype(f32), done[11])


def solution(mesh):
    rows, whole = P(("batch", "mlp"), None), P()
    columns, hidden, depth = P(None, "mlp"), P("mlp"), P("mlp", None)
    return jax.shard_map(
        shards,
        mesh=mesh,
        in_specs=(rows, rows) + (whole,) * 8 + (columns, hidden, depth, whole, rows),
        out_specs=(rows, rows) + (whole,) * 8 + (columns, hidden, depth, whole),
        check_vma=False,
    )
```

profile of v0, /device:TPU:0, one launch (start us, length us, event | category | flops | bytes accessed | tf_op | source)
XLA Modules:
  0.0 305.3 jit_solution(19845604530699664)
XLA Ops:
  11.1 3.0 collective-permute-start.33
  15.4 5.7 %fusion.22.q_ref.k_ref.v_ref = bf16[512,2304]{1,0:T(8,128)(2,1)} fusion(bf16[512,768]{1,0:T(8,128)(2,1)S(1)} %add_convert_fusion.9, bf16[768,2304]{1,0:T(8,128)(2,1)} %param.21, f32[2304]{0:T(1024)S(1)} %pad_maximum_fusion.10), kind=kOutput, calls=%fused_computation.129 | convolution fusion | flops 1814298624 | bytes 6693888 | tf_op jit(solution)/shard_map/dot_general | solution.py:27
  21.7 13.0 %local_attention.1 = (f32[256,768]{1,0:T(8,128)}, f32[6,8,512]{2,1,0:T(8,128)}, bf16[512,768]{1,0:T(8,128)(2,1)}, f32[512,768]{1,0:T(8,128)S(1)}, bf16[512,768]{1,0:T(8,128)(2,1)}) custom-call(s32[1,3]{1,0:T(1,128)S(1)} %copy-done.73, bf16[512,2304]{1,0:T(8,128)(2,1)} %fusion.22.q_ref.k_ref.v_ref, bf16[512,2304]{1,0:T(8,128)(2,1)} %fusion.22.q_ref.k_ref.v_ref, ...), custom_call_target="tpu_custom_call" | custom-call | flops 2415919104 | bytes 3145728 | tf_op jit(solution)/shard_map/local_attention/pallas_call | solution.py:118
  34.7 1.8 slice.144
  36.5 2.0 collective-permute-start.36
  39.8 3.3 %convolution_convert_fusion.3.kt_ref.vt_ref = bf16[256,1536]{1,0:T(8,128)(2,1)} fusion(bf16[256,768]{1,0:T(8,128)(2,1)S(1)} %add_convert_fusion.10, bf16[768,2304]{1,0:T(8,128)(2,1)} %param.21), kind=kOutput, calls=%fused_computation.132 | convolution fusion | flops 604372992 | bytes 3538944 | tf_op jit(solution)/shard_map/dot_general | solution.py:27
  43.8 11.8 %memory_attention.1 = (bf16[512,768]{1,0:T(8,128)(2,1)}, bf16[512,768]{1,0:T(8,128)(2,1)}, bf16[512,768]{1,0:T(8,128)(2,1)}, f32[6,8,256]{2,1,0:T(8,128)}, f32[5...) custom-call(s32[1,1]{1,0:T(1,128)S(6)} %select_n.279.reads, ...), custom_call_target="tpu_custom_call", output_to_operand_aliasing={{0}: (10, {}), {4}: (11, {}), {5}: (12, {})} | custom-call | flops 3221225472 | bytes 6291456 | tf_op jit(solution)/shard_map/memory_attention/pallas_call | solution.py:232
  55.6 1.8 slice.143
  58.6 8.8 %mlp_block.3 = (bf16[1024,1536]{1,0:T(8,128)(2,1)}, bf16[1024,1536]{1,0:T(8,128)(2,1)}, f32[8,1536]{1,0:T(8,128)}, bf16[256,768]{1,0:T(8,128)(2,1)}, bf16[256,768]{1,0:T(8,128)(2,1)}) custom-call(bf16[256,768]{1,0:T(8,128)(2,1)} %collective-permute-done.36.x_ref, bf16[512,768]{1,0:T(8,128)(2,1)} %collective-permute-done.34.ct_ref, bf16[768,1536]{1,0:T(8,128)(2,1)} %wi_ref.5, ...), custom_call_target="tpu_custom_call" | custom-call | flops 2415919104 | bytes 7864320 | tf_op jit(solution)/shard_map/mlp_block/pallas_call | solution.py:340
  69.6 8.8 %mlp_block.4 = (bf16[1024,1536]{1,0:T(8,128)(2,1)}, bf16[1024,1536]{1,0:T(8,128)(2,1)}, f32[8,1536]{1,0:T(8,128)}, bf16[256,768]{1,0:T(8,128)(2,1)}, bf16[256,768]{1,0:T(8,128)(2,1)}) custom-call(bf16[256,768]{1,0:T(8,128)(2,1)} %copy-done.36, bf16[512,768]{1,0:T(8,128)(2,1)} %collective-permute-done.34.ct_ref, ...), custom_call_target="tpu_custom_call", output_to_operand_aliasing={{0}: (5, {}), {1}: (6, {})} | custom-call | flops 2415919104 | bytes 7864320 | tf_op jit(solution)/shard_map/mlp_block/pallas_call | solution.py:340
  79.1 12.3 %mlp_block.5 = (bf16[1024,1536]{1,0:T(8,128)(2,1)}, bf16[1024,1536]{1,0:T(8,128)(2,1)}, f32[8,1536]{1,0:T(8,128)}, bf16[512,768]{1,0:T(8,128)(2,1)}, bf16[512,768]{1,0:T(8,128)(2,1)}) custom-call(bf16[512,768]{1,0:T(8,128)(2,1)} %get-tuple-element.223.x_ref, bf16[512,768]{1,0:T(8,128)(2,1)S(1)} %copy-done.9, ...), custom_call_target="tpu_custom_call", output_to_operand_aliasing={{0}: (5, {}), {1}: (6, {})} | custom-call | flops 4831838208 | bytes 11010048 | tf_op jit(solution)/shard_map/mlp_block/pallas_call | solution.py:340
  92.2 6.4 %convolution_convert_fusion.1 = bf16[1536,768]{1,0:T(8,128)(2,1)} fusion(bf16[1024,1536]{1,0:T(8,128)(2,1)} %get-tuple-element.263, bf16[512,768]{1,0:T(8,128)(2,1)} %collective-permute-done.34.ct_ref, bf16[512,768]{1,0:T(8,128)(2,1)S(1)} %copy-done.9), kind=kOutput, calls=%fused_computation.130 | convolution fusion | flops 2420244480 | bytes 7077888 | tf_op jit(solution)/shard_map/dot_general | solution.py:747
  98.6 5.2 %convolution_convert_fusion.2 = bf16[768,1536]{1,0:T(8,128)(2,1)} fusion(bf16[1024,1536]{1,0:T(8,128)(2,1)S(1)} %copy-done.12, bf16[256,768]{1,0:T(8,128)(2,1)} %collective-permute-done.36.x_ref, bf16[256,768]{1,0:T(8,128)(2,1)S(1)} %copy-done.37, bf16[512,768]{1,0:T(8,128)(2,1)S(1)} %copy-done.26), kind=kOutput, calls=%fused_computation.131 | convolution fusion | flops 2421817344 | bytes 7077888 | tf_op jit(solution)/shard_map/dot_general | solution.py:747
  106.1 183.8 %conditional.1 = (bf16[512,768]{1,0:T(8,128)(2,1)S(1)}, bf16[512,768]{1,0:T(8,128)(2,1)S(1)}, f32[768]{0:T(1024)S(1)}, f32[768]{0:T(1024)S(1)}, f32[768,2304]{1,...) conditional(s32[]{:T(128)} %bitcast.7, () %tuple.39, ...), branch_computations={%region_4.5_spmd, %region_5.25_spmd} | conditional | flops 14372846592 | bytes 324266624 | solution.py:899
  109.9 1.7 fusion.37
  111.6 2.6 convert_reduce_fusion.1
  114.2 1.8 fusion.2.refs_0_
  116.1 10.2 %attention_backward.2 = (bf16[3,512,256]{2,1,0:T(8,128)(2,1)}, bf16[2,256,256]{2,1,0:T(8,128)(2,1)}, f32[8,256]{1,0:T(8,128)}) custom-call(s32[1,3]{1,0:T(1,128)S(1)} %copy-done.74, bf16[512,2304]{1,0:T(8,128)(2,1)} %get-tuple-element.68.q_ref.k_ref.v_ref, bf16[512,2304]{1,0:T(8,128)(2,1)} %get-tuple-element.68.q_ref.k_ref.v_ref, ...), custom_call_target="tpu_custom_call" | custom-call | flops 3758096384 | bytes 2621440 | tf_op jit(solution)/shard_map/cond/branch_1_fun/attention_backward/pallas_call | solution.py:469
  126.2 6.8 %weight_grads.2 = (bf16[384,1536]{1,0:T(8,128)(2,1)}, bf16[384,1536]{1,0:T(8,128)(2,1)}) custom-call(s32[1]{0:T(128)} %bitcast.side_ref, bf16[512,768]{1,0:T(8,128)(2,1)} %get-tuple-element.81.n_ref, bf16[256,768]{1,0:T(8,128)(2,1)S(1)} %get-tuple-element.82.nt_ref, bf16[3,512,256]{2,1,0:T(8,128)(2,1)} %get-tuple-element.133.d_ref, ...), custom_call_target="tpu_custom_call" | custom-call | flops 1000 | bytes 1000 | tf_op jit(solution)/shard_map/cond/branch_1_fun/weight_grads/pallas_call | solution.py:642
  133.1 1.9 reduce_sum.195
  139.0 1.9 add_convert_fusion.1
  146.4 16.8 %attention_backward.3 = (bf16[3,512,512]{2,1,0:T(8,128)(2,1)}, bf16[2,256,512]{2,1,0:T(8,128)(2,1)}, f32[8,512]{1,0:T(8,128)}) custom-call(s32[1,3]{1,0:T(1,128)S(1)} %copy-done.75, bf16[512,2304]{1,0:T(8,128)(2,1)} %get-tuple-element.68.q_ref.k_ref.v_ref, bf16[512,2304]{1,0:T(8,128)(2,1)} %get-tuple-element.68.q_ref.k_ref.v_ref, ...), custom_call_target="tpu_custom_call" | custom-call | flops 7516192768 | bytes 5242880 | tf_op jit(solution)/shard_map/cond/branch_1_fun/attention_backward/pallas_call | solution.py:469
  167.0 7.3 %weight_grads.3 = (bf16[384,1536]{1,0:T(8,128)(2,1)}, bf16[384,1536]{1,0:T(8,128)(2,1)}) custom-call(s32[1]{0:T(128)} %bitcast.side_ref, bf16[512,768]{1,0:T(8,128)(2,1)} %get-tuple-element.81.n_ref, bf16[256,768]{1,0:T(8,128)(2,1)S(1)} %get-tuple-element.82.nt_ref, bf16[3,512,512]{2,1,0:T(8,128)(2,1)} %get-tuple-element.134.d_ref, ...), custom_call_target="tpu_custom_call" | custom-call | flops 1000 | bytes 1000 | tf_op jit(solution)/shard_map/cond/branch_1_fun/weight_grads/pallas_call | solution.py:642
  177.4 1.6 collective-permute-start.8
  182.5 2.0 fusion.10
  184.5 2.0 fusion.4
  191.7 2.7 collective-permute-start.10
  196.5 1.8 fusion.8
  200.4 2.0 add_add_fusion.2
  202.4 10.2 %collective-permute-done.7 = bf16[96,1536]{1,0:T(8,128)(2,1)S(1)} collective-permute-done((bf16[96,1536]{1,0:T(8,128)(2,1)}, bf16[96,1536]{1,0:T(8,128)(2,1)S(1)}, u32[]{:S(2)}, u32[]{:S(2)}) %collective-permute-start.7) | collective-permute-done | bytes 294944 | tf_op jit(solution)/shard_map/cond/branch_1_fun/ppermute | solution.py:521
  219.7 2.5 collective-permute-start.12
  224.3 3.4 %collective-permute-start.19 = (f32[12,768]{1,0:T(8,128)S(1)}, f32[12,768]{1,0:T(8,128)S(1)}, u32[]{:S(2)}, u32[]{:S(2)}) collective-permute-start(f32[12,768]{1,0:T(8,128)S(1)} %add.250), channel_id=1, source_target_pairs={{0,5},{1,4},{2,7},{3,6},{4,1},{5,0},{6,3},{7,2},{8,13},{9,12},{10,... | collective-permute-start | bytes 110600 | tf_op jit(solution)/shard_map/cond/branch_1_fun/ppermute | solution.py:521
  229.8 7.4 %collective-permute-done.11 = bf16[24,1536]{1,0:T(8,128)(2,1)S(1)} collective-permute-done((bf16[24,1536]{1,0:T(8,128)(2,1)S(1)}, bf16[24,1536]{1,0:T(8,128)(2,1)S(1)}, u32[]{:S(2)}, u32[]{:S(2)}) %collective-permute-start.11) | collective-permute-done | bytes 73760 | tf_op jit(solution)/shard_map/cond/branch_1_fun/ppermute | solution.py:521
  237.4 5.7 %collective-permute-done.14 = bf16[256,768]{1,0:T(8,128)(2,1)S(1)} collective-permute-done((bf16[256,768]{1,0:T(8,128)(2,1)}, bf16[256,768]{1,0:T(8,128)(2,1)S(1)}, u32[]{:S(2)}, u32[]{:S(2)}) %collective-permute-start.14) | collective-permute-done | bytes 393248 | tf_op jit(solution)/shard_map/cond/branch_1_fun/ppermute | solution.py:512
  243.8 3.3 %collective-permute-start.25 = (bf16[96,1536]{1,0:T(8,128)(2,1)S(1)}, bf16[96,1536]{1,0:T(8,128)(2,1)S(1)}, u32[]{:S(2)}, u32[]{:S(2)}) collective-permute-start(bf16[96,1536]{1,0:T(8,128)(2,1)S(1)} %pad_maximum_fusion.5), channel_id=1, source_target_pairs={{0,5},{1,4},{2,7},{3,6},{4,1},{5,0},{6,3},{7,2},{8,13},{9,12},{10,... | collective-permute-start | bytes 884744 | tf_op jit(solution)/shard_map/cond/branch_1_fun/ppermute | solution.py:521
  247.1 2.0 collective-permute-done.26
  250.7 4.4 %collective-permute-done.25 = bf16[96,1536]{1,0:T(8,128)(2,1)S(1)} collective-permute-done((bf16[96,1536]{1,0:T(8,128)(2,1)S(1)}, bf16[96,1536]{1,0:T(8,128)(2,1)S(1)}, u32[]{:S(2)}, u32[]{:S(2)}) %collective-permute-start.25) | collective-permute-done | bytes 294944 | tf_op jit(solution)/shard_map/cond/branch_1_fun/ppermute | solution.py:521
  256.1 3.1 %collective-permute-done.24 = bf16[96,1536]{1,0:T(8,128)(2,1)S(1)} collective-permute-done((bf16[96,1536]{1,0:T(8,128)(2,1)S(1)}, bf16[96,1536]{1,0:T(8,128)(2,1)S(1)}, u32[]{:S(2)}, u32[]{:S(2)}) %collective-permute-start.24) | collective-permute-done | bytes 294944 | tf_op jit(solution)/shard_map/cond/branch_1_fun/ppermute | solution.py:521
  259.2 2.1 collective-permute-start.28
  265.2 2.2 collective-permute-start.31
  268.9 2.1 collective-permute-start.20
  271.0 2.3 collective-permute-done.20
  273.3 2.4 collective-permute-start.21
  275.7 2.7 collective-permute-done.21
  283.8 1.6 fusion.3
  286.2 3.5 %convert_element_type.185 = f32[768,2304]{1,0:T(8,128)} convert(bf16[768,2304]{1,0:T(8,128)(2,1)S(1)} %fusion.17) | non-fusion elementwise | flops 1769472 | bytes 10616832 | tf_op jit(solution)/shard_map/cond/branch_1_fun/convert_element_type | solution.py:888
  291.1 4.6 %convert_element_type.224 = f32[768,1536]{1,0:T(8,128)} convert(bf16[768,1536]{1,0:T(8,128)(2,1)} %get-tuple-element.284) | non-fusion elementwise | flops 1179648 | bytes 7077888 | tf_op jit(solution)/shard_map/convert_element_type | solution.py:904
  295.7 2.5 convert_element_type.226
  (337 shorter events, 74.7 us)
Async XLA Ops:
  7.2 7.0 %copy-start = (bf16[512,768]{1,0:T(8,128)(2,1)S(1)}, bf16[512,768]{1,0:T(8,128)(2,1)}, u32[]{:S(2)}) copy-start(bf16[512,768]{1,0:T(8,128)(2,1)} %x_ref.3) | copy-start | bytes 2359300
  7.2 7.0 %copy-start.9 = (bf16[512,768]{1,0:T(8,128)(2,1)S(1)}, bf16[512,768]{1,0:T(8,128)(2,1)}, u32[]{:S(2)}) copy-start(bf16[512,768]{1,0:T(8,128)(2,1)} %ct_ref.1) | copy-start | bytes 2359300
  7.2 282.8 %all-reduce.4.cloned.1.call-start = ((), (), s32[]{:S(2)}) async-start(), calls=%async_computation | async-start | bytes 9437184 | tf_op jit(solution)/shard_map/psum | solution.py:764
  11.1 27.4 %collective-permute-start.33 = (bf16[272,768]{1,0:T(8,128)(2,1)}, bf16[272,768]{1,0:T(8,128)(2,1)S(1)}, u32[]{:S(2)}, u32[]{:S(2)}) collective-permute-start(bf16[272,768]{1,0:T(8,128)(2,1)} %concatenate.63), channel_id=1, source_target_pairs={{0,1},{1,0},{2,3},{3,2},{4,5},{5,4},{6,7},{7,6},{8,9},{9,8},{10,11... | collective-permute-start | bytes 1253384 | tf_op jit(solution)/shard_map/ppermute | solution.py:512
  14.1 29.0 %collective-permute-start.34 = (bf16[512,768]{1,0:T(8,128)(2,1)S(1)}, bf16[512,768]{1,0:T(8,128)(2,1)}, u32[]{:S(2)}, u32[]{:S(2)}) collective-permute-start(bf16[512,768]{1,0:T(8,128)(2,1)S(1)} %copy-done.9), channel_id=1, source_target_pairs={{0,1},{1,0},{2,3},{3,2},{4,5},{5,4},{6,7},{7,6},{8,9},{9,8},{10,11... | collective-permute-start | bytes 2359304 | tf_op jit(solution)/shard_map/ppermute | solution.py:512
  36.5 21.5 %collective-permute-start.36 = (bf16[256,768]{1,0:T(8,128)(2,1)}, bf16[256,768]{1,0:T(8,128)(2,1)}, u32[]{:S(2)}, u32[]{:S(2)}) collective-permute-start(bf16[256,768]{1,0:T(8,128)(2,1)} %slice.144), channel_id=1, source_target_pairs={{0,1},{1,0},{2,3},{3,2},{4,5},{5,4},{6,7},{7,6},{8,9},{9,8},{10,11... | collective-permute-start | bytes 1179656 | tf_op jit(solution)/shard_map/ppermute | solution.py:512
  43.8 14.3 %copy-start.67 = (bf16[1536]{0:T(1024)(128)(2,1)S(1)}, bf16[1536]{0:T(1024)(128)(2,1)}, u32[]{:S(2)}) copy-start(bf16[1536]{0:T(1024)(128)(2,1)} %param.28) | copy-start | bytes 9220
  57.3 11.5 %collective-permute-start.35 = (bf16[256,768]{1,0:T(8,128)(2,1)}, bf16[256,768]{1,0:T(8,128)(2,1)S(1)}, u32[]{:S(2)}, u32[]{:S(2)}) collective-permute-start(bf16[256,768]{1,0:T(8,128)(2,1)} %slice.143), channel_id=1, source_target_pairs={{0,1},{1,0},{2,3},{3,2},{4,5},{5,4},{6,7},{7,6},{8,9},{9,8},{10,11... | collective-permute-start | bytes 1179656 | tf_op jit(solution)/shard_map/ppermute | solution.py:512
  67.5 24.0 %collective-permute-start.37 = (bf16[256,768]{1,0:T(8,128)(2,1)}, bf16[256,768]{1,0:T(8,128)(2,1)}, u32[]{:S(2)}, u32[]{:S(2)}) collective-permute-start(bf16[256,768]{1,0:T(8,128)(2,1)} %get-tuple-element.234), channel_id=1, source_target_pairs={{0,1},{1,0},{2,3},{3,2},{4,5},{5,4},{6,7},{7,6},{8,9},{9,8},{10,11... | collective-permute-start | bytes 1179656 | tf_op jit(solution)/shard_map/ppermute | solution.py:512
  78.4 13.1 %collective-permute-start.38 = (bf16[256,768]{1,0:T(8,128)(2,1)}, bf16[256,768]{1,0:T(8,128)(2,1)S(1)}, u32[]{:S(2)}, u32[]{:S(2)}) collective-permute-start(bf16[256,768]{1,0:T(8,128)(2,1)} %get-tuple-element.235), channel_id=1, source_target_pairs={{0,1},{1,0},{2,3},{3,2},{4,5},{5,4},{6,7},{7,6},{8,9},{9,8},{10,11... | collective-permute-start | bytes 1179656 | tf_op jit(solution)/shard_map/ppermute | solution.py:512
  133.0 6.0 %collective-permute-start = (bf16[384,1536]{1,0:T(8,128)(2,1)}, bf16[384,1536]{1,0:T(8,128)(2,1)}, u32[]{:S(2)}, u32[]{:S(2)}) collective-permute-start(bf16[384,1536]{1,0:T(8,128)(2,1)} %get-tuple-element.86), channel_id=1, source_target_pairs={{0,2},{1,3},{2,0},{3,1},{4,6},{5,7},{6,4},{7,5},{8,10},{9,11},{10,... | collective-permute-start | bytes 3538952 | tf_op jit(solution)/shard_map/cond/branch_1_fun/ppermute | solution.py:521
  142.9 20.3 %collective-permute-start.1 = (bf16[96,1536]{1,0:T(8,128)(2,1)}, bf16[96,1536]{1,0:T(8,128)(2,1)}, u32[]{:S(2)}, u32[]{:S(2)}) collective-permute-start(bf16[96,1536]{1,0:T(8,128)(2,1)} %get-tuple-element.90), channel_id=1, source_target_pairs={{0,1},{1,0},{2,3},{3,2},{4,5},{5,4},{6,7},{7,6},{8,9},{9,8},{10,11... | collective-permute-start | bytes 884744 | tf_op jit(solution)/shard_map/cond/branch_1_fun/ppermute | solution.py:521
  144.3 19.0 %collective-permute-start.2 = (bf16[96,1536]{1,0:T(8,128)(2,1)}, bf16[96,1536]{1,0:T(8,128)(2,1)}, u32[]{:S(2)}, u32[]{:S(2)}) collective-permute-start(bf16[96,1536]{1,0:T(8,128)(2,1)} %get-tuple-element.91), channel_id=1, source_target_pairs={{0,4},{1,5},{2,6},{3,7},{4,0},{5,1},{6,2},{7,3},{8,12},{9,13},{10,... | collective-permute-start | bytes 884744 | tf_op jit(solution)/shard_map/cond/branch_1_fun/ppermute | solution.py:521
  145.8 18.5 %collective-permute-start.3 = (bf16[96,1536]{1,0:T(8,128)(2,1)}, bf16[96,1536]{1,0:T(8,128)(2,1)}, u32[]{:S(2)}, u32[]{:S(2)}) collective-permute-start(bf16[96,1536]{1,0:T(8,128)(2,1)} %get-tuple-element.92), channel_id=1, source_target_pairs={{0,5},{1,4},{2,7},{3,6},{4,1},{5,0},{6,3},{7,2},{8,13},{9,12},{10,... | collective-permute-start | bytes 884744 | tf_op jit(solution)/shard_map/cond/branch_1_fun/ppermute | solution.py:521
  167.0 9.4 %copy-start.58 = (f32[512]{0:T(512)S(1)}, f32[512]{0:T(512)}, u32[]{:S(2)}) copy-start(f32[512]{0:T(512)} %reduce_sum.162) | copy-start | bytes 6148 | tf_op jit(solution)/shard_map/cond
  174.3 4.7 %collective-permute-start.4 = (bf16[384,1536]{1,0:T(8,128)(2,1)}, bf16[384,1536]{1,0:T(8,128)(2,1)S(1)}, u32[]{:S(2)}, u32[]{:S(2)}) collective-permute-start(bf16[384,1536]{1,0:T(8,128)(2,1)} %get-tuple-element.109), channel_id=1, source_target_pairs={{0,2},{1,3},{2,0},{3,1},{4,6},{5,7},{6,4},{7,5},{8,10},{9,11},{10,... | collective-permute-start | bytes 3538952 | tf_op jit(solution)/shard_map/cond/branch_1_fun/ppermute | solution.py:521
  177.4 13.2 %collective-permute-start.8 = (bf16[48,1536]{1,0:T(8,128)(2,1)}, bf16[48,1536]{1,0:T(8,128)(2,1)}, u32[]{:S(2)}, u32[]{:S(2)}) collective-permute-start(bf16[48,1536]{1,0:T(8,128)(2,1)} %constant_dynamic-slice_fusion.6), channel_id=1, source_target_pairs={{0,8},{1,9},{2,10},{3,11},{4,12},{5,13},{6,14},{7,15},{8,0},{9,1},... | collective-permute-start | bytes 442376 | tf_op jit(solution)/shard_map/cond/branch_1_fun/ppermute | solution.py:521
  187.0 15.5 %collective-permute-start.5 = (bf16[96,1536]{1,0:T(8,128)(2,1)}, bf16[96,1536]{1,0:T(8,128)(2,1)S(1)}, u32[]{:S(2)}, u32[]{:S(2)}) collective-permute-start(bf16[96,1536]{1,0:T(8,128)(2,1)} %get-tuple-element.111), channel_id=1, source_target_pairs={{0,1},{1,0},{2,3},{3,2},{4,5},{5,4},{6,7},{7,6},{8,9},{9,8},{10,11... | collective-permute-start | bytes 884744 | tf_op jit(solution)/shard_map/cond/branch_1_fun/ppermute | solution.py:521
  188.3 14.1 %collective-permute-start.6 = (bf16[96,1536]{1,0:T(8,128)(2,1)}, bf16[96,1536]{1,0:T(8,128)(2,1)S(1)}, u32[]{:S(2)}, u32[]{:S(2)}) collective-permute-start(bf16[96,1536]{1,0:T(8,128)(2,1)} %get-tuple-element.112), channel_id=1, source_target_pairs={{0,4},{1,5},{2,6},{3,7},{4,0},{5,1},{6,2},{7,3},{8,12},{9,13},{10,... | collective-permute-start | bytes 884744 | tf_op jit(solution)/shard_map/cond/branch_1_fun/ppermute | solution.py:521
  189.8 22.8 %collective-permute-start.7 = (bf16[96,1536]{1,0:T(8,128)(2,1)}, bf16[96,1536]{1,0:T(8,128)(2,1)S(1)}, u32[]{:S(2)}, u32[]{:S(2)}) collective-permute-start(bf16[96,1536]{1,0:T(8,128)(2,1)} %get-tuple-element.113), channel_id=1, source_target_pairs={{0,5},{1,4},{2,7},{3,6},{4,1},{5,0},{6,3},{7,2},{8,13},{9,12},{10,... | collective-permute-start | bytes 884744 | tf_op jit(solution)/shard_map/cond/branch_1_fun/ppermute | solution.py:521
  190.5 7.8 %copy-start.39 = (bf16[768,2304]{1,0:T(8,128)(2,1)S(1)}, bf16[768,2304]{1,0:T(8,128)(2,1)}, u32[]{:S(2)}) copy-start(bf16[768,2304]{1,0:T(8,128)(2,1)} %get-tuple-element.135) | copy-start | bytes 10616836 | tf_op jit(solution)/shard_map/cond
  191.7 22.8 %collective-permute-start.10 = (bf16[24,1536]{1,0:T(8,128)(2,1)S(1)}, bf16[24,1536]{1,0:T(8,128)(2,1)S(1)}, u32[]{:S(2)}, u32[]{:S(2)}) collective-permute-start(bf16[24,1536]{1,0:T(8,128)(2,1)S(1)} %constant_dynamic-slice_fusion.2), channel_id=1, source_target_pairs={{0,16},{1,17},{2,18},{3,19},{4,20},{5,21},{6,22},{7,23},{8,24},{9,... | collective-permute-start | bytes 221192 | tf_op jit(solution)/shard_map/cond/branch_1_fun/ppermute | solution.py:521
  198.9 15.5 %collective-permute-start.15 = (bf16[256,768]{1,0:T(8,128)(2,1)S(1)}, bf16[256,768]{1,0:T(8,128)(2,1)S(1)}, u32[]{:S(2)}, u32[]{:S(2)}) collective-permute-start(bf16[256,768]{1,0:T(8,128)(2,1)S(1)} %get-tuple-element.314), channel_id=1, source_target_pairs={{0,1},{1,0},{2,3},{3,2},{4,5},{5,4},{6,7},{7,6},{8,9},{9,8},{10,11... | collective-permute-start | bytes 1179656 | tf_op jit(solution)/shard_map/cond/branch_1_fun/ppermute | solution.py:512
  214.5 13.2 %collective-permute-start.9 = (bf16[48,1536]{1,0:T(8,128)(2,1)}, bf16[48,1536]{1,0:T(8,128)(2,1)}, u32[]{:S(2)}, u32[]{:S(2)}) collective-permute-start(bf16[48,1536]{1,0:T(8,128)(2,1)} %constant_dynamic-slice_fusion.1), channel_id=1, source_target_pairs={{0,8},{1,9},{2,10},{3,11},{4,12},{5,13},{6,14},{7,15},{8,0},{9,1},... | collective-permute-start | bytes 442376 | tf_op jit(solution)/shard_map/cond/branch_1_fun/ppermute | solution.py:521
  219.6 4.7 %collective-permute-start.16 = (f32[12,768]{1,0:T(8,128)S(1)}, f32[12,768]{1,0:T(8,128)S(1)}, u32[]{:S(2)}, u32[]{:S(2)}) collective-permute-start(f32[12,768]{1,0:T(8,128)S(1)} %concatenate.49), channel_id=1, source_target_pairs={{0,2},{1,3},{2,0},{3,1},{4,6},{5,7},{6,4},{7,5},{8,10},{9,11},{10,... | collective-permute-start | bytes 110600 | tf_op jit(solution)/shard_map/cond/branch_1_fun/ppermute | solution.py:521
  219.7 9.0 %collective-permute-start.12 = (bf16[24,1536]{1,0:T(8,128)(2,1)S(1)}, bf16[24,1536]{1,0:T(8,128)(2,1)S(1)}, u32[]{:S(2)}, u32[]{:S(2)}) collective-permute-start(bf16[24,1536]{1,0:T(8,128)(2,1)S(1)} %add_convert_fusion.8), channel_id=1, source_target_pairs={{0,16},{1,17},{2,18},{3,19},{4,20},{5,21},{6,22},{7,23},{8,24},{9,... | collective-permute-start | bytes 221192 | tf_op jit(solution)/shard_map/cond/branch_1_fun/ppermute | solution.py:521
  222.3 15.2 %collective-permute-start.13 = (bf16[256,768]{1,0:T(8,128)(2,1)}, bf16[256,768]{1,0:T(8,128)(2,1)S(1)}, u32[]{:S(2)}, u32[]{:S(2)}) collective-permute-start(bf16[256,768]{1,0:T(8,128)(2,1)} %get-tuple-element.128), channel_id=1, source_target_pairs={{0,1},{1,0},{2,3},{3,2},{4,5},{5,4},{6,7},{7,6},{8,9},{9,8},{10,11... | collective-permute-start | bytes 1179656 | tf_op jit(solution)/shard_map/cond/branch_1_fun/ppermute | solution.py:512
  223.7 19.4 %collective-permute-start.14 = (bf16[256,768]{1,0:T(8,128)(2,1)}, bf16[256,768]{1,0:T(8,128)(2,1)S(1)}, u32[]{:S(2)}, u32[]{:S(2)}) collective-permute-start(bf16[256,768]{1,0:T(8,128)(2,1)} %get-tuple-element.129), channel_id=1, source_target_pairs={{0,1},{1,0},{2,3},{3,2},{4,5},{5,4},{6,7},{7,6},{8,9},{9,8},{10,11... | collective-permute-start | bytes 1179656 | tf_op jit(solution)/shard_map/cond/branch_1_fun/ppermute | solution.py:512
  224.3 43.4 %collective-permute-start.19 = (f32[12,768]{1,0:T(8,128)S(1)}, f32[12,768]{1,0:T(8,128)S(1)}, u32[]{:S(2)}, u32[]{:S(2)}) collective-permute-start(f32[12,768]{1,0:T(8,128)S(1)} %add.250), channel_id=1, source_target_pairs={{0,5},{1,4},{2,7},{3,6},{4,1},{5,0},{6,3},{7,2},{8,13},{9,12},{10,... | collective-permute-start | bytes 110600 | tf_op jit(solution)/shard_map/cond/branch_1_fun/ppermute | solution.py:521
  227.7 41.2 %collective-permute-start.18 = (f32[12,768]{1,0:T(8,128)S(1)}, f32[12,768]{1,0:T(8,128)S(1)}, u32[]{:S(2)}, u32[]{:S(2)}) collective-permute-start(f32[12,768]{1,0:T(8,128)S(1)} %add.250), channel_id=1, source_target_pairs={{0,4},{1,5},{2,6},{3,7},{4,0},{5,1},{6,2},{7,3},{8,12},{9,13},{10,... | collective-permute-start | bytes 110600 | tf_op jit(solution)/shard_map/cond/branch_1_fun/ppermute | solution.py:521
  228.7 8.5 %collective-permute-start.11 = (bf16[24,1536]{1,0:T(8,128)(2,1)S(1)}, bf16[24,1536]{1,0:T(8,128)(2,1)S(1)}, u32[]{:S(2)}, u32[]{:S(2)}) collective-permute-start(bf16[24,1536]{1,0:T(8,128)(2,1)S(1)} %constant_dynamic-slice_fusion), channel_id=1, source_target_pairs={{0,16},{1,17},{2,18},{3,19},{4,20},{5,21},{6,22},{7,23},{8,24},{9,... | collective-permute-start | bytes 221192 | tf_op jit(solution)/shard_map/cond/branch_1_fun/ppermute | solution.py:521
  237.2 6.5 %collective-permute-start.22 = (bf16[48,1536]{1,0:T(8,128)(2,1)S(1)}, bf16[48,1536]{1,0:T(8,128)(2,1)S(1)}, u32[]{:S(2)}, u32[]{:S(2)}) collective-permute-start(bf16[48,1536]{1,0:T(8,128)(2,1)S(1)} %pad_maximum_fusion.7), channel_id=1, source_target_pairs={{0,8},{1,9},{2,10},{3,11},{4,12},{5,13},{6,14},{7,15},{8,0},{9,1},... | collective-permute-start | bytes 442376 | tf_op jit(solution)/shard_map/cond/branch_1_fun/ppermute | solution.py:521
  237.4 23.8 %copy-start.42 = (bf16[256,768]{1,0:T(8,128)(2,1)}, bf16[256,768]{1,0:T(8,128)(2,1)S(1)}, u32[]{:S(2)}) copy-start(bf16[256,768]{1,0:T(8,128)(2,1)S(1)} %collective-permute-done.13) | copy-start | bytes 1179652 | tf_op jit(solution)/shard_map/cond
  243.2 18.1 %copy-start.44 = (bf16[256,768]{1,0:T(8,128)(2,1)}, bf16[256,768]{1,0:T(8,128)(2,1)S(1)}, u32[]{:S(2)}) copy-start(bf16[256,768]{1,0:T(8,128)(2,1)S(1)} %collective-permute-done.14) | copy-start | bytes 1179652 | tf_op jit(solution)/shard_map/cond
  243.2 5.9 %collective-permute-start.26 = (bf16[24,1536]{1,0:T(8,128)(2,1)S(1)}, bf16[24,1536]{1,0:T(8,128)(2,1)S(1)}, u32[]{:S(2)}, u32[]{:S(2)}) collective-permute-start(bf16[24,1536]{1,0:T(8,128)(2,1)S(1)} %add_convert_fusion.7), channel_id=1, source_target_pairs={{0,16},{1,17},{2,18},{3,19},{4,20},{5,21},{6,22},{7,23},{8,24},{9,... | collective-permute-start | bytes 221192 | tf_op jit(solution)/shard_map/cond/branch_1_fun/ppermute | solution.py:521
  243.8 11.2 %collective-permute-start.25 = (bf16[96,1536]{1,0:T(8,128)(2,1)S(1)}, bf16[96,1536]{1,0:T(8,128)(2,1)S(1)}, u32[]{:S(2)}, u32[]{:S(2)}) collective-permute-start(bf16[96,1536]{1,0:T(8,128)(2,1)S(1)} %pad_maximum_fusion.5), channel_id=1, source_target_pairs={{0,5},{1,4},{2,7},{3,6},{4,1},{5,0},{6,3},{7,2},{8,13},{9,12},{10,... | collective-permute-start | bytes 884744 | tf_op jit(solution)/shard_map/cond/branch_1_fun/ppermute | solution.py:521
  247.1 12.0 %collective-permute-start.24 = (bf16[96,1536]{1,0:T(8,128)(2,1)S(1)}, bf16[96,1536]{1,0:T(8,128)(2,1)S(1)}, u32[]{:S(2)}, u32[]{:S(2)}) collective-permute-start(bf16[96,1536]{1,0:T(8,128)(2,1)S(1)} %pad_maximum_fusion.5), channel_id=1, source_target_pairs={{0,4},{1,5},{2,6},{3,7},{4,0},{5,1},{6,2},{7,3},{8,12},{9,13},{10,... | collective-permute-start | bytes 884744 | tf_op jit(solution)/shard_map/cond/branch_1_fun/ppermute | solution.py:521
  249.1 12.1 %collective-permute-start.23 = (bf16[96,1536]{1,0:T(8,128)(2,1)S(1)}, bf16[96,1536]{1,0:T(8,128)(2,1)S(1)}, u32[]{:S(2)}, u32[]{:S(2)}) collective-permute-start(bf16[96,1536]{1,0:T(8,128)(2,1)S(1)} %pad_maximum_fusion.5), channel_id=1, source_target_pairs={{0,1},{1,0},{2,3},{3,2},{4,5},{5,4},{6,7},{7,6},{8,9},{9,8},{10,11... | collective-permute-start | bytes 884744 | tf_op jit(solution)/shard_map/cond/branch_1_fun/ppermute | solution.py:521
  255.0 13.8 %collective-permute-start.17 = (f32[12,768]{1,0:T(8,128)S(1)}, f32[12,768]{1,0:T(8,128)S(1)}, u32[]{:S(2)}, u32[]{:S(2)}) collective-permute-start(f32[12,768]{1,0:T(8,128)S(1)} %add.250), channel_id=1, source_target_pairs={{0,1},{1,0},{2,3},{3,2},{4,5},{5,4},{6,7},{7,6},{8,9},{9,8},{10,11... | collective-permute-start | bytes 110600 | tf_op jit(solution)/shard_map/cond/branch_1_fun/ppermute | solution.py:521
  259.2 5.2 %collective-permute-start.28 = (bf16[48,1536]{1,0:T(8,128)(2,1)S(1)}, bf16[48,1536]{1,0:T(8,128)(2,1)S(1)}, u32[]{:S(2)}, u32[]{:S(2)}) collective-permute-start(bf16[48,1536]{1,0:T(8,128)(2,1)S(1)} %pad_maximum_fusion.8), channel_id=1, source_target_pairs={{0,8},{1,9},{2,10},{3,11},{4,12},{5,13},{6,14},{7,15},{8,0},{9,1},... | collective-permute-start | bytes 442376 | tf_op jit(solution)/shard_map/cond/branch_1_fun/ppermute | solution.py:521
  261.8 13.9 %copy-start.70 = (bf16[768]{0:T(1024)(128)(2,1)S(1)}, bf16[768]{0:T(1024)(128)(2,1)}, u32[]{:S(2)}) copy-start(bf16[768]{0:T(1024)(128)(2,1)} %get-tuple-element.266) | copy-start | bytes 4612 | tf_op jit(solution)/shard_map/cond
  265.2 15.1 %collective-permute-start.31 = (bf16[96,1536]{1,0:T(8,128)(2,1)}, bf16[96,1536]{1,0:T(8,128)(2,1)S(1)}, u32[]{:S(2)}, u32[]{:S(2)}) collective-permute-start(bf16[96,1536]{1,0:T(8,128)(2,1)} %pad_maximum_fusion.6), channel_id=1, source_target_pairs={{0,5},{1,4},{2,7},{3,6},{4,1},{5,0},{6,3},{7,2},{8,13},{9,12},{10,... | collective-permute-start | bytes 884744 | tf_op jit(solution)/shard_map/cond/branch_1_fun/ppermute | solution.py:521
  267.4 12.9 %collective-permute-start.30 = (bf16[96,1536]{1,0:T(8,128)(2,1)}, bf16[96,1536]{1,0:T(8,128)(2,1)S(1)}, u32[]{:S(2)}, u32[]{:S(2)}) collective-permute-start(bf16[96,1536]{1,0:T(8,128)(2,1)} %pad_maximum_fusion.6), channel_id=1, source_target_pairs={{0,4},{1,5},{2,6},{3,7},{4,0},{5,1},{6,2},{7,3},{8,12},{9,13},{10,... | collective-permute-start | bytes 884744 | tf_op jit(solution)/shard_map/cond/branch_1_fun/ppermute | solution.py:521
  267.7 12.6 %collective-permute-start.29 = (bf16[96,1536]{1,0:T(8,128)(2,1)}, bf16[96,1536]{1,0:T(8,128)(2,1)S(1)}, u32[]{:S(2)}, u32[]{:S(2)}) collective-permute-start(bf16[96,1536]{1,0:T(8,128)(2,1)} %pad_maximum_fusion.6), channel_id=1, source_target_pairs={{0,1},{1,0},{2,3},{3,2},{4,5},{5,4},{6,7},{7,6},{8,9},{9,8},{10,11... | collective-permute-start | bytes 884744 | tf_op jit(solution)/shard_map/cond/branch_1_fun/ppermute | solution.py:521
  268.9 4.4 %collective-permute-start.20 = (f32[12,768]{1,0:T(8,128)S(1)}, f32[12,768]{1,0:T(8,128)S(1)}, u32[]{:S(2)}, u32[]{:S(2)}) collective-permute-start(f32[12,768]{1,0:T(8,128)S(1)} %add_add_fusion.3), channel_id=1, source_target_pairs={{0,8},{1,9},{2,10},{3,11},{4,12},{5,13},{6,14},{7,15},{8,0},{9,1},... | collective-permute-start | bytes 110600 | tf_op jit(solution)/shard_map/cond/branch_1_fun/ppermute | solution.py:521
  273.3 5.0 %collective-permute-start.21 = (f32[12,768]{1,0:T(8,128)S(1)}, f32[12,768]{1,0:T(8,128)S(1)}, u32[]{:S(2)}, u32[]{:S(2)}) collective-permute-start(f32[12,768]{1,0:T(8,128)S(1)} %add.254), channel_id=1, source_target_pairs={{0,16},{1,17},{2,18},{3,19},{4,20},{5,21},{6,22},{7,23},{8,24},{9,... | collective-permute-start | bytes 110600 | tf_op jit(solution)/shard_map/cond/branch_1_fun/ppermute | solution.py:521
  280.3 3.1 %collective-permute-start.27 = (bf16[384,1536]{1,0:T(8,128)(2,1)}, bf16[384,1536]{1,0:T(8,128)(2,1)S(1)}, u32[]{:S(2)}, u32[]{:S(2)}) collective-permute-start(bf16[384,1536]{1,0:T(8,128)(2,1)} %pad_maximum_fusion.2), channel_id=1, source_target_pairs={{0,2},{1,3},{2,0},{3,1},{4,6},{5,7},{6,4},{7,5},{8,10},{9,11},{10,... | collective-permute-start | bytes 3538952 | tf_op jit(solution)/shard_map/cond/branch_1_fun/ppermute | solution.py:521
  280.9 4.5 %collective-permute-start.32 = (bf16[384,1536]{1,0:T(8,128)(2,1)S(1)}, bf16[384,1536]{1,0:T(8,128)(2,1)S(1)}, u32[]{:S(2)}, u32[]{:S(2)}) collective-permute-start(bf16[384,1536]{1,0:T(8,128)(2,1)S(1)} %pad_maximum_fusion.3), channel_id=1, source_target_pairs={{0,2},{1,3},{2,0},{3,1},{4,6},{5,7},{6,4},{7,5},{8,10},{9,11},{10,... | collective-permute-start | bytes 3538952 | tf_op jit(solution)/shard_map/cond/branch_1_fun/ppermute | solution.py:521
  (70 other events, 195.0 us)
Sparse Core Ops, SparseCore 0:
  103.9 131.7 all-reduce.3
where the time goes:
time: 310 us; the launch traced here: 305 us
  Pallas kernels  95.8 us (31%)
  starting transfers between devices  47 us (15%)
  other arithmetic  46.2 us (15%)
  waiting for transfers between devices  40.5 us (13%)
  matrix products  30.7 us (10%)
  local copies, waits for them, and re-layouts  29.3 us (9%)
  between operations  14.7 us (5%)
    ppermute x30, starting transfers between devices, flipped(): return lax.ppermute(value, GRID, [(i, i ^ mask) for i in range(count)])  35.6 us
    ppermute x30, waiting for transfers between devices, flipped(): return lax.ppermute(value, GRID, [(i, i ^ mask) for i in range(count)])  34.7 us
    pallas_call x3, Pallas kernels, mlp_block(): pl.pallas_call(mlp_kernel, grid=(hidden // tile,), in_specs=[fixed, pl.Bl...  29.9 us
    pallas_call x2, Pallas kernels, attention_backward(): pl.pallas_call(backward_kernel, grid=(pairs,), in_specs=[pl.BlockSpec(mem...  27 us
    pallas_call x2, Pallas kernels, weight_grads(): pl.pallas_call(kernel, grid=(steps,), in_specs=in_specs, out_specs=[pl.Bl...  14 us
    dot_general x3, matrix products, shards(): lax.dot_general(a, b, (((0,), (0,)), ((), ())), preferred_element_type=f32)  13.4 us
    pallas_call x1, Pallas kernels, local_attention(): pl.pallas_call(local_kernel, grid=(PAIRS,), in_specs=[pl.BlockSpec(memory...  13 us
    pallas_call x1, Pallas kernels, memory_attention(): pl.pallas_call(memory_kernel, grid=(PAIRS,), in_specs=[pl.BlockSpec(memor...  11.8 us
  transfers between devices with their start and end apart: 40, of which 11 were waited for; matrix products, arithmetic and copies ran while one was open for 24% of the time, Pallas kernels for 31%

commit v1 on v0

--- a/solution.py
+++ b/solution.py
@@ -36,11 +36,6 @@
     centered = matrix - center
     spread = jnp.mean(centered * centered, axis=-1, keepdims=True)
     return centered * lax.rsqrt(spread + 1e-05) * gain_row + shift_row
-
-
-def norm_backward(matrix, gain_row, shift_row, upstream):
-    unused, pullback = jax.vjp(layer_norm, matrix, gain_row, shift_row)
-    return pullback(upstream)
 
 
 def head_lanes(matrix, head):
@@ -70,6 +65,7 @@
     mix_ref,
     middle_ref,
     normed_ref,
+    sent_ref,
     mask,
     turned,
     acc,
@@ -103,13 +99,15 @@
 
     @pl.when(step == PAIRS - 1)
     def _():
-        finish_middle(x_ref, acc, rows_ref, middle_ref, normed_ref)
-
-
-def finish_middle(x_ref, acc, rows_ref, middle_ref, normed_ref):
+        finish_middle(x_ref, acc, rows_ref, middle_ref, normed_ref, sent_ref)
+
+
+def finish_middle(x_ref, acc, rows_ref, middle_ref, normed_ref, sent_ref):
     middle = x_ref[...].astype(f32) + (acc[...] + rows_ref[0:1])
     middle_ref[...] = middle
-    normed_ref[...] = layer_norm(middle, rows_ref[1:2], rows_ref[2:3]).astype(bf16)
+    normed = layer_norm(middle, rows_ref[1:2], rows_ref[2:3]).astype(bf16)
+    normed_ref[...] = normed
+    sent_ref[...] = normed
 
 
 def local_attention(lens, qkv, attn_out, inputs, rows):
@@ -133,6 +131,7 @@
             pl.BlockSpec((HALF, LANES), lambda i: (1, i)),
             upper,
             upper,
+            pl.BlockSpec((HALF, D), lambda i: (0, 0)),
         ],
         out_shape=[
             jax.ShapeDtypeStruct((HALF, D), f32),
@@ -140,6 +139,7 @@
             jax.ShapeDtypeStruct((L, D), bf16),
             jax.ShapeDtypeStruct((L, D), f32),
             jax.ShapeDtypeStruct((L, D), bf16),
+            jax.ShapeDtypeStruct((HALF, D), bf16),
         ],
         scratch_shapes=[
             pltpu.VMEM((L, L), f32),
@@ -185,6 +185,7 @@
     middle_ref,
     normed_ref,
     basis_t_ref,
+    sent_ref,
     basis,
     turned,
     acc,
@@ -221,7 +222,7 @@
 
     @pl.when(step == PAIRS - 1)
     def _():
-        finish_middle(x_ref, acc, rows_ref, middle_ref, normed_ref)
+        finish_middle(x_ref, acc, rows_ref, middle_ref, normed_ref, sent_ref)
 
 
 def memory_attention(
@@ -255,6 +256,7 @@
             whole((HALF, D)),
             whole((HALF, D)),
             whole((HALF, NB)),
+            whole((HALF, D)),
         ],
         out_shape=[
             jax.ShapeDtypeStruct((L, D), bf16),
@@ -264,6 +266,7 @@
             jax.ShapeDtypeStruct((L, D), f32),
             jax.ShapeDtypeStruct((L, D), bf16),
             jax.ShapeDtypeStruct((HALF, NB), bf16),
+            jax.ShapeDtypeStruct((HALF, D), bf16),
         ],
         scratch_shapes=[
             pltpu.VMEM((NB, HALF), bf16),
@@ -507,6 +510,182 @@
     )(lens, qkv, qkv, qkv, mem_k, mem_v, d_branch, attn_out, lse_local, lse_mem, basis_t)
 
 
+def normalized(matrix):
+    centered = matrix - jnp.mean(matrix, axis=-1, keepdims=True)
+    scale = lax.rsqrt(jnp.mean(centered * centered, axis=-1, keepdims=True) + 1e-05)
+    return centered * scale, scale
+
+
+def norm_slope(unit, scale, grown):
+    inner = jnp.mean(grown * unit, axis=-1, keepdims=True)
+    return (grown - jnp.mean(grown, axis=-1, keepdims=True) - unit * inner) * scale
+
+
+def column_sum(matrix):
+    return jnp.sum(matrix, axis=0, keepdims=True)
+
+
+def middle_backward(d_own, returned, cotangent, middle, rows):
+    count = len(returned[0])
+
+    def kernel(d_ref, ct_ref, middle_ref, rows_ref, *refs):
+        shares = refs[: 2 * count]
+        d_middle_ref, d_branch_ref, sums_ref = refs[2 * count :]
+        part = pl.program_id(0)
+        total = d_ref[...].astype(f32)
+        for i in range(count):
+            total = total + jnp.where(part == 0, shares[i][...], shares[count + i][...]).astype(f32)
+        upstream = ct_ref[...].astype(f32)
+        unit, scale = normalized(middle_ref[...])
+        d_middle = upstream + norm_slope(unit, scale, total * rows_ref[1:2])
+        d_branch = d_middle.astype(bf16)
+        d_middle_ref[...] = d_middle
+        d_branch_ref[...] = d_branch
+        sums = jnp.concatenate(
+            [
+                column_sum(d_branch.astype(f32)),
+                column_sum(total * unit),
+                column_sum(total),
+                column_sum(upstream),
+                jnp.zeros((4, D), f32),
+            ],
+            axis=0,
+        )
+
+        @pl.when(part == 0)
+        def _():
+            sums_ref[...] = sums
+
+        @pl.when(part > 0)
+        def _():
+            sums_ref[...] += sums
+
+    half = pl.BlockSpec((HALF, D), lambda i: (i, 0))
+    fixed = pl.BlockSpec((HALF, D), lambda i: (0, 0))
+    eight = pl.BlockSpec((8, D), lambda i: (0, 0))
+    return pl.pallas_call(
+        kernel,
+        grid=(2,),
+        in_specs=[half, half, half, eight] + [fixed] * (2 * count),
+        out_specs=[half, half, eight],
+        out_shape=[
+            jax.ShapeDtypeStruct((L, D), f32),
+            jax.ShapeDtypeStruct((L, D), bf16),
+            jax.ShapeDtypeStruct((8, D), f32),
+        ],
+        cost_estimate=pl.CostEstimate(
+            flops=20 * L * D, bytes_accessed=14 * L * D, transcendentals=0
+        ),
+        name="middle_backward",
+    )(d_own, cotangent, middle, rows, *returned[0], *returned[1])
+
+
+def qkv_backward(d_one, d_two, d_tail_one, d_tail_two, attn_in, inputs, tail_rows):
+    cut = d_one.shape[2]
+
+    def kernel(
+        one_ref, two_ref, t_one_ref, t_two_ref, w_ref, x_ref, xt_ref, dn_ref, dt_ref, sums_ref, tail
+    ):
+        step = pl.program_id(0)
+        left, right = w_ref[:, :cut], w_ref[:, cut:]
+        part = dot_nt(one_ref[0], left) + dot_nt(two_ref[0], right)
+
+        @pl.when(step == 0)
+        def _():
+            dn_ref[...] = part
+            tail[...] = jnp.zeros_like(tail)
+
+        @pl.when(step > 0)
+        def _():
+            dn_ref[...] += part
+            tail[...] += dot_nt(t_one_ref[0], left) + dot_nt(t_two_ref[0], right)
+
+        @pl.when(step == 2)
+        def _():
+            dt_ref[...] = tail[...].astype(bf16)
+            unit, unused = normalized(x_ref[...].astype(f32))
+            tail_unit, unused = normalized(xt_ref[...].astype(f32))
+            sums_ref[0:1] = column_sum(dn_ref[...] * unit) + column_sum(tail[...] * tail_unit)
+            sums_ref[1:2] = column_sum(dn_ref[...]) + column_sum(tail[...])
+
+    fixed = lambda count: pl.BlockSpec((count, D), lambda i: (0, 0))
+    return pl.pallas_call(
+        kernel,
+        grid=(3,),
+        in_specs=[
+            pl.BlockSpec((1, L, cut), lambda i: (i, 0, 0)),
+            pl.BlockSpec((1, L, D - cut), lambda i: (i, 0, 0)),
+            pl.BlockSpec((1, HALF, cut), lambda i: (jnp.maximum(i - 1, 0), 0, 0)),
+            pl.BlockSpec((1, HALF, D - cut), lambda i: (jnp.maximum(i - 1, 0), 0, 0)),
+            pl.BlockSpec((D, D), lambda i: (0, i)),
+            fixed(L),
+            fixed(HALF),
+        ],
+        out_specs=[fixed(L), fixed(HALF), fixed(8)],
+        out_shape=[
+            jax.ShapeDtypeStruct((L, D), f32),
+            jax.ShapeDtypeStruct((HALF, D), bf16),
+            jax.ShapeDtypeStruct((8, D), f32),
+        ],
+        scratch_shapes=[pltpu.VMEM((HALF, D), f32)],
+        cost_estimate=pl.CostEstimate(
+            flops=8 * L * D * D, bytes_accessed=20 * L * D, transcendentals=0
+        ),
+        name="qkv_backward",
+    )(d_one, d_two, d_tail_one, d_tail_two, attn_in, inputs, tail_rows)
+
+
+def input_backward(d_normed, from_next, inputs, d_middle, gain):
+    def kernel(dn_ref, next_ref, x_ref, dm_ref, gain_ref, out_ref):
+        unit, scale = normalized(x_ref[...].astype(f32))
+        shared = jnp.where(pl.program_id(0) == 0, 0.0, next_ref[...].astype(f32))
+        grown = (dn_ref[...] + shared) * gain_ref[0:1]
+        out_ref[...] = (dm_ref[...] + norm_slope(unit, scale, grown)).astype(bf16)
+
+    half = pl.BlockSpec((HALF, D), lambda i: (i, 0))
+    return pl.pallas_call(
+        kernel,
+        grid=(2,),
+        in_specs=[
+            half,
+            pl.BlockSpec((HALF, D), lambda i: (0, 0)),
+            half,
+            half,
+            pl.BlockSpec((8, D), lambda i: (0, 0)),
+        ],
+        out_specs=half,
+        out_shape=jax.ShapeDtypeStruct((L, D), bf16),
+        cost_estimate=pl.CostEstimate(
+            flops=20 * L * D, bytes_accessed=12 * L * D, transcendentals=0
+        ),
+        name="input_backward",
+    )(d_normed, from_next, inputs, d_middle, gain)
+
+
+def widened(first, second):
+    steps = 6
+
+    def kernel(a_ref, b_ref, a_out, b_out):
+        a_out[...] = a_ref[...].astype(f32)
+        b_out[...] = b_ref[...].astype(f32)
+
+    specs = [
+        pl.BlockSpec((matrix.shape[0] // steps, matrix.shape[1]), lambda i: (i, 0))
+        for matrix in (first, second)
+    ]
+    return pl.pallas_call(
+        kernel,
+        grid=(steps,),
+        in_specs=specs,
+        out_specs=specs,
+        out_shape=[jax.ShapeDtypeStruct(matrix.shape, f32) for matrix in (first, second)],
+        cost_estimate=pl.CostEstimate(
+            flops=0, bytes_accessed=6 * (first.size + second.size), transcendentals=0
+        ),
+        name="widened",
+    )(first, second)
+
+
 def rotated(value, axis, by):
     count = lax.axis_size(axis)
     return lax.ppermute(value, axis, [(i, (i + by) % count) for i in range(count)])
@@ -583,10 +762,17 @@
         return False
 
 
-def sum_small(value, groups):
-    for bits in groups:
-        value = value + sum(flipped(value, mask) for mask in peers(bits))
-    return value
+class Total:
+    def __init__(self, value, bits):
+        self.value, self.bits = value, list(bits)
+
+    def fly(self):
+        self.got = flipped(self.value, 1 << self.bits.pop(0))
+
+    def land(self):
+        self.value = self.value + self.got
+        self.given = [self.value]
+        return bool(self.bits)
 
 
 def weight_grads(normed, normed_tail, d, d_tail, ready, side):
@@ -696,11 +882,11 @@
             jnp.zeros((5, D), f32),
         ]
     )
-    local, lse_local, mixture, middle, normed_two = local_attention(
+    local, lse_local, mixture, middle, normed_two, sent = local_attention(
         doc_lengths, qkv, attn_out, inputs, rows
     )
     steps = range(1, n_mlp)
-    arrived_hi = [rotated(normed_two[HALF:], "mlp", by) for by in steps]
+    arrived_hi = [rotated(sent, "mlp", by) for by in steps]
 
     tail_rows = tail[:HALF].astype(f32)
     normed_tail = layer_norm(tail_rows, gain_one, bias_one).astype(bf16)
@@ -708,7 +894,7 @@
     reads = jnp.where(place == 0, 0, doc_lengths[:, :1])
     value_bias = jnp.broadcast_to(qv_bias[1].astype(f32), (8, D))
     tail_kv, *cotangents[1:] = fence((tail_kv, *cotangents[1:]))
-    mixture, mem_k, mem_v, lse_mem, middle, normed_two, basis_t = memory_attention(
+    mixture, mem_k, mem_v, lse_mem, middle, normed_two, basis_t, sent = memory_attention(
         reads,
         tail[HALF:],
         qkv,
@@ -722,7 +908,7 @@
         middle,
         normed_two,
     )
-    arrived_lo = [rotated(normed_two[:HALF], "mlp", by) for by in steps]
+    arrived_lo = [rotated(sent, "mlp", by) for by in steps]
     mem_k, arrived_hi = fence((mem_k, arrived_hi))
 
     bias_rows = jnp.broadcast_to(mlp_in_bias.astype(f32), (8, mlp_in.shape[1]))
@@ -764,17 +950,8 @@
     d_mlp_in, d_mlp_out = lax.psum((d_mlp_in, d_mlp_out), "batch")
 
     def finish():
-        halves = [dx_own[:HALF].astype(f32), dx_own[HALF:].astype(f32)]
-        for (by, part), dx in zip(calls, returned_dx):
-            halves[part] = halves[part] + dx.astype(f32)
-        d_normed_two = jnp.concatenate(halves, axis=0)
-        upstream = cotangent.astype(f32)
-        d_out_bias = jnp.sum(upstream, axis=0)
-        d_middle_norm, d_ln2_gain, d_ln2_bias = norm_backward(middle, gain_two, bias_two, d_normed_two)
-        d_middle = upstream + d_middle_norm
-        d_branch = d_middle.astype(bf16)
-        d_attn_out_bias = jnp.sum(d_branch, axis=0, dtype=f32)
-
+        shares = [[dx for (by, part), dx in zip(calls, returned_dx) if part == half] for half in (0, 1)]
+        d_middle, d_branch, middle_sums = middle_backward(dx_own, shares, cotangent, middle, rows)
         backward = lambda first, pairs, d: attention_backward(
             first, pairs, doc_lengths, qkv, mem_k, mem_v, d, attn_out, lse_local, lse_mem, basis_t
         )
@@ -797,9 +974,10 @@
         chain_two = Chain(*weight_grads(normed, normed_tail, d_two, d_tail_two, None, side), groups)
         chain_two.fly()
         chain_two.land()
-        d_qkv, d_tail, sums, later, chain_two.given = fence(
+        d_one, d_two, d_tails, sums, later, chain_two.given = fence(
             (
-                (d_one, d_two),
+                d_one,
+                d_two,
                 (d_tail_one, d_tail_two),
                 (sums_one, sums_two),
                 (d_mlp_in_bias, returned_y, y_own),
@@ -808,58 +986,55 @@
         )
         bias_grad, y_given, y_mine = later
         chain_two.fly()
-
-        token = chain_two.given
-        flying = [chain_one, chain_two]
-        events = 0
+        d_normed, d_tail_rows, input_sums = qkv_backward(
+            d_one, d_two, *d_tails, attn_in, inputs, tail[:HALF]
+        )
+        chain_one.got, d_normed, d_tail_rows, input_sums = fence(
+            (chain_one.got, d_normed, d_tail_rows, input_sums)
+        )
+        chain_one.land()
+        chain_one.fly()
+        from_next = rotated(d_tail_rows, "mlp", -1)
+        placed_bias = lax.dynamic_update_slice(
+            jnp.zeros((n_mlp * hidden_count,), f32), bias_grad, (place * hidden_count,)
+        )
+        vectors = Total(
+            jnp.concatenate(
+                [
+                    input_sums[:2],
+                    middle_sums[:4],
+                    jnp.concatenate(sums, axis=1)[:2],
+                    placed_bias.reshape(-1, D),
+                ],
+                axis=0,
+            ),
+            core[0] + mlp_bits + rest,
+        )
+        vectors.fly()
+
+        token = chain_one.given
+        flying = [chain_one, chain_two, vectors]
+        turns = 0
         while flying:
             for chain in list(flying):
                 chain.got, token = fence((chain.got, token))
-                events += 1
-                if events == 2:
-                    chain.got, y_given = fence((chain.got, y_given))
-                    returned = [rotated(y, "mlp", -by) for (by, part), y in zip(calls, y_given)]
-                if events == 6:
-                    chain.got, returned = fence((chain.got, returned))
+                if chain is chain_two:
+                    turns += 1
+                    if turns == 1:
+                        chain.got, y_given = fence((chain.got, y_given))
+                        returned = [
+                            rotated(y, "mlp", -by) for (by, part), y in zip(calls, y_given)
+                        ]
+                    if turns == 3:
+                        chain.got, returned = fence((chain.got, returned))
                 if chain.land():
                     token = chain.given
                     chain.fly()
                 else:
                     flying.remove(chain)
 
-        d_qkv = jnp.concatenate(d_qkv, axis=2)
-        d_tail = jnp.concatenate(d_tail, axis=2)
-        sums = jnp.concatenate(sums, axis=1)
-        columns = [attn_in[:, i * D : (i + 1) * D] for i in range(3)]
-        d_tail_rows = dot_nt(d_tail[0], columns[1]) + dot_nt(d_tail[1], columns[2])
-        from_next = rotated(d_tail_rows.astype(bf16), "mlp", -1)
-        d_normed = (
-            dot_nt(d_qkv[0], columns[0]) + dot_nt(d_qkv[1], columns[1]) + dot_nt(d_qkv[2], columns[2])
-        )
-        unused, d_ln1_gain, d_ln1_bias = norm_backward(activations, gain_one, bias_one, d_normed)
-        unused, d_tail_gain, d_tail_bias = norm_backward(tail_rows, gain_one, bias_one, d_tail_rows)
-        d_ln1_gain, d_ln1_bias = d_ln1_gain + d_tail_gain, d_ln1_bias + d_tail_bias
-
-        placed_bias = lax.dynamic_update_slice(
-            jnp.zeros((n_mlp * hidden_count,), f32), bias_grad, (place * hidden_count,)
-        )
-        vectors = jnp.concatenate(
-            [
-                jnp.stack(
-                    [d_ln1_gain, d_ln1_bias, d_attn_out_bias, d_ln2_gain, d_ln2_bias, d_out_bias]
-                ),
-                sums[:2],
-                placed_bias.reshape(-1, D),
-            ],
-            axis=0,
-        )
-        vectors = sum_small(vectors, groups)
-
-        d_normed = jnp.concatenate(
-            [d_normed[:HALF], d_normed[HALF:] + from_next.astype(f32)], axis=0
-        )
-        d_in_norm, unused, unused = norm_backward(activations, gain_one, bias_one, d_normed)
-        input_grad = (d_middle + d_in_norm).astype(bf16)
+        gain = jnp.broadcast_to(gain_one, (8, D))
+        input_grad = input_backward(d_normed, from_next, inputs, d_middle, gain)
 
         halves = [y_mine[:HALF].astype(f32), y_mine[HALF:].astype(f32)]
         for (by, part), y in zip(calls, returned):
@@ -868,32 +1043,34 @@
         layer_output = (middle + (result + mlp_out_bias)).astype(bf16)
 
         width = early * LANES
-        rest = D - width
+        late = D - width
         d_attn_in = jnp.concatenate(
             [
                 piece
                 for i in range(3)
                 for piece in (
                     chain_one.value[:, i * width : (i + 1) * width],
-                    chain_two.value[:, i * rest : (i + 1) * rest],
+                    chain_two.value[:, i * late : (i + 1) * late],
                 )
             ],
             axis=1,
         )
+        summed = vectors.value
         return (
             layer_output,
             input_grad,
-            vectors[0],
-            vectors[1],
+            summed[0],
+            summed[1],
             d_attn_in.astype(f32),
-            vectors[6:8],
+            summed[6:8],
             chain_one.value[:, 3 * width :].astype(f32),
-            vectors[2],
-            vectors[3],
-            vectors[4],
-            lax.dynamic_slice(vectors[8:].reshape(-1), (place * hidden_count,), (hidden_count,)),
-            vectors[5],
+            summed[2],
+            summed[3],
+            summed[4],
+            lax.dynamic_slice(summed[8:].reshape(-1), (place * hidden_count,), (hidden_count,)),
+            summed[5],
         )
+
 
     shapes = jax.eval_shape(finish)
     done = lax.cond(
@@ -901,7 +1078,8 @@
         finish,
         lambda: jax.tree.map(lambda leaf: jnp.zeros(leaf.shape, leaf.dtype), shapes),
     )
-    return (*done[:10], d_mlp_in.astype(f32), done[10], d_mlp_out.astype(f32), done[11])
+    d_mlp_in, d_mlp_out = widened(d_mlp_in, d_mlp_out)
+    return (*done[:10], d_mlp_in, done[10], d_mlp_out, done[11])
 
 
 def solution(mesh):

time: 310 us -> 292 us (0.942)
  Pallas kernels: 95.8 us -> 119 us
  other arithmetic: 46.2 us -> 31.7 us
  local copies, waits for them, and re-layouts: 29.3 us -> 15.8 us
  matrix products: 30.7 us -> 20.3 us
  waiting for transfers between devices: 40.5 us -> 35.3 us
    pallas_call x0 -> x4, Pallas kernels: none -> 23.3 us  [the longest x1 8.18 us: qkv_backward(): pl.pallas_call(kernel, grid=(3,), in_specs=[pl.BlockSpec((1, L, cut), lam...]
    convert_element_type x5 -> x0, other arithmetic: 9.44 us -> none  [the longest x1 4.65 us: shards(): d_mlp_in.astype(f32)]
    reduce_sum x8 -> x0, other arithmetic: 9.27 us -> none  [the longest x4 3.06 us: layer_norm(): return centered * lax.rsqrt(spread + 1e-05) * gain_row + shift_row]
    dot_general x5 -> x0, matrix products: 8.28 us -> none  [dot_nt(): lax.dot_general(a, b, (((1,), (1,)), ((), ())), preferred_element_type=f32)]
    ppermute x30 -> x29, waiting for transfers between devices: 34.7 us -> 27.4 us  [flipped(): return lax.ppermute(value, GRID, [(i, i ^ mask) for i in range(count)])]
    cond x110 -> x66, local copies, waits for them, and re-layouts: 7.5 us -> 2.29 us
    dot_general x2, matrix products: 9.01 us -> 5.33 us  [dot(): return jnp.dot(a, b, preferred_element_type=f32)]
    ppermute x30 -> x29, starting transfers between devices: 35.6 us -> 36 us  [flipped(): return lax.ppermute(value, GRID, [(i, i ^ mask) for i in range(count)])]
  transfers between devices with their start and end apart: 40 -> 39, of which waited for: 11 -> 11; matrix products, arithmetic and copies ran while one was open for 24% -> 17% of each run, Pallas kernels for 31% -> 39%
where the time goes in v1:
time: 292 us; the launch traced here: 287 us
  Pallas kernels  119 us (41%)
  starting transfers between devices  48.8 us (17%)
  waiting for transfers between devices  35.3 us (12%)
  other arithmetic  31.7 us (11%)
  matrix products  20.3 us (7%)
  local copies, waits for them, and re-layouts  15.8 us (5%)
  between operations  15 us (5%)
    ppermute x29, starting transfers between devices, flipped(): return lax.ppermute(value, GRID, [(i, i ^ mask) for i in range(count)])  36 us
    pallas_call x3, Pallas kernels, mlp_block(): pl.pallas_call(mlp_kernel, grid=(hidden // tile,), in_specs=[fixed, pl.Bl...  30.1 us
    ppermute x29, waiting for transfers between devices, flipped(): return lax.ppermute(value, GRID, [(i, i ^ mask) for i in range(count)])  27.4 us
    pallas_call x2, Pallas kernels, attention_backward(): pl.pallas_call(backward_kernel, grid=(pairs,), in_specs=[pl.BlockSpec(mem...  26.3 us
    dot_general x3, matrix products, shards(): lax.dot_general(a, b, (((0,), (0,)), ((), ())), preferred_element_type=f32)  15 us
    pallas_call x2, Pallas kernels, weight_grads(): pl.pallas_call(kernel, grid=(steps,), in_specs=in_specs, out_specs=[pl.Bl...  13.8 us
    pallas_call x1, Pallas kernels, local_attention(): pl.pallas_call(local_kernel, grid=(PAIRS,), in_specs=[pl.BlockSpec(memory...  13.3 us
    ppermute x9, starting transfers between devices, rotated(): lax.ppermute(value, axis, [(i, (i + by) % count) for i in range(count)])  12.8 us
  transfers between devices with their start and end apart: 39, of which 11 were waited for; matrix products, arithmetic and copies ran while one was open for 17% of the time, Pallas kernels for 39%

profile of v1, /device:TPU:0, one launch (start us, length us, event | category | flops | bytes accessed | tf_op | source)
XLA Modules:
  0.0 286.8 jit_solution(14410219035124492409)
XLA Ops:
  9.7 1.6 concatenate.51
  11.3 3.0 %collective-permute-start.32 = (bf16[272,768]{1,0:T(8,128)(2,1)}, bf16[272,768]{1,0:T(8,128)(2,1)}, u32[]{:S(2)}, u32[]{:S(2)}) collective-permute-start(bf16[272,768]{1,0:T(8,128)(2,1)} %concatenate.51), channel_id=1, source_target_pairs={{0,1},{1,0},{2,3},{3,2},{4,5},{5,4},{6,7},{7,6},{8,9},{9,8},{10,11... | collective-permute-start | bytes 1253384 | tf_op jit(solution)/shard_map/ppermute | solution.py:691
  15.5 2.0 fusion.12.q_ref.k_ref.v_ref
  17.6 13.3 %local_attention.1 = (f32[256,768]{1,0:T(8,128)}, f32[6,8,512]{2,1,0:T(8,128)}, bf16[512,768]{1,0:T(8,128)(2,1)}, f32[512,768]{1,0:T(8,128)}, bf16[512,768]{1,0:T(8,128)(2,1)}, /*index=5*/bf16[256,768]{1,0:T(8,128)(2,1)}) custom-call(s32[1,3]{1,0:T(1,128)S(1)} %copy-done.47, bf16[512,2304]{1,0:T(8,128)(2,1)S(1)} %fusion.12.q_ref.k_ref.v_ref, ...), custom_call_target="tpu_custom_call" | custom-call | flops 2415919104 | bytes 3145728 | tf_op jit(solution)/shard_map/local_attention/pallas_call | solution.py:116
  30.9 2.1 collective-permute-start.35
  38.0 3.3 %convolution_convert_fusion.3.kt_ref.vt_ref = bf16[256,1536]{1,0:T(8,128)(2,1)} fusion(bf16[256,768]{1,0:T(8,128)(2,1)S(1)} %fusion.33, bf16[768,2304]{1,0:T(8,128)(2,1)} %param.21), kind=kOutput, calls=%fused_computation.83 | convolution fusion | flops 604372992 | bytes 3538944 | tf_op jit(solution)/shard_map/dot_general | solution.py:27
  42.5 12.0 %memory_attention.1 = (bf16[512,768]{1,0:T(8,128)(2,1)}, bf16[512,768]{1,0:T(8,128)(2,1)}, bf16[512,768]{1,0:T(8,128)(2,1)}, f32[6,8,256]{2,1,0:T(8,128)}, f32[5...) custom-call(s32[1,1]{1,0:T(1,128)S(6)} %select_n.279.reads, ...), custom_call_target="tpu_custom_call", output_to_operand_aliasing={{0}: (10, {}), {4}: (11, {}), {5}: (12, {})} | custom-call | flops 3221225472 | bytes 6291456 | tf_op jit(solution)/shard_map/memory_attention/pallas_call | solution.py:233
  54.5 2.1 collective-permute-start.34
  57.3 8.8 %mlp_block.3 = (bf16[1024,1536]{1,0:T(8,128)(2,1)}, bf16[1024,1536]{1,0:T(8,128)(2,1)}, f32[8,1536]{1,0:T(8,128)}, bf16[256,768]{1,0:T(8,128)(2,1)}, bf16[256,768]{1,0:T(8,128)(2,1)}) custom-call(bf16[256,768]{1,0:T(8,128)(2,1)} %collective-permute-done.35.x_ref, bf16[512,768]{1,0:T(8,128)(2,1)} %collective-permute-done.33.ct_ref, bf16[768,1536]{1,0:T(8,128)(2,1)} %wi_ref.5, ...), custom_call_target="tpu_custom_call" | custom-call | flops 2415919104 | bytes 7864320 | tf_op jit(solution)/shard_map/mlp_block/pallas_call | solution.py:343
  66.1 8.8 %mlp_block.4 = (bf16[1024,1536]{1,0:T(8,128)(2,1)}, bf16[1024,1536]{1,0:T(8,128)(2,1)}, f32[8,1536]{1,0:T(8,128)}, bf16[256,768]{1,0:T(8,128)(2,1)}, bf16[256,768]{1,0:T(8,128)(2,1)}) custom-call(bf16[256,768]{1,0:T(8,128)(2,1)} %collective-permute-done.34.x_ref, ...), custom_call_target="tpu_custom_call", output_to_operand_aliasing={{0}: (5, {}), {1}: (6, {})} | custom-call | flops 2415919104 | bytes 7864320 | tf_op jit(solution)/shard_map/mlp_block/pallas_call | solution.py:343
  74.9 2.1 collective-permute-start.37
  76.9 12.6 %mlp_block.5 = (bf16[1024,1536]{1,0:T(8,128)(2,1)}, bf16[1024,1536]{1,0:T(8,128)(2,1)}, f32[8,1536]{1,0:T(8,128)}, bf16[512,768]{1,0:T(8,128)(2,1)}, bf16[512,768]{1,0:T(8,128)(2,1)}) custom-call(bf16[512,768]{1,0:T(8,128)(2,1)} %get-tuple-element.240.x_ref, bf16[512,768]{1,0:T(8,128)(2,1)} %ct_ref.1, ...), custom_call_target="tpu_custom_call", output_to_operand_aliasing={{0}: (5, {}), {1}: (6, {})} | custom-call | flops 4831838208 | bytes 11010048 | tf_op jit(solution)/shard_map/mlp_block/pallas_call | solution.py:343
  89.6 6.5 %convolution_convert_fusion.1 = bf16[1536,768]{1,0:T(8,128)(2,1)} fusion(bf16[1024,1536]{1,0:T(8,128)(2,1)} %get-tuple-element.281, bf16[512,768]{1,0:T(8,128)(2,1)} %collective-permute-done.33.ct_ref, bf16[512,768]{1,0:T(8,128)(2,1)} %ct_ref.1), kind=kOutput, calls=%fused_computation.81 | convolution fusion | flops 2420244480 | bytes 7077888 | tf_op jit(solution)/shard_map/dot_general | solution.py:933
  96.1 5.1 %convolution_convert_fusion.2 = bf16[768,1536]{1,0:T(8,128)(2,1)} fusion(bf16[1024,1536]{1,0:T(8,128)(2,1)S(1)} %copy-done.5, bf16[256,768]{1,0:T(8,128)(2,1)} %collective-permute-done.35.x_ref, bf16[256,768]{1,0:T(8,128)(2,1)} %collective-permute-done.34.x_ref, bf16[512,768]{1,0:T(8,128)(2,1)S(1)} %copy-done.49), kind=kOutput, calls=%fused_computation.82 | convolution fusion | flops 2421817344 | bytes 7077888 | tf_op jit(solution)/shard_map/dot_general | solution.py:933
  101.2 170.8 %conditional.1 = (bf16[512,768]{1,0:T(8,128)(2,1)S(1)}, bf16[512,768]{1,0:T(8,128)(2,1)S(1)}, f32[768]{0:T(1024)S(1)}, f32[768]{0:T(1024)S(1)}, f32[768,2304]{1,...) conditional(s32[]{:T(128)} %bitcast.2, () %tuple.44, ...), branch_computations={%region_4.5_spmd, %region_5.6_spmd} | conditional | flops 14362497024 | bytes 199732928 | solution.py:1076
  101.2 4.6 %middle_backward.1 = (f32[512,768]{1,0:T(8,128)}, bf16[512,768]{1,0:T(8,128)(2,1)}, f32[8,768]{1,0:T(8,128)}) custom-call(bf16[512,768]{1,0:T(8,128)(2,1)} %get-tuple-element.71.d_ref, bf16[512,768]{1,0:T(8,128)(2,1)} %get-tuple-element.72.ct_ref, f32[512,768]{1,0:T(8,128)} %get-tuple-element.66.middle_ref, f32[8,768]{1,0:T(8,128)} %get-tuple-element.73.rows_ref, ...), custom_call_target="tpu_custom_call" | custom-call | flops 7864320 | bytes 5505024 | tf_op jit(solution)/shard_map/cond/branch_1_fun/middle_backward/pallas_call | solution.py:566
  105.8 3.4 %fusion.2.refs_0_ = bf16[768,768]{1,0:T(8,128)(2,1)} fusion(bf16[512,768]{1,0:T(8,128)(2,1)} %get-tuple-element.88.db_ref, bf16[512,768]{1,0:T(8,128)(2,1)} %get-tuple-element.85), kind=kOutput, calls=%fused_computation.10 | convolution fusion | flops 604569600 | bytes 2752512 | tf_op jit(solution)/shard_map/cond/branch_1_fun/dot_general | solution.py:933
  109.2 9.5 %attention_backward.2 = (bf16[3,512,256]{2,1,0:T(8,128)(2,1)}, bf16[2,256,256]{2,1,0:T(8,128)(2,1)}, f32[8,256]{1,0:T(8,128)}) custom-call(s32[1,3]{1,0:T(1,128)S(1)} %get-tuple-element.67.lens, bf16[512,2304]{1,0:T(8,128)(2,1)S(1)} %get-tuple-element.68.q_ref.k_ref.v_ref, bf16[512,2304]{1,0:T(8,128)(2,1)S(1)} %get-tuple-element.68.q_ref.k_ref.v_ref, ...), custom_call_target="tpu_custom_call" | custom-call | flops 3758096384 | bytes 2621440 | tf_op jit(solution)/shard_map/cond/branch_1_fun/attention_backward/pallas_call | solution.py:472
  118.7 6.8 %weight_grads.2 = (bf16[384,1536]{1,0:T(8,128)(2,1)}, bf16[384,1536]{1,0:T(8,128)(2,1)}) custom-call(s32[1]{0:T(128)} %bitcast.side_ref, bf16[512,768]{1,0:T(8,128)(2,1)} %get-tuple-element.82.n_ref, bf16[256,768]{1,0:T(8,128)(2,1)S(1)} %get-tuple-element.83.nt_ref, bf16[3,512,256]{2,1,0:T(8,128)(2,1)} %get-tuple-element.116.d_ref.one_ref, ...), custom_call_target="tpu_custom_call" | custom-call | flops 1000 | bytes 1000 | tf_op jit(solution)/shard_map/cond/branch_1_fun/weight_grads/pallas_call | solution.py:828
  125.5 3.3 %collective-permute-done = bf16[384,1536]{1,0:T(8,128)(2,1)} collective-permute-done((bf16[384,1536]{1,0:T(8,128)(2,1)}, bf16[384,1536]{1,0:T(8,128)(2,1)}, u32[]{:S(2)}, u32[]{:S(2)}) %collective-permute-start) | collective-permute-done | bytes 1179680 | tf_op jit(solution)/shard_map/cond/branch_1_fun/ppermute | solution.py:700
  128.8 1.9 add_convert_fusion.1
  132.7 1.8 collective-permute-start.2
  134.5 1.7 collective-permute-start.3
  136.2 16.8 %attention_backward.3 = (bf16[3,512,512]{2,1,0:T(8,128)(2,1)}, bf16[2,256,512]{2,1,0:T(8,128)(2,1)}, f32[8,512]{1,0:T(8,128)}) custom-call(s32[1,3]{1,0:T(1,128)S(1)} %get-tuple-element.67.lens, bf16[512,2304]{1,0:T(8,128)(2,1)S(1)} %get-tuple-element.68.q_ref.k_ref.v_ref, bf16[512,2304]{1,0:T(8,128)(2,1)S(1)} %get-tuple-element.68.q_ref.k_ref.v_ref, ...), custom_call_target="tpu_custom_call" | custom-call | flops 7516192768 | bytes 5242880 | tf_op jit(solution)/shard_map/cond/branch_1_fun/attention_backward/pallas_call | solution.py:472
  155.2 7.0 %weight_grads.3 = (bf16[384,1536]{1,0:T(8,128)(2,1)}, bf16[384,1536]{1,0:T(8,128)(2,1)}) custom-call(s32[1]{0:T(128)} %bitcast.side_ref, bf16[512,768]{1,0:T(8,128)(2,1)S(1)} %copy-done.2, bf16[256,768]{1,0:T(8,128)(2,1)S(1)} %get-tuple-element.83.nt_ref, bf16[3,512,512]{2,1,0:T(8,128)(2,1)} %get-tuple-element.117.d_ref.two_ref, ...), custom_call_target="tpu_custom_call" | custom-call | flops 1000 | bytes 1000 | tf_op jit(solution)/shard_map/cond/branch_1_fun/weight_grads/pallas_call | solution.py:828
  162.3 1.8 slice.74.xt_ref
  166.3 1.6 add_convert_fusion
  170.5 1.6 collective-permute-start.7
  172.1 8.2 %qkv_backward.1 = (f32[512,768]{1,0:T(8,128)}, bf16[256,768]{1,0:T(8,128)(2,1)}, f32[8,768]{1,0:T(8,128)}) custom-call(bf16[3,512,256]{2,1,0:T(8,128)(2,1)} %get-tuple-element.116.d_ref.one_ref, bf16[3,512,512]{2,1,0:T(8,128)(2,1)} %get-tuple-element.117.d_ref.two_ref, bf16[2,256,256]{2,1,0:T(8,128)(2,1)} %get-tuple-element.118.dt_ref.t_one_ref, ...), custom_call_target="tpu_custom_call" | custom-call | flops 2415919104 | bytes 7864320 | tf_op jit(solution)/shard_map/cond/branch_1_fun/qkv_backward/pallas_call | solution.py:612
  181.1 2.8 collective-permute-start.9
  184.0 4.0 %collective-permute-done.9 = bf16[24,1536]{1,0:T(8,128)(2,1)S(1)} collective-permute-done((bf16[24,1536]{1,0:T(8,128)(2,1)S(1)}, bf16[24,1536]{1,0:T(8,128)(2,1)S(1)}, u32[]{:S(2)}, u32[]{:S(2)}) %collective-permute-start.9) | collective-permute-done | bytes 73760 | tf_op jit(solution)/shard_map/cond/branch_1_fun/ppermute | solution.py:700
  196.2 4.1 %collective-permute-done.10 = bf16[48,1536]{1,0:T(8,128)(2,1)S(1)} collective-permute-done((bf16[48,1536]{1,0:T(8,128)(2,1)S(1)}, bf16[48,1536]{1,0:T(8,128)(2,1)S(1)}, u32[]{:S(2)}, u32[]{:S(2)}) %collective-permute-start.10) | collective-permute-done | bytes 147488 | tf_op jit(solution)/shard_map/cond/branch_1_fun/ppermute | solution.py:700
  200.4 1.7 collective-permute-start.13
  203.0 4.9 %collective-permute-done.14 = bf16[48,1536]{1,0:T(8,128)(2,1)S(1)} collective-permute-done((bf16[48,1536]{1,0:T(8,128)(2,1)S(1)}, bf16[48,1536]{1,0:T(8,128)(2,1)S(1)}, u32[]{:S(2)}, u32[]{:S(2)}) %collective-permute-start.14) | collective-permute-done | bytes 147488 | tf_op jit(solution)/shard_map/cond/branch_1_fun/ppermute | solution.py:700
  208.1 2.1 collective-permute-start.23
  211.6 7.3 %collective-permute-done.17 = bf16[256,768]{1,0:T(8,128)(2,1)S(1)} collective-permute-done((bf16[256,768]{1,0:T(8,128)(2,1)S(1)}, bf16[256,768]{1,0:T(8,128)(2,1)S(1)}, u32[]{:S(2)}, u32[]{:S(2)}) %collective-permute-start.17) | collective-permute-done | bytes 393248 | tf_op jit(solution)/shard_map/cond/branch_1_fun/ppermute | solution.py:691
  219.0 2.8 collective-permute-start.21
  222.6 4.4 %collective-permute-done.23 = bf16[96,1536]{1,0:T(8,128)(2,1)S(1)} collective-permute-done((bf16[96,1536]{1,0:T(8,128)(2,1)S(1)}, bf16[96,1536]{1,0:T(8,128)(2,1)S(1)}, u32[]{:S(2)}, u32[]{:S(2)}) %collective-permute-start.23) | collective-permute-done | bytes 294944 | tf_op jit(solution)/shard_map/cond/branch_1_fun/ppermute | solution.py:700
  231.4 4.5 %collective-permute-done.26 = bf16[48,1536]{1,0:T(8,128)(2,1)S(1)} collective-permute-done((bf16[48,1536]{1,0:T(8,128)(2,1)S(1)}, bf16[48,1536]{1,0:T(8,128)(2,1)S(1)}, u32[]{:S(2)}, u32[]{:S(2)}) %collective-permute-start.26) | collective-permute-done | bytes 147488 | tf_op jit(solution)/shard_map/cond/branch_1_fun/ppermute | solution.py:700
  237.2 2.0 collective-permute-start.29
  241.0 3.4 %input_backward.1 = bf16[512,768]{1,0:T(8,128)(2,1)} custom-call(f32[512,768]{1,0:T(8,128)} %get-tuple-element.153.dn_ref, bf16[256,768]{1,0:T(8,128)(2,1)} %copy-done.27, bf16[512,768]{1,0:T(8,128)(2,1)S(1)} %get-tuple-element.121.x_ref, f32[512,768]{1,0:T(8,128)} %get-tuple-element.155.dm_ref, f32[8,768]{1,0:T(8,128)} %broadcast_in_dim.1.gain_ref), custom_call_target="tpu_custom_call" | custom-call | flops 7864320 | bytes 4718592 | tf_op jit(solution)/shard_map/cond/branch_1_fun/input_backward/pallas_call | solution.py:646
  244.3 7.4 %collective-permute-start.20 = (f32[12,768]{1,0:T(8,128)}, f32[12,768]{1,0:T(8,128)S(1)}, u32[]{:S(2)}, u32[]{:S(2)}) collective-permute-start(f32[12,768]{1,0:T(8,128)} %add.176), channel_id=1, source_target_pairs={{0,8},{1,9},{2,10},{3,11},{4,12},{5,13},{6,14},{7,15},{8,0},{9,1},... | collective-permute-start | bytes 110600 | tf_op jit(solution)/shard_map/cond/branch_1_fun/ppermute | solution.py:700
  251.8 1.5 convert_add_fusion.1
  262.7 1.9 broadcast_select_fusion.3
  264.6 1.6 fusion.3
  266.2 1.7 broadcast_select_fusion
  268.3 3.5 %convert_element_type.150 = f32[768,2304]{1,0:T(8,128)} convert(bf16[768,2304]{1,0:T(8,128)(2,1)S(1)} %fusion.8) | non-fusion elementwise | flops 1769472 | bytes 10616832 | tf_op jit(solution)/shard_map/cond/branch_1_fun/convert_element_type | solution.py:1064
  272.2 7.2 %widened.1 = (f32[768,1536]{1,0:T(8,128)}, f32[1536,768]{1,0:T(8,128)}) custom-call(bf16[768,1536]{1,0:T(8,128)(2,1)} %get-tuple-element.296.a_ref, bf16[1536,768]{1,0:T(8,128)(2,1)} %get-tuple-element.297.b_ref), custom_call_target="tpu_custom_call" | custom-call | bytes 14155776 | tf_op jit(solution)/shard_map/widened/pallas_call | solution.py:676
  (244 shorter events, 49.0 us)
Async XLA Ops:
  7.2 265.0 %all-reduce.4.cloned.1.call-start = ((), (), s32[]{:S(2)}) async-start(), calls=%async_computation | async-start | bytes 9437184 | tf_op jit(solution)/shard_map/psum | solution.py:950
  11.3 21.8 %collective-permute-start.32 = (bf16[272,768]{1,0:T(8,128)(2,1)}, bf16[272,768]{1,0:T(8,128)(2,1)}, u32[]{:S(2)}, u32[]{:S(2)}) collective-permute-start(bf16[272,768]{1,0:T(8,128)(2,1)} %concatenate.51), channel_id=1, source_target_pairs={{0,1},{1,0},{2,3},{3,2},{4,5},{5,4},{6,7},{7,6},{8,9},{9,8},{10,11... | collective-permute-start | bytes 1253384 | tf_op jit(solution)/shard_map/ppermute | solution.py:691
  14.3 27.7 %collective-permute-start.33 = (bf16[512,768]{1,0:T(8,128)(2,1)}, bf16[512,768]{1,0:T(8,128)(2,1)}, u32[]{:S(2)}, u32[]{:S(2)}) collective-permute-start(bf16[512,768]{1,0:T(8,128)(2,1)} %ct_ref.1), channel_id=1, source_target_pairs={{0,1},{1,0},{2,3},{3,2},{4,5},{5,4},{6,7},{7,6},{8,9},{9,8},{10,11... | collective-permute-start | bytes 2359304 | tf_op jit(solution)/shard_map/ppermute | solution.py:691
  17.6 13.3 %copy-start.28 = (f32[8,768]{1,0:T(8,128)}, f32[8,768]{1,0:T(8,128)S(1)}, u32[]{:S(2)}) copy-start(f32[8,768]{1,0:T(8,128)S(1)} %maximum_maximum_fusion.rows_ref) | copy-start | bytes 73732
  30.9 25.7 %collective-permute-start.35 = (bf16[256,768]{1,0:T(8,128)(2,1)}, bf16[256,768]{1,0:T(8,128)(2,1)}, u32[]{:S(2)}, u32[]{:S(2)}) collective-permute-start(bf16[256,768]{1,0:T(8,128)(2,1)} %get-tuple-element.244), channel_id=1, source_target_pairs={{0,1},{1,0},{2,3},{3,2},{4,5},{5,4},{6,7},{7,6},{8,9},{9,8},{10,11... | collective-permute-start | bytes 1179656 | tf_op jit(solution)/shard_map/ppermute | solution.py:691
  42.5 14.1 %copy-start.40 = (bf16[1536]{0:T(1024)(128)(2,1)S(1)}, bf16[1536]{0:T(1024)(128)(2,1)}, u32[]{:S(2)}) copy-start(bf16[1536]{0:T(1024)(128)(2,1)} %param.28) | copy-start | bytes 9220
  54.5 11.6 %collective-permute-start.34 = (bf16[256,768]{1,0:T(8,128)(2,1)}, bf16[256,768]{1,0:T(8,128)(2,1)}, u32[]{:S(2)}, u32[]{:S(2)}) collective-permute-start(bf16[256,768]{1,0:T(8,128)(2,1)} %get-tuple-element.241), channel_id=1, source_target_pairs={{0,1},{1,0},{2,3},{3,2},{4,5},{5,4},{6,7},{7,6},{8,9},{9,8},{10,11... | collective-permute-start | bytes 1179656 | tf_op jit(solution)/shard_map/ppermute | solution.py:691
  66.0 23.5 %collective-permute-start.36 = (bf16[256,768]{1,0:T(8,128)(2,1)}, bf16[256,768]{1,0:T(8,128)(2,1)}, u32[]{:S(2)}, u32[]{:S(2)}) collective-permute-start(bf16[256,768]{1,0:T(8,128)(2,1)} %get-tuple-element.254), channel_id=1, source_target_pairs={{0,1},{1,0},{2,3},{3,2},{4,5},{5,4},{6,7},{7,6},{8,9},{9,8},{10,11... | collective-permute-start | bytes 1179656 | tf_op jit(solution)/shard_map/ppermute | solution.py:691
  74.9 14.6 %collective-permute-start.37 = (bf16[256,768]{1,0:T(8,128)(2,1)}, bf16[256,768]{1,0:T(8,128)(2,1)}, u32[]{:S(2)}, u32[]{:S(2)}) collective-permute-start(bf16[256,768]{1,0:T(8,128)(2,1)} %get-tuple-element.255), channel_id=1, source_target_pairs={{0,1},{1,0},{2,3},{3,2},{4,5},{5,4},{6,7},{7,6},{8,9},{9,8},{10,11... | collective-permute-start | bytes 1179656 | tf_op jit(solution)/shard_map/ppermute | solution.py:691
  125.5 3.3 %collective-permute-start = (bf16[384,1536]{1,0:T(8,128)(2,1)}, bf16[384,1536]{1,0:T(8,128)(2,1)}, u32[]{:S(2)}, u32[]{:S(2)}) collective-permute-start(bf16[384,1536]{1,0:T(8,128)(2,1)} %get-tuple-element.87), channel_id=1, source_target_pairs={{0,2},{1,3},{2,0},{3,1},{4,6},{5,7},{6,4},{7,5},{8,10},{9,11},{10,... | collective-permute-start | bytes 3538952 | tf_op jit(solution)/shard_map/cond/branch_1_fun/ppermute | solution.py:700
  132.7 20.3 %collective-permute-start.1 = (bf16[96,1536]{1,0:T(8,128)(2,1)}, bf16[96,1536]{1,0:T(8,128)(2,1)}, u32[]{:S(2)}, u32[]{:S(2)}) collective-permute-start(bf16[96,1536]{1,0:T(8,128)(2,1)} %get-tuple-element.91), channel_id=1, source_target_pairs={{0,1},{1,0},{2,3},{3,2},{4,5},{5,4},{6,7},{7,6},{8,9},{9,8},{10,11... | collective-permute-start | bytes 884744 | tf_op jit(solution)/shard_map/cond/branch_1_fun/ppermute | solution.py:700
  132.7 20.3 %collective-permute-start.2 = (bf16[96,1536]{1,0:T(8,128)(2,1)}, bf16[96,1536]{1,0:T(8,128)(2,1)}, u32[]{:S(2)}, u32[]{:S(2)}) collective-permute-start(bf16[96,1536]{1,0:T(8,128)(2,1)} %get-tuple-element.92), channel_id=1, source_target_pairs={{0,4},{1,5},{2,6},{3,7},{4,0},{5,1},{6,2},{7,3},{8,12},{9,13},{10,... | collective-permute-start | bytes 884744 | tf_op jit(solution)/shard_map/cond/branch_1_fun/ppermute | solution.py:700
  134.5 18.5 %collective-permute-start.3 = (bf16[96,1536]{1,0:T(8,128)(2,1)}, bf16[96,1536]{1,0:T(8,128)(2,1)}, u32[]{:S(2)}, u32[]{:S(2)}) collective-permute-start(bf16[96,1536]{1,0:T(8,128)(2,1)} %get-tuple-element.93), channel_id=1, source_target_pairs={{0,5},{1,4},{2,7},{3,6},{4,1},{5,0},{6,3},{7,2},{8,13},{9,12},{10,... | collective-permute-start | bytes 884744 | tf_op jit(solution)/shard_map/cond/branch_1_fun/ppermute | solution.py:700
  155.2 8.9 %copy-start.32 = (f32[8,768]{1,0:T(8,128)S(1)}, f32[8,768]{1,0:T(8,128)}, u32[]{:S(2)}) copy-start(f32[8,768]{1,0:T(8,128)} %get-tuple-element.137) | copy-start | bytes 73732 | tf_op jit(solution)/shard_map/cond
  162.2 4.1 %collective-permute-start.4 = (bf16[384,1536]{1,0:T(8,128)(2,1)}, bf16[384,1536]{1,0:T(8,128)(2,1)S(1)}, u32[]{:S(2)}, u32[]{:S(2)}) collective-permute-start(bf16[384,1536]{1,0:T(8,128)(2,1)} %get-tuple-element.110), channel_id=1, source_target_pairs={{0,2},{1,3},{2,0},{3,1},{4,6},{5,7},{6,4},{7,5},{8,10},{9,11},{10,... | collective-permute-start | bytes 3538952 | tf_op jit(solution)/shard_map/cond/branch_1_fun/ppermute | solution.py:700
  164.9 15.3 %collective-permute-start.8 = (bf16[48,1536]{1,0:T(8,128)(2,1)}, bf16[48,1536]{1,0:T(8,128)(2,1)S(1)}, u32[]{:S(2)}, u32[]{:S(2)}) collective-permute-start(bf16[48,1536]{1,0:T(8,128)(2,1)} %constant_dynamic-slice_fusion.6), channel_id=1, source_target_pairs={{0,8},{1,9},{2,10},{3,11},{4,12},{5,13},{6,14},{7,15},{8,0},{9,1},... | collective-permute-start | bytes 442376 | tf_op jit(solution)/shard_map/cond/branch_1_fun/ppermute | solution.py:700
  168.5 20.7 %collective-permute-start.5 = (bf16[96,1536]{1,0:T(8,128)(2,1)S(1)}, bf16[96,1536]{1,0:T(8,128)(2,1)}, u32[]{:S(2)}, u32[]{:S(2)}) collective-permute-start(bf16[96,1536]{1,0:T(8,128)(2,1)S(1)} %get-tuple-element.112), channel_id=1, source_target_pairs={{0,1},{1,0},{2,3},{3,2},{4,5},{5,4},{6,7},{7,6},{8,9},{9,8},{10,11... | collective-permute-start | bytes 884744 | tf_op jit(solution)/shard_map/cond/branch_1_fun/ppermute | solution.py:700
  169.1 20.2 %collective-permute-start.6 = (bf16[96,1536]{1,0:T(8,128)(2,1)S(1)}, bf16[96,1536]{1,0:T(8,128)(2,1)}, u32[]{:S(2)}, u32[]{:S(2)}) collective-permute-start(bf16[96,1536]{1,0:T(8,128)(2,1)S(1)} %get-tuple-element.113), channel_id=1, source_target_pairs={{0,4},{1,5},{2,6},{3,7},{4,0},{5,1},{6,2},{7,3},{8,12},{9,13},{10,... | collective-permute-start | bytes 884744 | tf_op jit(solution)/shard_map/cond/branch_1_fun/ppermute | solution.py:700
  170.5 18.7 %collective-permute-start.7 = (bf16[96,1536]{1,0:T(8,128)(2,1)S(1)}, bf16[96,1536]{1,0:T(8,128)(2,1)}, u32[]{:S(2)}, u32[]{:S(2)}) collective-permute-start(bf16[96,1536]{1,0:T(8,128)(2,1)S(1)} %get-tuple-element.114), channel_id=1, source_target_pairs={{0,5},{1,4},{2,7},{3,6},{4,1},{5,0},{6,3},{7,2},{8,13},{9,12},{10,... | collective-permute-start | bytes 884744 | tf_op jit(solution)/shard_map/cond/branch_1_fun/ppermute | solution.py:700
  172.1 8.9 %copy-start.20 = (bf16[96,1536]{1,0:T(8,128)(2,1)S(1)}, bf16[96,1536]{1,0:T(8,128)(2,1)}, u32[]{:S(2)}) copy-start(bf16[96,1536]{1,0:T(8,128)(2,1)} %copy-done.19) | copy-start | bytes 884740 | tf_op jit(solution)/shard_map/cond
  172.1 11.8 %copy-start.29 = (f32[8,512]{1,0:T(8,128)S(1)}, f32[8,512]{1,0:T(8,128)}, u32[]{:S(2)}) copy-start(f32[8,512]{1,0:T(8,128)} %get-tuple-element.139) | copy-start | bytes 49156 | tf_op jit(solution)/shard_map/cond
  172.1 11.8 %copy-start.31 = (f32[8,256]{1,0:T(8,128)S(1)}, f32[8,256]{1,0:T(8,128)}, u32[]{:S(2)}) copy-start(f32[8,256]{1,0:T(8,128)} %get-tuple-element.138) | copy-start | bytes 24580 | tf_op jit(solution)/shard_map/cond
  181.0 13.1 %copy-start.50 = (bf16[256,768]{1,0:T(8,128)(2,1)S(1)}, bf16[256,768]{1,0:T(8,128)(2,1)}, u32[]{:S(2)}) copy-start(bf16[256,768]{1,0:T(8,128)(2,1)} %get-tuple-element.148) | copy-start | bytes 1179652 | tf_op jit(solution)/shard_map/cond
  181.1 14.1 %copy-start.51 = (bf16[256,768]{1,0:T(8,128)(2,1)S(1)}, bf16[256,768]{1,0:T(8,128)(2,1)}, u32[]{:S(2)}) copy-start(bf16[256,768]{1,0:T(8,128)(2,1)} %get-tuple-element.149) | copy-start | bytes 1179652 | tf_op jit(solution)/shard_map/cond
  181.1 6.9 %collective-permute-start.9 = (bf16[24,1536]{1,0:T(8,128)(2,1)S(1)}, bf16[24,1536]{1,0:T(8,128)(2,1)S(1)}, u32[]{:S(2)}, u32[]{:S(2)}) collective-permute-start(bf16[24,1536]{1,0:T(8,128)(2,1)S(1)} %constant_dynamic-slice_fusion.2), channel_id=1, source_target_pairs={{0,16},{1,17},{2,18},{3,19},{4,20},{5,21},{6,22},{7,23},{8,24},{9,... | collective-permute-start | bytes 221192 | tf_op jit(solution)/shard_map/cond/branch_1_fun/ppermute | solution.py:700
  183.9 7.5 %collective-permute-start.12 = (f32[12,768]{1,0:T(8,128)S(1)}, f32[12,768]{1,0:T(8,128)S(1)}, u32[]{:S(2)}, u32[]{:S(2)}) collective-permute-start(f32[12,768]{1,0:T(8,128)S(1)} %fusion.10), channel_id=1, source_target_pairs={{0,2},{1,3},{2,0},{3,1},{4,6},{5,7},{6,4},{7,5},{8,10},{9,11},{10,... | collective-permute-start | bytes 110600 | tf_op jit(solution)/shard_map/cond/branch_1_fun/ppermute | solution.py:700
  188.0 6.0 %collective-permute-start.11 = (bf16[24,1536]{1,0:T(8,128)(2,1)S(1)}, bf16[24,1536]{1,0:T(8,128)(2,1)S(1)}, u32[]{:S(2)}, u32[]{:S(2)}) collective-permute-start(bf16[24,1536]{1,0:T(8,128)(2,1)S(1)} %add_convert_fusion.7), channel_id=1, source_target_pairs={{0,16},{1,17},{2,18},{3,19},{4,20},{5,21},{6,22},{7,23},{8,24},{9,... | collective-permute-start | bytes 221192 | tf_op jit(solution)/shard_map/cond/branch_1_fun/ppermute | solution.py:700
  190.6 9.7 %collective-permute-start.10 = (bf16[48,1536]{1,0:T(8,128)(2,1)S(1)}, bf16[48,1536]{1,0:T(8,128)(2,1)S(1)}, u32[]{:S(2)}, u32[]{:S(2)}) collective-permute-start(bf16[48,1536]{1,0:T(8,128)(2,1)S(1)} %constant_dynamic-slice_fusion.1), channel_id=1, source_target_pairs={{0,8},{1,9},{2,10},{3,11},{4,12},{5,13},{6,14},{7,15},{8,0},{9,1},... | collective-permute-start | bytes 442376 | tf_op jit(solution)/shard_map/cond/branch_1_fun/ppermute | solution.py:700
  191.5 10.6 %collective-permute-start.15 = (f32[12,768]{1,0:T(8,128)S(1)}, f32[12,768]{1,0:T(8,128)S(1)}, u32[]{:S(2)}, u32[]{:S(2)}) collective-permute-start(f32[12,768]{1,0:T(8,128)S(1)} %add.167), channel_id=1, source_target_pairs={{0,1},{1,0},{2,3},{3,2},{4,5},{5,4},{6,7},{7,6},{8,9},{9,8},{10,11... | collective-permute-start | bytes 110600 | tf_op jit(solution)/shard_map/cond/branch_1_fun/ppermute | solution.py:700
  194.0 13.9 %collective-permute-start.14 = (bf16[48,1536]{1,0:T(8,128)(2,1)S(1)}, bf16[48,1536]{1,0:T(8,128)(2,1)S(1)}, u32[]{:S(2)}, u32[]{:S(2)}) collective-permute-start(bf16[48,1536]{1,0:T(8,128)(2,1)S(1)} %pad_maximum_fusion.6), channel_id=1, source_target_pairs={{0,8},{1,9},{2,10},{3,11},{4,12},{5,13},{6,14},{7,15},{8,0},{9,1},... | collective-permute-start | bytes 442376 | tf_op jit(solution)/shard_map/cond/branch_1_fun/ppermute | solution.py:700
  194.1 16.1 %collective-permute-start.16 = (bf16[256,768]{1,0:T(8,128)(2,1)S(1)}, bf16[256,768]{1,0:T(8,128)(2,1)S(1)}, u32[]{:S(2)}, u32[]{:S(2)}) collective-permute-start(bf16[256,768]{1,0:T(8,128)(2,1)S(1)} %copy-done.50), channel_id=1, source_target_pairs={{0,1},{1,0},{2,3},{3,2},{4,5},{5,4},{6,7},{7,6},{8,9},{9,8},{10,11... | collective-permute-start | bytes 1179656 | tf_op jit(solution)/shard_map/cond/branch_1_fun/ppermute | solution.py:691
  195.2 23.7 %collective-permute-start.17 = (bf16[256,768]{1,0:T(8,128)(2,1)S(1)}, bf16[256,768]{1,0:T(8,128)(2,1)S(1)}, u32[]{:S(2)}, u32[]{:S(2)}) collective-permute-start(bf16[256,768]{1,0:T(8,128)(2,1)S(1)} %copy-done.51), channel_id=1, source_target_pairs={{0,1},{1,0},{2,3},{3,2},{4,5},{5,4},{6,7},{7,6},{8,9},{9,8},{10,11... | collective-permute-start | bytes 1179656 | tf_op jit(solution)/shard_map/cond/branch_1_fun/ppermute | solution.py:691
  200.4 7.7 %collective-permute-start.13 = (bf16[24,1536]{1,0:T(8,128)(2,1)S(1)}, bf16[24,1536]{1,0:T(8,128)(2,1)S(1)}, u32[]{:S(2)}, u32[]{:S(2)}) collective-permute-start(bf16[24,1536]{1,0:T(8,128)(2,1)S(1)} %constant_dynamic-slice_fusion), channel_id=1, source_target_pairs={{0,16},{1,17},{2,18},{3,19},{4,20},{5,21},{6,22},{7,23},{8,24},{9,... | collective-permute-start | bytes 221192 | tf_op jit(solution)/shard_map/cond/branch_1_fun/ppermute | solution.py:700
  202.1 19.6 %collective-permute-start.19 = (f32[12,768]{1,0:T(8,128)S(1)}, f32[12,768]{1,0:T(8,128)S(1)}, u32[]{:S(2)}, u32[]{:S(2)}) collective-permute-start(f32[12,768]{1,0:T(8,128)S(1)} %add.169), channel_id=1, source_target_pairs={{0,4},{1,5},{2,6},{3,7},{4,0},{5,1},{6,2},{7,3},{8,12},{9,13},{10,... | collective-permute-start | bytes 110600 | tf_op jit(solution)/shard_map/cond/branch_1_fun/ppermute | solution.py:700
  208.0 14.6 %collective-permute-start.24 = (bf16[96,1536]{1,0:T(8,128)(2,1)S(1)}, bf16[96,1536]{1,0:T(8,128)(2,1)S(1)}, u32[]{:S(2)}, u32[]{:S(2)}) collective-permute-start(bf16[96,1536]{1,0:T(8,128)(2,1)S(1)} %pad_maximum_fusion.4), channel_id=1, source_target_pairs={{0,5},{1,4},{2,7},{3,6},{4,1},{5,0},{6,3},{7,2},{8,13},{9,12},{10,... | collective-permute-start | bytes 884744 | tf_op jit(solution)/shard_map/cond/branch_1_fun/ppermute | solution.py:700
  208.1 19.0 %collective-permute-start.23 = (bf16[96,1536]{1,0:T(8,128)(2,1)S(1)}, bf16[96,1536]{1,0:T(8,128)(2,1)S(1)}, u32[]{:S(2)}, u32[]{:S(2)}) collective-permute-start(bf16[96,1536]{1,0:T(8,128)(2,1)S(1)} %pad_maximum_fusion.4), channel_id=1, source_target_pairs={{0,4},{1,5},{2,6},{3,7},{4,0},{5,1},{6,2},{7,3},{8,12},{9,13},{10,... | collective-permute-start | bytes 884744 | tf_op jit(solution)/shard_map/cond/branch_1_fun/ppermute | solution.py:700
  210.2 16.9 %copy-start.25 = (bf16[256,768]{1,0:T(8,128)(2,1)}, bf16[256,768]{1,0:T(8,128)(2,1)S(1)}, u32[]{:S(2)}) copy-start(bf16[256,768]{1,0:T(8,128)(2,1)S(1)} %collective-permute-done.16) | copy-start | bytes 1179652 | tf_op jit(solution)/shard_map/cond
  210.2 16.9 %collective-permute-start.22 = (bf16[96,1536]{1,0:T(8,128)(2,1)S(1)}, bf16[96,1536]{1,0:T(8,128)(2,1)S(1)}, u32[]{:S(2)}, u32[]{:S(2)}) collective-permute-start(bf16[96,1536]{1,0:T(8,128)(2,1)S(1)} %pad_maximum_fusion.4), channel_id=1, source_target_pairs={{0,1},{1,0},{2,3},{3,2},{4,5},{5,4},{6,7},{7,6},{8,9},{9,8},{10,11... | collective-permute-start | bytes 884744 | tf_op jit(solution)/shard_map/cond/branch_1_fun/ppermute | solution.py:700
  219.0 9.7 %collective-permute-start.21 = (bf16[24,1536]{1,0:T(8,128)(2,1)S(1)}, bf16[24,1536]{1,0:T(8,128)(2,1)S(1)}, u32[]{:S(2)}, u32[]{:S(2)}) collective-permute-start(bf16[24,1536]{1,0:T(8,128)(2,1)S(1)} %add_convert_fusion.6), channel_id=1, source_target_pairs={{0,16},{1,17},{2,18},{3,19},{4,20},{5,21},{6,22},{7,23},{8,24},{9,... | collective-permute-start | bytes 221192 | tf_op jit(solution)/shard_map/cond/branch_1_fun/ppermute | solution.py:700
  228.7 7.1 %collective-permute-start.26 = (bf16[48,1536]{1,0:T(8,128)(2,1)S(1)}, bf16[48,1536]{1,0:T(8,128)(2,1)S(1)}, u32[]{:S(2)}, u32[]{:S(2)}) collective-permute-start(bf16[48,1536]{1,0:T(8,128)(2,1)S(1)} %pad_maximum_fusion.7), channel_id=1, source_target_pairs={{0,8},{1,9},{2,10},{3,11},{4,12},{5,13},{6,14},{7,15},{8,0},{9,1},... | collective-permute-start | bytes 442376 | tf_op jit(solution)/shard_map/cond/branch_1_fun/ppermute | solution.py:700
  230.0 10.2 %collective-permute-start.18 = (bf16[256,768]{1,0:T(8,128)(2,1)S(1)}, bf16[256,768]{1,0:T(8,128)(2,1)S(1)}, u32[]{:S(2)}, u32[]{:S(2)}) collective-permute-start(bf16[256,768]{1,0:T(8,128)(2,1)S(1)} %copy-done.52), channel_id=1, source_target_pairs={{0,1},{1,0},{2,3},{3,2},{4,5},{5,4},{6,7},{7,6},{8,9},{9,8},{10,11... | collective-permute-start | bytes 1179656 | tf_op jit(solution)/shard_map/cond/branch_1_fun/ppermute | solution.py:691
  236.7 18.2 %collective-permute-start.30 = (bf16[96,1536]{1,0:T(8,128)(2,1)}, bf16[96,1536]{1,0:T(8,128)(2,1)S(1)}, u32[]{:S(2)}, u32[]{:S(2)}) collective-permute-start(bf16[96,1536]{1,0:T(8,128)(2,1)} %pad_maximum_fusion.5), channel_id=1, source_target_pairs={{0,5},{1,4},{2,7},{3,6},{4,1},{5,0},{6,3},{7,2},{8,13},{9,12},{10,... | collective-permute-start | bytes 884744 | tf_op jit(solution)/shard_map/cond/branch_1_fun/ppermute | solution.py:700
  237.2 17.7 %collective-permute-start.29 = (bf16[96,1536]{1,0:T(8,128)(2,1)}, bf16[96,1536]{1,0:T(8,128)(2,1)S(1)}, u32[]{:S(2)}, u32[]{:S(2)}) collective-permute-start(bf16[96,1536]{1,0:T(8,128)(2,1)} %pad_maximum_fusion.5), channel_id=1, source_target_pairs={{0,4},{1,5},{2,6},{3,7},{4,0},{5,1},{6,2},{7,3},{8,12},{9,13},{10,... | collective-permute-start | bytes 884744 | tf_op jit(solution)/shard_map/cond/branch_1_fun/ppermute | solution.py:700
  239.2 15.7 %collective-permute-start.28 = (bf16[96,1536]{1,0:T(8,128)(2,1)}, bf16[96,1536]{1,0:T(8,128)(2,1)}, u32[]{:S(2)}, u32[]{:S(2)}) collective-permute-start(bf16[96,1536]{1,0:T(8,128)(2,1)} %pad_maximum_fusion.5), channel_id=1, source_target_pairs={{0,1},{1,0},{2,3},{3,2},{4,5},{5,4},{6,7},{7,6},{8,9},{9,8},{10,11... | collective-permute-start | bytes 884744 | tf_op jit(solution)/shard_map/cond/branch_1_fun/ppermute | solution.py:700
  244.3 9.7 %collective-permute-start.20 = (f32[12,768]{1,0:T(8,128)}, f32[12,768]{1,0:T(8,128)S(1)}, u32[]{:S(2)}, u32[]{:S(2)}) collective-permute-start(f32[12,768]{1,0:T(8,128)} %add.176), channel_id=1, source_target_pairs={{0,8},{1,9},{2,10},{3,11},{4,12},{5,13},{6,14},{7,15},{8,0},{9,1},... | collective-permute-start | bytes 110600 | tf_op jit(solution)/shard_map/cond/branch_1_fun/ppermute | solution.py:700
  253.4 9.3 %collective-permute-start.27 = (bf16[384,1536]{1,0:T(8,128)(2,1)}, bf16[384,1536]{1,0:T(8,128)(2,1)}, u32[]{:S(2)}, u32[]{:S(2)}) collective-permute-start(bf16[384,1536]{1,0:T(8,128)(2,1)} %pad_maximum_fusion.1), channel_id=1, source_target_pairs={{0,2},{1,3},{2,0},{3,1},{4,6},{5,7},{6,4},{7,5},{8,10},{9,11},{10,... | collective-permute-start | bytes 3538952 | tf_op jit(solution)/shard_map/cond/branch_1_fun/ppermute | solution.py:700
  254.9 5.8 %collective-permute-start.25 = (f32[12,768]{1,0:T(8,128)S(1)}, f32[12,768]{1,0:T(8,128)S(1)}, u32[]{:S(2)}, u32[]{:S(2)}) collective-permute-start(f32[12,768]{1,0:T(8,128)S(1)} %add.177), channel_id=1, source_target_pairs={{0,16},{1,17},{2,18},{3,19},{4,20},{5,21},{6,22},{7,23},{8,24},{9,... | collective-permute-start | bytes 110600 | tf_op jit(solution)/shard_map/cond/branch_1_fun/ppermute | solution.py:700
  258.6 7.7 %collective-permute-start.31 = (bf16[384,1536]{1,0:T(8,128)(2,1)}, bf16[384,1536]{1,0:T(8,128)(2,1)}, u32[]{:S(2)}, u32[]{:S(2)}) collective-permute-start(bf16[384,1536]{1,0:T(8,128)(2,1)} %pad_maximum_fusion.2), channel_id=1, source_target_pairs={{0,2},{1,3},{2,0},{3,1},{4,6},{5,7},{6,4},{7,5},{8,10},{9,11},{10,... | collective-permute-start | bytes 3538952 | tf_op jit(solution)/shard_map/cond/branch_1_fun/ppermute | solution.py:700
  (44 other events, 205.0 us)
Sparse Core Ops, SparseCore 0:
  101.3 134.0 all-reduce.3

commit v2 on v1

--- a/solution.py
+++ b/solution.py
@@ -162,6 +162,35 @@
     distances = (slot + 0.5) / NB * last_len - offsets
     weights = jnp.where(offsets > 0.0, jnp.exp(-0.5 * distances * distances), 0.0)
     return weights / jnp.sum(weights, axis=place_dim, keepdims=True)
+
+
+def tail_projection(tail, first_rows, attn_in):
+    tile = D // 2
+
+    def kernel(x_ref, rows_ref, w_ref, normed_ref, kv_ref):
+        @pl.when(pl.program_id(0) == 0)
+        def _():
+            normed_ref[...] = layer_norm(
+                x_ref[...].astype(f32), rows_ref[0:1], rows_ref[1:2]
+            ).astype(bf16)
+
+        kv_ref[...] = dot(normed_ref[...], w_ref[...]).astype(bf16)
+
+    fixed = lambda count: pl.BlockSpec((count, D), lambda i: (0, 0))
+    return pl.pallas_call(
+        kernel,
+        grid=(4,),
+        in_specs=[fixed(HALF), fixed(8), pl.BlockSpec((D, tile), lambda i: (0, 2 + i))],
+        out_specs=[fixed(HALF), pl.BlockSpec((HALF, tile), lambda i: (0, i))],
+        out_shape=[
+            jax.ShapeDtypeStruct((HALF, D), bf16),
+            jax.ShapeDtypeStruct((HALF, 2 * D), bf16),
+        ],
+        cost_estimate=pl.CostEstimate(
+            flops=4 * HALF * D * D, bytes_accessed=4 * D * D, transcendentals=0
+        ),
+        name="tail_projection",
+    )(tail, first_rows, attn_in)
 
 
 def memory_kernel(
@@ -235,7 +264,7 @@
         grid=(PAIRS,),
         in_specs=[
             pl.BlockSpec(memory_space=pltpu.SMEM),
-            whole((16, D)),
+            whole((16, LANES)),
             pl.BlockSpec((HALF, LANES), lambda i: (0, i)),
             pl.BlockSpec((HALF, LANES), lambda i: (0, i)),
             pl.BlockSpec((HALF, LANES), lambda i: (0, PAIRS + i)),
@@ -720,6 +749,9 @@
         self.turn()
         self.kept, self.given = kept, [given]
 
+    def left(self):
+        return len(self.stages) + 1
+
     def turn(self):
         self.scatters, self.bits = self.stages.pop(0)
         self.place = place_in(self.bits)
@@ -741,7 +773,20 @@
         given = self.given if self.scatters else self.given * len(masks)
         self.got = [flipped(piece, mask) for piece, mask in zip(given, masks)]
 
+    @classmethod
+    def gathering(cls, value, groups):
+        chain = cls.__new__(cls)
+        chain.stages = [(False, bits) for bits in groups]
+        chain.turn()
+        chain.kept, chain.given = value, [value]
+        return chain
+
     def land(self):
+        if self.scatters and self.stages[0][0] and len(self.stages[0][1]) > 1:
+            kept, got = self.kept, self.got[0]
+            self.turn()
+            self.kept, *self.given = split_sum(kept, got, self.place, 1 << len(self.bits))
+            return True
         if self.scatters:
             total = self.kept.astype(f32)
             for piece in self.got:
@@ -772,24 +817,32 @@
     def land(self):
         self.value = self.value + self.got
         self.given = [self.value]
-        return bool(self.bits)
-
-
-def weight_grads(normed, normed_tail, d, d_tail, ready, side):
+
+    def left(self):
+        return len(self.bits)
+
+
+def weight_grads(turned, d, d_tail, ready, side):
     width = d.shape[2]
-    tile = 256
+    tile = width if ready is None else 256
     each = width // tile
     extra = 0 if ready is None else ready.shape[1] // tile
     half = D // 2
+    fresh = turned[0].shape[0] == L
 
     def kernel(side_ref, n_ref, nt_ref, d_ref, dt_ref, *refs):
-        kept_ref, given_ref, turned, tail_turned = refs[-4:]
         step = pl.program_id(0)
-
-        @pl.when(step == 0)
-        def _():
-            turned[...] = n_ref[...].T
-            tail_turned[...] = nt_ref[...].T
+        kept_ref, given_ref = refs[extra > 0 : (extra > 0) + 2]
+        if fresh:
+            turn_refs = refs[-2:]
+
+            @pl.when(step == 0)
+            def _():
+                turn_refs[0][...] = n_ref[...].T
+                turn_refs[1][...] = nt_ref[...].T
+
+        else:
+            turn_refs = (n_ref, nt_ref)
 
         def rows(which, ref):
             return ref[pl.ds(pl.multiple_of(which * half, half), half), :]
@@ -798,12 +851,13 @@
 
             @pl.when(step < each)
             def _():
-                out_ref[...] = dot(rows(which, turned), d_ref[0]).astype(bf16)
+                out_ref[...] = dot(rows(which, turn_refs[0]), d_ref[0]).astype(bf16)
 
             @pl.when((step >= each) & (step < 3 * each))
             def _():
                 out_ref[...] = (
-                    dot(rows(which, turned), d_ref[0]) + dot(rows(which, tail_turned), dt_ref[0])
+                    dot(rows(which, turn_refs[0]), d_ref[0])
+                    + dot(rows(which, turn_refs[1]), dt_ref[0])
                 ).astype(bf16)
 
             if extra:
@@ -813,28 +867,56 @@
                     out_ref[...] = rows(which, refs[0])
 
     column = lambda i: jnp.where(i < 3 * each, i % each, each - 1)
+    fixed = lambda matrix: pl.BlockSpec(matrix.shape, lambda i: (0, 0))
     in_specs = [
         pl.BlockSpec(memory_space=pltpu.SMEM),
-        pl.BlockSpec((L, D), lambda i: (0, 0)),
-        pl.BlockSpec((HALF, D), lambda i: (0, 0)),
+        fixed(turned[0]),
+        fixed(turned[1]),
         pl.BlockSpec((1, L, tile), lambda i: (jnp.minimum(i // each, 2), 0, column(i))),
         pl.BlockSpec((1, HALF, tile), lambda i: (jnp.clip(i // each - 1, 0, 1), 0, column(i))),
     ]
-    operands = [side, normed, normed_tail, d, d_tail]
+    operands = [side, *turned, d, d_tail]
     if extra:
         in_specs.append(pl.BlockSpec((D, tile), lambda i: (0, jnp.maximum(i - 3 * each, 0))))
         operands.append(ready)
     steps = 3 * each + extra
-    return pl.pallas_call(
+    shapes = [jax.ShapeDtypeStruct((half, steps * tile), bf16)] * 2
+    specs = [pl.BlockSpec((half, tile), lambda i: (0, i))] * 2
+    if fresh:
+        turns = [jax.ShapeDtypeStruct((D, L), bf16), jax.ShapeDtypeStruct((D, HALF), bf16)]
+        shapes, specs = shapes + turns, specs + [fixed(turn) for turn in turns]
+    kept, given, *turns = pl.pallas_call(
         kernel,
         grid=(steps,),
         in_specs=in_specs,
-        out_specs=[pl.BlockSpec((half, tile), lambda i: (0, i))] * 2,
-        out_shape=[jax.ShapeDtypeStruct((half, steps * tile), bf16)] * 2,
-        scratch_shapes=[pltpu.VMEM((D, L), bf16), pltpu.VMEM((D, HALF), bf16)],
+        out_specs=specs,
+        out_shape=shapes,
         cost_estimate=HIDDEN,
         name="weight_grads",
     )(*operands)
+    return kept, given, turns or turned
+
+
+def split_sum(kept, got, number, count):
+    size = kept.shape[0] // count
+
+    def kernel(number_ref, kept_ref, got_ref, *outs):
+        for q, out_ref in enumerate(outs):
+            rows = pl.ds(pl.multiple_of((number_ref[0] ^ q) * size, size), size)
+            out_ref[...] = (kept_ref[rows, :].astype(f32) + got_ref[rows, :].astype(f32)).astype(
+                out_ref.dtype
+            )
+
+    whole = lambda matrix: pl.BlockSpec(matrix.shape, lambda: (0, 0))
+    out = jax.ShapeDtypeStruct((size, kept.shape[1]), kept.dtype)
+    return pl.pallas_call(
+        kernel,
+        in_specs=[pl.BlockSpec(memory_space=pltpu.SMEM), whole(kept), whole(got)],
+        out_specs=[whole(out)] * count,
+        out_shape=[out] * count,
+        cost_estimate=HIDDEN,
+        name="split_sum",
+    )(number.reshape(1), kept, got)
 
 
 def shards(
@@ -861,18 +943,15 @@
     gain_two = ln2_gain.astype(f32)
     bias_two = second_norm_bias.astype(f32)
 
-    own_tail = jnp.concatenate(
-        [
-            inputs[HALF:],
-            jnp.broadcast_to(doc_lengths[:, NDOC - 1 :].astype(bf16), (16, D)),
-        ],
-        axis=0,
-    )
-    tail = rotated(own_tail, "mlp", 1)
+    tail = rotated(inputs[HALF:], "mlp", 1)
+    last_len = rotated(
+        jnp.broadcast_to(doc_lengths[:, NDOC - 1 :].astype(bf16), (16, LANES)), "mlp", 1
+    )
     cotangents = [cotangent] + [rotated(cotangent, "mlp", by) for by in range(1, n_mlp)]
 
     activations = inputs.astype(f32)
     normed = layer_norm(activations, gain_one, bias_one).astype(bf16)
+    first_rows = jnp.concatenate([jnp.stack([gain_one, bias_one]), jnp.zeros((6, D), f32)])
     zeros = jnp.zeros((D,), f32)
     qkv_bias = jnp.concatenate([qv_bias[0].astype(f32), zeros, qv_bias[1].astype(f32)])
     qkv = (dot(normed, attn_in) + qkv_bias).astype(bf16)
@@ -888,15 +967,13 @@
     steps = range(1, n_mlp)
     arrived_hi = [rotated(sent, "mlp", by) for by in steps]
 
-    tail_rows = tail[:HALF].astype(f32)
-    normed_tail = layer_norm(tail_rows, gain_one, bias_one).astype(bf16)
-    tail_kv = dot(normed_tail, attn_in[:, D:]).astype(bf16)
+    normed_tail, tail_kv = tail_projection(tail, first_rows, attn_in)
     reads = jnp.where(place == 0, 0, doc_lengths[:, :1])
     value_bias = jnp.broadcast_to(qv_bias[1].astype(f32), (8, D))
     tail_kv, *cotangents[1:] = fence((tail_kv, *cotangents[1:]))
     mixture, mem_k, mem_v, lse_mem, middle, normed_two, basis_t, sent = memory_attention(
         reads,
-        tail[HALF:],
+        last_len,
         qkv,
         tail_kv,
         value_bias,
@@ -959,9 +1036,10 @@
         side = place_in(core[0]).reshape(1)
         d_one, d_tail_one, sums_one = backward(0, early, d_branch)
         d_attn_out = over_rows(mixture, d_branch).astype(bf16)
-        chain_one = Chain(
-            *weight_grads(normed, normed_tail, d_one, d_tail_one, d_attn_out, side), groups
+        kept, given, turned = weight_grads(
+            (normed, normed_tail), d_one, d_tail_one, d_attn_out, side
         )
+        chain_one = Chain(kept, given, groups)
         chain_one.fly()
         chain_one.land()
         d_branch, chain_one.given = fence((d_branch, chain_one.given))
@@ -971,7 +1049,8 @@
         chain_one.land()
         d_two, d_tail_two, chain_one.given = fence((d_two, d_tail_two, chain_one.given))
         chain_one.fly()
-        chain_two = Chain(*weight_grads(normed, normed_tail, d_two, d_tail_two, None, side), groups)
+        kept, given, turned = weight_grads(turned, d_two, d_tail_two, None, side)
+        chain_two = Chain(kept, given, groups)
         chain_two.fly()
         chain_two.land()
         d_one, d_two, d_tails, sums, later, chain_two.given = fence(
@@ -987,10 +1066,10 @@
         bias_grad, y_given, y_mine = later
         chain_two.fly()
         d_normed, d_tail_rows, input_sums = qkv_backward(
-            d_one, d_two, *d_tails, attn_in, inputs, tail[:HALF]
+            d_one, d_two, *d_tails, attn_in, inputs, tail
         )
-        chain_one.got, d_normed, d_tail_rows, input_sums = fence(
-            (chain_one.got, d_normed, d_tail_rows, input_sums)
+        chain_one.got, chain_two.got[0], d_normed, d_tail_rows, input_sums = fence(
+            (chain_one.got, chain_two.got[0], d_normed, d_tail_rows, input_sums)
         )
         chain_one.land()
         chain_one.fly()
@@ -1014,6 +1093,7 @@
 
         token = chain_one.given
         flying = [chain_one, chain_two, vectors]
+        held = {chain_one: 1, chain_two: 2, vectors: 1}
         turns = 0
         while flying:
             for chain in list(flying):
@@ -1027,50 +1107,20 @@
                         ]
                     if turns == 3:
                         chain.got, returned = fence((chain.got, returned))
-                if chain.land():
-                    token = chain.given
+                chain.land()
+                token = chain.given
+                if chain.left() > held[chain]:
                     chain.fly()
                 else:
                     flying.remove(chain)
 
-        gain = jnp.broadcast_to(gain_one, (8, D))
-        input_grad = input_backward(d_normed, from_next, inputs, d_middle, gain)
-
-        halves = [y_mine[:HALF].astype(f32), y_mine[HALF:].astype(f32)]
-        for (by, part), y in zip(calls, returned):
-            halves[part] = halves[part] + y.astype(f32)
-        result = jnp.concatenate(halves, axis=0)
-        layer_output = (middle + (result + mlp_out_bias)).astype(bf16)
-
-        width = early * LANES
-        late = D - width
-        d_attn_in = jnp.concatenate(
-            [
-                piece
-                for i in range(3)
-                for piece in (
-                    chain_one.value[:, i * width : (i + 1) * width],
-                    chain_two.value[:, i * late : (i + 1) * late],
-                )
-            ],
-            axis=1,
+        return (
+            chain_one.value,
+            chain_two.value,
+            vectors.value,
+            (d_normed, from_next, d_middle),
+            (y_mine, returned),
         )
-        summed = vectors.value
-        return (
-            layer_output,
-            input_grad,
-            summed[0],
-            summed[1],
-            d_attn_in.astype(f32),
-            summed[6:8],
-            chain_one.value[:, 3 * width :].astype(f32),
-            summed[2],
-            summed[3],
-            summed[4],
-            lax.dynamic_slice(summed[8:].reshape(-1), (place * hidden_count,), (hidden_count,)),
-            summed[5],
-        )
-
 
     shapes = jax.eval_shape(finish)
     done = lax.cond(
@@ -1078,8 +1128,61 @@
         finish,
         lambda: jax.tree.map(lambda leaf: jnp.zeros(leaf.shape, leaf.dtype), shapes),
     )
+    one, two, summed, (d_normed, from_next, d_middle), (y_own, returned) = done
+    chain_two = Chain.gathering(two, [groups[1], core[0]])
+    chain_two.fly()
+    chain_one = Chain.gathering(one, core)
+    chain_one.fly()
+    vectors = Total(summed, (core[0] + mlp_bits + rest)[-1:])
+    vectors.fly()
+
+    gain = jnp.broadcast_to(gain_one, (8, D))
+    input_grad = input_backward(d_normed, from_next, inputs, d_middle, gain)
+    halves = [y_own[:HALF].astype(f32), y_own[HALF:].astype(f32)]
+    for (by, part), y in zip(calls, returned):
+        halves[part] = halves[part] + y.astype(f32)
+    result = jnp.concatenate(halves, axis=0)
+    layer_output = (middle + (result + mlp_out_bias)).astype(bf16)
     d_mlp_in, d_mlp_out = widened(d_mlp_in, d_mlp_out)
-    return (*done[:10], d_mlp_in, done[10], d_mlp_out, done[11])
+    chain_two.got, vectors.got, layer_output, input_grad, d_mlp_in, d_mlp_out = fence(
+        (chain_two.got, vectors.got, layer_output, input_grad, d_mlp_in, d_mlp_out)
+    )
+    chain_two.land()
+    chain_two.fly()
+    chain_one.land()
+    chain_two.land()
+    vectors.land()
+    summed = vectors.value
+
+    width = PAIRS // 3 * LANES
+    late = D - width
+    d_attn_in = jnp.concatenate(
+        [
+            piece
+            for i in range(3)
+            for piece in (
+                chain_one.value[:, i * width : (i + 1) * width],
+                chain_two.value[:, i * late : (i + 1) * late],
+            )
+        ],
+        axis=1,
+    )
+    return (
+        layer_output,
+        input_grad,
+        summed[0],
+        summed[1],
+        d_attn_in.astype(f32),
+        summed[6:8],
+        chain_one.value[:, 3 * width :].astype(f32),
+        summed[2],
+        summed[3],
+        summed[4],
+        d_mlp_in,
+        lax.dynamic_slice(summed[8:].reshape(-1), (place * hidden_count,), (hidden_count,)),
+        d_mlp_out,
+        summed[5],
+    )
 
 
 def solution(mesh):

time: 292 us -> 288 us (0.986)
  Pallas kernels: 119 us -> 128 us
  starting transfers between devices: 48.8 us -> 41 us
  other arithmetic: 31.7 us -> 27.2 us
  waiting for transfers between devices: 35.3 us -> 39.2 us
    ppermute x29, waiting for transfers between devices: 27.4 us -> 37.1 us  [flipped(): return lax.ppermute(value, GRID, [(i, i ^ mask) for i in range(count)])]
    pallas_call x2 -> x5, Pallas kernels: 13.8 us -> 23.2 us  [the longest x2 12.8 us: weight_grads(): pl.pallas_call(kernel, grid=(steps,), in_specs=in_specs, out_specs=specs,...]
    ppermute x29, starting transfers between devices: 36 us -> 28.9 us  [flipped(): return lax.ppermute(value, GRID, [(i, i ^ mask) for i in range(count)])]
    ppermute x9 -> x10, waiting for transfers between devices: 7.93 us -> 2.09 us  [rotated(): lax.ppermute(value, axis, [(i, (i + by) % count) for i in range(count)])]
    convert_element_type x8 -> x6, other arithmetic: 6.38 us -> 1.57 us  [land(): self.value = total.astype(self.kept.dtype)]
    slice x6 -> x4, local copies, waits for them, and re-layouts: 5.46 us -> 2.33 us  [the longest x1 1.08 us: shards(): tail = rotated(inputs[HALF:], 'mlp', 1)]
    unnamed x40 -> x46, local copies, waits for them, and re-layouts: 0.11 us -> 3.04 us
    ppermute x9 -> x10, starting transfers between devices: 12.8 us -> 12.1 us  [rotated(): lax.ppermute(value, axis, [(i, (i + by) % count) for i in range(count)])]
  transfers between devices with their start and end apart: 39 -> 40, of which waited for: 11 -> 12; matrix products, arithmetic and copies ran while one was open for 17% -> 13% of each run, Pallas kernels for 39% -> 45%
where the time goes in v2:
time: 288 us; the launch traced here: 284 us
  Pallas kernels  128 us (44%)
  starting transfers between devices  41 us (14%)
  waiting for transfers between devices  39.2 us (14%)
  other arithmetic  27.2 us (9%)
  matrix products  19.3 us (7%)
  between operations  15.5 us (5%)
  local copies, waits for them, and re-layouts  13.2 us (5%)
    ppermute x29, waiting for transfers between devices, flipped(): return lax.ppermute(value, GRID, [(i, i ^ mask) for i in range(count)])  37.1 us
    pallas_call x3, Pallas kernels, mlp_block(): pl.pallas_call(mlp_kernel, grid=(hidden // tile,), in_specs=[fixed, pl.Bl...  30 us
    ppermute x29, starting transfers between devices, flipped(): return lax.ppermute(value, GRID, [(i, i ^ mask) for i in range(count)])  28.9 us
    pallas_call x2, Pallas kernels, attention_backward(): pl.pallas_call(backward_kernel, grid=(pairs,), in_specs=[pl.BlockSpec(mem...  26.3 us
    dot_general x3, matrix products, shards(): lax.dot_general(a, b, (((0,), (0,)), ((), ())), preferred_element_type=f32)  15 us
    pallas_call x1, Pallas kernels, local_attention(): pl.pallas_call(local_kernel, grid=(PAIRS,), in_specs=[pl.BlockSpec(memory...  13.7 us
    pallas_call x2, Pallas kernels, weight_grads(): pl.pallas_call(kernel, grid=(steps,), in_specs=in_specs, out_specs=specs,...  12.8 us
    ppermute x10, starting transfers between devices, rotated(): lax.ppermute(value, axis, [(i, (i + by) % count) for i in range(count)])  12.1 us
  transfers between devices with their start and end apart: 40, of which 12 were waited for; matrix products, arithmetic and copies ran while one was open for 13% of the time, Pallas kernels for 45%

profile of v2, /device:TPU:0, one launch (start us, length us, event | category | flops | bytes accessed | tf_op | source)
XLA Modules:
  0.0 283.9 jit_solution(1477879527192238309)
XLA Ops:
  8.4 3.1 %collective-permute-start.27 = (bf16[256,768]{1,0:T(8,128)(2,1)S(1)}, bf16[256,768]{1,0:T(8,128)(2,1)}, u32[]{:S(2)}, u32[]{:S(2)}) collective-permute-start(bf16[256,768]{1,0:T(8,128)(2,1)S(1)} %slice.94), channel_id=1, source_target_pairs={{0,1},{1,0},{2,3},{3,2},{4,5},{5,4},{6,7},{7,6},{8,9},{9,8},{10,11... | collective-permute-start | bytes 1179656 | tf_op jit(solution)/shard_map/ppermute | solution.py:720
  14.0 1.9 collective-permute-start.26
  18.1 4.3 %fusion.4.q_ref.k_ref.v_ref = bf16[512,2304]{1,0:T(8,128)(2,1)S(1)} fusion(bf16[512,768]{1,0:T(8,128)(2,1)S(1)} %fusion.10, bf16[768,2304]{1,0:T(8,128)(2,1)} %w_ref.1, f32[2304]{0:T(1024)S(1)} %pad_maximum_fusion.8), kind=kOutput, calls=%fused_computation.37 | convolution fusion | flops 1814298624 | bytes 6693888 | tf_op jit(solution)/shard_map/dot_general | solution.py:27
  23.3 13.7 %local_attention.1 = (f32[256,768]{1,0:T(8,128)}, f32[6,8,512]{2,1,0:T(8,128)}, bf16[512,768]{1,0:T(8,128)(2,1)}, f32[512,768]{1,0:T(8,128)}, bf16[512,768]{1,0:T(8,128)(2,1)}, /*index=5*/bf16[256,768]{1,0:T(8,128)(2,1)}) custom-call(s32[1,3]{1,0:T(1,128)S(1)} %copy-done.27, bf16[512,2304]{1,0:T(8,128)(2,1)S(1)} %fusion.4.q_ref.k_ref.v_ref, ...), custom_call_target="tpu_custom_call" | custom-call | flops 2415919104 | bytes 3145728 | tf_op jit(solution)/shard_map/local_attention/pallas_call | solution.py:116
  40.4 4.7 %tail_projection.1 = (bf16[256,768]{1,0:T(8,128)(2,1)}, bf16[256,1536]{1,0:T(8,128)(2,1)}) custom-call(bf16[256,768]{1,0:T(8,128)(2,1)} %collective-permute-done.27.x_ref, f32[8,768]{1,0:T(8,128)} %maximum_maximum_fusion.rows_ref, bf16[768,2304]{1,0:T(8,128)(2,1)} %w_ref.1), custom_call_target="tpu_custom_call" | custom-call | flops 603979776 | bytes 2359296 | tf_op jit(solution)/shard_map/tail_projection/pallas_call | solution.py:180
  45.7 12.0 %memory_attention.1 = (bf16[512,768]{1,0:T(8,128)(2,1)}, bf16[512,768]{1,0:T(8,128)(2,1)}, bf16[512,768]{1,0:T(8,128)(2,1)}, f32[6,8,256]{2,1,0:T(8,128)}, f32[5...) custom-call(s32[1,1]{1,0:T(1,128)S(6)} %select_n.313.reads, ...), custom_call_target="tpu_custom_call", output_to_operand_aliasing={{0}: (10, {}), {4}: (11, {}), {5}: (12, {})} | custom-call | flops 3221225472 | bytes 6291456 | tf_op jit(solution)/shard_map/memory_attention/pallas_call | solution.py:262
  57.8 2.0 collective-permute-start.29
  60.4 8.7 %mlp_block.3 = (bf16[1024,1536]{1,0:T(8,128)(2,1)}, bf16[1024,1536]{1,0:T(8,128)(2,1)}, f32[8,1536]{1,0:T(8,128)}, bf16[256,768]{1,0:T(8,128)(2,1)}, bf16[256,768]{1,0:T(8,128)(2,1)}) custom-call(bf16[256,768]{1,0:T(8,128)(2,1)} %collective-permute-done.30.x_ref, bf16[512,768]{1,0:T(8,128)(2,1)} %collective-permute-done.28.ct_ref, bf16[768,1536]{1,0:T(8,128)(2,1)} %wi_ref.5, ...), custom_call_target="tpu_custom_call" | custom-call | flops 2415919104 | bytes 7864320 | tf_op jit(solution)/shard_map/mlp_block/pallas_call | solution.py:372
  70.1 8.7 %mlp_block.4 = (bf16[1024,1536]{1,0:T(8,128)(2,1)}, bf16[1024,1536]{1,0:T(8,128)(2,1)}, f32[8,1536]{1,0:T(8,128)}, bf16[256,768]{1,0:T(8,128)(2,1)}, bf16[256,768]{1,0:T(8,128)(2,1)}) custom-call(bf16[256,768]{1,0:T(8,128)(2,1)} %copy-done.10, bf16[512,768]{1,0:T(8,128)(2,1)} %collective-permute-done.28.ct_ref, ...), custom_call_target="tpu_custom_call", output_to_operand_aliasing={{0}: (5, {}), {1}: (6, {})} | custom-call | flops 2415919104 | bytes 7864320 | tf_op jit(solution)/shard_map/mlp_block/pallas_call | solution.py:372
  78.8 2.0 collective-permute-start.32
  80.8 12.6 %mlp_block.5 = (bf16[1024,1536]{1,0:T(8,128)(2,1)}, bf16[1024,1536]{1,0:T(8,128)(2,1)}, f32[8,1536]{1,0:T(8,128)}, bf16[512,768]{1,0:T(8,128)(2,1)}, bf16[512,768]{1,0:T(8,128)(2,1)}) custom-call(bf16[512,768]{1,0:T(8,128)(2,1)} %get-tuple-element.250.x_ref, bf16[512,768]{1,0:T(8,128)(2,1)} %ct_ref.1, ...), custom_call_target="tpu_custom_call", output_to_operand_aliasing={{0}: (5, {}), {1}: (6, {})} | custom-call | flops 4831838208 | bytes 11010048 | tf_op jit(solution)/shard_map/mlp_block/pallas_call | solution.py:372
  93.4 6.5 %convolution_convert_fusion.1 = bf16[1536,768]{1,0:T(8,128)(2,1)} fusion(bf16[1024,1536]{1,0:T(8,128)(2,1)} %get-tuple-element.290, bf16[512,768]{1,0:T(8,128)(2,1)} %collective-permute-done.28.ct_ref, bf16[512,768]{1,0:T(8,128)(2,1)} %ct_ref.1), kind=kOutput, calls=%fused_computation.38 | convolution fusion | flops 2420244480 | bytes 7077888 | tf_op jit(solution)/shard_map/dot_general | solution.py:1010
  100.0 4.9 %convolution_convert_fusion.2 = bf16[768,1536]{1,0:T(8,128)(2,1)} fusion(bf16[1024,1536]{1,0:T(8,128)(2,1)S(1)} %copy-done.5, bf16[256,768]{1,0:T(8,128)(2,1)} %collective-permute-done.30.x_ref, bf16[256,768]{1,0:T(8,128)(2,1)S(1)} %copy-done.11, bf16[512,768]{1,0:T(8,128)(2,1)S(1)} %copy-done.29), kind=kOutput, calls=%fused_computation.39 | convolution fusion | flops 2421817344 | bytes 7077888 | tf_op jit(solution)/shard_map/dot_general | solution.py:1010
  105.7 135.2 %conditional.1 = (bf16[384,1536]{1,0:T(8,128)(2,1)}, bf16[96,1536]{1,0:T(8,128)(2,1)S(1)}, f32[12,768]{1,0:T(8,128)}, f32[512,768]{1,0:T(8,128)}, bf16[256,768]{...) conditional(s32[]{:T(128)} %bitcast.3, () %tuple.44, ...), branch_computations={%region_2.3_spmd, %region_3.4_spmd} | conditional | flops 14316875776 | bytes 84455432 | solution.py:1126
  105.7 4.4 %middle_backward.1 = (f32[512,768]{1,0:T(8,128)}, bf16[512,768]{1,0:T(8,128)(2,1)}, f32[8,768]{1,0:T(8,128)}) custom-call(bf16[512,768]{1,0:T(8,128)(2,1)} %get-tuple-element.70.d_ref, bf16[512,768]{1,0:T(8,128)(2,1)} %get-tuple-element.71.ct_ref, f32[512,768]{1,0:T(8,128)} %get-tuple-element.72.middle_ref, f32[8,768]{1,0:T(8,128)} %get-tuple-element.73.rows_ref, ...), custom_call_target="tpu_custom_call" | custom-call | flops 7864320 | bytes 5505024 | tf_op jit(solution)/shard_map/cond/branch_1_fun/middle_backward/pallas_call | solution.py:595
  110.1 3.6 %fusion.refs_0_ = bf16[768,768]{1,0:T(8,128)(2,1)} fusion(bf16[512,768]{1,0:T(8,128)(2,1)} %get-tuple-element.90.db_ref, bf16[512,768]{1,0:T(8,128)(2,1)} %get-tuple-element.83), kind=kOutput, calls=%fused_computation.1 | convolution fusion | flops 604569600 | bytes 2752512 | tf_op jit(solution)/shard_map/cond/branch_1_fun/dot_general | solution.py:1010
  113.7 9.5 %attention_backward.2 = (bf16[3,512,256]{2,1,0:T(8,128)(2,1)}, bf16[2,256,256]{2,1,0:T(8,128)(2,1)}, f32[8,256]{1,0:T(8,128)}) custom-call(s32[1,3]{1,0:T(1,128)S(1)} %get-tuple-element.66.lens, bf16[512,2304]{1,0:T(8,128)(2,1)S(1)} %get-tuple-element.67.q_ref.k_ref.v_ref, bf16[512,2304]{1,0:T(8,128)(2,1)S(1)} %get-tuple-element.67.q_ref.k_ref.v_ref, ...), custom_call_target="tpu_custom_call" | custom-call | flops 3758096384 | bytes 2621440 | tf_op jit(solution)/shard_map/cond/branch_1_fun/attention_backward/pallas_call | solution.py:501
  123.2 7.3 %weight_grads.2 = (bf16[384,1536]{1,0:T(8,128)(2,1)}, bf16[384,1536]{1,0:T(8,128)(2,1)}, bf16[768,512]{1,0:T(8,128)(2,1)}, bf16[768,256]{1,0:T(8,128)(2,1)}) custom-call(s32[1]{0:T(128)} %bitcast.1.side_ref, bf16[512,768]{1,0:T(8,128)(2,1)} %get-tuple-element.64.n_ref, bf16[256,768]{1,0:T(8,128)(2,1)S(1)} %copy-done.12, ...), custom_call_target="tpu_custom_call" | custom-call | flops 1000 | bytes 1000 | tf_op jit(solution)/shard_map/cond/branch_1_fun/weight_grads/pallas_call | solution.py:888
  130.6 3.2 %collective-permute-done.got_ref = bf16[384,1536]{1,0:T(8,128)(2,1)} collective-permute-done((bf16[384,1536]{1,0:T(8,128)(2,1)}, bf16[384,1536]{1,0:T(8,128)(2,1)}, u32[]{:S(2)}, u32[]{:S(2)}) %collective-permute-start) | collective-permute-done | bytes 1179680 | tf_op jit(solution)/shard_map/cond/branch_1_fun/ppermute | solution.py:729
  133.8 2.9 %split_sum.2 = (bf16[96,1536]{1,0:T(8,128)(2,1)}, bf16[96,1536]{1,0:T(8,128)(2,1)}, bf16[96,1536]{1,0:T(8,128)(2,1)}, bf16[96,1536]{1,0:T(8,128)(2,1)}) custom-call(s32[1]{0:T(128)} %bitcast.number_ref, bf16[384,1536]{1,0:T(8,128)(2,1)} %get-tuple-element.84.kept_ref, bf16[384,1536]{1,0:T(8,128)(2,1)} %collective-permute-done.got_ref), custom_call_target="tpu_custom_call" | custom-call | flops 1000 | bytes 1000 | tf_op jit(solution)/shard_map/cond/branch_1_fun/split_sum/pallas_call | solution.py:912
  136.6 1.7 collective-permute-start.2
  138.4 1.8 collective-permute-start.3
  140.1 16.8 %attention_backward.3 = (bf16[3,512,512]{2,1,0:T(8,128)(2,1)}, bf16[2,256,512]{2,1,0:T(8,128)(2,1)}, f32[8,512]{1,0:T(8,128)}) custom-call(s32[1,3]{1,0:T(1,128)S(1)} %get-tuple-element.66.lens, bf16[512,2304]{1,0:T(8,128)(2,1)S(1)} %get-tuple-element.67.q_ref.k_ref.v_ref, bf16[512,2304]{1,0:T(8,128)(2,1)S(1)} %get-tuple-element.67.q_ref.k_ref.v_ref, ...), custom_call_target="tpu_custom_call" | custom-call | flops 7516192768 | bytes 5242880 | tf_op jit(solution)/shard_map/cond/branch_1_fun/attention_backward/pallas_call | solution.py:501
  158.3 5.5 %weight_grads.3 = (bf16[384,1536]{1,0:T(8,128)(2,1)}, bf16[384,1536]{1,0:T(8,128)(2,1)}) custom-call(s32[1]{0:T(128)} %bitcast.1.side_ref, bf16[768,512]{1,0:T(8,128)(2,1)} %get-tuple-element.112.n_ref, bf16[768,256]{1,0:T(8,128)(2,1)} %get-tuple-element.113.nt_ref, bf16[3,512,512]{2,1,0:T(8,128)(2,1)} %get-tuple-element.121.d_ref.two_ref, ...), custom_call_target="tpu_custom_call" | custom-call | flops 1000 | bytes 1000 | tf_op jit(solution)/shard_map/cond/branch_1_fun/weight_grads/pallas_call | solution.py:888
  164.7 2.2 collective-permute-done.5.got_ref
  167.9 2.9 %split_sum.3 = (bf16[96,1536]{1,0:T(8,128)(2,1)}, bf16[96,1536]{1,0:T(8,128)(2,1)}, bf16[96,1536]{1,0:T(8,128)(2,1)}, bf16[96,1536]{1,0:T(8,128)(2,1)}) custom-call(s32[1]{0:T(128)} %bitcast.number_ref, bf16[384,1536]{1,0:T(8,128)(2,1)} %get-tuple-element.114.kept_ref, bf16[384,1536]{1,0:T(8,128)(2,1)} %copy-done.7), custom_call_target="tpu_custom_call" | custom-call | flops 1000 | bytes 1000 | tf_op jit(solution)/shard_map/cond/branch_1_fun/split_sum/pallas_call | solution.py:912
  176.1 8.4 %qkv_backward.1 = (f32[512,768]{1,0:T(8,128)}, bf16[256,768]{1,0:T(8,128)(2,1)}, f32[8,768]{1,0:T(8,128)}) custom-call(bf16[3,512,256]{2,1,0:T(8,128)(2,1)} %get-tuple-element.120.d_ref.one_ref, bf16[3,512,512]{2,1,0:T(8,128)(2,1)} %get-tuple-element.121.d_ref.two_ref, bf16[2,256,256]{2,1,0:T(8,128)(2,1)} %get-tuple-element.122.dt_ref.t_one_ref, ...), custom_call_target="tpu_custom_call" | custom-call | flops 2415919104 | bytes 7864320 | tf_op jit(solution)/shard_map/cond/branch_1_fun/qkv_backward/pallas_call | solution.py:641
  184.5 3.0 %collective-permute-start.7 = (bf16[24,1536]{1,0:T(8,128)(2,1)S(1)}, bf16[24,1536]{1,0:T(8,128)(2,1)S(1)}, u32[]{:S(2)}, u32[]{:S(2)}) collective-permute-start(bf16[24,1536]{1,0:T(8,128)(2,1)S(1)} %constant_dynamic-slice_fusion.2), channel_id=1, source_target_pairs={{0,16},{1,17},{2,18},{3,19},{4,20},{5,21},{6,22},{7,23},{8,24},{9,... | collective-permute-start | bytes 221192 | tf_op jit(solution)/shard_map/cond/branch_1_fun/ppermute | solution.py:729
  188.4 3.6 %collective-permute-done.7 = bf16[24,1536]{1,0:T(8,128)(2,1)S(1)} collective-permute-done((bf16[24,1536]{1,0:T(8,128)(2,1)S(1)}, bf16[24,1536]{1,0:T(8,128)(2,1)S(1)}, u32[]{:S(2)}, u32[]{:S(2)}) %collective-permute-start.7) | collective-permute-done | bytes 73760 | tf_op jit(solution)/shard_map/cond/branch_1_fun/ppermute | solution.py:729
  193.9 1.8 collective-permute-start.13
  195.9 1.8 collective-permute-start.21
  198.1 6.5 %collective-permute-done.14 = bf16[48,1536]{1,0:T(8,128)(2,1)S(1)} collective-permute-done((bf16[48,1536]{1,0:T(8,128)(2,1)S(1)}, bf16[48,1536]{1,0:T(8,128)(2,1)S(1)}, u32[]{:S(2)}, u32[]{:S(2)}) %collective-permute-start.14) | collective-permute-done | bytes 147488 | tf_op jit(solution)/shard_map/cond/branch_1_fun/ppermute | solution.py:729
  205.0 5.6 %collective-permute-done.12 = bf16[48,1536]{1,0:T(8,128)(2,1)S(1)} collective-permute-done((bf16[48,1536]{1,0:T(8,128)(2,1)S(1)}, bf16[48,1536]{1,0:T(8,128)(2,1)S(1)}, u32[]{:S(2)}, u32[]{:S(2)}) %collective-permute-start.12) | collective-permute-done | bytes 147488 | tf_op jit(solution)/shard_map/cond/branch_1_fun/ppermute | solution.py:729
  212.0 2.3 collective-permute-start.17
  214.3 2.1 collective-permute-done.21
  216.4 2.1 collective-permute-start.22
  218.5 2.9 %collective-permute-done.15 = bf16[96,1536]{1,0:T(8,128)(2,1)S(1)} collective-permute-done((bf16[96,1536]{1,0:T(8,128)(2,1)S(1)}, bf16[96,1536]{1,0:T(8,128)(2,1)S(1)}, u32[]{:S(2)}, u32[]{:S(2)}) %collective-permute-start.15) | collective-permute-done | bytes 294944 | tf_op jit(solution)/shard_map/cond/branch_1_fun/ppermute | solution.py:729
  221.4 3.3 %collective-permute-done.16 = bf16[96,1536]{1,0:T(8,128)(2,1)S(1)} collective-permute-done((bf16[96,1536]{1,0:T(8,128)(2,1)S(1)}, bf16[96,1536]{1,0:T(8,128)(2,1)S(1)}, u32[]{:S(2)}, u32[]{:S(2)}) %collective-permute-start.16) | collective-permute-done | bytes 294944 | tf_op jit(solution)/shard_map/cond/branch_1_fun/ppermute | solution.py:729
  224.7 4.0 %collective-permute-done.17 = bf16[96,1536]{1,0:T(8,128)(2,1)S(1)} collective-permute-done((bf16[96,1536]{1,0:T(8,128)(2,1)S(1)}, bf16[96,1536]{1,0:T(8,128)(2,1)S(1)}, u32[]{:S(2)}, u32[]{:S(2)}) %collective-permute-start.17) | collective-permute-done | bytes 294944 | tf_op jit(solution)/shard_map/cond/branch_1_fun/ppermute | solution.py:729
  234.9 5.0 %collective-permute-done.24 = f32[12,768]{1,0:T(8,128)S(1)} collective-permute-done((f32[12,768]{1,0:T(8,128)S(1)}, f32[12,768]{1,0:T(8,128)S(1)}, u32[]{:S(2)}, u32[]{:S(2)}) %collective-permute-start.24) | collective-permute-done | bytes 36896 | tf_op jit(solution)/shard_map/cond/branch_1_fun/ppermute | solution.py:729
  242.2 2.3 collective-permute-start.35
  244.5 2.3 collective-permute-start.36
  246.8 1.9 convert_add_fusion.1
  250.6 3.1 %input_backward.1 = bf16[512,768]{1,0:T(8,128)(2,1)} custom-call(f32[512,768]{1,0:T(8,128)S(1)} %copy-done.2, bf16[256,768]{1,0:T(8,128)(2,1)} %get-tuple-element.287.next_ref, bf16[512,768]{1,0:T(8,128)(2,1)S(1)} %copy-done, f32[512,768]{1,0:T(8,128)} %get-tuple-element.288.dm_ref, f32[8,768]{1,0:T(8,128)} %broadcast_in_dim.46.gain_ref), custom_call_target="tpu_custom_call" | custom-call | flops 7864320 | bytes 4718592 | tf_op jit(solution)/shard_map/input_backward/pallas_call | solution.py:675
  253.7 6.8 %widened.1 = (f32[768,1536]{1,0:T(8,128)}, f32[1536,768]{1,0:T(8,128)}) custom-call(bf16[768,1536]{1,0:T(8,128)(2,1)} %get-tuple-element.310.a_ref, bf16[1536,768]{1,0:T(8,128)(2,1)} %get-tuple-element.311.b_ref), custom_call_target="tpu_custom_call" | custom-call | bytes 14155776 | tf_op jit(solution)/shard_map/widened/pallas_call | solution.py:705
  263.8 1.8 broadcast_select_fusion.11
  270.6 1.9 broadcast_select_fusion.8
  273.3 3.5 %convert_element_type.165 = f32[768,2304]{1,0:T(8,128)} convert(bf16[768,2304]{1,0:T(8,128)(2,1)S(1)} %fusion.26) | non-fusion elementwise | flops 1769472 | bytes 10616832 | tf_op jit(solution)/shard_map/convert_element_type | solution.py:1175
  (205 shorter events, 45.1 us)
Async XLA Ops:
  7.2 10.5 %copy-start.18 = (bf16[2,768]{1,0:T(2,128)(2,1)S(1)}, bf16[2,768]{1,0:T(2,128)(2,1)}, u32[]{:S(2)}) copy-start(bf16[2,768]{1,0:T(2,128)(2,1)} %param.22) | copy-start | bytes 9220
  7.2 246.5 %all-reduce.3.cloned.1.call-start = ((), (), s32[]{:S(2)}) async-start(), calls=%async_computation | async-start | bytes 9437184 | tf_op jit(solution)/shard_map/psum | solution.py:1027
  8.4 32.0 %collective-permute-start.27 = (bf16[256,768]{1,0:T(8,128)(2,1)S(1)}, bf16[256,768]{1,0:T(8,128)(2,1)}, u32[]{:S(2)}, u32[]{:S(2)}) collective-permute-start(bf16[256,768]{1,0:T(8,128)(2,1)S(1)} %slice.94), channel_id=1, source_target_pairs={{0,1},{1,0},{2,3},{3,2},{4,5},{5,4},{6,7},{7,6},{8,9},{9,8},{10,11... | collective-permute-start | bytes 1179656 | tf_op jit(solution)/shard_map/ppermute | solution.py:720
  11.4 33.7 %collective-permute-start.28 = (bf16[512,768]{1,0:T(8,128)(2,1)}, bf16[512,768]{1,0:T(8,128)(2,1)}, u32[]{:S(2)}, u32[]{:S(2)}) collective-permute-start(bf16[512,768]{1,0:T(8,128)(2,1)} %ct_ref.1), channel_id=1, source_target_pairs={{0,1},{1,0},{2,3},{3,2},{4,5},{5,4},{6,7},{7,6},{8,9},{9,8},{10,11... | collective-permute-start | bytes 2359304 | tf_op jit(solution)/shard_map/ppermute | solution.py:720
  14.0 31.1 %collective-permute-start.26 = (bf16[16,128]{1,0:T(8,128)(2,1)}, bf16[16,128]{1,0:T(8,128)(2,1)}, u32[]{:S(2)}, u32[]{:S(2)}) collective-permute-start(bf16[16,128]{1,0:T(8,128)(2,1)} %broadcast_in_dim.38), channel_id=1, source_target_pairs={{0,1},{1,0},{2,3},{3,2},{4,5},{5,4},{6,7},{7,6},{8,9},{9,8},{10,11... | collective-permute-start | bytes 12296 | tf_op jit(solution)/shard_map/ppermute | solution.py:720
  37.0 22.8 %collective-permute-start.30 = (bf16[256,768]{1,0:T(8,128)(2,1)}, bf16[256,768]{1,0:T(8,128)(2,1)}, u32[]{:S(2)}, u32[]{:S(2)}) collective-permute-start(bf16[256,768]{1,0:T(8,128)(2,1)} %get-tuple-element.254), channel_id=1, source_target_pairs={{0,1},{1,0},{2,3},{3,2},{4,5},{5,4},{6,7},{7,6},{8,9},{9,8},{10,11... | collective-permute-start | bytes 1179656 | tf_op jit(solution)/shard_map/ppermute | solution.py:720
  45.7 14.0 %copy-start.22 = (bf16[1536]{0:T(1024)(128)(2,1)S(1)}, bf16[1536]{0:T(1024)(128)(2,1)}, u32[]{:S(2)}) copy-start(bf16[1536]{0:T(1024)(128)(2,1)} %param.28) | copy-start | bytes 9220
  57.8 11.5 %collective-permute-start.29 = (bf16[256,768]{1,0:T(8,128)(2,1)}, bf16[256,768]{1,0:T(8,128)(2,1)S(1)}, u32[]{:S(2)}, u32[]{:S(2)}) collective-permute-start(bf16[256,768]{1,0:T(8,128)(2,1)} %get-tuple-element.251), channel_id=1, source_target_pairs={{0,1},{1,0},{2,3},{3,2},{4,5},{5,4},{6,7},{7,6},{8,9},{9,8},{10,11... | collective-permute-start | bytes 1179656 | tf_op jit(solution)/shard_map/ppermute | solution.py:720
  69.1 24.2 %collective-permute-start.31 = (bf16[256,768]{1,0:T(8,128)(2,1)}, bf16[256,768]{1,0:T(8,128)(2,1)}, u32[]{:S(2)}, u32[]{:S(2)}) collective-permute-start(bf16[256,768]{1,0:T(8,128)(2,1)} %get-tuple-element.264), channel_id=1, source_target_pairs={{0,1},{1,0},{2,3},{3,2},{4,5},{5,4},{6,7},{7,6},{8,9},{9,8},{10,11... | collective-permute-start | bytes 1179656 | tf_op jit(solution)/shard_map/ppermute | solution.py:720
  78.8 14.6 %collective-permute-start.32 = (bf16[256,768]{1,0:T(8,128)(2,1)}, bf16[256,768]{1,0:T(8,128)(2,1)S(1)}, u32[]{:S(2)}, u32[]{:S(2)}) collective-permute-start(bf16[256,768]{1,0:T(8,128)(2,1)} %get-tuple-element.265), channel_id=1, source_target_pairs={{0,1},{1,0},{2,3},{3,2},{4,5},{5,4},{6,7},{7,6},{8,9},{9,8},{10,11... | collective-permute-start | bytes 1179656 | tf_op jit(solution)/shard_map/ppermute | solution.py:720
  130.5 3.3 %collective-permute-start = (bf16[384,1536]{1,0:T(8,128)(2,1)}, bf16[384,1536]{1,0:T(8,128)(2,1)}, u32[]{:S(2)}, u32[]{:S(2)}) collective-permute-start(bf16[384,1536]{1,0:T(8,128)(2,1)} %get-tuple-element.85), channel_id=1, source_target_pairs={{0,2},{1,3},{2,0},{3,1},{4,6},{5,7},{6,4},{7,5},{8,10},{9,11},{10,... | collective-permute-start | bytes 3538952 | tf_op jit(solution)/shard_map/cond/branch_1_fun/ppermute | solution.py:729
  136.6 20.3 %copy-start.14 = (bf16[96,1536]{1,0:T(8,128)(2,1)S(1)}, bf16[96,1536]{1,0:T(8,128)(2,1)}, u32[]{:S(2)}) copy-start(bf16[96,1536]{1,0:T(8,128)(2,1)} %get-tuple-element.86) | copy-start | bytes 884740 | tf_op jit(solution)/shard_map/cond
  136.6 20.3 %collective-permute-start.1 = (bf16[96,1536]{1,0:T(8,128)(2,1)}, bf16[96,1536]{1,0:T(8,128)(2,1)}, u32[]{:S(2)}, u32[]{:S(2)}) collective-permute-start(bf16[96,1536]{1,0:T(8,128)(2,1)} %get-tuple-element.93), channel_id=1, source_target_pairs={{0,1},{1,0},{2,3},{3,2},{4,5},{5,4},{6,7},{7,6},{8,9},{9,8},{10,11... | collective-permute-start | bytes 884744 | tf_op jit(solution)/shard_map/cond/branch_1_fun/ppermute | solution.py:729
  136.6 20.3 %collective-permute-start.2 = (bf16[96,1536]{1,0:T(8,128)(2,1)}, bf16[96,1536]{1,0:T(8,128)(2,1)}, u32[]{:S(2)}, u32[]{:S(2)}) collective-permute-start(bf16[96,1536]{1,0:T(8,128)(2,1)} %get-tuple-element.94), channel_id=1, source_target_pairs={{0,4},{1,5},{2,6},{3,7},{4,0},{5,1},{6,2},{7,3},{8,12},{9,13},{10,... | collective-permute-start | bytes 884744 | tf_op jit(solution)/shard_map/cond/branch_1_fun/ppermute | solution.py:729
  138.4 18.6 %collective-permute-start.3 = (bf16[96,1536]{1,0:T(8,128)(2,1)}, bf16[96,1536]{1,0:T(8,128)(2,1)}, u32[]{:S(2)}, u32[]{:S(2)}) collective-permute-start(bf16[96,1536]{1,0:T(8,128)(2,1)} %get-tuple-element.95), channel_id=1, source_target_pairs={{0,5},{1,4},{2,7},{3,6},{4,1},{5,0},{6,3},{7,2},{8,13},{9,12},{10,... | collective-permute-start | bytes 884744 | tf_op jit(solution)/shard_map/cond/branch_1_fun/ppermute | solution.py:729
  163.8 3.1 %collective-permute-start.5 = (bf16[384,1536]{1,0:T(8,128)(2,1)}, bf16[384,1536]{1,0:T(8,128)(2,1)S(1)}, u32[]{:S(2)}, u32[]{:S(2)}) collective-permute-start(bf16[384,1536]{1,0:T(8,128)(2,1)} %get-tuple-element.115), channel_id=1, source_target_pairs={{0,2},{1,3},{2,0},{3,1},{4,6},{5,7},{6,4},{7,5},{8,10},{9,11},{10,... | collective-permute-start | bytes 3538952 | tf_op jit(solution)/shard_map/cond/branch_1_fun/ppermute | solution.py:729
  170.8 13.7 %collective-permute-start.6 = (bf16[96,1536]{1,0:T(8,128)(2,1)}, bf16[96,1536]{1,0:T(8,128)(2,1)S(1)}, u32[]{:S(2)}, u32[]{:S(2)}) collective-permute-start(bf16[96,1536]{1,0:T(8,128)(2,1)} %get-tuple-element.119), channel_id=1, source_target_pairs={{0,1},{1,0},{2,3},{3,2},{4,5},{5,4},{6,7},{7,6},{8,9},{9,8},{10,11... | collective-permute-start | bytes 884744 | tf_op jit(solution)/shard_map/cond/branch_1_fun/ppermute | solution.py:729
  170.9 13.5 %collective-permute-start.4 = (bf16[48,1536]{1,0:T(8,128)(2,1)S(1)}, bf16[48,1536]{1,0:T(8,128)(2,1)S(1)}, u32[]{:S(2)}, u32[]{:S(2)}) collective-permute-start(bf16[48,1536]{1,0:T(8,128)(2,1)S(1)} %constant_dynamic-slice_fusion.3), channel_id=1, source_target_pairs={{0,8},{1,9},{2,10},{3,11},{4,12},{5,13},{6,14},{7,15},{8,0},{9,1},... | collective-permute-start | bytes 442376 | tf_op jit(solution)/shard_map/cond/branch_1_fun/ppermute | solution.py:729
  172.5 20.4 %collective-permute-start.10 = (bf16[96,1536]{1,0:T(8,128)(2,1)}, bf16[96,1536]{1,0:T(8,128)(2,1)S(1)}, u32[]{:S(2)}, u32[]{:S(2)}) collective-permute-start(bf16[96,1536]{1,0:T(8,128)(2,1)} %get-tuple-element.140), channel_id=1, source_target_pairs={{0,4},{1,5},{2,6},{3,7},{4,0},{5,1},{6,2},{7,3},{8,12},{9,13},{10,... | collective-permute-start | bytes 884744 | tf_op jit(solution)/shard_map/cond/branch_1_fun/ppermute | solution.py:729
  174.2 18.7 %collective-permute-start.11 = (bf16[96,1536]{1,0:T(8,128)(2,1)}, bf16[96,1536]{1,0:T(8,128)(2,1)S(1)}, u32[]{:S(2)}, u32[]{:S(2)}) collective-permute-start(bf16[96,1536]{1,0:T(8,128)(2,1)} %get-tuple-element.141), channel_id=1, source_target_pairs={{0,5},{1,4},{2,7},{3,6},{4,1},{5,0},{6,3},{7,2},{8,13},{9,12},{10,... | collective-permute-start | bytes 884744 | tf_op jit(solution)/shard_map/cond/branch_1_fun/ppermute | solution.py:729
  176.0 12.2 %copy-start.17 = (f32[8,512]{1,0:T(8,128)S(1)}, f32[8,512]{1,0:T(8,128)}, u32[]{:S(2)}) copy-start(f32[8,512]{1,0:T(8,128)} %get-tuple-element.135) | copy-start | bytes 49156 | tf_op jit(solution)/shard_map/cond
  176.0 12.2 %copy-start.19 = (f32[8,256]{1,0:T(8,128)S(1)}, f32[8,256]{1,0:T(8,128)}, u32[]{:S(2)}) copy-start(f32[8,256]{1,0:T(8,128)} %get-tuple-element.134) | copy-start | bytes 24580 | tf_op jit(solution)/shard_map/cond
  176.1 16.8 %copy-start.13 = (bf16[96,1536]{1,0:T(8,128)(2,1)S(1)}, bf16[96,1536]{1,0:T(8,128)(2,1)}, u32[]{:S(2)}) copy-start(bf16[96,1536]{1,0:T(8,128)(2,1)} %get-tuple-element.138) | copy-start | bytes 884740 | tf_op jit(solution)/shard_map/cond
  184.4 11.3 %copy-start.30 = (bf16[256,768]{1,0:T(8,128)(2,1)S(1)}, bf16[256,768]{1,0:T(8,128)(2,1)}, u32[]{:S(2)}) copy-start(bf16[256,768]{1,0:T(8,128)(2,1)} %get-tuple-element.156) | copy-start | bytes 1179652 | tf_op jit(solution)/shard_map/cond
  184.4 11.5 %copy-start.31 = (bf16[256,768]{1,0:T(8,128)(2,1)S(1)}, bf16[256,768]{1,0:T(8,128)(2,1)}, u32[]{:S(2)}) copy-start(bf16[256,768]{1,0:T(8,128)(2,1)} %get-tuple-element.157) | copy-start | bytes 1179652 | tf_op jit(solution)/shard_map/cond
  184.5 7.5 %collective-permute-start.7 = (bf16[24,1536]{1,0:T(8,128)(2,1)S(1)}, bf16[24,1536]{1,0:T(8,128)(2,1)S(1)}, u32[]{:S(2)}, u32[]{:S(2)}) collective-permute-start(bf16[24,1536]{1,0:T(8,128)(2,1)S(1)} %constant_dynamic-slice_fusion.2), channel_id=1, source_target_pairs={{0,16},{1,17},{2,18},{3,19},{4,20},{5,21},{6,22},{7,23},{8,24},{9,... | collective-permute-start | bytes 221192 | tf_op jit(solution)/shard_map/cond/branch_1_fun/ppermute | solution.py:729
  188.3 5.6 %collective-permute-start.9 = (f32[12,768]{1,0:T(8,128)S(1)}, f32[12,768]{1,0:T(8,128)S(1)}, u32[]{:S(2)}, u32[]{:S(2)}) collective-permute-start(f32[12,768]{1,0:T(8,128)S(1)} %fusion.2), channel_id=1, source_target_pairs={{0,2},{1,3},{2,0},{3,1},{4,6},{5,7},{6,4},{7,5},{8,10},{9,11},{10,... | collective-permute-start | bytes 110600 | tf_op jit(solution)/shard_map/cond/branch_1_fun/ppermute | solution.py:729
  192.0 6.0 %collective-permute-start.8 = (bf16[24,1536]{1,0:T(8,128)(2,1)S(1)}, bf16[24,1536]{1,0:T(8,128)(2,1)S(1)}, u32[]{:S(2)}, u32[]{:S(2)}) collective-permute-start(bf16[24,1536]{1,0:T(8,128)(2,1)S(1)} %add_convert_fusion.5), channel_id=1, source_target_pairs={{0,16},{1,17},{2,18},{3,19},{4,20},{5,21},{6,22},{7,23},{8,24},{9,... | collective-permute-start | bytes 221192 | tf_op jit(solution)/shard_map/cond/branch_1_fun/ppermute | solution.py:729
  193.1 11.5 %collective-permute-start.14 = (bf16[48,1536]{1,0:T(8,128)(2,1)S(1)}, bf16[48,1536]{1,0:T(8,128)(2,1)S(1)}, u32[]{:S(2)}, u32[]{:S(2)}) collective-permute-start(bf16[48,1536]{1,0:T(8,128)(2,1)S(1)} %constant_dynamic-slice_fusion.1), channel_id=1, source_target_pairs={{0,8},{1,9},{2,10},{3,11},{4,12},{5,13},{6,14},{7,15},{8,0},{9,1},... | collective-permute-start | bytes 442376 | tf_op jit(solution)/shard_map/cond/branch_1_fun/ppermute | solution.py:729
  193.9 10.9 %collective-permute-start.13 = (f32[12,768]{1,0:T(8,128)S(1)}, f32[12,768]{1,0:T(8,128)S(1)}, u32[]{:S(2)}, u32[]{:S(2)}) collective-permute-start(f32[12,768]{1,0:T(8,128)S(1)} %add.133), channel_id=1, source_target_pairs={{0,1},{1,0},{2,3},{3,2},{4,5},{5,4},{6,7},{7,6},{8,9},{9,8},{10,11... | collective-permute-start | bytes 110600 | tf_op jit(solution)/shard_map/cond/branch_1_fun/ppermute | solution.py:729
  195.7 16.3 %collective-permute-start.20 = (bf16[256,768]{1,0:T(8,128)(2,1)S(1)}, bf16[256,768]{1,0:T(8,128)(2,1)S(1)}, u32[]{:S(2)}, u32[]{:S(2)}) collective-permute-start(bf16[256,768]{1,0:T(8,128)(2,1)S(1)} %copy-done.30), channel_id=1, source_target_pairs={{0,1},{1,0},{2,3},{3,2},{4,5},{5,4},{6,7},{7,6},{8,9},{9,8},{10,11... | collective-permute-start | bytes 1179656 | tf_op jit(solution)/shard_map/cond/branch_1_fun/ppermute | solution.py:720
  195.9 20.4 %collective-permute-start.21 = (bf16[256,768]{1,0:T(8,128)(2,1)S(1)}, bf16[256,768]{1,0:T(8,128)(2,1)S(1)}, u32[]{:S(2)}, u32[]{:S(2)}) collective-permute-start(bf16[256,768]{1,0:T(8,128)(2,1)S(1)} %copy-done.31), channel_id=1, source_target_pairs={{0,1},{1,0},{2,3},{3,2},{4,5},{5,4},{6,7},{7,6},{8,9},{9,8},{10,11... | collective-permute-start | bytes 1179656 | tf_op jit(solution)/shard_map/cond/branch_1_fun/ppermute | solution.py:720
  198.1 12.5 %collective-permute-start.12 = (bf16[48,1536]{1,0:T(8,128)(2,1)S(1)}, bf16[48,1536]{1,0:T(8,128)(2,1)S(1)}, u32[]{:S(2)}, u32[]{:S(2)}) collective-permute-start(bf16[48,1536]{1,0:T(8,128)(2,1)S(1)} %pad_maximum_fusion.3), channel_id=1, source_target_pairs={{0,8},{1,9},{2,10},{3,11},{4,12},{5,13},{6,14},{7,15},{8,0},{9,1},... | collective-permute-start | bytes 442376 | tf_op jit(solution)/shard_map/cond/branch_1_fun/ppermute | solution.py:729
  204.7 6.9 %collective-permute-start.19 = (bf16[24,1536]{1,0:T(8,128)(2,1)S(1)}, bf16[24,1536]{1,0:T(8,128)(2,1)S(1)}, u32[]{:S(2)}, u32[]{:S(2)}) collective-permute-start(bf16[24,1536]{1,0:T(8,128)(2,1)S(1)} %constant_dynamic-slice_fusion), channel_id=1, source_target_pairs={{0,16},{1,17},{2,18},{3,19},{4,20},{5,21},{6,22},{7,23},{8,24},{9,... | collective-permute-start | bytes 221192 | tf_op jit(solution)/shard_map/cond/branch_1_fun/ppermute | solution.py:729
  204.8 13.7 %collective-permute-start.18 = (f32[12,768]{1,0:T(8,128)S(1)}, f32[12,768]{1,0:T(8,128)S(1)}, u32[]{:S(2)}, u32[]{:S(2)}) collective-permute-start(f32[12,768]{1,0:T(8,128)S(1)} %add.135), channel_id=1, source_target_pairs={{0,4},{1,5},{2,6},{3,7},{4,0},{5,1},{6,2},{7,3},{8,12},{9,13},{10,... | collective-permute-start | bytes 110600 | tf_op jit(solution)/shard_map/cond/branch_1_fun/ppermute | solution.py:729
  210.7 10.7 %collective-permute-start.15 = (bf16[96,1536]{1,0:T(8,128)(2,1)S(1)}, bf16[96,1536]{1,0:T(8,128)(2,1)S(1)}, u32[]{:S(2)}, u32[]{:S(2)}) collective-permute-start(bf16[96,1536]{1,0:T(8,128)(2,1)S(1)} %pad_maximum_fusion.1), channel_id=1, source_target_pairs={{0,1},{1,0},{2,3},{3,2},{4,5},{5,4},{6,7},{7,6},{8,9},{9,8},{10,11... | collective-permute-start | bytes 884744 | tf_op jit(solution)/shard_map/cond/branch_1_fun/ppermute | solution.py:729
  211.6 13.1 %collective-permute-start.16 = (bf16[96,1536]{1,0:T(8,128)(2,1)S(1)}, bf16[96,1536]{1,0:T(8,128)(2,1)S(1)}, u32[]{:S(2)}, u32[]{:S(2)}) collective-permute-start(bf16[96,1536]{1,0:T(8,128)(2,1)S(1)} %pad_maximum_fusion.1), channel_id=1, source_target_pairs={{0,4},{1,5},{2,6},{3,7},{4,0},{5,1},{6,2},{7,3},{8,12},{9,13},{10,... | collective-permute-start | bytes 884744 | tf_op jit(solution)/shard_map/cond/branch_1_fun/ppermute | solution.py:729
  212.0 16.7 %collective-permute-start.17 = (bf16[96,1536]{1,0:T(8,128)(2,1)S(1)}, bf16[96,1536]{1,0:T(8,128)(2,1)S(1)}, u32[]{:S(2)}, u32[]{:S(2)}) collective-permute-start(bf16[96,1536]{1,0:T(8,128)(2,1)S(1)} %pad_maximum_fusion.1), channel_id=1, source_target_pairs={{0,5},{1,4},{2,7},{3,6},{4,1},{5,0},{6,3},{7,2},{8,13},{9,12},{10,... | collective-permute-start | bytes 884744 | tf_op jit(solution)/shard_map/cond/branch_1_fun/ppermute | solution.py:729
  216.4 13.9 %collective-permute-start.22 = (bf16[24,1536]{1,0:T(8,128)(2,1)S(1)}, bf16[24,1536]{1,0:T(8,128)(2,1)S(1)}, u32[]{:S(2)}, u32[]{:S(2)}) collective-permute-start(bf16[24,1536]{1,0:T(8,128)(2,1)S(1)} %add_convert_fusion.4), channel_id=1, source_target_pairs={{0,16},{1,17},{2,18},{3,19},{4,20},{5,21},{6,22},{7,23},{8,24},{9,... | collective-permute-start | bytes 221192 | tf_op jit(solution)/shard_map/cond/branch_1_fun/ppermute | solution.py:729
  230.3 10.2 %collective-permute-start.23 = (bf16[48,1536]{1,0:T(8,128)(2,1)S(1)}, bf16[48,1536]{1,0:T(8,128)(2,1)S(1)}, u32[]{:S(2)}, u32[]{:S(2)}) collective-permute-start(bf16[48,1536]{1,0:T(8,128)(2,1)S(1)} %pad_maximum_fusion.4), channel_id=1, source_target_pairs={{0,8},{1,9},{2,10},{3,11},{4,12},{5,13},{6,14},{7,15},{8,0},{9,1},... | collective-permute-start | bytes 442376 | tf_op jit(solution)/shard_map/cond/branch_1_fun/ppermute | solution.py:729
  231.3 8.6 %collective-permute-start.24 = (f32[12,768]{1,0:T(8,128)S(1)}, f32[12,768]{1,0:T(8,128)S(1)}, u32[]{:S(2)}, u32[]{:S(2)}) collective-permute-start(f32[12,768]{1,0:T(8,128)S(1)} %add.137), channel_id=1, source_target_pairs={{0,8},{1,9},{2,10},{3,11},{4,12},{5,13},{6,14},{7,15},{8,0},{9,1},... | collective-permute-start | bytes 110600 | tf_op jit(solution)/shard_map/cond/branch_1_fun/ppermute | solution.py:729
  232.4 8.2 %collective-permute-start.25 = (bf16[256,768]{1,0:T(8,128)(2,1)S(1)}, bf16[256,768]{1,0:T(8,128)(2,1)}, u32[]{:S(2)}, u32[]{:S(2)}) collective-permute-start(bf16[256,768]{1,0:T(8,128)(2,1)S(1)} %copy-done.32), channel_id=1, source_target_pairs={{0,1},{1,0},{2,3},{3,2},{4,5},{5,4},{6,7},{7,6},{8,9},{9,8},{10,11... | collective-permute-start | bytes 1179656 | tf_op jit(solution)/shard_map/cond/branch_1_fun/ppermute | solution.py:720
  240.9 19.6 %collective-permute-start.33 = (bf16[96,1536]{1,0:T(8,128)(2,1)S(1)}, bf16[96,1536]{1,0:T(8,128)(2,1)S(1)}, u32[]{:S(2)}, u32[]{:S(2)}) collective-permute-start(bf16[96,1536]{1,0:T(8,128)(2,1)S(1)} %get-tuple-element.281), channel_id=1, source_target_pairs={{0,1},{1,0},{2,3},{3,2},{4,5},{5,4},{6,7},{7,6},{8,9},{9,8},{10,11... | collective-permute-start | bytes 884744 | tf_op jit(solution)/shard_map/ppermute | solution.py:729
  241.7 18.8 %collective-permute-start.34 = (bf16[96,1536]{1,0:T(8,128)(2,1)S(1)}, bf16[96,1536]{1,0:T(8,128)(2,1)S(1)}, u32[]{:S(2)}, u32[]{:S(2)}) collective-permute-start(bf16[96,1536]{1,0:T(8,128)(2,1)S(1)} %get-tuple-element.281), channel_id=1, source_target_pairs={{0,4},{1,5},{2,6},{3,7},{4,0},{5,1},{6,2},{7,3},{8,12},{9,13},{10,... | collective-permute-start | bytes 884744 | tf_op jit(solution)/shard_map/ppermute | solution.py:729
  242.2 18.4 %collective-permute-start.35 = (bf16[96,1536]{1,0:T(8,128)(2,1)S(1)}, bf16[96,1536]{1,0:T(8,128)(2,1)}, u32[]{:S(2)}, u32[]{:S(2)}) collective-permute-start(bf16[96,1536]{1,0:T(8,128)(2,1)S(1)} %get-tuple-element.281), channel_id=1, source_target_pairs={{0,5},{1,4},{2,7},{3,6},{4,1},{5,0},{6,3},{7,2},{8,13},{9,12},{10,... | collective-permute-start | bytes 884744 | tf_op jit(solution)/shard_map/ppermute | solution.py:729
  244.4 19.3 %collective-permute-start.37 = (bf16[384,1536]{1,0:T(8,128)(2,1)}, bf16[384,1536]{1,0:T(8,128)(2,1)}, u32[]{:S(2)}, u32[]{:S(2)}) collective-permute-start(bf16[384,1536]{1,0:T(8,128)(2,1)} %get-tuple-element.296), channel_id=1, source_target_pairs={{0,2},{1,3},{2,0},{3,1},{4,6},{5,7},{6,4},{7,5},{8,10},{9,11},{10,... | collective-permute-start | bytes 3538952 | tf_op jit(solution)/shard_map/ppermute | solution.py:729
  244.5 16.1 %collective-permute-start.36 = (f32[12,768]{1,0:T(8,128)}, f32[12,768]{1,0:T(8,128)S(1)}, u32[]{:S(2)}, u32[]{:S(2)}) collective-permute-start(f32[12,768]{1,0:T(8,128)} %get-tuple-element.282), channel_id=1, source_target_pairs={{0,16},{1,17},{2,18},{3,19},{4,20},{5,21},{6,22},{7,23},{8,24},{9,... | collective-permute-start | bytes 110600 | tf_op jit(solution)/shard_map/ppermute | solution.py:729
  263.5 7.1 %collective-permute-start.38 = (bf16[384,1536]{1,0:T(8,128)(2,1)}, bf16[384,1536]{1,0:T(8,128)(2,1)}, u32[]{:S(2)}, u32[]{:S(2)}) collective-permute-start(bf16[384,1536]{1,0:T(8,128)(2,1)} %pad_maximum_fusion.6), channel_id=1, source_target_pairs={{0,2},{1,3},{2,0},{3,1},{4,6},{5,7},{6,4},{7,5},{8,10},{9,11},{10,... | collective-permute-start | bytes 3538952 | tf_op jit(solution)/shard_map/ppermute | solution.py:729
  (26 other events, 133.1 us)
Sparse Core Ops, SparseCore 0:
  105.1 135.2 all-reduce.2

commit v3 on v2

--- a/solution.py
+++ b/solution.py
@@ -164,14 +164,14 @@
     return weights / jnp.sum(weights, axis=place_dim, keepdims=True)
 
 
-def tail_projection(tail, first_rows, attn_in):
+def tail_projection(tail, rows, attn_in):
     tile = D // 2
 
     def kernel(x_ref, rows_ref, w_ref, normed_ref, kv_ref):
         @pl.when(pl.program_id(0) == 0)
         def _():
             normed_ref[...] = layer_norm(
-                x_ref[...].astype(f32), rows_ref[0:1], rows_ref[1:2]
+                x_ref[...].astype(f32), rows_ref[3:4], rows_ref[4:5]
             ).astype(bf16)
 
         kv_ref[...] = dot(normed_ref[...], w_ref[...]).astype(bf16)
@@ -190,7 +190,7 @@
             flops=4 * HALF * D * D, bytes_accessed=4 * D * D, transcendentals=0
         ),
         name="tail_projection",
-    )(tail, first_rows, attn_in)
+    )(tail, rows, attn_in)
 
 
 def memory_kernel(
@@ -229,7 +229,7 @@
         acc[...] = jnp.zeros_like(acc)
 
     mem_k = dot(basis[...], kt_ref[...]).astype(bf16)
-    mem_v = (dot(basis[...], vt_ref[...]) + vb_ref[0:1]).astype(bf16)
+    mem_v = (dot(basis[...], vt_ref[...]) + vb_ref[5:6]).astype(bf16)
     mk_ref[...] = mem_k
     mv_ref[...] = mem_v
     v_t = mem_v.T
@@ -366,7 +366,7 @@
 
 def mlp_block(rows, cotangent, part, mlp_in, bias_rows, mlp_out, total, place, kept):
     count, hidden = rows.shape[0], mlp_in.shape[1]
-    tile = 256 if hidden % 256 == 0 else 128
+    tile = next(t for t in (768 if count <= HALF else 512, 384, 256, 128) if hidden % t == 0)
     fixed = pl.BlockSpec((count, D), lambda i: (0, 0))
     across = pl.BlockSpec((count, tile), lambda i: (place, i))
     return pl.pallas_call(
@@ -664,11 +664,11 @@
     )(d_one, d_two, d_tail_one, d_tail_two, attn_in, inputs, tail_rows)
 
 
-def input_backward(d_normed, from_next, inputs, d_middle, gain):
-    def kernel(dn_ref, next_ref, x_ref, dm_ref, gain_ref, out_ref):
+def input_backward(d_normed, from_next, inputs, d_middle, rows):
+    def kernel(dn_ref, next_ref, x_ref, dm_ref, rows_ref, out_ref):
         unit, scale = normalized(x_ref[...].astype(f32))
         shared = jnp.where(pl.program_id(0) == 0, 0.0, next_ref[...].astype(f32))
-        grown = (dn_ref[...] + shared) * gain_ref[0:1]
+        grown = (dn_ref[...] + shared) * rows_ref[3:4]
         out_ref[...] = (dm_ref[...] + norm_slope(unit, scale, grown)).astype(bf16)
 
     half = pl.BlockSpec((HALF, D), lambda i: (i, 0))
@@ -688,7 +688,7 @@
             flops=20 * L * D, bytes_accessed=12 * L * D, transcendentals=0
         ),
         name="input_backward",
-    )(d_normed, from_next, inputs, d_middle, gain)
+    )(d_normed, from_next, inputs, d_middle, rows)
 
 
 def widened(first, second):
@@ -891,7 +891,9 @@
         in_specs=in_specs,
         out_specs=specs,
         out_shape=shapes,
-        cost_estimate=HIDDEN,
+        cost_estimate=pl.CostEstimate(
+            flops=8 * L * D * width, bytes_accessed=8 * D * width, transcendentals=0
+        ),
         name="weight_grads",
     )(*operands)
     return kept, given, turns or turned
@@ -944,21 +946,26 @@
     bias_two = second_norm_bias.astype(f32)
 
     tail = rotated(inputs[HALF:], "mlp", 1)
-    last_len = rotated(
-        jnp.broadcast_to(doc_lengths[:, NDOC - 1 :].astype(bf16), (16, LANES)), "mlp", 1
-    )
     cotangents = [cotangent] + [rotated(cotangent, "mlp", by) for by in range(1, n_mlp)]
 
     activations = inputs.astype(f32)
     normed = layer_norm(activations, gain_one, bias_one).astype(bf16)
-    first_rows = jnp.concatenate([jnp.stack([gain_one, bias_one]), jnp.zeros((6, D), f32)])
     zeros = jnp.zeros((D,), f32)
     qkv_bias = jnp.concatenate([qv_bias[0].astype(f32), zeros, qv_bias[1].astype(f32)])
     qkv = (dot(normed, attn_in) + qkv_bias).astype(bf16)
     rows = jnp.concatenate(
         [
-            jnp.stack([attn_out_bias.astype(f32), gain_two, bias_two]),
-            jnp.zeros((5, D), f32),
+            jnp.stack(
+                [
+                    attn_out_bias.astype(f32),
+                    gain_two,
+                    bias_two,
+                    gain_one,
+                    bias_one,
+                    qv_bias[1].astype(f32),
+                ]
+            ),
+            jnp.zeros((2, D), f32),
         ]
     )
     local, lse_local, mixture, middle, normed_two, sent = local_attention(
@@ -967,16 +974,17 @@
     steps = range(1, n_mlp)
     arrived_hi = [rotated(sent, "mlp", by) for by in steps]
 
-    normed_tail, tail_kv = tail_projection(tail, first_rows, attn_in)
+    own_len, local = fence((doc_lengths[:, NDOC - 1 :], local))
+    last_len = rotated(jnp.broadcast_to(own_len.astype(bf16), (16, LANES)), "mlp", 1)
+    normed_tail, tail_kv = tail_projection(tail, rows, attn_in)
     reads = jnp.where(place == 0, 0, doc_lengths[:, :1])
-    value_bias = jnp.broadcast_to(qv_bias[1].astype(f32), (8, D))
     tail_kv, *cotangents[1:] = fence((tail_kv, *cotangents[1:]))
     mixture, mem_k, mem_v, lse_mem, middle, normed_two, basis_t, sent = memory_attention(
         reads,
         last_len,
         qkv,
         tail_kv,
-        value_bias,
+        rows,
         local,
         attn_out,
         inputs,
@@ -1065,14 +1073,26 @@
         )
         bias_grad, y_given, y_mine = later
         chain_two.fly()
+        chain_one.got, unused = fence((chain_one.got, chain_two.given))
+        chain_one.land()
+        d_one, chain_one.given = fence((d_one, chain_one.given))
+        chain_one.fly()
         d_normed, d_tail_rows, input_sums = qkv_backward(
             d_one, d_two, *d_tails, attn_in, inputs, tail
         )
-        chain_one.got, chain_two.got[0], d_normed, d_tail_rows, input_sums = fence(
-            (chain_one.got, chain_two.got[0], d_normed, d_tail_rows, input_sums)
+        chain_one.got, chain_two.got, d_normed, d_tail_rows, input_sums = fence(
+            (chain_one.got, chain_two.got, d_normed, d_tail_rows, input_sums)
         )
         chain_one.land()
         chain_one.fly()
+        chain_two.land()
+        chain_two.fly()
+        y_given, unused = fence((y_given, chain_two.given))
+        shares = [
+            jnp.concatenate([y for (by, part), y in zip(calls, y_given) if by == step][::-1], axis=0)
+            for step in steps
+        ]
+        returned = [rotated(y, "mlp", -step) for step, y in zip(steps, shares)]
         from_next = rotated(d_tail_rows, "mlp", -1)
         placed_bias = lax.dynamic_update_slice(
             jnp.zeros((n_mlp * hidden_count,), f32), bias_grad, (place * hidden_count,)
@@ -1091,36 +1111,35 @@
         )
         vectors.fly()
 
-        token = chain_one.given
-        flying = [chain_one, chain_two, vectors]
-        held = {chain_one: 1, chain_two: 2, vectors: 1}
+        chains = {"one": chain_one, "two": chain_two, "all": vectors}
+        held = {"one": 1, "two": 2, "all": 1}
+        order = ["two", "one", "all"] * 2 + ["two", "all"] * 2 + ["one"]
+        token = chain_two.given
+        input_grad = layer_output = None
         turns = 0
-        while flying:
-            for chain in list(flying):
+        while any(chains[name].left() > held[name] or name in order for name in chains):
+            for name in order:
+                chain = chains[name]
                 chain.got, token = fence((chain.got, token))
-                if chain is chain_two:
-                    turns += 1
-                    if turns == 1:
-                        chain.got, y_given = fence((chain.got, y_given))
-                        returned = [
-                            rotated(y, "mlp", -by) for (by, part), y in zip(calls, y_given)
-                        ]
-                    if turns == 3:
-                        chain.got, returned = fence((chain.got, returned))
+                turns += 1
+                if turns == 7:
+                    chain.got, returned = fence((chain.got, returned))
+                if turns == 9:
+                    input_grad = input_backward(d_normed, from_next, inputs, d_middle, rows)
+                    chain.got, input_grad = fence((chain.got, input_grad))
+                if turns == 11:
+                    result = y_mine.astype(f32)
+                    for y in returned:
+                        result = result + y.astype(f32)
+                    layer_output = (middle + (result + mlp_out_bias)).astype(bf16)
+                    chain.got, layer_output = fence((chain.got, layer_output))
                 chain.land()
                 token = chain.given
-                if chain.left() > held[chain]:
+                if chain.left() > held[name]:
                     chain.fly()
-                else:
-                    flying.remove(chain)
-
-        return (
-            chain_one.value,
-            chain_two.value,
-            vectors.value,
-            (d_normed, from_next, d_middle),
-            (y_mine, returned),
-        )
+            order = [name for name in chains if chains[name].left() > held[name]]
+
+        return chain_one.value, chain_two.value, vectors.value, input_grad, layer_output
 
     shapes = jax.eval_shape(finish)
     done = lax.cond(
@@ -1128,31 +1147,26 @@
         finish,
         lambda: jax.tree.map(lambda leaf: jnp.zeros(leaf.shape, leaf.dtype), shapes),
     )
-    one, two, summed, (d_normed, from_next, d_middle), (y_own, returned) = done
+    one, two, summed, input_grad, layer_output = done
     chain_two = Chain.gathering(two, [groups[1], core[0]])
     chain_two.fly()
     chain_one = Chain.gathering(one, core)
     chain_one.fly()
     vectors = Total(summed, (core[0] + mlp_bits + rest)[-1:])
     vectors.fly()
-
-    gain = jnp.broadcast_to(gain_one, (8, D))
-    input_grad = input_backward(d_normed, from_next, inputs, d_middle, gain)
-    halves = [y_own[:HALF].astype(f32), y_own[HALF:].astype(f32)]
-    for (by, part), y in zip(calls, returned):
-        halves[part] = halves[part] + y.astype(f32)
-    result = jnp.concatenate(halves, axis=0)
-    layer_output = (middle + (result + mlp_out_bias)).astype(bf16)
+    vectors.land()
+    bias_grad = lax.dynamic_slice(
+        vectors.value[8:].reshape(-1), (place * hidden_count,), (hidden_count,)
+    )
+    summed = [vectors.value[i] for i in range(6)] + [vectors.value[6:8], bias_grad]
     d_mlp_in, d_mlp_out = widened(d_mlp_in, d_mlp_out)
-    chain_two.got, vectors.got, layer_output, input_grad, d_mlp_in, d_mlp_out = fence(
-        (chain_two.got, vectors.got, layer_output, input_grad, d_mlp_in, d_mlp_out)
+    chain_two.got, summed, d_mlp_in, d_mlp_out = fence(
+        (chain_two.got, summed, d_mlp_in, d_mlp_out)
     )
     chain_two.land()
     chain_two.fly()
     chain_one.land()
     chain_two.land()
-    vectors.land()
-    summed = vectors.value
 
     width = PAIRS // 3 * LANES
     late = D - width
@@ -1173,13 +1187,13 @@
         summed[0],
         summed[1],
         d_attn_in.astype(f32),
-        summed[6:8],
+        summed[6],
         chain_one.value[:, 3 * width :].astype(f32),
         summed[2],
         summed[3],
         summed[4],
         d_mlp_in,
-        lax.dynamic_slice(summed[8:].reshape(-1), (place * hidden_count,), (hidden_count,)),
+        summed[7],
         d_mlp_out,
         summed[5],
     )

time: 288 us -> 275 us (0.955)
  waiting for transfers between devices: 39.2 us -> 29.4 us
  starting transfers between devices: 41 us -> 48.9 us
  local copies, waits for them, and re-layouts: 13.2 us -> 7.96 us
  Pallas kernels: 128 us -> 123 us
    ppermute x29, waiting for transfers between devices: 37.1 us -> 28 us  [flipped(): return lax.ppermute(value, GRID, [(i, i ^ mask) for i in range(count)])]
    ppermute x29, starting transfers between devices: 28.9 us -> 37 us  [flipped(): return lax.ppermute(value, GRID, [(i, i ^ mask) for i in range(count)])]
    pallas_call x3, Pallas kernels: 30 us -> 24.5 us  [mlp_block(): pl.pallas_call(mlp_kernel, grid=(hidden // tile,), in_specs=[fixed, pl.Bl...]
    ppermute x10 -> x9, starting transfers between devices: 12.1 us -> 11.9 us  [rotated(): lax.ppermute(value, axis, [(i, (i + by) % count) for i in range(count)])]
  transfers between devices with their start and end apart: 40 -> 39, of which waited for: 12 -> 12; matrix products, arithmetic and copies ran while one was open for 13% -> 12% of each run, Pallas kernels for 45% -> 45%
where the time goes in v3:
time: 275 us; the launch traced here: 271 us
  Pallas kernels  123 us (45%)
  starting transfers between devices  48.9 us (18%)
  waiting for transfers between devices  29.4 us (11%)
  other arithmetic  25.6 us (9%)
  matrix products  19.3 us (7%)
  between operations  16.7 us (6%)
  local copies, waits for them, and re-layouts  7.96 us (3%)
    ppermute x29, starting transfers between devices, flipped(): return lax.ppermute(value, GRID, [(i, i ^ mask) for i in range(count)])  37 us
    ppermute x29, waiting for transfers between devices, flipped(): return lax.ppermute(value, GRID, [(i, i ^ mask) for i in range(count)])  28 us
    pallas_call x2, Pallas kernels, attention_backward(): pl.pallas_call(backward_kernel, grid=(pairs,), in_specs=[pl.BlockSpec(mem...  26.2 us
    pallas_call x3, Pallas kernels, mlp_block(): pl.pallas_call(mlp_kernel, grid=(hidden // tile,), in_specs=[fixed, pl.Bl...  24.5 us
    dot_general x3, matrix products, shards(): lax.dot_general(a, b, (((0,), (0,)), ((), ())), preferred_element_type=f32)  15 us
    pallas_call x1, Pallas kernels, local_attention(): pl.pallas_call(local_kernel, grid=(PAIRS,), in_specs=[pl.BlockSpec(memory...  13.5 us
    pallas_call x2, Pallas kernels, weight_grads(): pl.pallas_call(kernel, grid=(steps,), in_specs=in_specs, out_specs=specs,...  12.9 us
    pallas_call x1, Pallas kernels, memory_attention(): pl.pallas_call(memory_kernel, grid=(PAIRS,), in_specs=[pl.BlockSpec(memor...  12 us
  transfers between devices with their start and end apart: 39, of which 12 were waited for; matrix products, arithmetic and copies ran while one was open for 12% of the time, Pallas kernels for 45%

profile of v3, /device:TPU:0, one launch (start us, length us, event | category | flops | bytes accessed | tf_op | source)
XLA Modules:
  0.0 271.2 jit_solution(5481127814551448880)
XLA Ops:
  7.3 1.8 slice.87
  9.1 3.0 %collective-permute-start.26 = (bf16[256,768]{1,0:T(8,128)(2,1)}, bf16[256,768]{1,0:T(8,128)(2,1)}, u32[]{:S(2)}, u32[]{:S(2)}) collective-permute-start(bf16[256,768]{1,0:T(8,128)(2,1)} %slice.87), channel_id=1, source_target_pairs={{0,1},{1,0},{2,3},{3,2},{4,5},{5,4},{6,7},{7,6},{8,9},{9,8},{10,11... | collective-permute-start | bytes 1179656 | tf_op jit(solution)/shard_map/ppermute | solution.py:720
  14.3 4.3 %fusion.4.q_ref.k_ref.v_ref = bf16[512,2304]{1,0:T(8,128)(2,1)S(1)} fusion(bf16[512,768]{1,0:T(8,128)(2,1)S(1)} %fusion.10, bf16[768,2304]{1,0:T(8,128)(2,1)} %w_ref.1, f32[2304]{0:T(1024)S(1)} %pad_maximum_fusion.9), kind=kOutput, calls=%fused_computation.39 | convolution fusion | flops 1814298624 | bytes 6693888 | tf_op jit(solution)/shard_map/dot_general | solution.py:27
  19.4 13.5 %local_attention.1 = (f32[256,768]{1,0:T(8,128)}, f32[6,8,512]{2,1,0:T(8,128)}, bf16[512,768]{1,0:T(8,128)(2,1)}, f32[512,768]{1,0:T(8,128)}, bf16[512,768]{1,0:T(8,128)(2,1)}, /*index=5*/bf16[256,768]{1,0:T(8,128)(2,1)}) custom-call(s32[1,3]{1,0:T(1,128)S(1)} %copy-done.20, bf16[512,2304]{1,0:T(8,128)(2,1)S(1)} %fusion.4.q_ref.k_ref.v_ref, ...), custom_call_target="tpu_custom_call" | custom-call | flops 2415919104 | bytes 3145728 | tf_op jit(solution)/shard_map/local_attention/pallas_call | solution.py:116
  33.6 2.1 collective-permute-start.25
  36.4 4.7 %tail_projection.1 = (bf16[256,768]{1,0:T(8,128)(2,1)}, bf16[256,1536]{1,0:T(8,128)(2,1)}) custom-call(bf16[256,768]{1,0:T(8,128)(2,1)} %collective-permute-done.26.x_ref, f32[8,768]{1,0:T(8,128)S(1)} %concatenate.49.rows_ref.vb_ref, bf16[768,2304]{1,0:T(8,128)(2,1)} %w_ref.1), custom_call_target="tpu_custom_call" | custom-call | flops 603979776 | bytes 2359296 | tf_op jit(solution)/shard_map/tail_projection/pallas_call | solution.py:180
  41.7 12.0 %memory_attention.1 = (bf16[512,768]{1,0:T(8,128)(2,1)}, bf16[512,768]{1,0:T(8,128)(2,1)}, bf16[512,768]{1,0:T(8,128)(2,1)}, f32[6,8,256]{2,1,0:T(8,128)}, f32[5...) custom-call(s32[1,1]{1,0:T(1,128)S(6)} %select_n.313.reads, ...), custom_call_target="tpu_custom_call", output_to_operand_aliasing={{0}: (10, {}), {4}: (11, {}), {5}: (12, {})} | custom-call | flops 3221225472 | bytes 6291456 | tf_op jit(solution)/shard_map/memory_attention/pallas_call | solution.py:262
  53.7 2.0 collective-permute-start.28
  56.3 6.5 %mlp_block.3 = (bf16[1024,1536]{1,0:T(8,128)(2,1)}, bf16[1024,1536]{1,0:T(8,128)(2,1)}, f32[8,1536]{1,0:T(8,128)}, bf16[256,768]{1,0:T(8,128)(2,1)}, bf16[256,768]{1,0:T(8,128)(2,1)}) custom-call(bf16[256,768]{1,0:T(8,128)(2,1)} %collective-permute-done.29.x_ref, bf16[512,768]{1,0:T(8,128)(2,1)} %collective-permute-done.27.ct_ref, bf16[768,1536]{1,0:T(8,128)(2,1)} %wi_ref.5, ...), custom_call_target="tpu_custom_call" | custom-call | flops 2415919104 | bytes 7864320 | tf_op jit(solution)/shard_map/mlp_block/pallas_call | solution.py:372
  64.4 6.5 %mlp_block.4 = (bf16[1024,1536]{1,0:T(8,128)(2,1)}, bf16[1024,1536]{1,0:T(8,128)(2,1)}, f32[8,1536]{1,0:T(8,128)}, bf16[256,768]{1,0:T(8,128)(2,1)}, bf16[256,768]{1,0:T(8,128)(2,1)}) custom-call(bf16[256,768]{1,0:T(8,128)(2,1)} %collective-permute-done.28.x_ref, ...), custom_call_target="tpu_custom_call", output_to_operand_aliasing={{0}: (5, {}), {1}: (6, {})} | custom-call | flops 2415919104 | bytes 7864320 | tf_op jit(solution)/shard_map/mlp_block/pallas_call | solution.py:372
  70.9 2.5 collective-permute-start.31
  73.4 11.5 %mlp_block.5 = (bf16[1024,1536]{1,0:T(8,128)(2,1)}, bf16[1024,1536]{1,0:T(8,128)(2,1)}, f32[8,1536]{1,0:T(8,128)}, bf16[512,768]{1,0:T(8,128)(2,1)}, bf16[512,768]{1,0:T(8,128)(2,1)}) custom-call(bf16[512,768]{1,0:T(8,128)(2,1)} %get-tuple-element.259.x_ref, bf16[512,768]{1,0:T(8,128)(2,1)} %ct_ref.1, ...), custom_call_target="tpu_custom_call", output_to_operand_aliasing={{0}: (5, {}), {1}: (6, {})} | custom-call | flops 4831838208 | bytes 11010048 | tf_op jit(solution)/shard_map/mlp_block/pallas_call | solution.py:372
  85.0 6.5 %convolution_convert_fusion.1 = bf16[1536,768]{1,0:T(8,128)(2,1)} fusion(bf16[1024,1536]{1,0:T(8,128)(2,1)} %get-tuple-element.295, bf16[512,768]{1,0:T(8,128)(2,1)} %collective-permute-done.27.ct_ref, bf16[512,768]{1,0:T(8,128)(2,1)} %ct_ref.1), kind=kOutput, calls=%fused_computation.40 | convolution fusion | flops 2420244480 | bytes 7077888 | tf_op jit(solution)/shard_map/dot_general | solution.py:1018
  91.5 5.1 %convolution_convert_fusion.2 = bf16[768,1536]{1,0:T(8,128)(2,1)} fusion(bf16[1024,1536]{1,0:T(8,128)(2,1)S(1)} %copy-done.3, bf16[256,768]{1,0:T(8,128)(2,1)} %collective-permute-done.29.x_ref, bf16[256,768]{1,0:T(8,128)(2,1)} %collective-permute-done.28.x_ref, bf16[512,768]{1,0:T(8,128)(2,1)S(1)} %copy-done.26), kind=kOutput, calls=%fused_computation.41 | convolution fusion | flops 2421817344 | bytes 7077888 | tf_op jit(solution)/shard_map/dot_general | solution.py:1018
  97.3 137.7 %conditional.1 = (bf16[384,1536]{1,0:T(8,128)(2,1)}, bf16[96,1536]{1,0:T(8,128)(2,1)}, f32[12,768]{1,0:T(8,128)}, bf16[512,768]{1,0:T(8,128)(2,1)}, bf16[512,768]{1,0:T(8,128)(2,1)}) conditional(s32[]{:T(128)} %bitcast.3, () %tuple.43, (bf16[512,768]{1,0:T(8,128)(2,1)}, bf16[512,768]{1,0:T(8,128)(2,1)}, f32[512,768]{1,0:T(8,128)}, ...), branch_computations={%region_2.3_spmd, %region_3.4_spmd} | conditional | flops 16744197120 | bytes 105596568 | solution.py:1145
  97.3 4.6 %middle_backward.1 = (f32[512,768]{1,0:T(8,128)}, bf16[512,768]{1,0:T(8,128)(2,1)}, f32[8,768]{1,0:T(8,128)}) custom-call(bf16[512,768]{1,0:T(8,128)(2,1)} %get-tuple-element.70.d_ref, bf16[512,768]{1,0:T(8,128)(2,1)} %get-tuple-element.71.ct_ref, f32[512,768]{1,0:T(8,128)} %get-tuple-element.72.middle_ref, f32[8,768]{1,0:T(8,128)S(1)} %get-tuple-element.73.rows_ref, ...), custom_call_target="tpu_custom_call" | custom-call | flops 7864320 | bytes 5505024 | tf_op jit(solution)/shard_map/cond/branch_1_fun/middle_backward/pallas_call | solution.py:595
  101.9 3.4 %fusion.refs_0_ = bf16[768,768]{1,0:T(8,128)(2,1)} fusion(bf16[512,768]{1,0:T(8,128)(2,1)} %get-tuple-element.90.db_ref, bf16[512,768]{1,0:T(8,128)(2,1)} %get-tuple-element.83), kind=kOutput, calls=%fused_computation.2 | convolution fusion | flops 604569600 | bytes 2752512 | tf_op jit(solution)/shard_map/cond/branch_1_fun/dot_general | solution.py:1018
  105.3 9.5 %attention_backward.2 = (bf16[3,512,256]{2,1,0:T(8,128)(2,1)}, bf16[2,256,256]{2,1,0:T(8,128)(2,1)}, f32[8,256]{1,0:T(8,128)}) custom-call(s32[1,3]{1,0:T(1,128)S(1)} %get-tuple-element.66.lens, bf16[512,2304]{1,0:T(8,128)(2,1)S(1)} %get-tuple-element.67.q_ref.k_ref.v_ref, bf16[512,2304]{1,0:T(8,128)(2,1)S(1)} %get-tuple-element.67.q_ref.k_ref.v_ref, ...), custom_call_target="tpu_custom_call" | custom-call | flops 3758096384 | bytes 2621440 | tf_op jit(solution)/shard_map/cond/branch_1_fun/attention_backward/pallas_call | solution.py:501
  114.8 7.3 %weight_grads.2 = (bf16[384,1536]{1,0:T(8,128)(2,1)}, bf16[384,1536]{1,0:T(8,128)(2,1)}, bf16[768,512]{1,0:T(8,128)(2,1)}, bf16[768,256]{1,0:T(8,128)(2,1)}) custom-call(s32[1]{0:T(128)} %bitcast.1.side_ref, bf16[512,768]{1,0:T(8,128)(2,1)} %get-tuple-element.64.n_ref, bf16[256,768]{1,0:T(8,128)(2,1)S(1)} %copy-done.9, ...), custom_call_target="tpu_custom_call" | custom-call | flops 805306368 | bytes 1572864 | tf_op jit(solution)/shard_map/cond/branch_1_fun/weight_grads/pallas_call | solution.py:888
  122.2 3.2 %collective-permute-done.got_ref = bf16[384,1536]{1,0:T(8,128)(2,1)} collective-permute-done((bf16[384,1536]{1,0:T(8,128)(2,1)}, bf16[384,1536]{1,0:T(8,128)(2,1)}, u32[]{:S(2)}, u32[]{:S(2)}) %collective-permute-start) | collective-permute-done | bytes 1179680 | tf_op jit(solution)/shard_map/cond/branch_1_fun/ppermute | solution.py:729
  125.4 2.9 %split_sum.2 = (bf16[96,1536]{1,0:T(8,128)(2,1)}, bf16[96,1536]{1,0:T(8,128)(2,1)}, bf16[96,1536]{1,0:T(8,128)(2,1)}, bf16[96,1536]{1,0:T(8,128)(2,1)}) custom-call(s32[1]{0:T(128)} %bitcast.number_ref, bf16[384,1536]{1,0:T(8,128)(2,1)} %get-tuple-element.84.kept_ref, bf16[384,1536]{1,0:T(8,128)(2,1)} %collective-permute-done.got_ref), custom_call_target="tpu_custom_call" | custom-call | flops 1000 | bytes 1000 | tf_op jit(solution)/shard_map/cond/branch_1_fun/split_sum/pallas_call | solution.py:914
  128.3 1.7 collective-permute-start.2
  130.0 1.8 collective-permute-start.3
  131.8 16.7 %attention_backward.3 = (bf16[3,512,512]{2,1,0:T(8,128)(2,1)}, bf16[2,256,512]{2,1,0:T(8,128)(2,1)}, f32[8,512]{1,0:T(8,128)}) custom-call(s32[1,3]{1,0:T(1,128)S(1)} %get-tuple-element.66.lens, bf16[512,2304]{1,0:T(8,128)(2,1)S(1)} %get-tuple-element.67.q_ref.k_ref.v_ref, bf16[512,2304]{1,0:T(8,128)(2,1)S(1)} %get-tuple-element.67.q_ref.k_ref.v_ref, ...), custom_call_target="tpu_custom_call" | custom-call | flops 7516192768 | bytes 5242880 | tf_op jit(solution)/shard_map/cond/branch_1_fun/attention_backward/pallas_call | solution.py:501
  149.9 5.6 %weight_grads.3 = (bf16[384,1536]{1,0:T(8,128)(2,1)}, bf16[384,1536]{1,0:T(8,128)(2,1)}) custom-call(s32[1]{0:T(128)} %bitcast.1.side_ref, bf16[768,512]{1,0:T(8,128)(2,1)} %get-tuple-element.112.n_ref, bf16[768,256]{1,0:T(8,128)(2,1)} %get-tuple-element.113.nt_ref, bf16[3,512,512]{2,1,0:T(8,128)(2,1)} %get-tuple-element.126.d_ref.two_ref, ...), custom_call_target="tpu_custom_call" | custom-call | flops 1610612736 | bytes 3145728 | tf_op jit(solution)/shard_map/cond/branch_1_fun/weight_grads/pallas_call | solution.py:888
  155.5 1.7 collective-permute-start.4
  159.6 2.8 %split_sum.3 = (bf16[96,1536]{1,0:T(8,128)(2,1)}, bf16[96,1536]{1,0:T(8,128)(2,1)}, bf16[96,1536]{1,0:T(8,128)(2,1)}, bf16[96,1536]{1,0:T(8,128)(2,1)}) custom-call(s32[1]{0:T(128)} %bitcast.number_ref, bf16[384,1536]{1,0:T(8,128)(2,1)} %get-tuple-element.114.kept_ref, bf16[384,1536]{1,0:T(8,128)(2,1)} %copy-done.4), custom_call_target="tpu_custom_call" | custom-call | flops 1000 | bytes 1000 | tf_op jit(solution)/shard_map/cond/branch_1_fun/split_sum/pallas_call | solution.py:914
  162.6 2.0 collective-permute-start.8
  166.1 2.6 collective-permute-start.6
  168.7 8.4 %qkv_backward.1 = (f32[512,768]{1,0:T(8,128)}, bf16[256,768]{1,0:T(8,128)(2,1)}, f32[8,768]{1,0:T(8,128)}) custom-call(bf16[3,512,256]{2,1,0:T(8,128)(2,1)} %get-tuple-element.125.d_ref.one_ref, bf16[3,512,512]{2,1,0:T(8,128)(2,1)} %get-tuple-element.126.d_ref.two_ref, bf16[2,256,256]{2,1,0:T(8,128)(2,1)} %get-tuple-element.127.dt_ref.t_one_ref, ...), custom_call_target="tpu_custom_call" | custom-call | flops 2415919104 | bytes 7864320 | tf_op jit(solution)/shard_map/cond/branch_1_fun/qkv_backward/pallas_call | solution.py:641
  177.5 6.3 %collective-permute-done.9 = bf16[96,1536]{1,0:T(8,128)(2,1)S(1)} collective-permute-done((bf16[96,1536]{1,0:T(8,128)(2,1)}, bf16[96,1536]{1,0:T(8,128)(2,1)S(1)}, u32[]{:S(2)}, u32[]{:S(2)}) %collective-permute-start.9) | collective-permute-done | bytes 294944 | tf_op jit(solution)/shard_map/cond/branch_1_fun/ppermute | solution.py:729
  187.7 2.8 %collective-permute-start.10 = (bf16[24,1536]{1,0:T(8,128)(2,1)S(1)}, bf16[24,1536]{1,0:T(8,128)(2,1)S(1)}, u32[]{:S(2)}, u32[]{:S(2)}) collective-permute-start(bf16[24,1536]{1,0:T(8,128)(2,1)S(1)} %add_convert_fusion.6), channel_id=1, source_target_pairs={{0,16},{1,17},{2,18},{3,19},{4,20},{5,21},{6,22},{7,23},{8,24},{9,... | collective-permute-start | bytes 221192 | tf_op jit(solution)/shard_map/cond/branch_1_fun/ppermute | solution.py:729
  190.5 1.7 collective-permute-start.24
  192.3 2.6 collective-permute-start.13
  195.0 2.1 collective-permute-done.10
  198.1 2.2 collective-permute-start.18
  202.7 4.5 %collective-permute-done.12 = bf16[48,1536]{1,0:T(8,128)(2,1)S(1)} collective-permute-done((bf16[48,1536]{1,0:T(8,128)(2,1)S(1)}, bf16[48,1536]{1,0:T(8,128)(2,1)S(1)}, u32[]{:S(2)}, u32[]{:S(2)}) %collective-permute-start.12) | collective-permute-done | bytes 147488 | tf_op jit(solution)/shard_map/cond/branch_1_fun/ppermute | solution.py:729
  208.0 3.6 %collective-permute-start.15 = (bf16[96,1536]{1,0:T(8,128)(2,1)}, bf16[96,1536]{1,0:T(8,128)(2,1)S(1)}, u32[]{:S(2)}, u32[]{:S(2)}) collective-permute-start(bf16[96,1536]{1,0:T(8,128)(2,1)} %pad_maximum_fusion.2), channel_id=1, source_target_pairs={{0,1},{1,0},{2,3},{3,2},{4,5},{5,4},{6,7},{7,6},{8,9},{9,8},{10,11... | collective-permute-start | bytes 884744 | tf_op jit(solution)/shard_map/cond/branch_1_fun/ppermute | solution.py:729
  211.6 5.0 %collective-permute-done.18 = f32[12,768]{1,0:T(8,128)S(1)} collective-permute-done((f32[12,768]{1,0:T(8,128)S(1)}, f32[12,768]{1,0:T(8,128)S(1)}, u32[]{:S(2)}, u32[]{:S(2)}) %collective-permute-start.18) | collective-permute-done | bytes 36896 | tf_op jit(solution)/shard_map/cond/branch_1_fun/ppermute | solution.py:729
  220.2 3.5 %input_backward.1 = bf16[512,768]{1,0:T(8,128)(2,1)} custom-call(f32[512,768]{1,0:T(8,128)} %get-tuple-element.160.dn_ref, bf16[256,768]{1,0:T(8,128)(2,1)} %copy-done.6, bf16[512,768]{1,0:T(8,128)(2,1)S(1)} %get-tuple-element.130.x_ref, f32[512,768]{1,0:T(8,128)} %get-tuple-element.162.dm_ref, f32[8,768]{1,0:T(8,128)} %copy-done.5), custom_call_target="tpu_custom_call" | custom-call | flops 7864320 | bytes 4718592 | tf_op jit(solution)/shard_map/cond/branch_1_fun/input_backward/pallas_call | solution.py:675
  225.1 1.9 collective-permute-done.19
  228.3 2.5 add_convert_fusion
  235.0 1.9 collective-permute-start.32
  238.5 2.7 %collective-permute-start.35 = (f32[12,768]{1,0:T(8,128)}, f32[12,768]{1,0:T(8,128)S(1)}, u32[]{:S(2)}, u32[]{:S(2)}) collective-permute-start(f32[12,768]{1,0:T(8,128)} %get-tuple-element.293), channel_id=1, source_target_pairs={{0,16},{1,17},{2,18},{3,19},{4,20},{5,21},{6,22},{7,23},{8,24},{9,... | collective-permute-start | bytes 110600 | tf_op jit(solution)/shard_map/ppermute | solution.py:729
  241.2 2.5 collective-permute-done.35
  246.5 6.7 %widened.1 = (f32[768,1536]{1,0:T(8,128)}, f32[1536,768]{1,0:T(8,128)}) custom-call(bf16[768,1536]{1,0:T(8,128)(2,1)} %get-tuple-element.322.a_ref, bf16[1536,768]{1,0:T(8,128)(2,1)} %get-tuple-element.323.b_ref), custom_call_target="tpu_custom_call" | custom-call | bytes 14155776 | tf_op jit(solution)/shard_map/widened/pallas_call | solution.py:705
  258.6 1.7 broadcast_select_fusion.8
  260.6 3.5 %convert_element_type.157 = f32[768,2304]{1,0:T(8,128)} convert(bf16[768,2304]{1,0:T(8,128)(2,1)S(1)} %fusion.24) | non-fusion elementwise | flops 1769472 | bytes 10616832 | tf_op jit(solution)/shard_map/convert_element_type | solution.py:1189
  (187 shorter events, 39.6 us)
Async XLA Ops:
  7.2 239.3 %all-reduce.3.cloned.1.call-start = ((), (), s32[]{:S(2)}) async-start(), calls=%async_computation | async-start | bytes 9437184 | tf_op jit(solution)/shard_map/psum | solution.py:1035
  9.1 27.3 %collective-permute-start.26 = (bf16[256,768]{1,0:T(8,128)(2,1)}, bf16[256,768]{1,0:T(8,128)(2,1)}, u32[]{:S(2)}, u32[]{:S(2)}) collective-permute-start(bf16[256,768]{1,0:T(8,128)(2,1)} %slice.87), channel_id=1, source_target_pairs={{0,1},{1,0},{2,3},{3,2},{4,5},{5,4},{6,7},{7,6},{8,9},{9,8},{10,11... | collective-permute-start | bytes 1179656 | tf_op jit(solution)/shard_map/ppermute | solution.py:720
  12.1 29.0 %collective-permute-start.27 = (bf16[512,768]{1,0:T(8,128)(2,1)}, bf16[512,768]{1,0:T(8,128)(2,1)}, u32[]{:S(2)}, u32[]{:S(2)}) collective-permute-start(bf16[512,768]{1,0:T(8,128)(2,1)} %ct_ref.1), channel_id=1, source_target_pairs={{0,1},{1,0},{2,3},{3,2},{4,5},{5,4},{6,7},{7,6},{8,9},{9,8},{10,11... | collective-permute-start | bytes 2359304 | tf_op jit(solution)/shard_map/ppermute | solution.py:720
  33.6 7.5 %collective-permute-start.25 = (bf16[16,128]{1,0:T(8,128)(2,1)S(1)}, bf16[16,128]{1,0:T(8,128)(2,1)S(1)}, u32[]{:S(2)}, u32[]{:S(2)}) collective-permute-start(bf16[16,128]{1,0:T(8,128)(2,1)S(1)} %broadcast_in_dim.33), channel_id=1, source_target_pairs={{0,1},{1,0},{2,3},{3,2},{4,5},{5,4},{6,7},{7,6},{8,9},{9,8},{10,11... | collective-permute-start | bytes 12296 | tf_op jit(solution)/shard_map/ppermute | solution.py:720
  35.6 20.1 %collective-permute-start.29 = (bf16[256,768]{1,0:T(8,128)(2,1)}, bf16[256,768]{1,0:T(8,128)(2,1)}, u32[]{:S(2)}, u32[]{:S(2)}) collective-permute-start(bf16[256,768]{1,0:T(8,128)(2,1)} %get-tuple-element.263), channel_id=1, source_target_pairs={{0,1},{1,0},{2,3},{3,2},{4,5},{5,4},{6,7},{7,6},{8,9},{9,8},{10,11... | collective-permute-start | bytes 1179656 | tf_op jit(solution)/shard_map/ppermute | solution.py:720
  41.7 14.0 %copy-start.21 = (bf16[1536]{0:T(1024)(128)(2,1)S(1)}, bf16[1536]{0:T(1024)(128)(2,1)}, u32[]{:S(2)}) copy-start(bf16[1536]{0:T(1024)(128)(2,1)} %param.28) | copy-start | bytes 9220
  53.7 10.7 %collective-permute-start.28 = (bf16[256,768]{1,0:T(8,128)(2,1)}, bf16[256,768]{1,0:T(8,128)(2,1)}, u32[]{:S(2)}, u32[]{:S(2)}) collective-permute-start(bf16[256,768]{1,0:T(8,128)(2,1)} %get-tuple-element.260), channel_id=1, source_target_pairs={{0,1},{1,0},{2,3},{3,2},{4,5},{5,4},{6,7},{7,6},{8,9},{9,8},{10,11... | collective-permute-start | bytes 1179656 | tf_op jit(solution)/shard_map/ppermute | solution.py:720
  62.8 22.1 %collective-permute-start.30 = (bf16[256,768]{1,0:T(8,128)(2,1)}, bf16[256,768]{1,0:T(8,128)(2,1)}, u32[]{:S(2)}, u32[]{:S(2)}) collective-permute-start(bf16[256,768]{1,0:T(8,128)(2,1)} %get-tuple-element.273), channel_id=1, source_target_pairs={{0,1},{1,0},{2,3},{3,2},{4,5},{5,4},{6,7},{7,6},{8,9},{9,8},{10,11... | collective-permute-start | bytes 1179656 | tf_op jit(solution)/shard_map/ppermute | solution.py:720
  70.9 14.0 %collective-permute-start.31 = (bf16[256,768]{1,0:T(8,128)(2,1)}, bf16[256,768]{1,0:T(8,128)(2,1)}, u32[]{:S(2)}, u32[]{:S(2)}) collective-permute-start(bf16[256,768]{1,0:T(8,128)(2,1)} %get-tuple-element.274), channel_id=1, source_target_pairs={{0,1},{1,0},{2,3},{3,2},{4,5},{5,4},{6,7},{7,6},{8,9},{9,8},{10,11... | collective-permute-start | bytes 1179656 | tf_op jit(solution)/shard_map/ppermute | solution.py:720
  105.3 9.5 %copy-start.9 = (bf16[256,768]{1,0:T(8,128)(2,1)S(1)}, bf16[256,768]{1,0:T(8,128)(2,1)}, u32[]{:S(2)}) copy-start(bf16[256,768]{1,0:T(8,128)(2,1)} %get-tuple-element.65.nt_ref) | copy-start | bytes 1179652 | tf_op jit(solution)/shard_map/cond
  122.1 9.7 %copy-start.28 = (f32[6,8,512]{2,1,0:T(8,128)S(1)}, f32[6,8,512]{2,1,0:T(8,128)}, u32[]{:S(2)}) copy-start(f32[6,8,512]{2,1,0:T(8,128)} %get-tuple-element.78.ll_ref) | copy-start | bytes 294916 | tf_op jit(solution)/shard_map/cond
  122.1 3.3 %collective-permute-start = (bf16[384,1536]{1,0:T(8,128)(2,1)}, bf16[384,1536]{1,0:T(8,128)(2,1)}, u32[]{:S(2)}, u32[]{:S(2)}) collective-permute-start(bf16[384,1536]{1,0:T(8,128)(2,1)} %get-tuple-element.85), channel_id=1, source_target_pairs={{0,2},{1,3},{2,0},{3,1},{4,6},{5,7},{6,4},{7,5},{8,10},{9,11},{10,... | collective-permute-start | bytes 3538952 | tf_op jit(solution)/shard_map/cond/branch_1_fun/ppermute | solution.py:729
  128.3 20.3 %copy-start.12 = (bf16[96,1536]{1,0:T(8,128)(2,1)S(1)}, bf16[96,1536]{1,0:T(8,128)(2,1)}, u32[]{:S(2)}) copy-start(bf16[96,1536]{1,0:T(8,128)(2,1)} %get-tuple-element.86) | copy-start | bytes 884740 | tf_op jit(solution)/shard_map/cond
  128.3 20.2 %collective-permute-start.1 = (bf16[96,1536]{1,0:T(8,128)(2,1)}, bf16[96,1536]{1,0:T(8,128)(2,1)}, u32[]{:S(2)}, u32[]{:S(2)}) collective-permute-start(bf16[96,1536]{1,0:T(8,128)(2,1)} %get-tuple-element.93), channel_id=1, source_target_pairs={{0,1},{1,0},{2,3},{3,2},{4,5},{5,4},{6,7},{7,6},{8,9},{9,8},{10,11... | collective-permute-start | bytes 884744 | tf_op jit(solution)/shard_map/cond/branch_1_fun/ppermute | solution.py:729
  128.3 20.2 %collective-permute-start.2 = (bf16[96,1536]{1,0:T(8,128)(2,1)}, bf16[96,1536]{1,0:T(8,128)(2,1)}, u32[]{:S(2)}, u32[]{:S(2)}) collective-permute-start(bf16[96,1536]{1,0:T(8,128)(2,1)} %get-tuple-element.94), channel_id=1, source_target_pairs={{0,4},{1,5},{2,6},{3,7},{4,0},{5,1},{6,2},{7,3},{8,12},{9,13},{10,... | collective-permute-start | bytes 884744 | tf_op jit(solution)/shard_map/cond/branch_1_fun/ppermute | solution.py:729
  130.0 18.5 %collective-permute-start.3 = (bf16[96,1536]{1,0:T(8,128)(2,1)}, bf16[96,1536]{1,0:T(8,128)(2,1)}, u32[]{:S(2)}, u32[]{:S(2)}) collective-permute-start(bf16[96,1536]{1,0:T(8,128)(2,1)} %get-tuple-element.95), channel_id=1, source_target_pairs={{0,5},{1,4},{2,7},{3,6},{4,1},{5,0},{6,3},{7,2},{8,13},{9,12},{10,... | collective-permute-start | bytes 884744 | tf_op jit(solution)/shard_map/cond/branch_1_fun/ppermute | solution.py:729
  155.5 3.1 %collective-permute-start.5 = (bf16[384,1536]{1,0:T(8,128)(2,1)}, bf16[384,1536]{1,0:T(8,128)(2,1)S(1)}, u32[]{:S(2)}, u32[]{:S(2)}) collective-permute-start(bf16[384,1536]{1,0:T(8,128)(2,1)} %get-tuple-element.115), channel_id=1, source_target_pairs={{0,2},{1,3},{2,0},{3,1},{4,6},{5,7},{6,4},{7,5},{8,10},{9,11},{10,... | collective-permute-start | bytes 3538952 | tf_op jit(solution)/shard_map/cond/branch_1_fun/ppermute | solution.py:729
  155.5 10.6 %collective-permute-start.4 = (bf16[48,1536]{1,0:T(8,128)(2,1)S(1)}, bf16[48,1536]{1,0:T(8,128)(2,1)S(1)}, u32[]{:S(2)}, u32[]{:S(2)}) collective-permute-start(bf16[48,1536]{1,0:T(8,128)(2,1)S(1)} %constant_dynamic-slice_fusion.3), channel_id=1, source_target_pairs={{0,8},{1,9},{2,10},{3,11},{4,12},{5,13},{6,14},{7,15},{8,0},{9,1},... | collective-permute-start | bytes 442376 | tf_op jit(solution)/shard_map/cond/branch_1_fun/ppermute | solution.py:729
  162.4 15.1 %collective-permute-start.7 = (bf16[96,1536]{1,0:T(8,128)(2,1)}, bf16[96,1536]{1,0:T(8,128)(2,1)S(1)}, u32[]{:S(2)}, u32[]{:S(2)}) collective-permute-start(bf16[96,1536]{1,0:T(8,128)(2,1)} %get-tuple-element.119), channel_id=1, source_target_pairs={{0,1},{1,0},{2,3},{3,2},{4,5},{5,4},{6,7},{7,6},{8,9},{9,8},{10,11... | collective-permute-start | bytes 884744 | tf_op jit(solution)/shard_map/cond/branch_1_fun/ppermute | solution.py:729
  162.6 14.8 %collective-permute-start.8 = (bf16[96,1536]{1,0:T(8,128)(2,1)}, bf16[96,1536]{1,0:T(8,128)(2,1)S(1)}, u32[]{:S(2)}, u32[]{:S(2)}) collective-permute-start(bf16[96,1536]{1,0:T(8,128)(2,1)} %get-tuple-element.120), channel_id=1, source_target_pairs={{0,4},{1,5},{2,6},{3,7},{4,0},{5,1},{6,2},{7,3},{8,12},{9,13},{10,... | collective-permute-start | bytes 884744 | tf_op jit(solution)/shard_map/cond/branch_1_fun/ppermute | solution.py:729
  164.6 19.2 %collective-permute-start.9 = (bf16[96,1536]{1,0:T(8,128)(2,1)}, bf16[96,1536]{1,0:T(8,128)(2,1)S(1)}, u32[]{:S(2)}, u32[]{:S(2)}) collective-permute-start(bf16[96,1536]{1,0:T(8,128)(2,1)} %get-tuple-element.121), channel_id=1, source_target_pairs={{0,5},{1,4},{2,7},{3,6},{4,1},{5,0},{6,3},{7,2},{8,13},{9,12},{10,... | collective-permute-start | bytes 884744 | tf_op jit(solution)/shard_map/cond/branch_1_fun/ppermute | solution.py:729
  166.1 11.3 %collective-permute-start.6 = (bf16[24,1536]{1,0:T(8,128)(2,1)S(1)}, bf16[24,1536]{1,0:T(8,128)(2,1)S(1)}, u32[]{:S(2)}, u32[]{:S(2)}) collective-permute-start(bf16[24,1536]{1,0:T(8,128)(2,1)S(1)} %constant_dynamic-slice_fusion.2), channel_id=1, source_target_pairs={{0,16},{1,17},{2,18},{3,19},{4,20},{5,21},{6,22},{7,23},{8,24},{9,... | collective-permute-start | bytes 221192 | tf_op jit(solution)/shard_map/cond/branch_1_fun/ppermute | solution.py:729
  168.7 15.1 %copy-start.11 = (bf16[96,1536]{1,0:T(8,128)(2,1)S(1)}, bf16[96,1536]{1,0:T(8,128)(2,1)}, u32[]{:S(2)}) copy-start(bf16[96,1536]{1,0:T(8,128)(2,1)} %get-tuple-element.136) | copy-start | bytes 884740 | tf_op jit(solution)/shard_map/cond
  177.1 8.5 %copy-start.7 = (bf16[256,768]{1,0:T(8,128)(2,1)S(1)}, bf16[256,768]{1,0:T(8,128)(2,1)}, u32[]{:S(2)}) copy-start(bf16[256,768]{1,0:T(8,128)(2,1)} %get-tuple-element.156) | copy-start | bytes 1179652 | tf_op jit(solution)/shard_map/cond
  177.1 8.5 %copy-start.8 = (bf16[256,768]{1,0:T(8,128)(2,1)S(1)}, bf16[256,768]{1,0:T(8,128)(2,1)}, u32[]{:S(2)}) copy-start(bf16[256,768]{1,0:T(8,128)(2,1)} %get-tuple-element.155) | copy-start | bytes 1179652 | tf_op jit(solution)/shard_map/cond
  184.0 8.3 %collective-permute-start.11 = (bf16[48,1536]{1,0:T(8,128)(2,1)S(1)}, bf16[48,1536]{1,0:T(8,128)(2,1)S(1)}, u32[]{:S(2)}, u32[]{:S(2)}) collective-permute-start(bf16[48,1536]{1,0:T(8,128)(2,1)S(1)} %constant_dynamic-slice_fusion.1), channel_id=1, source_target_pairs={{0,8},{1,9},{2,10},{3,11},{4,12},{5,13},{6,14},{7,15},{8,0},{9,1},... | collective-permute-start | bytes 442376 | tf_op jit(solution)/shard_map/cond/branch_1_fun/ppermute | solution.py:729
  186.5 37.2 %collective-permute-start.21 = (bf16[512,768]{1,0:T(8,128)(2,1)}, bf16[512,768]{1,0:T(8,128)(2,1)}, u32[]{:S(2)}, u32[]{:S(2)}) collective-permute-start(bf16[512,768]{1,0:T(8,128)(2,1)} %pad_maximum_fusion.1), channel_id=1, source_target_pairs={{0,1},{1,0},{2,3},{3,2},{4,5},{5,4},{6,7},{7,6},{8,9},{9,8},{10,11... | collective-permute-start | bytes 2359304 | tf_op jit(solution)/shard_map/cond/branch_1_fun/ppermute | solution.py:720
  187.6 10.5 %collective-permute-start.14 = (f32[12,768]{1,0:T(8,128)S(1)}, f32[12,768]{1,0:T(8,128)S(1)}, u32[]{:S(2)}, u32[]{:S(2)}) collective-permute-start(f32[12,768]{1,0:T(8,128)S(1)} %fusion.2), channel_id=1, source_target_pairs={{0,2},{1,3},{2,0},{3,1},{4,6},{5,7},{6,4},{7,5},{8,10},{9,11},{10,... | collective-permute-start | bytes 110600 | tf_op jit(solution)/shard_map/cond/branch_1_fun/ppermute | solution.py:729
  187.7 9.4 %collective-permute-start.10 = (bf16[24,1536]{1,0:T(8,128)(2,1)S(1)}, bf16[24,1536]{1,0:T(8,128)(2,1)S(1)}, u32[]{:S(2)}, u32[]{:S(2)}) collective-permute-start(bf16[24,1536]{1,0:T(8,128)(2,1)S(1)} %add_convert_fusion.6), channel_id=1, source_target_pairs={{0,16},{1,17},{2,18},{3,19},{4,20},{5,21},{6,22},{7,23},{8,24},{9,... | collective-permute-start | bytes 221192 | tf_op jit(solution)/shard_map/cond/branch_1_fun/ppermute | solution.py:729
  190.5 28.8 %collective-permute-start.24 = (bf16[256,768]{1,0:T(8,128)(2,1)S(1)}, bf16[256,768]{1,0:T(8,128)(2,1)S(1)}, u32[]{:S(2)}, u32[]{:S(2)}) collective-permute-start(bf16[256,768]{1,0:T(8,128)(2,1)S(1)} %copy-done.27), channel_id=1, source_target_pairs={{0,1},{1,0},{2,3},{3,2},{4,5},{5,4},{6,7},{7,6},{8,9},{9,8},{10,11... | collective-permute-start | bytes 1179656 | tf_op jit(solution)/shard_map/cond/branch_1_fun/ppermute | solution.py:720
  192.3 8.7 %collective-permute-start.13 = (bf16[24,1536]{1,0:T(8,128)(2,1)S(1)}, bf16[24,1536]{1,0:T(8,128)(2,1)S(1)}, u32[]{:S(2)}, u32[]{:S(2)}) collective-permute-start(bf16[24,1536]{1,0:T(8,128)(2,1)S(1)} %constant_dynamic-slice_fusion), channel_id=1, source_target_pairs={{0,16},{1,17},{2,18},{3,19},{4,20},{5,21},{6,22},{7,23},{8,24},{9,... | collective-permute-start | bytes 221192 | tf_op jit(solution)/shard_map/cond/branch_1_fun/ppermute | solution.py:729
  197.2 10.0 %collective-permute-start.12 = (bf16[48,1536]{1,0:T(8,128)(2,1)S(1)}, bf16[48,1536]{1,0:T(8,128)(2,1)S(1)}, u32[]{:S(2)}, u32[]{:S(2)}) collective-permute-start(bf16[48,1536]{1,0:T(8,128)(2,1)S(1)} %pad_maximum_fusion.4), channel_id=1, source_target_pairs={{0,8},{1,9},{2,10},{3,11},{4,12},{5,13},{6,14},{7,15},{8,0},{9,1},... | collective-permute-start | bytes 442376 | tf_op jit(solution)/shard_map/cond/branch_1_fun/ppermute | solution.py:729
  198.1 18.6 %collective-permute-start.18 = (f32[12,768]{1,0:T(8,128)S(1)}, f32[12,768]{1,0:T(8,128)S(1)}, u32[]{:S(2)}, u32[]{:S(2)}) collective-permute-start(f32[12,768]{1,0:T(8,128)S(1)} %add.132), channel_id=1, source_target_pairs={{0,1},{1,0},{2,3},{3,2},{4,5},{5,4},{6,7},{7,6},{8,9},{9,8},{10,11... | collective-permute-start | bytes 110600 | tf_op jit(solution)/shard_map/cond/branch_1_fun/ppermute | solution.py:729
  201.1 19.1 %copy-start.10 = (bf16[24,1536]{1,0:T(8,128)(2,1)}, bf16[24,1536]{1,0:T(8,128)(2,1)S(1)}, u32[]{:S(2)}) copy-start(bf16[24,1536]{1,0:T(8,128)(2,1)S(1)} %add_convert_fusion.5) | copy-start | bytes 221188 | tf_op jit(solution)/shard_map/cond
  201.1 17.1 %collective-permute-start.20 = (bf16[24,1536]{1,0:T(8,128)(2,1)S(1)}, bf16[24,1536]{1,0:T(8,128)(2,1)S(1)}, u32[]{:S(2)}, u32[]{:S(2)}) collective-permute-start(bf16[24,1536]{1,0:T(8,128)(2,1)S(1)} %add_convert_fusion.5), channel_id=1, source_target_pairs={{0,16},{1,17},{2,18},{3,19},{4,20},{5,21},{6,22},{7,23},{8,24},{9,... | collective-permute-start | bytes 221192 | tf_op jit(solution)/shard_map/cond/branch_1_fun/ppermute | solution.py:729
  208.0 25.2 %collective-permute-start.15 = (bf16[96,1536]{1,0:T(8,128)(2,1)}, bf16[96,1536]{1,0:T(8,128)(2,1)S(1)}, u32[]{:S(2)}, u32[]{:S(2)}) collective-permute-start(bf16[96,1536]{1,0:T(8,128)(2,1)} %pad_maximum_fusion.2), channel_id=1, source_target_pairs={{0,1},{1,0},{2,3},{3,2},{4,5},{5,4},{6,7},{7,6},{8,9},{9,8},{10,11... | collective-permute-start | bytes 884744 | tf_op jit(solution)/shard_map/cond/branch_1_fun/ppermute | solution.py:729
  216.6 16.5 %collective-permute-start.16 = (bf16[96,1536]{1,0:T(8,128)(2,1)}, bf16[96,1536]{1,0:T(8,128)(2,1)S(1)}, u32[]{:S(2)}, u32[]{:S(2)}) collective-permute-start(bf16[96,1536]{1,0:T(8,128)(2,1)} %pad_maximum_fusion.2), channel_id=1, source_target_pairs={{0,4},{1,5},{2,6},{3,7},{4,0},{5,1},{6,2},{7,3},{8,12},{9,13},{10,... | collective-permute-start | bytes 884744 | tf_op jit(solution)/shard_map/cond/branch_1_fun/ppermute | solution.py:729
  218.2 8.9 %collective-permute-start.19 = (f32[12,768]{1,0:T(8,128)}, f32[12,768]{1,0:T(8,128)}, u32[]{:S(2)}, u32[]{:S(2)}) collective-permute-start(f32[12,768]{1,0:T(8,128)} %add.134), channel_id=1, source_target_pairs={{0,4},{1,5},{2,6},{3,7},{4,0},{5,1},{6,2},{7,3},{8,12},{9,13},{10,... | collective-permute-start | bytes 110600 | tf_op jit(solution)/shard_map/cond/branch_1_fun/ppermute | solution.py:729
  219.3 13.9 %collective-permute-start.17 = (bf16[96,1536]{1,0:T(8,128)(2,1)}, bf16[96,1536]{1,0:T(8,128)(2,1)S(1)}, u32[]{:S(2)}, u32[]{:S(2)}) collective-permute-start(bf16[96,1536]{1,0:T(8,128)(2,1)} %pad_maximum_fusion.2), channel_id=1, source_target_pairs={{0,5},{1,4},{2,7},{3,6},{4,1},{5,0},{6,3},{7,2},{8,13},{9,12},{10,... | collective-permute-start | bytes 884744 | tf_op jit(solution)/shard_map/cond/branch_1_fun/ppermute | solution.py:729
  220.2 8.1 %copy-start.1 = (f32[512,768]{1,0:T(8,128)S(1)}, f32[512,768]{1,0:T(8,128)}, u32[]{:S(2)}) copy-start(f32[512,768]{1,0:T(8,128)} %get-tuple-element.72.middle_ref) | copy-start | bytes 4718596 | tf_op jit(solution)/shard_map/cond
  224.7 7.0 %collective-permute-start.23 = (bf16[48,1536]{1,0:T(8,128)(2,1)S(1)}, bf16[48,1536]{1,0:T(8,128)(2,1)S(1)}, u32[]{:S(2)}, u32[]{:S(2)}) collective-permute-start(bf16[48,1536]{1,0:T(8,128)(2,1)S(1)} %pad_maximum_fusion.5), channel_id=1, source_target_pairs={{0,8},{1,9},{2,10},{3,11},{4,12},{5,13},{6,14},{7,15},{8,0},{9,1},... | collective-permute-start | bytes 442376 | tf_op jit(solution)/shard_map/cond/branch_1_fun/ppermute | solution.py:729
  227.9 4.6 %collective-permute-start.22 = (f32[12,768]{1,0:T(8,128)S(1)}, f32[12,768]{1,0:T(8,128)S(1)}, u32[]{:S(2)}, u32[]{:S(2)}) collective-permute-start(f32[12,768]{1,0:T(8,128)S(1)} %add.135), channel_id=1, source_target_pairs={{0,8},{1,9},{2,10},{3,11},{4,12},{5,13},{6,14},{7,15},{8,0},{9,1},... | collective-permute-start | bytes 110600 | tf_op jit(solution)/shard_map/cond/branch_1_fun/ppermute | solution.py:729
  235.0 18.3 %collective-permute-start.32 = (bf16[96,1536]{1,0:T(8,128)(2,1)}, bf16[96,1536]{1,0:T(8,128)(2,1)S(1)}, u32[]{:S(2)}, u32[]{:S(2)}) collective-permute-start(bf16[96,1536]{1,0:T(8,128)(2,1)} %get-tuple-element.292), channel_id=1, source_target_pairs={{0,1},{1,0},{2,3},{3,2},{4,5},{5,4},{6,7},{7,6},{8,9},{9,8},{10,11... | collective-permute-start | bytes 884744 | tf_op jit(solution)/shard_map/ppermute | solution.py:729
  236.8 16.4 %collective-permute-start.33 = (bf16[96,1536]{1,0:T(8,128)(2,1)}, bf16[96,1536]{1,0:T(8,128)(2,1)S(1)}, u32[]{:S(2)}, u32[]{:S(2)}) collective-permute-start(bf16[96,1536]{1,0:T(8,128)(2,1)} %get-tuple-element.292), channel_id=1, source_target_pairs={{0,4},{1,5},{2,6},{3,7},{4,0},{5,1},{6,2},{7,3},{8,12},{9,13},{10,... | collective-permute-start | bytes 884744 | tf_op jit(solution)/shard_map/ppermute | solution.py:729
  238.2 15.1 %collective-permute-start.34 = (bf16[96,1536]{1,0:T(8,128)(2,1)}, bf16[96,1536]{1,0:T(8,128)(2,1)S(1)}, u32[]{:S(2)}, u32[]{:S(2)}) collective-permute-start(bf16[96,1536]{1,0:T(8,128)(2,1)} %get-tuple-element.292), channel_id=1, source_target_pairs={{0,5},{1,4},{2,7},{3,6},{4,1},{5,0},{6,3},{7,2},{8,13},{9,12},{10,... | collective-permute-start | bytes 884744 | tf_op jit(solution)/shard_map/ppermute | solution.py:729
  238.5 5.2 %collective-permute-start.35 = (f32[12,768]{1,0:T(8,128)}, f32[12,768]{1,0:T(8,128)S(1)}, u32[]{:S(2)}, u32[]{:S(2)}) collective-permute-start(f32[12,768]{1,0:T(8,128)} %get-tuple-element.293), channel_id=1, source_target_pairs={{0,16},{1,17},{2,18},{3,19},{4,20},{5,21},{6,22},{7,23},{8,24},{9,... | collective-permute-start | bytes 110600 | tf_op jit(solution)/shard_map/ppermute | solution.py:729
  241.2 14.2 %collective-permute-start.36 = (bf16[384,1536]{1,0:T(8,128)(2,1)}, bf16[384,1536]{1,0:T(8,128)(2,1)S(1)}, u32[]{:S(2)}, u32[]{:S(2)}) collective-permute-start(bf16[384,1536]{1,0:T(8,128)(2,1)} %get-tuple-element.300), channel_id=1, source_target_pairs={{0,2},{1,3},{2,0},{3,1},{4,6},{5,7},{6,4},{7,5},{8,10},{9,11},{10,... | collective-permute-start | bytes 3538952 | tf_op jit(solution)/shard_map/ppermute | solution.py:729
  255.4 3.2 %collective-permute-start.37 = (bf16[384,1536]{1,0:T(8,128)(2,1)}, bf16[384,1536]{1,0:T(8,128)(2,1)}, u32[]{:S(2)}, u32[]{:S(2)}) collective-permute-start(bf16[384,1536]{1,0:T(8,128)(2,1)} %pad_maximum_fusion.7), channel_id=1, source_target_pairs={{0,2},{1,3},{2,0},{3,1},{4,6},{5,7},{6,4},{7,5},{8,10},{9,11},{10,... | collective-permute-start | bytes 3538952 | tf_op jit(solution)/shard_map/ppermute | solution.py:729
  (21 other events, 92.9 us)
Sparse Core Ops, SparseCore 0:
  96.7 135.0 all-reduce.2

commit v4 on v3

--- a/solution.py
+++ b/solution.py
@@ -195,7 +195,7 @@
 
 def memory_kernel(
     reads,
-    last_ref,
+    tail_lengths,
     q_ref,
     kt_ref,
     vt_ref,
@@ -223,7 +223,7 @@
 
     @pl.when(step == 0)
     def _():
-        last_len = last_ref[0:1, 0:1]
+        last_len = tail_lengths[0, NDOC - 1].astype(f32)
         basis[...] = basis_rows(last_len, False).astype(bf16)
         basis_t_ref[...] = basis_rows(last_len, True).astype(bf16)
         acc[...] = jnp.zeros_like(acc)
@@ -255,7 +255,7 @@
 
 
 def memory_attention(
-    reads, last_rows, qkv, tail_kv, value_bias, local, attn_out, inputs, rows, mixture, middle, normed
+    reads, tail_lengths, qkv, tail_kv, value_bias, local, attn_out, inputs, rows, mixture, middle, normed
 ):
     whole = lambda shape: pl.BlockSpec(shape, lambda i: (0,) * len(shape))
     untouched = pl.BlockSpec(memory_space=pl.ANY)
@@ -264,7 +264,7 @@
         grid=(PAIRS,),
         in_specs=[
             pl.BlockSpec(memory_space=pltpu.SMEM),
-            whole((16, LANES)),
+            pl.BlockSpec(memory_space=pltpu.SMEM),
             pl.BlockSpec((HALF, LANES), lambda i: (0, i)),
             pl.BlockSpec((HALF, LANES), lambda i: (0, i)),
             pl.BlockSpec((HALF, LANES), lambda i: (0, PAIRS + i)),
@@ -309,7 +309,7 @@
         name="memory_attention",
     )(
         reads,
-        last_rows,
+        tail_lengths,
         qkv,
         tail_kv,
         tail_kv,
@@ -822,19 +822,26 @@
         return len(self.bits)
 
 
-def weight_grads(turned, d, d_tail, ready, side):
+def weight_grads(turned, d, d_tail, pair, side):
     width = d.shape[2]
-    tile = width if ready is None else 256
+    tile = width if pair is None else 256
     each = width // tile
-    extra = 0 if ready is None else ready.shape[1] // tile
+    extra = 0 if pair is None else pair[1].shape[1] // tile
+    paired = 2 if extra else 0
     half = D // 2
     fresh = turned[0].shape[0] == L
 
     def kernel(side_ref, n_ref, nt_ref, d_ref, dt_ref, *refs):
         step = pl.program_id(0)
-        kept_ref, given_ref = refs[extra > 0 : (extra > 0) + 2]
+        kept_ref, given_ref = refs[paired : paired + 2]
+        if extra:
+
+            @pl.when(step == 0)
+            def _():
+                refs[-1][...] = refs[0][...].T
+
         if fresh:
-            turn_refs = refs[-2:]
+            turn_refs = refs[paired + 2 : paired + 4]
 
             @pl.when(step == 0)
             def _():
@@ -864,7 +871,7 @@
 
                 @pl.when(step >= 3 * each)
                 def _():
-                    out_ref[...] = rows(which, refs[0])
+                    out_ref[...] = dot(rows(which, refs[-1]), refs[1][...]).astype(bf16)
 
     column = lambda i: jnp.where(i < 3 * each, i % each, each - 1)
     fixed = lambda matrix: pl.BlockSpec(matrix.shape, lambda i: (0, 0))
@@ -877,8 +884,9 @@
     ]
     operands = [side, *turned, d, d_tail]
     if extra:
-        in_specs.append(pl.BlockSpec((D, tile), lambda i: (0, jnp.maximum(i - 3 * each, 0))))
-        operands.append(ready)
+        in_specs.append(fixed(pair[0]))
+        in_specs.append(pl.BlockSpec((L, tile), lambda i: (0, jnp.maximum(i - 3 * each, 0))))
+        operands += pair
     steps = 3 * each + extra
     shapes = [jax.ShapeDtypeStruct((half, steps * tile), bf16)] * 2
     specs = [pl.BlockSpec((half, tile), lambda i: (0, i))] * 2
@@ -891,6 +899,7 @@
         in_specs=in_specs,
         out_specs=specs,
         out_shape=shapes,
+        scratch_shapes=[pltpu.VMEM((D, L), bf16)] if extra else [],
         cost_estimate=pl.CostEstimate(
             flops=8 * L * D * width, bytes_accessed=8 * D * width, transcendentals=0
         ),
@@ -946,6 +955,7 @@
     bias_two = second_norm_bias.astype(f32)
 
     tail = rotated(inputs[HALF:], "mlp", 1)
+    tail_lengths = rotated(doc_lengths, "mlp", 1)
     cotangents = [cotangent] + [rotated(cotangent, "mlp", by) for by in range(1, n_mlp)]
 
     activations = inputs.astype(f32)
@@ -974,14 +984,12 @@
     steps = range(1, n_mlp)
     arrived_hi = [rotated(sent, "mlp", by) for by in steps]
 
-    own_len, local = fence((doc_lengths[:, NDOC - 1 :], local))
-    last_len = rotated(jnp.broadcast_to(own_len.astype(bf16), (16, LANES)), "mlp", 1)
     normed_tail, tail_kv = tail_projection(tail, rows, attn_in)
     reads = jnp.where(place == 0, 0, doc_lengths[:, :1])
     tail_kv, *cotangents[1:] = fence((tail_kv, *cotangents[1:]))
     mixture, mem_k, mem_v, lse_mem, middle, normed_two, basis_t, sent = memory_attention(
         reads,
-        last_len,
+        tail_lengths,
         qkv,
         tail_kv,
         rows,
@@ -1043,9 +1051,8 @@
         early = PAIRS // 3
         side = place_in(core[0]).reshape(1)
         d_one, d_tail_one, sums_one = backward(0, early, d_branch)
-        d_attn_out = over_rows(mixture, d_branch).astype(bf16)
         kept, given, turned = weight_grads(
-            (normed, normed_tail), d_one, d_tail_one, d_attn_out, side
+            (normed, normed_tail), d_one, d_tail_one, (mixture, d_branch), side
         )
         chain_one = Chain(kept, given, groups)
         chain_one.fly()
@@ -1107,7 +1114,7 @@
                 ],
                 axis=0,
             ),
-            core[0] + mlp_bits + rest,
+            core[0] + rest + mlp_bits,
         )
         vectors.fly()
 
@@ -1152,7 +1159,7 @@
     chain_two.fly()
     chain_one = Chain.gathering(one, core)
     chain_one.fly()
-    vectors = Total(summed, (core[0] + mlp_bits + rest)[-1:])
+    vectors = Total(summed, mlp_bits[-1:])
     vectors.fly()
     vectors.land()
     bias_grad = lax.dynamic_slice(

time: 275 us -> 274 us (level)
  waiting for transfers between devices: 29.4 us -> 35.8 us
  matrix products: 19.3 us -> 15.9 us
  starting transfers between devices: 48.9 us -> 46 us
    ppermute x29, waiting for transfers between devices: 28 us -> 31.4 us  [flipped(): return lax.ppermute(value, GRID, [(i, i ^ mask) for i in range(count)])]
    dot_general x3 -> x2, matrix products: 15 us -> 11.6 us  [shards(): lax.dot_general(a, b, (((0,), (0,)), ((), ())), preferred_element_type=f32)]
    ppermute x9, waiting for transfers between devices: 1.39 us -> 4.35 us  [rotated(): lax.ppermute(value, axis, [(i, (i + by) % count) for i in range(count)])]
    ppermute x29, starting transfers between devices: 37 us -> 34.1 us  [flipped(): return lax.ppermute(value, GRID, [(i, i ^ mask) for i in range(count)])]
  transfers between devices with their start and end apart: 39 -> 39, of which waited for: 12 -> 11; matrix products, arithmetic and copies ran while one was open for 12% -> 10% of each run, Pallas kernels for 45% -> 46%
where the time goes in v4:
time: 274 us; the launch traced here: 270 us
  Pallas kernels  124 us (45%)
  starting transfers between devices  46 us (17%)
  waiting for transfers between devices  35.8 us (13%)
  other arithmetic  25.6 us (9%)
  matrix products  15.9 us (6%)
  between operations  14.8 us (5%)
  local copies, waits for them, and re-layouts  7.93 us (3%)
    ppermute x29, starting transfers between devices, flipped(): return lax.ppermute(value, GRID, [(i, i ^ mask) for i in range(count)])  34.1 us
    ppermute x29, waiting for transfers between devices, flipped(): return lax.ppermute(value, GRID, [(i, i ^ mask) for i in range(count)])  31.4 us
    pallas_call x2, Pallas kernels, attention_backward(): pl.pallas_call(backward_kernel, grid=(pairs,), in_specs=[pl.BlockSpec(mem...  26.4 us
    pallas_call x3, Pallas kernels, mlp_block(): pl.pallas_call(mlp_kernel, grid=(hidden // tile,), in_specs=[fixed, pl.Bl...  24.5 us
    pallas_call x2, Pallas kernels, weight_grads(): pl.pallas_call(kernel, grid=(steps,), in_specs=in_specs, out_specs=specs,...  13.6 us
    pallas_call x1, Pallas kernels, local_attention(): pl.pallas_call(local_kernel, grid=(PAIRS,), in_specs=[pl.BlockSpec(memory...  13.5 us
    pallas_call x1, Pallas kernels, memory_attention(): pl.pallas_call(memory_kernel, grid=(PAIRS,), in_specs=[pl.BlockSpec(memor...  12 us
    ppermute x9, starting transfers between devices, rotated(): lax.ppermute(value, axis, [(i, (i + by) % count) for i in range(count)])  11.9 us
  transfers between devices with their start and end apart: 39, of which 11 were waited for; matrix products, arithmetic and copies ran while one was open for 10% of the time, Pallas kernels for 46%

profile of v4, /device:TPU:0, one launch (start us, length us, event | category | flops | bytes accessed | tf_op | source)
XLA Modules:
  0.0 270.3 jit_solution(3554331297635551073)
XLA Ops:
  7.3 1.8 slice.83
  9.1 3.0 %collective-permute-start.26 = (bf16[256,768]{1,0:T(8,128)(2,1)}, bf16[256,768]{1,0:T(8,128)(2,1)}, u32[]{:S(2)}, u32[]{:S(2)}) collective-permute-start(bf16[256,768]{1,0:T(8,128)(2,1)} %slice.83), channel_id=1, source_target_pairs={{0,1},{1,0},{2,3},{3,2},{4,5},{5,4},{6,7},{7,6},{8,9},{9,8},{10,11... | collective-permute-start | bytes 1179656 | tf_op jit(solution)/shard_map/ppermute | solution.py:720
  12.1 2.0 collective-permute-start.25
  16.3 4.3 %fusion.3.q_ref.k_ref.v_ref = bf16[512,2304]{1,0:T(8,128)(2,1)S(1)} fusion(bf16[512,768]{1,0:T(8,128)(2,1)S(1)} %fusion.9, bf16[768,2304]{1,0:T(8,128)(2,1)} %w_ref.1, f32[2304]{0:T(1024)S(1)} %pad_maximum_fusion.9), kind=kOutput, calls=%fused_computation.37 | convolution fusion | flops 1814298624 | bytes 6693888 | tf_op jit(solution)/shard_map/dot_general | solution.py:27
  20.8 13.5 %local_attention.1 = (f32[256,768]{1,0:T(8,128)}, f32[6,8,512]{2,1,0:T(8,128)}, bf16[512,768]{1,0:T(8,128)(2,1)}, f32[512,768]{1,0:T(8,128)}, bf16[512,768]{1,0:T(8,128)(2,1)}, /*index=5*/bf16[256,768]{1,0:T(8,128)(2,1)}) custom-call(s32[1,3]{1,0:T(1,128)S(1)} %copy-done.25, bf16[512,2304]{1,0:T(8,128)(2,1)S(1)} %fusion.3.q_ref.k_ref.v_ref, ...), custom_call_target="tpu_custom_call" | custom-call | flops 2415919104 | bytes 3145728 | tf_op jit(solution)/shard_map/local_attention/pallas_call | solution.py:116
  34.5 4.7 %tail_projection.1 = (bf16[256,768]{1,0:T(8,128)(2,1)}, bf16[256,1536]{1,0:T(8,128)(2,1)}) custom-call(bf16[256,768]{1,0:T(8,128)(2,1)} %collective-permute-done.26.x_ref, f32[8,768]{1,0:T(8,128)S(1)} %concatenate.49.rows_ref.vb_ref, bf16[768,2304]{1,0:T(8,128)(2,1)} %w_ref.1), custom_call_target="tpu_custom_call" | custom-call | flops 603979776 | bytes 2359296 | tf_op jit(solution)/shard_map/tail_projection/pallas_call | solution.py:180
  39.7 12.0 %memory_attention.1 = (bf16[512,768]{1,0:T(8,128)(2,1)}, bf16[512,768]{1,0:T(8,128)(2,1)}, bf16[512,768]{1,0:T(8,128)(2,1)}, f32[6,8,256]{2,1,0:T(8,128)}, f32[5...) custom-call(s32[1,1]{1,0:T(1,128)S(6)} %select_n.313.reads, ...), custom_call_target="tpu_custom_call", output_to_operand_aliasing={{0}: (10, {}), {4}: (11, {}), {5}: (12, {})} | custom-call | flops 3221225472 | bytes 6291456 | tf_op jit(solution)/shard_map/memory_attention/pallas_call | solution.py:262
  51.7 2.1 collective-permute-start.28
  54.4 6.5 %mlp_block.3 = (bf16[1024,1536]{1,0:T(8,128)(2,1)}, bf16[1024,1536]{1,0:T(8,128)(2,1)}, f32[8,1536]{1,0:T(8,128)}, bf16[256,768]{1,0:T(8,128)(2,1)}, bf16[256,768]{1,0:T(8,128)(2,1)}) custom-call(bf16[256,768]{1,0:T(8,128)(2,1)} %collective-permute-done.29.x_ref, bf16[512,768]{1,0:T(8,128)(2,1)} %collective-permute-done.27.ct_ref, bf16[768,1536]{1,0:T(8,128)(2,1)} %wi_ref.5, ...), custom_call_target="tpu_custom_call" | custom-call | flops 2415919104 | bytes 7864320 | tf_op jit(solution)/shard_map/mlp_block/pallas_call | solution.py:372
  62.5 6.5 %mlp_block.4 = (bf16[1024,1536]{1,0:T(8,128)(2,1)}, bf16[1024,1536]{1,0:T(8,128)(2,1)}, f32[8,1536]{1,0:T(8,128)}, bf16[256,768]{1,0:T(8,128)(2,1)}, bf16[256,768]{1,0:T(8,128)(2,1)}) custom-call(bf16[256,768]{1,0:T(8,128)(2,1)} %collective-permute-done.28.x_ref, ...), custom_call_target="tpu_custom_call", output_to_operand_aliasing={{0}: (5, {}), {1}: (6, {})} | custom-call | flops 2415919104 | bytes 7864320 | tf_op jit(solution)/shard_map/mlp_block/pallas_call | solution.py:372
  69.1 2.6 collective-permute-start.31
  71.6 11.5 %mlp_block.5 = (bf16[1024,1536]{1,0:T(8,128)(2,1)}, bf16[1024,1536]{1,0:T(8,128)(2,1)}, f32[8,1536]{1,0:T(8,128)}, bf16[512,768]{1,0:T(8,128)(2,1)}, bf16[512,768]{1,0:T(8,128)(2,1)}) custom-call(bf16[512,768]{1,0:T(8,128)(2,1)} %get-tuple-element.255.x_ref, bf16[512,768]{1,0:T(8,128)(2,1)} %ct_ref.1, ...), custom_call_target="tpu_custom_call", output_to_operand_aliasing={{0}: (5, {}), {1}: (6, {})} | custom-call | flops 4831838208 | bytes 11010048 | tf_op jit(solution)/shard_map/mlp_block/pallas_call | solution.py:372
  83.1 6.5 %convolution_convert_fusion = bf16[1536,768]{1,0:T(8,128)(2,1)} fusion(bf16[1024,1536]{1,0:T(8,128)(2,1)} %get-tuple-element.291, bf16[512,768]{1,0:T(8,128)(2,1)} %collective-permute-done.27.ct_ref, bf16[512,768]{1,0:T(8,128)(2,1)} %ct_ref.1), kind=kOutput, calls=%fused_computation.38 | convolution fusion | flops 2420244480 | bytes 7077888 | tf_op jit(solution)/shard_map/dot_general | solution.py:1026
  89.7 5.1 %convolution_convert_fusion.1 = bf16[768,1536]{1,0:T(8,128)(2,1)} fusion(bf16[1024,1536]{1,0:T(8,128)(2,1)S(1)} %copy-done.2, bf16[256,768]{1,0:T(8,128)(2,1)} %collective-permute-done.29.x_ref, bf16[256,768]{1,0:T(8,128)(2,1)} %collective-permute-done.28.x_ref, bf16[512,768]{1,0:T(8,128)(2,1)S(1)} %copy-done.26), kind=kOutput, calls=%fused_computation.39 | convolution fusion | flops 2421817344 | bytes 7077888 | tf_op jit(solution)/shard_map/dot_general | solution.py:1026
  95.4 133.7 %conditional.1 = (bf16[384,1536]{1,0:T(8,128)(2,1)}, bf16[96,1536]{1,0:T(8,128)(2,1)}, f32[12,768]{1,0:T(8,128)}, bf16[512,768]{1,0:T(8,128)(2,1)}, bf16[512,768]{1,0:T(8,128)(2,1)}) conditional(s32[]{:T(128)} %bitcast.2, () %tuple.42, (bf16[512,768]{1,0:T(8,128)(2,1)}, bf16[512,768]{1,0:T(8,128)(2,1)}, f32[512,768]{1,0:T(8,128)}, ...), branch_computations={%region_2.3_spmd, %region_3.4_spmd} | conditional | flops 16139627520 | bytes 102844040 | solution.py:1152
  95.4 4.6 %middle_backward.1 = (f32[512,768]{1,0:T(8,128)}, bf16[512,768]{1,0:T(8,128)(2,1)}, f32[8,768]{1,0:T(8,128)}) custom-call(bf16[512,768]{1,0:T(8,128)(2,1)} %get-tuple-element.70.d_ref, bf16[512,768]{1,0:T(8,128)(2,1)} %get-tuple-element.71.ct_ref, f32[512,768]{1,0:T(8,128)} %get-tuple-element.72.middle_ref, f32[8,768]{1,0:T(8,128)S(1)} %get-tuple-element.73.rows_ref, ...), custom_call_target="tpu_custom_call" | custom-call | flops 7864320 | bytes 5505024 | tf_op jit(solution)/shard_map/cond/branch_1_fun/middle_backward/pallas_call | solution.py:595
  100.0 9.6 %attention_backward.2 = (bf16[3,512,256]{2,1,0:T(8,128)(2,1)}, bf16[2,256,256]{2,1,0:T(8,128)(2,1)}, f32[8,256]{1,0:T(8,128)}) custom-call(s32[1,3]{1,0:T(1,128)S(1)} %get-tuple-element.66.lens, bf16[512,2304]{1,0:T(8,128)(2,1)S(1)} %get-tuple-element.67.q_ref.k_ref.v_ref, bf16[512,2304]{1,0:T(8,128)(2,1)S(1)} %get-tuple-element.67.q_ref.k_ref.v_ref, ...), custom_call_target="tpu_custom_call" | custom-call | flops 3758096384 | bytes 2621440 | tf_op jit(solution)/shard_map/cond/branch_1_fun/attention_backward/pallas_call | solution.py:501
  109.7 8.0 %weight_grads.2 = (bf16[384,1536]{1,0:T(8,128)(2,1)}, bf16[384,1536]{1,0:T(8,128)(2,1)}, bf16[768,512]{1,0:T(8,128)(2,1)}, bf16[768,256]{1,0:T(8,128)(2,1)}) custom-call(s32[1]{0:T(128)} %bitcast.1.side_ref, bf16[512,768]{1,0:T(8,128)(2,1)} %get-tuple-element.64.n_ref, bf16[256,768]{1,0:T(8,128)(2,1)S(1)} %copy-done.6, ...), custom_call_target="tpu_custom_call" | custom-call | flops 805306368 | bytes 1572864 | tf_op jit(solution)/shard_map/cond/branch_1_fun/weight_grads/pallas_call | solution.py:896
  117.8 3.3 %collective-permute-done.got_ref = bf16[384,1536]{1,0:T(8,128)(2,1)} collective-permute-done((bf16[384,1536]{1,0:T(8,128)(2,1)}, bf16[384,1536]{1,0:T(8,128)(2,1)}, u32[]{:S(2)}, u32[]{:S(2)}) %collective-permute-start) | collective-permute-done | bytes 1179680 | tf_op jit(solution)/shard_map/cond/branch_1_fun/ppermute | solution.py:729
  121.1 2.9 %split_sum.2 = (bf16[96,1536]{1,0:T(8,128)(2,1)}, bf16[96,1536]{1,0:T(8,128)(2,1)}, bf16[96,1536]{1,0:T(8,128)(2,1)}, bf16[96,1536]{1,0:T(8,128)(2,1)}) custom-call(s32[1]{0:T(128)} %bitcast.number_ref, bf16[384,1536]{1,0:T(8,128)(2,1)} %get-tuple-element.84.kept_ref, bf16[384,1536]{1,0:T(8,128)(2,1)} %collective-permute-done.got_ref), custom_call_target="tpu_custom_call" | custom-call | flops 1000 | bytes 1000 | tf_op jit(solution)/shard_map/cond/branch_1_fun/split_sum/pallas_call | solution.py:923
  124.0 1.7 collective-permute-start.2
  125.7 1.8 collective-permute-start.3
  127.5 16.8 %attention_backward.3 = (bf16[3,512,512]{2,1,0:T(8,128)(2,1)}, bf16[2,256,512]{2,1,0:T(8,128)(2,1)}, f32[8,512]{1,0:T(8,128)}) custom-call(s32[1,3]{1,0:T(1,128)S(1)} %get-tuple-element.66.lens, bf16[512,2304]{1,0:T(8,128)(2,1)S(1)} %get-tuple-element.67.q_ref.k_ref.v_ref, bf16[512,2304]{1,0:T(8,128)(2,1)S(1)} %get-tuple-element.67.q_ref.k_ref.v_ref, ...), custom_call_target="tpu_custom_call" | custom-call | flops 7516192768 | bytes 5242880 | tf_op jit(solution)/shard_map/cond/branch_1_fun/attention_backward/pallas_call | solution.py:501
  145.7 5.6 %weight_grads.3 = (bf16[384,1536]{1,0:T(8,128)(2,1)}, bf16[384,1536]{1,0:T(8,128)(2,1)}) custom-call(s32[1]{0:T(128)} %bitcast.1.side_ref, bf16[768,512]{1,0:T(8,128)(2,1)} %get-tuple-element.112.n_ref, bf16[768,256]{1,0:T(8,128)(2,1)} %get-tuple-element.113.nt_ref, bf16[3,512,512]{2,1,0:T(8,128)(2,1)} %get-tuple-element.126.d_ref.two_ref, ...), custom_call_target="tpu_custom_call" | custom-call | flops 1610612736 | bytes 3145728 | tf_op jit(solution)/shard_map/cond/branch_1_fun/weight_grads/pallas_call | solution.py:896
  151.2 1.6 collective-permute-start.4
  155.4 2.8 %split_sum.3 = (bf16[96,1536]{1,0:T(8,128)(2,1)}, bf16[96,1536]{1,0:T(8,128)(2,1)}, bf16[96,1536]{1,0:T(8,128)(2,1)}, bf16[96,1536]{1,0:T(8,128)(2,1)}) custom-call(s32[1]{0:T(128)} %bitcast.number_ref, bf16[384,1536]{1,0:T(8,128)(2,1)} %get-tuple-element.114.kept_ref, bf16[384,1536]{1,0:T(8,128)(2,1)} %copy-done.4), custom_call_target="tpu_custom_call" | custom-call | flops 1000 | bytes 1000 | tf_op jit(solution)/shard_map/cond/branch_1_fun/split_sum/pallas_call | solution.py:923
  159.9 1.8 collective-permute-start.9
  161.8 2.6 collective-permute-start.6
  164.4 8.4 %qkv_backward.1 = (f32[512,768]{1,0:T(8,128)}, bf16[256,768]{1,0:T(8,128)(2,1)}, f32[8,768]{1,0:T(8,128)}) custom-call(bf16[3,512,256]{2,1,0:T(8,128)(2,1)} %get-tuple-element.125.d_ref.one_ref, bf16[3,512,512]{2,1,0:T(8,128)(2,1)} %get-tuple-element.126.d_ref.two_ref, bf16[2,256,256]{2,1,0:T(8,128)(2,1)} %get-tuple-element.127.dt_ref.t_one_ref, ...), custom_call_target="tpu_custom_call" | custom-call | flops 2415919104 | bytes 7864320 | tf_op jit(solution)/shard_map/cond/branch_1_fun/qkv_backward/pallas_call | solution.py:641
  173.1 6.0 %collective-permute-done.9 = bf16[96,1536]{1,0:T(8,128)(2,1)S(1)} collective-permute-done((bf16[96,1536]{1,0:T(8,128)(2,1)}, bf16[96,1536]{1,0:T(8,128)(2,1)S(1)}, u32[]{:S(2)}, u32[]{:S(2)}) %collective-permute-start.9) | collective-permute-done | bytes 294944 | tf_op jit(solution)/shard_map/cond/branch_1_fun/ppermute | solution.py:729
  179.4 1.6 collective-permute-start.11
  183.1 2.7 %collective-permute-start.10 = (bf16[24,1536]{1,0:T(8,128)(2,1)S(1)}, bf16[24,1536]{1,0:T(8,128)(2,1)S(1)}, u32[]{:S(2)}, u32[]{:S(2)}) collective-permute-start(bf16[24,1536]{1,0:T(8,128)(2,1)S(1)} %add_convert_fusion.6), channel_id=1, source_target_pairs={{0,16},{1,17},{2,18},{3,19},{4,20},{5,21},{6,22},{7,23},{8,24},{9,... | collective-permute-start | bytes 221192 | tf_op jit(solution)/shard_map/cond/branch_1_fun/ppermute | solution.py:729
  185.8 1.7 collective-permute-start.24
  189.0 3.3 %collective-permute-done.10 = bf16[24,1536]{1,0:T(8,128)(2,1)S(1)} collective-permute-done((bf16[24,1536]{1,0:T(8,128)(2,1)S(1)}, bf16[24,1536]{1,0:T(8,128)(2,1)S(1)}, u32[]{:S(2)}, u32[]{:S(2)}) %collective-permute-start.10) | collective-permute-done | bytes 73760 | tf_op jit(solution)/shard_map/cond/branch_1_fun/ppermute | solution.py:729
  192.4 1.9 collective-permute-start.18
  194.3 2.2 collective-permute-done.13
  197.8 4.1 %collective-permute-done.12 = bf16[48,1536]{1,0:T(8,128)(2,1)S(1)} collective-permute-done((bf16[48,1536]{1,0:T(8,128)(2,1)S(1)}, bf16[48,1536]{1,0:T(8,128)(2,1)S(1)}, u32[]{:S(2)}, u32[]{:S(2)}) %collective-permute-start.12) | collective-permute-done | bytes 147488 | tf_op jit(solution)/shard_map/cond/branch_1_fun/ppermute | solution.py:729
  202.6 4.1 %collective-permute-start.15 = (bf16[96,1536]{1,0:T(8,128)(2,1)}, bf16[96,1536]{1,0:T(8,128)(2,1)S(1)}, u32[]{:S(2)}, u32[]{:S(2)}) collective-permute-start(bf16[96,1536]{1,0:T(8,128)(2,1)} %pad_maximum_fusion.2), channel_id=1, source_target_pairs={{0,1},{1,0},{2,3},{3,2},{4,5},{5,4},{6,7},{7,6},{8,9},{9,8},{10,11... | collective-permute-start | bytes 884744 | tf_op jit(solution)/shard_map/cond/branch_1_fun/ppermute | solution.py:729
  208.1 2.9 %collective-permute-done.24.next_ref = bf16[256,768]{1,0:T(8,128)(2,1)S(1)} collective-permute-done((bf16[256,768]{1,0:T(8,128)(2,1)S(1)}, bf16[256,768]{1,0:T(8,128)(2,1)S(1)}, u32[]{:S(2)}, u32[]{:S(2)}) %collective-permute-start.24) | collective-permute-done | bytes 393248 | tf_op jit(solution)/shard_map/cond/branch_1_fun/ppermute | solution.py:720
  212.0 3.5 %input_backward.1 = bf16[512,768]{1,0:T(8,128)(2,1)} custom-call(f32[512,768]{1,0:T(8,128)} %get-tuple-element.160.dn_ref, bf16[256,768]{1,0:T(8,128)(2,1)} %copy-done.7, bf16[512,768]{1,0:T(8,128)(2,1)S(1)} %get-tuple-element.130.x_ref, f32[512,768]{1,0:T(8,128)} %get-tuple-element.162.dm_ref, f32[8,768]{1,0:T(8,128)} %copy-done.5), custom_call_target="tpu_custom_call" | custom-call | flops 7864320 | bytes 4718592 | tf_op jit(solution)/shard_map/cond/branch_1_fun/input_backward/pallas_call | solution.py:675
  217.7 2.6 collective-permute-start.22
  220.4 2.6 add_convert_fusion
  222.9 3.0 %collective-permute-done.23 = bf16[48,1536]{1,0:T(8,128)(2,1)S(1)} collective-permute-done((bf16[48,1536]{1,0:T(8,128)(2,1)S(1)}, bf16[48,1536]{1,0:T(8,128)(2,1)S(1)}, u32[]{:S(2)}, u32[]{:S(2)}) %collective-permute-start.23) | collective-permute-done | bytes 147488 | tf_op jit(solution)/shard_map/cond/branch_1_fun/ppermute | solution.py:729
  234.1 8.7 %collective-permute-done.35 = f32[12,768]{1,0:T(8,128)S(1)} collective-permute-done((f32[12,768]{1,0:T(8,128)}, f32[12,768]{1,0:T(8,128)S(1)}, u32[]{:S(2)}, u32[]{:S(2)}) %collective-permute-start.35) | collective-permute-done | bytes 36896 | tf_op jit(solution)/shard_map/ppermute | solution.py:729
  245.6 6.7 %widened.1 = (f32[768,1536]{1,0:T(8,128)}, f32[1536,768]{1,0:T(8,128)}) custom-call(bf16[768,1536]{1,0:T(8,128)(2,1)} %get-tuple-element.318.a_ref, bf16[1536,768]{1,0:T(8,128)(2,1)} %get-tuple-element.319.b_ref), custom_call_target="tpu_custom_call" | custom-call | bytes 14155776 | tf_op jit(solution)/shard_map/widened/pallas_call | solution.py:705
  256.0 1.6 fusion.18
  257.7 1.7 broadcast_select_fusion.8
  259.7 3.5 %convert_element_type.148 = f32[768,2304]{1,0:T(8,128)} convert(bf16[768,2304]{1,0:T(8,128)(2,1)S(1)} %fusion.23) | non-fusion elementwise | flops 1769472 | bytes 10616832 | tf_op jit(solution)/shard_map/convert_element_type | solution.py:1196
  (184 shorter events, 36.8 us)
Async XLA Ops:
  7.2 8.6 %copy-start.17 = (bf16[768]{0:T(1024)(128)(2,1)S(1)}, bf16[768]{0:T(1024)(128)(2,1)}, u32[]{:S(2)}) copy-start(bf16[768]{0:T(1024)(128)(2,1)} %param.19) | copy-start | bytes 4612
  7.2 8.6 %copy-start.18 = (bf16[768]{0:T(1024)(128)(2,1)S(1)}, bf16[768]{0:T(1024)(128)(2,1)}, u32[]{:S(2)}) copy-start(bf16[768]{0:T(1024)(128)(2,1)} %param.20) | copy-start | bytes 4612
  7.2 8.6 %copy-start.14 = (bf16[2,768]{1,0:T(2,128)(2,1)S(1)}, bf16[2,768]{1,0:T(2,128)(2,1)}, u32[]{:S(2)}) copy-start(bf16[2,768]{1,0:T(2,128)(2,1)} %param.22) | copy-start | bytes 9220
  7.2 238.4 %all-reduce.3.cloned.1.call-start = ((), (), s32[]{:S(2)}) async-start(), calls=%async_computation | async-start | bytes 9437184 | tf_op jit(solution)/shard_map/psum | solution.py:1043
  9.1 25.4 %collective-permute-start.26 = (bf16[256,768]{1,0:T(8,128)(2,1)}, bf16[256,768]{1,0:T(8,128)(2,1)}, u32[]{:S(2)}, u32[]{:S(2)}) collective-permute-start(bf16[256,768]{1,0:T(8,128)(2,1)} %slice.83), channel_id=1, source_target_pairs={{0,1},{1,0},{2,3},{3,2},{4,5},{5,4},{6,7},{7,6},{8,9},{9,8},{10,11... | collective-permute-start | bytes 1179656 | tf_op jit(solution)/shard_map/ppermute | solution.py:720
  12.1 27.1 %collective-permute-start.27 = (bf16[512,768]{1,0:T(8,128)(2,1)}, bf16[512,768]{1,0:T(8,128)(2,1)}, u32[]{:S(2)}, u32[]{:S(2)}) collective-permute-start(bf16[512,768]{1,0:T(8,128)(2,1)} %ct_ref.1), channel_id=1, source_target_pairs={{0,1},{1,0},{2,3},{3,2},{4,5},{5,4},{6,7},{7,6},{8,9},{9,8},{10,11... | collective-permute-start | bytes 2359304 | tf_op jit(solution)/shard_map/ppermute | solution.py:720
  12.1 27.1 %collective-permute-start.25 = (s32[1,3]{1,0:T(1,128)}, s32[1,3]{1,0:T(1,128)S(1)}, u32[]{:S(2)}, u32[]{:S(2)}) collective-permute-start(s32[1,3]{1,0:T(1,128)} %lens.1), channel_id=1, source_target_pairs={{0,1},{1,0},{2,3},{3,2},{4,5},{5,4},{6,7},{7,6},{8,9},{9,8},{10,11... | collective-permute-start | bytes 44 | tf_op jit(solution)/shard_map/ppermute | solution.py:720
  34.3 19.5 %collective-permute-start.29 = (bf16[256,768]{1,0:T(8,128)(2,1)}, bf16[256,768]{1,0:T(8,128)(2,1)}, u32[]{:S(2)}, u32[]{:S(2)}) collective-permute-start(bf16[256,768]{1,0:T(8,128)(2,1)} %get-tuple-element.259), channel_id=1, source_target_pairs={{0,1},{1,0},{2,3},{3,2},{4,5},{5,4},{6,7},{7,6},{8,9},{9,8},{10,11... | collective-permute-start | bytes 1179656 | tf_op jit(solution)/shard_map/ppermute | solution.py:720
  39.7 14.1 %copy-start.20 = (bf16[1536]{0:T(1024)(128)(2,1)S(1)}, bf16[1536]{0:T(1024)(128)(2,1)}, u32[]{:S(2)}) copy-start(bf16[1536]{0:T(1024)(128)(2,1)} %param.28) | copy-start | bytes 9220
  51.7 10.8 %collective-permute-start.28 = (bf16[256,768]{1,0:T(8,128)(2,1)}, bf16[256,768]{1,0:T(8,128)(2,1)}, u32[]{:S(2)}, u32[]{:S(2)}) collective-permute-start(bf16[256,768]{1,0:T(8,128)(2,1)} %get-tuple-element.256), channel_id=1, source_target_pairs={{0,1},{1,0},{2,3},{3,2},{4,5},{5,4},{6,7},{7,6},{8,9},{9,8},{10,11... | collective-permute-start | bytes 1179656 | tf_op jit(solution)/shard_map/ppermute | solution.py:720
  61.0 22.1 %collective-permute-start.30 = (bf16[256,768]{1,0:T(8,128)(2,1)}, bf16[256,768]{1,0:T(8,128)(2,1)}, u32[]{:S(2)}, u32[]{:S(2)}) collective-permute-start(bf16[256,768]{1,0:T(8,128)(2,1)} %get-tuple-element.269), channel_id=1, source_target_pairs={{0,1},{1,0},{2,3},{3,2},{4,5},{5,4},{6,7},{7,6},{8,9},{9,8},{10,11... | collective-permute-start | bytes 1179656 | tf_op jit(solution)/shard_map/ppermute | solution.py:720
  69.1 14.1 %collective-permute-start.31 = (bf16[256,768]{1,0:T(8,128)(2,1)}, bf16[256,768]{1,0:T(8,128)(2,1)}, u32[]{:S(2)}, u32[]{:S(2)}) collective-permute-start(bf16[256,768]{1,0:T(8,128)(2,1)} %get-tuple-element.270), channel_id=1, source_target_pairs={{0,1},{1,0},{2,3},{3,2},{4,5},{5,4},{6,7},{7,6},{8,9},{9,8},{10,11... | collective-permute-start | bytes 1179656 | tf_op jit(solution)/shard_map/ppermute | solution.py:720
  100.0 9.6 %copy-start.6 = (bf16[256,768]{1,0:T(8,128)(2,1)S(1)}, bf16[256,768]{1,0:T(8,128)(2,1)}, u32[]{:S(2)}) copy-start(bf16[256,768]{1,0:T(8,128)(2,1)} %get-tuple-element.65.nt_ref) | copy-start | bytes 1179652 | tf_op jit(solution)/shard_map/cond
  117.7 9.8 %copy-start.28 = (f32[6,8,512]{2,1,0:T(8,128)S(1)}, f32[6,8,512]{2,1,0:T(8,128)}, u32[]{:S(2)}) copy-start(f32[6,8,512]{2,1,0:T(8,128)} %get-tuple-element.78.ll_ref) | copy-start | bytes 294916 | tf_op jit(solution)/shard_map/cond
  117.7 3.4 %collective-permute-start = (bf16[384,1536]{1,0:T(8,128)(2,1)}, bf16[384,1536]{1,0:T(8,128)(2,1)}, u32[]{:S(2)}, u32[]{:S(2)}) collective-permute-start(bf16[384,1536]{1,0:T(8,128)(2,1)} %get-tuple-element.85), channel_id=1, source_target_pairs={{0,2},{1,3},{2,0},{3,1},{4,6},{5,7},{6,4},{7,5},{8,10},{9,11},{10,... | collective-permute-start | bytes 3538952 | tf_op jit(solution)/shard_map/cond/branch_1_fun/ppermute | solution.py:729
  124.0 20.3 %copy-start.12 = (bf16[96,1536]{1,0:T(8,128)(2,1)S(1)}, bf16[96,1536]{1,0:T(8,128)(2,1)}, u32[]{:S(2)}) copy-start(bf16[96,1536]{1,0:T(8,128)(2,1)} %get-tuple-element.86) | copy-start | bytes 884740 | tf_op jit(solution)/shard_map/cond
  124.0 20.3 %collective-permute-start.1 = (bf16[96,1536]{1,0:T(8,128)(2,1)}, bf16[96,1536]{1,0:T(8,128)(2,1)}, u32[]{:S(2)}, u32[]{:S(2)}) collective-permute-start(bf16[96,1536]{1,0:T(8,128)(2,1)} %get-tuple-element.93), channel_id=1, source_target_pairs={{0,1},{1,0},{2,3},{3,2},{4,5},{5,4},{6,7},{7,6},{8,9},{9,8},{10,11... | collective-permute-start | bytes 884744 | tf_op jit(solution)/shard_map/cond/branch_1_fun/ppermute | solution.py:729
  124.0 20.3 %collective-permute-start.2 = (bf16[96,1536]{1,0:T(8,128)(2,1)}, bf16[96,1536]{1,0:T(8,128)(2,1)}, u32[]{:S(2)}, u32[]{:S(2)}) collective-permute-start(bf16[96,1536]{1,0:T(8,128)(2,1)} %get-tuple-element.94), channel_id=1, source_target_pairs={{0,4},{1,5},{2,6},{3,7},{4,0},{5,1},{6,2},{7,3},{8,12},{9,13},{10,... | collective-permute-start | bytes 884744 | tf_op jit(solution)/shard_map/cond/branch_1_fun/ppermute | solution.py:729
  125.7 18.6 %collective-permute-start.3 = (bf16[96,1536]{1,0:T(8,128)(2,1)}, bf16[96,1536]{1,0:T(8,128)(2,1)}, u32[]{:S(2)}, u32[]{:S(2)}) collective-permute-start(bf16[96,1536]{1,0:T(8,128)(2,1)} %get-tuple-element.95), channel_id=1, source_target_pairs={{0,5},{1,4},{2,7},{3,6},{4,1},{5,0},{6,3},{7,2},{8,13},{9,12},{10,... | collective-permute-start | bytes 884744 | tf_op jit(solution)/shard_map/cond/branch_1_fun/ppermute | solution.py:729
  151.2 3.1 %collective-permute-start.5 = (bf16[384,1536]{1,0:T(8,128)(2,1)}, bf16[384,1536]{1,0:T(8,128)(2,1)S(1)}, u32[]{:S(2)}, u32[]{:S(2)}) collective-permute-start(bf16[384,1536]{1,0:T(8,128)(2,1)} %get-tuple-element.115), channel_id=1, source_target_pairs={{0,2},{1,3},{2,0},{3,1},{4,6},{5,7},{6,4},{7,5},{8,10},{9,11},{10,... | collective-permute-start | bytes 3538952 | tf_op jit(solution)/shard_map/cond/branch_1_fun/ppermute | solution.py:729
  151.2 10.4 %collective-permute-start.4 = (bf16[48,1536]{1,0:T(8,128)(2,1)S(1)}, bf16[48,1536]{1,0:T(8,128)(2,1)S(1)}, u32[]{:S(2)}, u32[]{:S(2)}) collective-permute-start(bf16[48,1536]{1,0:T(8,128)(2,1)S(1)} %constant_dynamic-slice_fusion.3), channel_id=1, source_target_pairs={{0,8},{1,9},{2,10},{3,11},{4,12},{5,13},{6,14},{7,15},{8,0},{9,1},... | collective-permute-start | bytes 442376 | tf_op jit(solution)/shard_map/cond/branch_1_fun/ppermute | solution.py:729
  158.2 14.9 %collective-permute-start.7 = (bf16[96,1536]{1,0:T(8,128)(2,1)}, bf16[96,1536]{1,0:T(8,128)(2,1)S(1)}, u32[]{:S(2)}, u32[]{:S(2)}) collective-permute-start(bf16[96,1536]{1,0:T(8,128)(2,1)} %get-tuple-element.119), channel_id=1, source_target_pairs={{0,1},{1,0},{2,3},{3,2},{4,5},{5,4},{6,7},{7,6},{8,9},{9,8},{10,11... | collective-permute-start | bytes 884744 | tf_op jit(solution)/shard_map/cond/branch_1_fun/ppermute | solution.py:729
  158.4 14.7 %collective-permute-start.8 = (bf16[96,1536]{1,0:T(8,128)(2,1)}, bf16[96,1536]{1,0:T(8,128)(2,1)S(1)}, u32[]{:S(2)}, u32[]{:S(2)}) collective-permute-start(bf16[96,1536]{1,0:T(8,128)(2,1)} %get-tuple-element.120), channel_id=1, source_target_pairs={{0,4},{1,5},{2,6},{3,7},{4,0},{5,1},{6,2},{7,3},{8,12},{9,13},{10,... | collective-permute-start | bytes 884744 | tf_op jit(solution)/shard_map/cond/branch_1_fun/ppermute | solution.py:729
  159.9 19.3 %collective-permute-start.9 = (bf16[96,1536]{1,0:T(8,128)(2,1)}, bf16[96,1536]{1,0:T(8,128)(2,1)S(1)}, u32[]{:S(2)}, u32[]{:S(2)}) collective-permute-start(bf16[96,1536]{1,0:T(8,128)(2,1)} %get-tuple-element.121), channel_id=1, source_target_pairs={{0,5},{1,4},{2,7},{3,6},{4,1},{5,0},{6,3},{7,2},{8,13},{9,12},{10,... | collective-permute-start | bytes 884744 | tf_op jit(solution)/shard_map/cond/branch_1_fun/ppermute | solution.py:729
  161.8 11.4 %collective-permute-start.6 = (bf16[24,1536]{1,0:T(8,128)(2,1)S(1)}, bf16[24,1536]{1,0:T(8,128)(2,1)S(1)}, u32[]{:S(2)}, u32[]{:S(2)}) collective-permute-start(bf16[24,1536]{1,0:T(8,128)(2,1)S(1)} %constant_dynamic-slice_fusion.2), channel_id=1, source_target_pairs={{0,16},{1,17},{2,18},{3,19},{4,20},{5,21},{6,22},{7,23},{8,24},{9,... | collective-permute-start | bytes 221192 | tf_op jit(solution)/shard_map/cond/branch_1_fun/ppermute | solution.py:729
  164.4 14.8 %copy-start.11 = (bf16[96,1536]{1,0:T(8,128)(2,1)S(1)}, bf16[96,1536]{1,0:T(8,128)(2,1)}, u32[]{:S(2)}) copy-start(bf16[96,1536]{1,0:T(8,128)(2,1)} %get-tuple-element.136) | copy-start | bytes 884740 | tf_op jit(solution)/shard_map/cond
  179.4 8.2 %collective-permute-start.11 = (bf16[48,1536]{1,0:T(8,128)(2,1)S(1)}, bf16[48,1536]{1,0:T(8,128)(2,1)S(1)}, u32[]{:S(2)}, u32[]{:S(2)}) collective-permute-start(bf16[48,1536]{1,0:T(8,128)(2,1)S(1)} %constant_dynamic-slice_fusion.1), channel_id=1, source_target_pairs={{0,8},{1,9},{2,10},{3,11},{4,12},{5,13},{6,14},{7,15},{8,0},{9,1},... | collective-permute-start | bytes 442376 | tf_op jit(solution)/shard_map/cond/branch_1_fun/ppermute | solution.py:729
  181.9 33.7 %collective-permute-start.21 = (bf16[512,768]{1,0:T(8,128)(2,1)}, bf16[512,768]{1,0:T(8,128)(2,1)}, u32[]{:S(2)}, u32[]{:S(2)}) collective-permute-start(bf16[512,768]{1,0:T(8,128)(2,1)} %pad_maximum_fusion.1), channel_id=1, source_target_pairs={{0,1},{1,0},{2,3},{3,2},{4,5},{5,4},{6,7},{7,6},{8,9},{9,8},{10,11... | collective-permute-start | bytes 2359304 | tf_op jit(solution)/shard_map/cond/branch_1_fun/ppermute | solution.py:720
  183.0 9.4 %collective-permute-start.14 = (f32[12,768]{1,0:T(8,128)S(1)}, f32[12,768]{1,0:T(8,128)S(1)}, u32[]{:S(2)}, u32[]{:S(2)}) collective-permute-start(f32[12,768]{1,0:T(8,128)S(1)} %fusion.1), channel_id=1, source_target_pairs={{0,2},{1,3},{2,0},{3,1},{4,6},{5,7},{6,4},{7,5},{8,10},{9,11},{10,... | collective-permute-start | bytes 110600 | tf_op jit(solution)/shard_map/cond/branch_1_fun/ppermute | solution.py:729
  183.1 9.2 %collective-permute-start.10 = (bf16[24,1536]{1,0:T(8,128)(2,1)S(1)}, bf16[24,1536]{1,0:T(8,128)(2,1)S(1)}, u32[]{:S(2)}, u32[]{:S(2)}) collective-permute-start(bf16[24,1536]{1,0:T(8,128)(2,1)S(1)} %add_convert_fusion.6), channel_id=1, source_target_pairs={{0,16},{1,17},{2,18},{3,19},{4,20},{5,21},{6,22},{7,23},{8,24},{9,... | collective-permute-start | bytes 221192 | tf_op jit(solution)/shard_map/cond/branch_1_fun/ppermute | solution.py:729
  185.8 25.2 %collective-permute-start.24 = (bf16[256,768]{1,0:T(8,128)(2,1)S(1)}, bf16[256,768]{1,0:T(8,128)(2,1)S(1)}, u32[]{:S(2)}, u32[]{:S(2)}) collective-permute-start(bf16[256,768]{1,0:T(8,128)(2,1)S(1)} %copy-done.27), channel_id=1, source_target_pairs={{0,1},{1,0},{2,3},{3,2},{4,5},{5,4},{6,7},{7,6},{8,9},{9,8},{10,11... | collective-permute-start | bytes 1179656 | tf_op jit(solution)/shard_map/cond/branch_1_fun/ppermute | solution.py:720
  187.6 8.9 %collective-permute-start.13 = (bf16[24,1536]{1,0:T(8,128)(2,1)S(1)}, bf16[24,1536]{1,0:T(8,128)(2,1)S(1)}, u32[]{:S(2)}, u32[]{:S(2)}) collective-permute-start(bf16[24,1536]{1,0:T(8,128)(2,1)S(1)} %constant_dynamic-slice_fusion), channel_id=1, source_target_pairs={{0,16},{1,17},{2,18},{3,19},{4,20},{5,21},{6,22},{7,23},{8,24},{9,... | collective-permute-start | bytes 221192 | tf_op jit(solution)/shard_map/cond/branch_1_fun/ppermute | solution.py:729
  192.3 9.5 %collective-permute-start.12 = (bf16[48,1536]{1,0:T(8,128)(2,1)S(1)}, bf16[48,1536]{1,0:T(8,128)(2,1)S(1)}, u32[]{:S(2)}, u32[]{:S(2)}) collective-permute-start(bf16[48,1536]{1,0:T(8,128)(2,1)S(1)} %pad_maximum_fusion.4), channel_id=1, source_target_pairs={{0,8},{1,9},{2,10},{3,11},{4,12},{5,13},{6,14},{7,15},{8,0},{9,1},... | collective-permute-start | bytes 442376 | tf_op jit(solution)/shard_map/cond/branch_1_fun/ppermute | solution.py:729
  192.4 14.3 %collective-permute-start.18 = (f32[12,768]{1,0:T(8,128)S(1)}, f32[12,768]{1,0:T(8,128)S(1)}, u32[]{:S(2)}, u32[]{:S(2)}) collective-permute-start(f32[12,768]{1,0:T(8,128)S(1)} %add.132), channel_id=1, source_target_pairs={{0,4},{1,5},{2,6},{3,7},{4,0},{5,1},{6,2},{7,3},{8,12},{9,13},{10,... | collective-permute-start | bytes 110600 | tf_op jit(solution)/shard_map/cond/branch_1_fun/ppermute | solution.py:729
  196.6 15.5 %copy-start.10 = (bf16[24,1536]{1,0:T(8,128)(2,1)}, bf16[24,1536]{1,0:T(8,128)(2,1)S(1)}, u32[]{:S(2)}) copy-start(bf16[24,1536]{1,0:T(8,128)(2,1)S(1)} %add_convert_fusion.5) | copy-start | bytes 221188 | tf_op jit(solution)/shard_map/cond
  196.6 11.5 %collective-permute-start.20 = (bf16[24,1536]{1,0:T(8,128)(2,1)S(1)}, bf16[24,1536]{1,0:T(8,128)(2,1)S(1)}, u32[]{:S(2)}, u32[]{:S(2)}) collective-permute-start(bf16[24,1536]{1,0:T(8,128)(2,1)S(1)} %add_convert_fusion.5), channel_id=1, source_target_pairs={{0,16},{1,17},{2,18},{3,19},{4,20},{5,21},{6,22},{7,23},{8,24},{9,... | collective-permute-start | bytes 221192 | tf_op jit(solution)/shard_map/cond/branch_1_fun/ppermute | solution.py:729
  202.6 24.7 %collective-permute-start.15 = (bf16[96,1536]{1,0:T(8,128)(2,1)}, bf16[96,1536]{1,0:T(8,128)(2,1)S(1)}, u32[]{:S(2)}, u32[]{:S(2)}) collective-permute-start(bf16[96,1536]{1,0:T(8,128)(2,1)} %pad_maximum_fusion.2), channel_id=1, source_target_pairs={{0,1},{1,0},{2,3},{3,2},{4,5},{5,4},{6,7},{7,6},{8,9},{9,8},{10,11... | collective-permute-start | bytes 884744 | tf_op jit(solution)/shard_map/cond/branch_1_fun/ppermute | solution.py:729
  206.8 20.6 %collective-permute-start.16 = (bf16[96,1536]{1,0:T(8,128)(2,1)}, bf16[96,1536]{1,0:T(8,128)(2,1)S(1)}, u32[]{:S(2)}, u32[]{:S(2)}) collective-permute-start(bf16[96,1536]{1,0:T(8,128)(2,1)} %pad_maximum_fusion.2), channel_id=1, source_target_pairs={{0,4},{1,5},{2,6},{3,7},{4,0},{5,1},{6,2},{7,3},{8,12},{9,13},{10,... | collective-permute-start | bytes 884744 | tf_op jit(solution)/shard_map/cond/branch_1_fun/ppermute | solution.py:729
  208.1 8.8 %collective-permute-start.19 = (f32[12,768]{1,0:T(8,128)}, f32[12,768]{1,0:T(8,128)}, u32[]{:S(2)}, u32[]{:S(2)}) collective-permute-start(f32[12,768]{1,0:T(8,128)} %add.134), channel_id=1, source_target_pairs={{0,8},{1,9},{2,10},{3,11},{4,12},{5,13},{6,14},{7,15},{8,0},{9,1},... | collective-permute-start | bytes 110600 | tf_op jit(solution)/shard_map/cond/branch_1_fun/ppermute | solution.py:729
  211.0 16.4 %collective-permute-start.17 = (bf16[96,1536]{1,0:T(8,128)(2,1)}, bf16[96,1536]{1,0:T(8,128)(2,1)S(1)}, u32[]{:S(2)}, u32[]{:S(2)}) collective-permute-start(bf16[96,1536]{1,0:T(8,128)(2,1)} %pad_maximum_fusion.2), channel_id=1, source_target_pairs={{0,5},{1,4},{2,7},{3,6},{4,1},{5,0},{6,3},{7,2},{8,13},{9,12},{10,... | collective-permute-start | bytes 884744 | tf_op jit(solution)/shard_map/cond/branch_1_fun/ppermute | solution.py:729
  216.5 9.4 %collective-permute-start.23 = (bf16[48,1536]{1,0:T(8,128)(2,1)S(1)}, bf16[48,1536]{1,0:T(8,128)(2,1)S(1)}, u32[]{:S(2)}, u32[]{:S(2)}) collective-permute-start(bf16[48,1536]{1,0:T(8,128)(2,1)S(1)} %pad_maximum_fusion.5), channel_id=1, source_target_pairs={{0,8},{1,9},{2,10},{3,11},{4,12},{5,13},{6,14},{7,15},{8,0},{9,1},... | collective-permute-start | bytes 442376 | tf_op jit(solution)/shard_map/cond/branch_1_fun/ppermute | solution.py:729
  217.7 9.0 %collective-permute-start.22 = (f32[12,768]{1,0:T(8,128)S(1)}, f32[12,768]{1,0:T(8,128)S(1)}, u32[]{:S(2)}, u32[]{:S(2)}) collective-permute-start(f32[12,768]{1,0:T(8,128)S(1)} %add.135), channel_id=1, source_target_pairs={{0,16},{1,17},{2,18},{3,19},{4,20},{5,21},{6,22},{7,23},{8,24},{9,... | collective-permute-start | bytes 110600 | tf_op jit(solution)/shard_map/cond/branch_1_fun/ppermute | solution.py:729
  229.2 23.2 %collective-permute-start.32 = (bf16[96,1536]{1,0:T(8,128)(2,1)}, bf16[96,1536]{1,0:T(8,128)(2,1)S(1)}, u32[]{:S(2)}, u32[]{:S(2)}) collective-permute-start(bf16[96,1536]{1,0:T(8,128)(2,1)} %get-tuple-element.288), channel_id=1, source_target_pairs={{0,1},{1,0},{2,3},{3,2},{4,5},{5,4},{6,7},{7,6},{8,9},{9,8},{10,11... | collective-permute-start | bytes 884744 | tf_op jit(solution)/shard_map/ppermute | solution.py:729
  230.6 21.7 %collective-permute-start.33 = (bf16[96,1536]{1,0:T(8,128)(2,1)}, bf16[96,1536]{1,0:T(8,128)(2,1)S(1)}, u32[]{:S(2)}, u32[]{:S(2)}) collective-permute-start(bf16[96,1536]{1,0:T(8,128)(2,1)} %get-tuple-element.288), channel_id=1, source_target_pairs={{0,4},{1,5},{2,6},{3,7},{4,0},{5,1},{6,2},{7,3},{8,12},{9,13},{10,... | collective-permute-start | bytes 884744 | tf_op jit(solution)/shard_map/ppermute | solution.py:729
  231.4 20.9 %collective-permute-start.34 = (bf16[96,1536]{1,0:T(8,128)(2,1)}, bf16[96,1536]{1,0:T(8,128)(2,1)S(1)}, u32[]{:S(2)}, u32[]{:S(2)}) collective-permute-start(bf16[96,1536]{1,0:T(8,128)(2,1)} %get-tuple-element.288), channel_id=1, source_target_pairs={{0,5},{1,4},{2,7},{3,6},{4,1},{5,0},{6,3},{7,2},{8,13},{9,12},{10,... | collective-permute-start | bytes 884744 | tf_op jit(solution)/shard_map/ppermute | solution.py:729
  232.7 10.1 %collective-permute-start.35 = (f32[12,768]{1,0:T(8,128)}, f32[12,768]{1,0:T(8,128)S(1)}, u32[]{:S(2)}, u32[]{:S(2)}) collective-permute-start(f32[12,768]{1,0:T(8,128)} %get-tuple-element.289), channel_id=1, source_target_pairs={{0,1},{1,0},{2,3},{3,2},{4,5},{5,4},{6,7},{7,6},{8,9},{9,8},{10,11... | collective-permute-start | bytes 110600 | tf_op jit(solution)/shard_map/ppermute | solution.py:729
  234.1 20.4 %collective-permute-start.36 = (bf16[384,1536]{1,0:T(8,128)(2,1)}, bf16[384,1536]{1,0:T(8,128)(2,1)S(1)}, u32[]{:S(2)}, u32[]{:S(2)}) collective-permute-start(bf16[384,1536]{1,0:T(8,128)(2,1)} %get-tuple-element.296), channel_id=1, source_target_pairs={{0,2},{1,3},{2,0},{3,1},{4,6},{5,7},{6,4},{7,5},{8,10},{9,11},{10,... | collective-permute-start | bytes 3538952 | tf_op jit(solution)/shard_map/ppermute | solution.py:729
  254.5 3.2 %collective-permute-start.37 = (bf16[384,1536]{1,0:T(8,128)(2,1)}, bf16[384,1536]{1,0:T(8,128)(2,1)}, u32[]{:S(2)}, u32[]{:S(2)}) collective-permute-start(bf16[384,1536]{1,0:T(8,128)(2,1)} %pad_maximum_fusion.7), channel_id=1, source_target_pairs={{0,2},{1,3},{2,0},{3,1},{4,6},{5,7},{6,4},{7,5},{8,10},{9,11},{10,... | collective-permute-start | bytes 3538952 | tf_op jit(solution)/shard_map/ppermute | solution.py:729
  (21 other events, 101.4 us)
Sparse Core Ops, SparseCore 0:
  94.9 134.4 all-reduce.2

commit v5 on v4

--- a/solution.py
+++ b/solution.py
@@ -1094,11 +1094,11 @@
         chain_one.fly()
         chain_two.land()
         chain_two.fly()
-        y_given, unused = fence((y_given, chain_two.given))
         shares = [
             jnp.concatenate([y for (by, part), y in zip(calls, y_given) if by == step][::-1], axis=0)
             for step in steps
         ]
+        shares, unused = fence((shares, chain_two.given))
         returned = [rotated(y, "mlp", -step) for step, y in zip(steps, shares)]
         from_next = rotated(d_tail_rows, "mlp", -1)
         placed_bias = lax.dynamic_update_slice(
@@ -1161,12 +1161,13 @@
     chain_one.fly()
     vectors = Total(summed, mlp_bits[-1:])
     vectors.fly()
+    d_mlp_in, d_mlp_out = widened(d_mlp_in, d_mlp_out)
+    vectors.got, d_mlp_in, d_mlp_out = fence((vectors.got, d_mlp_in, d_mlp_out))
     vectors.land()
     bias_grad = lax.dynamic_slice(
         vectors.value[8:].reshape(-1), (place * hidden_count,), (hidden_count,)
     )
     summed = [vectors.value[i] for i in range(6)] + [vectors.value[6:8], bias_grad]
-    d_mlp_in, d_mlp_out = widened(d_mlp_in, d_mlp_out)
     chain_two.got, summed, d_mlp_in, d_mlp_out = fence(
         (chain_two.got, summed, d_mlp_in, d_mlp_out)
     )

time: 274 us -> 273 us (level)
  waiting for transfers between devices: 35.8 us -> 31.9 us
    ppermute x29, waiting for transfers between devices: 31.4 us -> 17 us  [flipped(): return lax.ppermute(value, GRID, [(i, i ^ mask) for i in range(count)])]
    ppermute x9, waiting for transfers between devices: 4.35 us -> 14.9 us  [rotated(): lax.ppermute(value, axis, [(i, (i + by) % count) for i in range(count)])]
  transfers between devices with their start and end apart: 39 -> 39, of which waited for: 11 -> 12; matrix products, arithmetic and copies ran while one was open for 10% -> 11% of each run, Pallas kernels for 46% -> 46%
where the time goes in v5:
time: 273 us; the launch traced here: 268 us
  Pallas kernels  124 us (45%)
  starting transfers between devices  47.4 us (17%)
  waiting for transfers between devices  31.9 us (12%)
  other arithmetic  25.6 us (9%)
  matrix products  15.9 us (6%)
  between operations  14.8 us (5%)
  local copies, waits for them, and re-layouts  8.09 us (3%)
    ppermute x29, starting transfers between devices, flipped(): return lax.ppermute(value, GRID, [(i, i ^ mask) for i in range(count)])  36.1 us
    pallas_call x2, Pallas kernels, attention_backward(): pl.pallas_call(backward_kernel, grid=(pairs,), in_specs=[pl.BlockSpec(mem...  26.5 us
    pallas_call x3, Pallas kernels, mlp_block(): pl.pallas_call(mlp_kernel, grid=(hidden // tile,), in_specs=[fixed, pl.Bl...  24.5 us
    ppermute x29, waiting for transfers between devices, flipped(): return lax.ppermute(value, GRID, [(i, i ^ mask) for i in range(count)])  17 us
    ppermute x9, waiting for transfers between devices, rotated(): lax.ppermute(value, axis, [(i, (i + by) % count) for i in range(count)])  14.9 us
    pallas_call x2, Pallas kernels, weight_grads(): pl.pallas_call(kernel, grid=(steps,), in_specs=in_specs, out_specs=specs,...  13.6 us
    pallas_call x1, Pallas kernels, local_attention(): pl.pallas_call(local_kernel, grid=(PAIRS,), in_specs=[pl.BlockSpec(memory...  13.5 us
    pallas_call x1, Pallas kernels, memory_attention(): pl.pallas_call(memory_kernel, grid=(PAIRS,), in_specs=[pl.BlockSpec(memor...  12 us
  transfers between devices with their start and end apart: 39, of which 12 were waited for; matrix products, arithmetic and copies ran while one was open for 11% of the time, Pallas kernels for 46%

profile of v5, /device:TPU:0, one launch (start us, length us, event | category | flops | bytes accessed | tf_op | source)
XLA Modules:
  0.0 268.1 jit_solution(12313053437642879799)
XLA Ops:
  7.3 3.1 %collective-permute-start.25 = (s32[1,3]{1,0:T(1,128)}, s32[1,3]{1,0:T(1,128)S(1)}, u32[]{:S(2)}, u32[]{:S(2)}) collective-permute-start(s32[1,3]{1,0:T(1,128)} %lens.1), channel_id=1, source_target_pairs={{0,1},{1,0},{2,3},{3,2},{4,5},{5,4},{6,7},{7,6},{8,9},{9,8},{10,11... | collective-permute-start | bytes 44 | tf_op jit(solution)/shard_map/ppermute | solution.py:720
  10.3 1.8 slice.83
  12.2 1.9 collective-permute-start.27
  16.3 4.3 %fusion.3.q_ref.k_ref.v_ref = bf16[512,2304]{1,0:T(8,128)(2,1)S(1)} fusion(bf16[512,768]{1,0:T(8,128)(2,1)S(1)} %fusion.9, bf16[768,2304]{1,0:T(8,128)(2,1)} %w_ref.1, f32[2304]{0:T(1024)S(1)} %pad_maximum_fusion.9), kind=kOutput, calls=%fused_computation.37 | convolution fusion | flops 1814298624 | bytes 6693888 | tf_op jit(solution)/shard_map/dot_general | solution.py:27
  20.8 13.5 %local_attention.1 = (f32[256,768]{1,0:T(8,128)}, f32[6,8,512]{2,1,0:T(8,128)}, bf16[512,768]{1,0:T(8,128)(2,1)}, f32[512,768]{1,0:T(8,128)}, bf16[512,768]{1,0:T(8,128)(2,1)}, /*index=5*/bf16[256,768]{1,0:T(8,128)(2,1)}) custom-call(s32[1,3]{1,0:T(1,128)S(1)} %copy-done.25, bf16[512,2304]{1,0:T(8,128)(2,1)S(1)} %fusion.3.q_ref.k_ref.v_ref, ...), custom_call_target="tpu_custom_call" | custom-call | flops 2415919104 | bytes 3145728 | tf_op jit(solution)/shard_map/local_attention/pallas_call | solution.py:116
  34.6 4.7 %tail_projection.1 = (bf16[256,768]{1,0:T(8,128)(2,1)}, bf16[256,1536]{1,0:T(8,128)(2,1)}) custom-call(bf16[256,768]{1,0:T(8,128)(2,1)} %collective-permute-done.26.x_ref, f32[8,768]{1,0:T(8,128)S(1)} %concatenate.49.rows_ref.vb_ref, bf16[768,2304]{1,0:T(8,128)(2,1)} %w_ref.1), custom_call_target="tpu_custom_call" | custom-call | flops 603979776 | bytes 2359296 | tf_op jit(solution)/shard_map/tail_projection/pallas_call | solution.py:180
  39.3 1.9 collective-permute-done.27.ct_ref
  41.8 12.0 %memory_attention.1 = (bf16[512,768]{1,0:T(8,128)(2,1)}, bf16[512,768]{1,0:T(8,128)(2,1)}, bf16[512,768]{1,0:T(8,128)(2,1)}, f32[6,8,256]{2,1,0:T(8,128)}, f32[5...) custom-call(s32[1,1]{1,0:T(1,128)S(6)} %select_n.313.reads, ...), custom_call_target="tpu_custom_call", output_to_operand_aliasing={{0}: (10, {}), {4}: (11, {}), {5}: (12, {})} | custom-call | flops 3221225472 | bytes 6291456 | tf_op jit(solution)/shard_map/memory_attention/pallas_call | solution.py:262
  54.6 6.5 %mlp_block.3 = (bf16[1024,1536]{1,0:T(8,128)(2,1)}, bf16[1024,1536]{1,0:T(8,128)(2,1)}, f32[8,1536]{1,0:T(8,128)}, bf16[256,768]{1,0:T(8,128)(2,1)}, bf16[256,768]{1,0:T(8,128)(2,1)}) custom-call(bf16[256,768]{1,0:T(8,128)(2,1)} %collective-permute-done.29.x_ref, bf16[512,768]{1,0:T(8,128)(2,1)} %collective-permute-done.27.ct_ref, bf16[768,1536]{1,0:T(8,128)(2,1)} %wi_ref.5, ...), custom_call_target="tpu_custom_call" | custom-call | flops 2415919104 | bytes 7864320 | tf_op jit(solution)/shard_map/mlp_block/pallas_call | solution.py:372
  61.1 2.0 collective-permute-start.30
  63.1 6.5 %mlp_block.4 = (bf16[1024,1536]{1,0:T(8,128)(2,1)}, bf16[1024,1536]{1,0:T(8,128)(2,1)}, f32[8,1536]{1,0:T(8,128)}, bf16[256,768]{1,0:T(8,128)(2,1)}, bf16[256,768]{1,0:T(8,128)(2,1)}) custom-call(bf16[256,768]{1,0:T(8,128)(2,1)} %collective-permute-done.28.x_ref, ...), custom_call_target="tpu_custom_call", output_to_operand_aliasing={{0}: (5, {}), {1}: (6, {})} | custom-call | flops 2415919104 | bytes 7864320 | tf_op jit(solution)/shard_map/mlp_block/pallas_call | solution.py:372
  69.6 1.7 collective-permute-start.31
  71.3 11.5 %mlp_block.5 = (bf16[1024,1536]{1,0:T(8,128)(2,1)}, bf16[1024,1536]{1,0:T(8,128)(2,1)}, f32[8,1536]{1,0:T(8,128)}, bf16[512,768]{1,0:T(8,128)(2,1)}, bf16[512,768]{1,0:T(8,128)(2,1)}) custom-call(bf16[512,768]{1,0:T(8,128)(2,1)} %get-tuple-element.257.x_ref, bf16[512,768]{1,0:T(8,128)(2,1)} %ct_ref.1, ...), custom_call_target="tpu_custom_call", output_to_operand_aliasing={{0}: (5, {}), {1}: (6, {})} | custom-call | flops 4831838208 | bytes 11010048 | tf_op jit(solution)/shard_map/mlp_block/pallas_call | solution.py:372
  82.8 6.5 %convolution_convert_fusion = bf16[1536,768]{1,0:T(8,128)(2,1)} fusion(bf16[1024,1536]{1,0:T(8,128)(2,1)} %get-tuple-element.293, bf16[512,768]{1,0:T(8,128)(2,1)} %collective-permute-done.27.ct_ref, bf16[512,768]{1,0:T(8,128)(2,1)} %ct_ref.1), kind=kOutput, calls=%fused_computation.38 | convolution fusion | flops 2420244480 | bytes 7077888 | tf_op jit(solution)/shard_map/dot_general | solution.py:1026
  89.4 5.1 %convolution_convert_fusion.1 = bf16[768,1536]{1,0:T(8,128)(2,1)} fusion(bf16[1024,1536]{1,0:T(8,128)(2,1)S(1)} %copy-done.2, bf16[256,768]{1,0:T(8,128)(2,1)} %collective-permute-done.29.x_ref, bf16[256,768]{1,0:T(8,128)(2,1)} %collective-permute-done.28.x_ref, bf16[512,768]{1,0:T(8,128)(2,1)S(1)} %copy-done.26), kind=kOutput, calls=%fused_computation.39 | convolution fusion | flops 2421817344 | bytes 7077888 | tf_op jit(solution)/shard_map/dot_general | solution.py:1026
  95.1 140.2 %conditional.1 = (bf16[384,1536]{1,0:T(8,128)(2,1)}, bf16[96,1536]{1,0:T(8,128)(2,1)}, f32[12,768]{1,0:T(8,128)}, bf16[512,768]{1,0:T(8,128)(2,1)}, bf16[512,768]{1,0:T(8,128)(2,1)}) conditional(s32[]{:T(128)} %bitcast.2, () %tuple.43, (bf16[512,768]{1,0:T(8,128)(2,1)}, bf16[512,768]{1,0:T(8,128)(2,1)}, f32[512,768]{1,0:T(8,128)}, ...), branch_computations={%region_2.3_spmd, %region_3.4_spmd} | conditional | flops 16139627520 | bytes 102844040 | solution.py:1152
  95.1 4.6 %middle_backward.1 = (f32[512,768]{1,0:T(8,128)}, bf16[512,768]{1,0:T(8,128)(2,1)}, f32[8,768]{1,0:T(8,128)}) custom-call(bf16[512,768]{1,0:T(8,128)(2,1)} %get-tuple-element.70.d_ref, bf16[512,768]{1,0:T(8,128)(2,1)} %get-tuple-element.71.ct_ref, f32[512,768]{1,0:T(8,128)} %get-tuple-element.72.middle_ref, f32[8,768]{1,0:T(8,128)S(1)} %get-tuple-element.73.rows_ref, ...), custom_call_target="tpu_custom_call" | custom-call | flops 7864320 | bytes 5505024 | tf_op jit(solution)/shard_map/cond/branch_1_fun/middle_backward/pallas_call | solution.py:595
  99.7 9.7 %attention_backward.2 = (bf16[3,512,256]{2,1,0:T(8,128)(2,1)}, bf16[2,256,256]{2,1,0:T(8,128)(2,1)}, f32[8,256]{1,0:T(8,128)}) custom-call(s32[1,3]{1,0:T(1,128)S(1)} %get-tuple-element.66.lens, bf16[512,2304]{1,0:T(8,128)(2,1)S(1)} %get-tuple-element.67.q_ref.k_ref.v_ref, bf16[512,2304]{1,0:T(8,128)(2,1)S(1)} %get-tuple-element.67.q_ref.k_ref.v_ref, ...), custom_call_target="tpu_custom_call" | custom-call | flops 3758096384 | bytes 2621440 | tf_op jit(solution)/shard_map/cond/branch_1_fun/attention_backward/pallas_call | solution.py:501
  109.4 8.0 %weight_grads.2 = (bf16[384,1536]{1,0:T(8,128)(2,1)}, bf16[384,1536]{1,0:T(8,128)(2,1)}, bf16[768,512]{1,0:T(8,128)(2,1)}, bf16[768,256]{1,0:T(8,128)(2,1)}) custom-call(s32[1]{0:T(128)} %bitcast.1.side_ref, bf16[512,768]{1,0:T(8,128)(2,1)} %get-tuple-element.64.n_ref, bf16[256,768]{1,0:T(8,128)(2,1)S(1)} %copy-done.6, ...), custom_call_target="tpu_custom_call" | custom-call | flops 805306368 | bytes 1572864 | tf_op jit(solution)/shard_map/cond/branch_1_fun/weight_grads/pallas_call | solution.py:896
  117.6 3.3 %collective-permute-done.got_ref = bf16[384,1536]{1,0:T(8,128)(2,1)} collective-permute-done((bf16[384,1536]{1,0:T(8,128)(2,1)}, bf16[384,1536]{1,0:T(8,128)(2,1)}, u32[]{:S(2)}, u32[]{:S(2)}) %collective-permute-start) | collective-permute-done | bytes 1179680 | tf_op jit(solution)/shard_map/cond/branch_1_fun/ppermute | solution.py:729
  120.9 2.9 %split_sum.2 = (bf16[96,1536]{1,0:T(8,128)(2,1)}, bf16[96,1536]{1,0:T(8,128)(2,1)}, bf16[96,1536]{1,0:T(8,128)(2,1)}, bf16[96,1536]{1,0:T(8,128)(2,1)}) custom-call(s32[1]{0:T(128)} %bitcast.number_ref, bf16[384,1536]{1,0:T(8,128)(2,1)} %get-tuple-element.84.kept_ref, bf16[384,1536]{1,0:T(8,128)(2,1)} %collective-permute-done.got_ref), custom_call_target="tpu_custom_call" | custom-call | flops 1000 | bytes 1000 | tf_op jit(solution)/shard_map/cond/branch_1_fun/split_sum/pallas_call | solution.py:923
  124.0 1.6 collective-permute-start.2
  125.6 1.7 collective-permute-start.3
  127.3 16.8 %attention_backward.3 = (bf16[3,512,512]{2,1,0:T(8,128)(2,1)}, bf16[2,256,512]{2,1,0:T(8,128)(2,1)}, f32[8,512]{1,0:T(8,128)}) custom-call(s32[1,3]{1,0:T(1,128)S(1)} %get-tuple-element.66.lens, bf16[512,2304]{1,0:T(8,128)(2,1)S(1)} %get-tuple-element.67.q_ref.k_ref.v_ref, bf16[512,2304]{1,0:T(8,128)(2,1)S(1)} %get-tuple-element.67.q_ref.k_ref.v_ref, ...), custom_call_target="tpu_custom_call" | custom-call | flops 7516192768 | bytes 5242880 | tf_op jit(solution)/shard_map/cond/branch_1_fun/attention_backward/pallas_call | solution.py:501
  145.5 5.6 %weight_grads.3 = (bf16[384,1536]{1,0:T(8,128)(2,1)}, bf16[384,1536]{1,0:T(8,128)(2,1)}) custom-call(s32[1]{0:T(128)} %bitcast.1.side_ref, bf16[768,512]{1,0:T(8,128)(2,1)} %get-tuple-element.112.n_ref, bf16[768,256]{1,0:T(8,128)(2,1)} %get-tuple-element.113.nt_ref, bf16[3,512,512]{2,1,0:T(8,128)(2,1)} %get-tuple-element.126.d_ref.two_ref, ...), custom_call_target="tpu_custom_call" | custom-call | flops 1610612736 | bytes 3145728 | tf_op jit(solution)/shard_map/cond/branch_1_fun/weight_grads/pallas_call | solution.py:896
  151.0 1.7 collective-permute-start.4
  155.2 2.9 %split_sum.3 = (bf16[96,1536]{1,0:T(8,128)(2,1)}, bf16[96,1536]{1,0:T(8,128)(2,1)}, bf16[96,1536]{1,0:T(8,128)(2,1)}, bf16[96,1536]{1,0:T(8,128)(2,1)}) custom-call(s32[1]{0:T(128)} %bitcast.number_ref, bf16[384,1536]{1,0:T(8,128)(2,1)} %get-tuple-element.114.kept_ref, bf16[384,1536]{1,0:T(8,128)(2,1)} %copy-done.4), custom_call_target="tpu_custom_call" | custom-call | flops 1000 | bytes 1000 | tf_op jit(solution)/shard_map/cond/branch_1_fun/split_sum/pallas_call | solution.py:923
  159.8 1.7 collective-permute-start.9
  161.6 2.7 %collective-permute-start.6 = (bf16[24,1536]{1,0:T(8,128)(2,1)S(1)}, bf16[24,1536]{1,0:T(8,128)(2,1)S(1)}, u32[]{:S(2)}, u32[]{:S(2)}) collective-permute-start(bf16[24,1536]{1,0:T(8,128)(2,1)S(1)} %constant_dynamic-slice_fusion.2), channel_id=1, source_target_pairs={{0,16},{1,17},{2,18},{3,19},{4,20},{5,21},{6,22},{7,23},{8,24},{9,... | collective-permute-start | bytes 221192 | tf_op jit(solution)/shard_map/cond/branch_1_fun/ppermute | solution.py:729
  164.6 8.4 %qkv_backward.1 = (f32[512,768]{1,0:T(8,128)}, bf16[256,768]{1,0:T(8,128)(2,1)}, f32[8,768]{1,0:T(8,128)}) custom-call(bf16[3,512,256]{2,1,0:T(8,128)(2,1)} %get-tuple-element.125.d_ref.one_ref, bf16[3,512,512]{2,1,0:T(8,128)(2,1)} %get-tuple-element.126.d_ref.two_ref, bf16[2,256,256]{2,1,0:T(8,128)(2,1)} %get-tuple-element.127.dt_ref.t_one_ref, ...), custom_call_target="tpu_custom_call" | custom-call | flops 2415919104 | bytes 7864320 | tf_op jit(solution)/shard_map/cond/branch_1_fun/qkv_backward/pallas_call | solution.py:641
  174.0 5.1 %collective-permute-done.9 = bf16[96,1536]{1,0:T(8,128)(2,1)S(1)} collective-permute-done((bf16[96,1536]{1,0:T(8,128)(2,1)}, bf16[96,1536]{1,0:T(8,128)(2,1)S(1)}, u32[]{:S(2)}, u32[]{:S(2)}) %collective-permute-start.9) | collective-permute-done | bytes 294944 | tf_op jit(solution)/shard_map/cond/branch_1_fun/ppermute | solution.py:729
  179.2 1.7 collective-permute-start.11
  181.0 2.7 %collective-permute-start.10 = (bf16[24,1536]{1,0:T(8,128)(2,1)S(1)}, bf16[24,1536]{1,0:T(8,128)(2,1)S(1)}, u32[]{:S(2)}, u32[]{:S(2)}) collective-permute-start(bf16[24,1536]{1,0:T(8,128)(2,1)S(1)} %add_convert_fusion.6), channel_id=1, source_target_pairs={{0,16},{1,17},{2,18},{3,19},{4,20},{5,21},{6,22},{7,23},{8,24},{9,... | collective-permute-start | bytes 221192 | tf_op jit(solution)/shard_map/cond/branch_1_fun/ppermute | solution.py:729
  184.8 1.7 collective-permute-start.24
  187.1 4.5 %collective-permute-start.13 = (bf16[24,1536]{1,0:T(8,128)(2,1)S(1)}, bf16[24,1536]{1,0:T(8,128)(2,1)S(1)}, u32[]{:S(2)}, u32[]{:S(2)}) collective-permute-start(bf16[24,1536]{1,0:T(8,128)(2,1)S(1)} %constant_dynamic-slice_fusion), channel_id=1, source_target_pairs={{0,16},{1,17},{2,18},{3,19},{4,20},{5,21},{6,22},{7,23},{8,24},{9,... | collective-permute-start | bytes 221192 | tf_op jit(solution)/shard_map/cond/branch_1_fun/ppermute | solution.py:729
  191.6 2.5 collective-permute-start.12
  196.0 3.3 %collective-permute-start.20 = (bf16[24,1536]{1,0:T(8,128)(2,1)S(1)}, bf16[24,1536]{1,0:T(8,128)(2,1)S(1)}, u32[]{:S(2)}, u32[]{:S(2)}) collective-permute-start(bf16[24,1536]{1,0:T(8,128)(2,1)S(1)} %add_convert_fusion.5), channel_id=1, source_target_pairs={{0,16},{1,17},{2,18},{3,19},{4,20},{5,21},{6,22},{7,23},{8,24},{9,... | collective-permute-start | bytes 221192 | tf_op jit(solution)/shard_map/cond/branch_1_fun/ppermute | solution.py:729
  199.3 2.7 %collective-permute-done.12 = bf16[48,1536]{1,0:T(8,128)(2,1)S(1)} collective-permute-done((bf16[48,1536]{1,0:T(8,128)(2,1)S(1)}, bf16[48,1536]{1,0:T(8,128)(2,1)S(1)}, u32[]{:S(2)}, u32[]{:S(2)}) %collective-permute-start.12) | collective-permute-done | bytes 147488 | tf_op jit(solution)/shard_map/cond/branch_1_fun/ppermute | solution.py:729
  203.8 3.1 %collective-permute-start.17 = (bf16[96,1536]{1,0:T(8,128)(2,1)}, bf16[96,1536]{1,0:T(8,128)(2,1)S(1)}, u32[]{:S(2)}, u32[]{:S(2)}) collective-permute-start(bf16[96,1536]{1,0:T(8,128)(2,1)} %pad_maximum_fusion.2), channel_id=1, source_target_pairs={{0,5},{1,4},{2,7},{3,6},{4,1},{5,0},{6,3},{7,2},{8,13},{9,12},{10,... | collective-permute-start | bytes 884744 | tf_op jit(solution)/shard_map/cond/branch_1_fun/ppermute | solution.py:729
  206.9 13.0 %collective-permute-done.24.next_ref = bf16[256,768]{1,0:T(8,128)(2,1)S(1)} collective-permute-done((bf16[256,768]{1,0:T(8,128)(2,1)S(1)}, bf16[256,768]{1,0:T(8,128)(2,1)S(1)}, u32[]{:S(2)}, u32[]{:S(2)}) %collective-permute-start.24) | collective-permute-done | bytes 393248 | tf_op jit(solution)/shard_map/cond/branch_1_fun/ppermute | solution.py:720
  220.7 3.5 %input_backward.1 = bf16[512,768]{1,0:T(8,128)(2,1)} custom-call(f32[512,768]{1,0:T(8,128)} %get-tuple-element.159.dn_ref, bf16[256,768]{1,0:T(8,128)(2,1)} %copy-done.7, bf16[512,768]{1,0:T(8,128)(2,1)S(1)} %get-tuple-element.130.x_ref, f32[512,768]{1,0:T(8,128)} %get-tuple-element.161.dm_ref, f32[8,768]{1,0:T(8,128)} %copy-done.5), custom_call_target="tpu_custom_call" | custom-call | flops 7864320 | bytes 4718592 | tf_op jit(solution)/shard_map/cond/branch_1_fun/input_backward/pallas_call | solution.py:675
  227.3 2.5 add_convert_fusion
  231.1 1.7 collective-permute-done.22
  236.7 2.2 collective-permute-start.34
  239.1 6.8 %widened.1 = (f32[768,1536]{1,0:T(8,128)}, f32[1536,768]{1,0:T(8,128)}) custom-call(bf16[768,1536]{1,0:T(8,128)(2,1)} %get-tuple-element.323.a_ref, bf16[1536,768]{1,0:T(8,128)(2,1)} %get-tuple-element.324.b_ref), custom_call_target="tpu_custom_call" | custom-call | bytes 14155776 | tf_op jit(solution)/shard_map/widened/pallas_call | solution.py:705
  253.8 1.6 fusion.18
  255.6 1.7 broadcast_select_fusion.8
  257.5 3.5 %convert_element_type.148 = f32[768,2304]{1,0:T(8,128)} convert(bf16[768,2304]{1,0:T(8,128)(2,1)S(1)} %fusion.23) | non-fusion elementwise | flops 1769472 | bytes 10616832 | tf_op jit(solution)/shard_map/convert_element_type | solution.py:1197
  (184 shorter events, 34.4 us)
Async XLA Ops:
  7.2 231.9 %all-reduce.3.cloned.1.call-start = ((), (), s32[]{:S(2)}) async-start(), calls=%async_computation | async-start | bytes 9437184 | tf_op jit(solution)/shard_map/psum | solution.py:1043
  7.3 34.0 %collective-permute-start.25 = (s32[1,3]{1,0:T(1,128)}, s32[1,3]{1,0:T(1,128)S(1)}, u32[]{:S(2)}, u32[]{:S(2)}) collective-permute-start(s32[1,3]{1,0:T(1,128)} %lens.1), channel_id=1, source_target_pairs={{0,1},{1,0},{2,3},{3,2},{4,5},{5,4},{6,7},{7,6},{8,9},{9,8},{10,11... | collective-permute-start | bytes 44 | tf_op jit(solution)/shard_map/ppermute | solution.py:720
  12.1 22.5 %collective-permute-start.26 = (bf16[256,768]{1,0:T(8,128)(2,1)}, bf16[256,768]{1,0:T(8,128)(2,1)}, u32[]{:S(2)}, u32[]{:S(2)}) collective-permute-start(bf16[256,768]{1,0:T(8,128)(2,1)} %slice.83), channel_id=1, source_target_pairs={{0,1},{1,0},{2,3},{3,2},{4,5},{5,4},{6,7},{7,6},{8,9},{9,8},{10,11... | collective-permute-start | bytes 1179656 | tf_op jit(solution)/shard_map/ppermute | solution.py:720
  12.2 29.0 %collective-permute-start.27 = (bf16[512,768]{1,0:T(8,128)(2,1)}, bf16[512,768]{1,0:T(8,128)(2,1)}, u32[]{:S(2)}, u32[]{:S(2)}) collective-permute-start(bf16[512,768]{1,0:T(8,128)(2,1)} %ct_ref.1), channel_id=1, source_target_pairs={{0,1},{1,0},{2,3},{3,2},{4,5},{5,4},{6,7},{7,6},{8,9},{9,8},{10,11... | collective-permute-start | bytes 2359304 | tf_op jit(solution)/shard_map/ppermute | solution.py:720
  34.3 19.6 %collective-permute-start.29 = (bf16[256,768]{1,0:T(8,128)(2,1)}, bf16[256,768]{1,0:T(8,128)(2,1)}, u32[]{:S(2)}, u32[]{:S(2)}) collective-permute-start(bf16[256,768]{1,0:T(8,128)(2,1)} %get-tuple-element.261), channel_id=1, source_target_pairs={{0,1},{1,0},{2,3},{3,2},{4,5},{5,4},{6,7},{7,6},{8,9},{9,8},{10,11... | collective-permute-start | bytes 1179656 | tf_op jit(solution)/shard_map/ppermute | solution.py:720
  41.8 12.2 %copy-start.20 = (bf16[1536]{0:T(1024)(128)(2,1)S(1)}, bf16[1536]{0:T(1024)(128)(2,1)}, u32[]{:S(2)}) copy-start(bf16[1536]{0:T(1024)(128)(2,1)} %param.28) | copy-start | bytes 9220
  53.7 9.3 %collective-permute-start.28 = (bf16[256,768]{1,0:T(8,128)(2,1)}, bf16[256,768]{1,0:T(8,128)(2,1)}, u32[]{:S(2)}, u32[]{:S(2)}) collective-permute-start(bf16[256,768]{1,0:T(8,128)(2,1)} %get-tuple-element.258), channel_id=1, source_target_pairs={{0,1},{1,0},{2,3},{3,2},{4,5},{5,4},{6,7},{7,6},{8,9},{9,8},{10,11... | collective-permute-start | bytes 1179656 | tf_op jit(solution)/shard_map/ppermute | solution.py:720
  61.1 21.7 %collective-permute-start.30 = (bf16[256,768]{1,0:T(8,128)(2,1)}, bf16[256,768]{1,0:T(8,128)(2,1)}, u32[]{:S(2)}, u32[]{:S(2)}) collective-permute-start(bf16[256,768]{1,0:T(8,128)(2,1)} %get-tuple-element.271), channel_id=1, source_target_pairs={{0,1},{1,0},{2,3},{3,2},{4,5},{5,4},{6,7},{7,6},{8,9},{9,8},{10,11... | collective-permute-start | bytes 1179656 | tf_op jit(solution)/shard_map/ppermute | solution.py:720
  69.6 13.2 %collective-permute-start.31 = (bf16[256,768]{1,0:T(8,128)(2,1)}, bf16[256,768]{1,0:T(8,128)(2,1)}, u32[]{:S(2)}, u32[]{:S(2)}) collective-permute-start(bf16[256,768]{1,0:T(8,128)(2,1)} %get-tuple-element.272), channel_id=1, source_target_pairs={{0,1},{1,0},{2,3},{3,2},{4,5},{5,4},{6,7},{7,6},{8,9},{9,8},{10,11... | collective-permute-start | bytes 1179656 | tf_op jit(solution)/shard_map/ppermute | solution.py:720
  99.7 9.7 %copy-start.6 = (bf16[256,768]{1,0:T(8,128)(2,1)S(1)}, bf16[256,768]{1,0:T(8,128)(2,1)}, u32[]{:S(2)}) copy-start(bf16[256,768]{1,0:T(8,128)(2,1)} %get-tuple-element.65.nt_ref) | copy-start | bytes 1179652 | tf_op jit(solution)/shard_map/cond
  117.5 9.8 %copy-start.28 = (f32[6,8,512]{2,1,0:T(8,128)S(1)}, f32[6,8,512]{2,1,0:T(8,128)}, u32[]{:S(2)}) copy-start(f32[6,8,512]{2,1,0:T(8,128)} %get-tuple-element.78.ll_ref) | copy-start | bytes 294916 | tf_op jit(solution)/shard_map/cond
  117.5 3.4 %collective-permute-start = (bf16[384,1536]{1,0:T(8,128)(2,1)}, bf16[384,1536]{1,0:T(8,128)(2,1)}, u32[]{:S(2)}, u32[]{:S(2)}) collective-permute-start(bf16[384,1536]{1,0:T(8,128)(2,1)} %get-tuple-element.85), channel_id=1, source_target_pairs={{0,2},{1,3},{2,0},{3,1},{4,6},{5,7},{6,4},{7,5},{8,10},{9,11},{10,... | collective-permute-start | bytes 3538952 | tf_op jit(solution)/shard_map/cond/branch_1_fun/ppermute | solution.py:729
  123.8 20.3 %copy-start.12 = (bf16[96,1536]{1,0:T(8,128)(2,1)S(1)}, bf16[96,1536]{1,0:T(8,128)(2,1)}, u32[]{:S(2)}) copy-start(bf16[96,1536]{1,0:T(8,128)(2,1)} %get-tuple-element.86) | copy-start | bytes 884740 | tf_op jit(solution)/shard_map/cond
  123.8 20.3 %collective-permute-start.1 = (bf16[96,1536]{1,0:T(8,128)(2,1)}, bf16[96,1536]{1,0:T(8,128)(2,1)}, u32[]{:S(2)}, u32[]{:S(2)}) collective-permute-start(bf16[96,1536]{1,0:T(8,128)(2,1)} %get-tuple-element.93), channel_id=1, source_target_pairs={{0,1},{1,0},{2,3},{3,2},{4,5},{5,4},{6,7},{7,6},{8,9},{9,8},{10,11... | collective-permute-start | bytes 884744 | tf_op jit(solution)/shard_map/cond/branch_1_fun/ppermute | solution.py:729
  124.0 20.1 %collective-permute-start.2 = (bf16[96,1536]{1,0:T(8,128)(2,1)}, bf16[96,1536]{1,0:T(8,128)(2,1)}, u32[]{:S(2)}, u32[]{:S(2)}) collective-permute-start(bf16[96,1536]{1,0:T(8,128)(2,1)} %get-tuple-element.94), channel_id=1, source_target_pairs={{0,4},{1,5},{2,6},{3,7},{4,0},{5,1},{6,2},{7,3},{8,12},{9,13},{10,... | collective-permute-start | bytes 884744 | tf_op jit(solution)/shard_map/cond/branch_1_fun/ppermute | solution.py:729
  125.6 18.5 %collective-permute-start.3 = (bf16[96,1536]{1,0:T(8,128)(2,1)}, bf16[96,1536]{1,0:T(8,128)(2,1)}, u32[]{:S(2)}, u32[]{:S(2)}) collective-permute-start(bf16[96,1536]{1,0:T(8,128)(2,1)} %get-tuple-element.95), channel_id=1, source_target_pairs={{0,5},{1,4},{2,7},{3,6},{4,1},{5,0},{6,3},{7,2},{8,13},{9,12},{10,... | collective-permute-start | bytes 884744 | tf_op jit(solution)/shard_map/cond/branch_1_fun/ppermute | solution.py:729
  151.0 3.1 %collective-permute-start.5 = (bf16[384,1536]{1,0:T(8,128)(2,1)}, bf16[384,1536]{1,0:T(8,128)(2,1)S(1)}, u32[]{:S(2)}, u32[]{:S(2)}) collective-permute-start(bf16[384,1536]{1,0:T(8,128)(2,1)} %get-tuple-element.115), channel_id=1, source_target_pairs={{0,2},{1,3},{2,0},{3,1},{4,6},{5,7},{6,4},{7,5},{8,10},{9,11},{10,... | collective-permute-start | bytes 3538952 | tf_op jit(solution)/shard_map/cond/branch_1_fun/ppermute | solution.py:729
  151.0 10.5 %collective-permute-start.4 = (bf16[48,1536]{1,0:T(8,128)(2,1)S(1)}, bf16[48,1536]{1,0:T(8,128)(2,1)S(1)}, u32[]{:S(2)}, u32[]{:S(2)}) collective-permute-start(bf16[48,1536]{1,0:T(8,128)(2,1)S(1)} %constant_dynamic-slice_fusion.3), channel_id=1, source_target_pairs={{0,8},{1,9},{2,10},{3,11},{4,12},{5,13},{6,14},{7,15},{8,0},{9,1},... | collective-permute-start | bytes 442376 | tf_op jit(solution)/shard_map/cond/branch_1_fun/ppermute | solution.py:729
  158.1 15.9 %collective-permute-start.7 = (bf16[96,1536]{1,0:T(8,128)(2,1)}, bf16[96,1536]{1,0:T(8,128)(2,1)S(1)}, u32[]{:S(2)}, u32[]{:S(2)}) collective-permute-start(bf16[96,1536]{1,0:T(8,128)(2,1)} %get-tuple-element.119), channel_id=1, source_target_pairs={{0,1},{1,0},{2,3},{3,2},{4,5},{5,4},{6,7},{7,6},{8,9},{9,8},{10,11... | collective-permute-start | bytes 884744 | tf_op jit(solution)/shard_map/cond/branch_1_fun/ppermute | solution.py:729
  158.3 15.6 %collective-permute-start.8 = (bf16[96,1536]{1,0:T(8,128)(2,1)}, bf16[96,1536]{1,0:T(8,128)(2,1)S(1)}, u32[]{:S(2)}, u32[]{:S(2)}) collective-permute-start(bf16[96,1536]{1,0:T(8,128)(2,1)} %get-tuple-element.120), channel_id=1, source_target_pairs={{0,4},{1,5},{2,6},{3,7},{4,0},{5,1},{6,2},{7,3},{8,12},{9,13},{10,... | collective-permute-start | bytes 884744 | tf_op jit(solution)/shard_map/cond/branch_1_fun/ppermute | solution.py:729
  159.8 19.2 %collective-permute-start.9 = (bf16[96,1536]{1,0:T(8,128)(2,1)}, bf16[96,1536]{1,0:T(8,128)(2,1)S(1)}, u32[]{:S(2)}, u32[]{:S(2)}) collective-permute-start(bf16[96,1536]{1,0:T(8,128)(2,1)} %get-tuple-element.121), channel_id=1, source_target_pairs={{0,5},{1,4},{2,7},{3,6},{4,1},{5,0},{6,3},{7,2},{8,13},{9,12},{10,... | collective-permute-start | bytes 884744 | tf_op jit(solution)/shard_map/cond/branch_1_fun/ppermute | solution.py:729
  161.6 12.3 %collective-permute-start.6 = (bf16[24,1536]{1,0:T(8,128)(2,1)S(1)}, bf16[24,1536]{1,0:T(8,128)(2,1)S(1)}, u32[]{:S(2)}, u32[]{:S(2)}) collective-permute-start(bf16[24,1536]{1,0:T(8,128)(2,1)S(1)} %constant_dynamic-slice_fusion.2), channel_id=1, source_target_pairs={{0,16},{1,17},{2,18},{3,19},{4,20},{5,21},{6,22},{7,23},{8,24},{9,... | collective-permute-start | bytes 221192 | tf_op jit(solution)/shard_map/cond/branch_1_fun/ppermute | solution.py:729
  173.0 11.4 %copy-start.15 = (f32[8,512]{1,0:T(8,128)S(1)}, f32[8,512]{1,0:T(8,128)}, u32[]{:S(2)}) copy-start(f32[8,512]{1,0:T(8,128)} %get-tuple-element.145) | copy-start | bytes 49156 | tf_op jit(solution)/shard_map/cond
  173.0 11.4 %copy-start.16 = (f32[8,256]{1,0:T(8,128)S(1)}, f32[8,256]{1,0:T(8,128)}, u32[]{:S(2)}) copy-start(f32[8,256]{1,0:T(8,128)} %get-tuple-element.144) | copy-start | bytes 24580 | tf_op jit(solution)/shard_map/cond
  173.0 11.8 %copy-start.27 = (bf16[256,768]{1,0:T(8,128)(2,1)S(1)}, bf16[256,768]{1,0:T(8,128)(2,1)}, u32[]{:S(2)}) copy-start(bf16[256,768]{1,0:T(8,128)(2,1)} %get-tuple-element.160) | copy-start | bytes 1179652 | tf_op jit(solution)/shard_map/cond
  179.2 7.8 %collective-permute-start.11 = (bf16[48,1536]{1,0:T(8,128)(2,1)S(1)}, bf16[48,1536]{1,0:T(8,128)(2,1)S(1)}, u32[]{:S(2)}, u32[]{:S(2)}) collective-permute-start(bf16[48,1536]{1,0:T(8,128)(2,1)S(1)} %constant_dynamic-slice_fusion.1), channel_id=1, source_target_pairs={{0,8},{1,9},{2,10},{3,11},{4,12},{5,13},{6,14},{7,15},{8,0},{9,1},... | collective-permute-start | bytes 442376 | tf_op jit(solution)/shard_map/cond/branch_1_fun/ppermute | solution.py:729
  181.0 10.6 %collective-permute-start.10 = (bf16[24,1536]{1,0:T(8,128)(2,1)S(1)}, bf16[24,1536]{1,0:T(8,128)(2,1)S(1)}, u32[]{:S(2)}, u32[]{:S(2)}) collective-permute-start(bf16[24,1536]{1,0:T(8,128)(2,1)S(1)} %add_convert_fusion.6), channel_id=1, source_target_pairs={{0,16},{1,17},{2,18},{3,19},{4,20},{5,21},{6,22},{7,23},{8,24},{9,... | collective-permute-start | bytes 221192 | tf_op jit(solution)/shard_map/cond/branch_1_fun/ppermute | solution.py:729
  184.4 9.8 %collective-permute-start.14 = (f32[12,768]{1,0:T(8,128)S(1)}, f32[12,768]{1,0:T(8,128)S(1)}, u32[]{:S(2)}, u32[]{:S(2)}) collective-permute-start(f32[12,768]{1,0:T(8,128)S(1)} %fusion.1), channel_id=1, source_target_pairs={{0,2},{1,3},{2,0},{3,1},{4,6},{5,7},{6,4},{7,5},{8,10},{9,11},{10,... | collective-permute-start | bytes 110600 | tf_op jit(solution)/shard_map/cond/branch_1_fun/ppermute | solution.py:729
  184.5 39.7 %collective-permute-start.21 = (bf16[512,768]{1,0:T(8,128)(2,1)}, bf16[512,768]{1,0:T(8,128)(2,1)}, u32[]{:S(2)}, u32[]{:S(2)}) collective-permute-start(bf16[512,768]{1,0:T(8,128)(2,1)} %pad_maximum_fusion.1), channel_id=1, source_target_pairs={{0,1},{1,0},{2,3},{3,2},{4,5},{5,4},{6,7},{7,6},{8,9},{9,8},{10,11... | collective-permute-start | bytes 2359304 | tf_op jit(solution)/shard_map/cond/branch_1_fun/ppermute | solution.py:720
  184.8 35.1 %collective-permute-start.24 = (bf16[256,768]{1,0:T(8,128)(2,1)S(1)}, bf16[256,768]{1,0:T(8,128)(2,1)S(1)}, u32[]{:S(2)}, u32[]{:S(2)}) collective-permute-start(bf16[256,768]{1,0:T(8,128)(2,1)S(1)} %copy-done.27), channel_id=1, source_target_pairs={{0,1},{1,0},{2,3},{3,2},{4,5},{5,4},{6,7},{7,6},{8,9},{9,8},{10,11... | collective-permute-start | bytes 1179656 | tf_op jit(solution)/shard_map/cond/branch_1_fun/ppermute | solution.py:720
  187.1 8.9 %collective-permute-start.13 = (bf16[24,1536]{1,0:T(8,128)(2,1)S(1)}, bf16[24,1536]{1,0:T(8,128)(2,1)S(1)}, u32[]{:S(2)}, u32[]{:S(2)}) collective-permute-start(bf16[24,1536]{1,0:T(8,128)(2,1)S(1)} %constant_dynamic-slice_fusion), channel_id=1, source_target_pairs={{0,16},{1,17},{2,18},{3,19},{4,20},{5,21},{6,22},{7,23},{8,24},{9,... | collective-permute-start | bytes 221192 | tf_op jit(solution)/shard_map/cond/branch_1_fun/ppermute | solution.py:729
  191.6 10.4 %collective-permute-start.12 = (bf16[48,1536]{1,0:T(8,128)(2,1)S(1)}, bf16[48,1536]{1,0:T(8,128)(2,1)S(1)}, u32[]{:S(2)}, u32[]{:S(2)}) collective-permute-start(bf16[48,1536]{1,0:T(8,128)(2,1)S(1)} %pad_maximum_fusion.4), channel_id=1, source_target_pairs={{0,8},{1,9},{2,10},{3,11},{4,12},{5,13},{6,14},{7,15},{8,0},{9,1},... | collective-permute-start | bytes 442376 | tf_op jit(solution)/shard_map/cond/branch_1_fun/ppermute | solution.py:729
  194.2 8.6 %collective-permute-start.18 = (f32[12,768]{1,0:T(8,128)S(1)}, f32[12,768]{1,0:T(8,128)S(1)}, u32[]{:S(2)}, u32[]{:S(2)}) collective-permute-start(f32[12,768]{1,0:T(8,128)S(1)} %add.132), channel_id=1, source_target_pairs={{0,4},{1,5},{2,6},{3,7},{4,0},{5,1},{6,2},{7,3},{8,12},{9,13},{10,... | collective-permute-start | bytes 110600 | tf_op jit(solution)/shard_map/cond/branch_1_fun/ppermute | solution.py:729
  196.0 24.4 %copy-start.10 = (bf16[24,1536]{1,0:T(8,128)(2,1)}, bf16[24,1536]{1,0:T(8,128)(2,1)S(1)}, u32[]{:S(2)}) copy-start(bf16[24,1536]{1,0:T(8,128)(2,1)S(1)} %add_convert_fusion.5) | copy-start | bytes 221188 | tf_op jit(solution)/shard_map/cond
  196.0 7.9 %collective-permute-start.20 = (bf16[24,1536]{1,0:T(8,128)(2,1)S(1)}, bf16[24,1536]{1,0:T(8,128)(2,1)S(1)}, u32[]{:S(2)}, u32[]{:S(2)}) collective-permute-start(bf16[24,1536]{1,0:T(8,128)(2,1)S(1)} %add_convert_fusion.5), channel_id=1, source_target_pairs={{0,16},{1,17},{2,18},{3,19},{4,20},{5,21},{6,22},{7,23},{8,24},{9,... | collective-permute-start | bytes 221192 | tf_op jit(solution)/shard_map/cond/branch_1_fun/ppermute | solution.py:729
  202.8 30.7 %collective-permute-start.15 = (bf16[96,1536]{1,0:T(8,128)(2,1)}, bf16[96,1536]{1,0:T(8,128)(2,1)S(1)}, u32[]{:S(2)}, u32[]{:S(2)}) collective-permute-start(bf16[96,1536]{1,0:T(8,128)(2,1)} %pad_maximum_fusion.2), channel_id=1, source_target_pairs={{0,1},{1,0},{2,3},{3,2},{4,5},{5,4},{6,7},{7,6},{8,9},{9,8},{10,11... | collective-permute-start | bytes 884744 | tf_op jit(solution)/shard_map/cond/branch_1_fun/ppermute | solution.py:729
  202.8 30.7 %collective-permute-start.16 = (bf16[96,1536]{1,0:T(8,128)(2,1)}, bf16[96,1536]{1,0:T(8,128)(2,1)S(1)}, u32[]{:S(2)}, u32[]{:S(2)}) collective-permute-start(bf16[96,1536]{1,0:T(8,128)(2,1)} %pad_maximum_fusion.2), channel_id=1, source_target_pairs={{0,4},{1,5},{2,6},{3,7},{4,0},{5,1},{6,2},{7,3},{8,12},{9,13},{10,... | collective-permute-start | bytes 884744 | tf_op jit(solution)/shard_map/cond/branch_1_fun/ppermute | solution.py:729
  203.8 16.5 %copy-start.13 = (bf16[24,1536]{1,0:T(8,128)(2,1)}, bf16[24,1536]{1,0:T(8,128)(2,1)S(1)}, u32[]{:S(2)}) copy-start(bf16[24,1536]{1,0:T(8,128)(2,1)S(1)} %collective-permute-done.20) | copy-start | bytes 221188 | tf_op jit(solution)/shard_map/cond
  203.8 29.6 %collective-permute-start.17 = (bf16[96,1536]{1,0:T(8,128)(2,1)}, bf16[96,1536]{1,0:T(8,128)(2,1)S(1)}, u32[]{:S(2)}, u32[]{:S(2)}) collective-permute-start(bf16[96,1536]{1,0:T(8,128)(2,1)} %pad_maximum_fusion.2), channel_id=1, source_target_pairs={{0,5},{1,4},{2,7},{3,6},{4,1},{5,0},{6,3},{7,2},{8,13},{9,12},{10,... | collective-permute-start | bytes 884744 | tf_op jit(solution)/shard_map/cond/branch_1_fun/ppermute | solution.py:729
  219.9 6.6 %collective-permute-start.19 = (f32[12,768]{1,0:T(8,128)}, f32[12,768]{1,0:T(8,128)}, u32[]{:S(2)}, u32[]{:S(2)}) collective-permute-start(f32[12,768]{1,0:T(8,128)} %add.134), channel_id=1, source_target_pairs={{0,8},{1,9},{2,10},{3,11},{4,12},{5,13},{6,14},{7,15},{8,0},{9,1},... | collective-permute-start | bytes 110600 | tf_op jit(solution)/shard_map/cond/branch_1_fun/ppermute | solution.py:729
  225.1 5.2 %collective-permute-start.23 = (bf16[48,1536]{1,0:T(8,128)(2,1)S(1)}, bf16[48,1536]{1,0:T(8,128)(2,1)S(1)}, u32[]{:S(2)}, u32[]{:S(2)}) collective-permute-start(bf16[48,1536]{1,0:T(8,128)(2,1)S(1)} %pad_maximum_fusion.5), channel_id=1, source_target_pairs={{0,8},{1,9},{2,10},{3,11},{4,12},{5,13},{6,14},{7,15},{8,0},{9,1},... | collective-permute-start | bytes 442376 | tf_op jit(solution)/shard_map/cond/branch_1_fun/ppermute | solution.py:729
  227.3 5.5 %collective-permute-start.22 = (f32[12,768]{1,0:T(8,128)S(1)}, f32[12,768]{1,0:T(8,128)S(1)}, u32[]{:S(2)}, u32[]{:S(2)}) collective-permute-start(f32[12,768]{1,0:T(8,128)S(1)} %add.135), channel_id=1, source_target_pairs={{0,16},{1,17},{2,18},{3,19},{4,20},{5,21},{6,22},{7,23},{8,24},{9,... | collective-permute-start | bytes 110600 | tf_op jit(solution)/shard_map/cond/branch_1_fun/ppermute | solution.py:729
  235.3 14.9 %collective-permute-start.32 = (bf16[96,1536]{1,0:T(8,128)(2,1)}, bf16[96,1536]{1,0:T(8,128)(2,1)S(1)}, u32[]{:S(2)}, u32[]{:S(2)}) collective-permute-start(bf16[96,1536]{1,0:T(8,128)(2,1)} %get-tuple-element.290), channel_id=1, source_target_pairs={{0,1},{1,0},{2,3},{3,2},{4,5},{5,4},{6,7},{7,6},{8,9},{9,8},{10,11... | collective-permute-start | bytes 884744 | tf_op jit(solution)/shard_map/ppermute | solution.py:729
  235.6 14.5 %collective-permute-start.33 = (bf16[96,1536]{1,0:T(8,128)(2,1)}, bf16[96,1536]{1,0:T(8,128)(2,1)S(1)}, u32[]{:S(2)}, u32[]{:S(2)}) collective-permute-start(bf16[96,1536]{1,0:T(8,128)(2,1)} %get-tuple-element.290), channel_id=1, source_target_pairs={{0,4},{1,5},{2,6},{3,7},{4,0},{5,1},{6,2},{7,3},{8,12},{9,13},{10,... | collective-permute-start | bytes 884744 | tf_op jit(solution)/shard_map/ppermute | solution.py:729
  236.7 13.5 %collective-permute-start.34 = (bf16[96,1536]{1,0:T(8,128)(2,1)}, bf16[96,1536]{1,0:T(8,128)(2,1)S(1)}, u32[]{:S(2)}, u32[]{:S(2)}) collective-permute-start(bf16[96,1536]{1,0:T(8,128)(2,1)} %get-tuple-element.290), channel_id=1, source_target_pairs={{0,5},{1,4},{2,7},{3,6},{4,1},{5,0},{6,3},{7,2},{8,13},{9,12},{10,... | collective-permute-start | bytes 884744 | tf_op jit(solution)/shard_map/ppermute | solution.py:729
  238.8 8.6 %collective-permute-start.35 = (f32[12,768]{1,0:T(8,128)}, f32[12,768]{1,0:T(8,128)S(1)}, u32[]{:S(2)}, u32[]{:S(2)}) collective-permute-start(f32[12,768]{1,0:T(8,128)} %get-tuple-element.291), channel_id=1, source_target_pairs={{0,1},{1,0},{2,3},{3,2},{4,5},{5,4},{6,7},{7,6},{8,9},{9,8},{10,11... | collective-permute-start | bytes 110600 | tf_op jit(solution)/shard_map/ppermute | solution.py:729
  239.1 13.3 %collective-permute-start.36 = (bf16[384,1536]{1,0:T(8,128)(2,1)}, bf16[384,1536]{1,0:T(8,128)(2,1)S(1)}, u32[]{:S(2)}, u32[]{:S(2)}) collective-permute-start(bf16[384,1536]{1,0:T(8,128)(2,1)} %get-tuple-element.301), channel_id=1, source_target_pairs={{0,2},{1,3},{2,0},{3,1},{4,6},{5,7},{6,4},{7,5},{8,10},{9,11},{10,... | collective-permute-start | bytes 3538952 | tf_op jit(solution)/shard_map/ppermute | solution.py:729
  252.4 3.2 %collective-permute-start.37 = (bf16[384,1536]{1,0:T(8,128)(2,1)}, bf16[384,1536]{1,0:T(8,128)(2,1)}, u32[]{:S(2)}, u32[]{:S(2)}) collective-permute-start(bf16[384,1536]{1,0:T(8,128)(2,1)} %pad_maximum_fusion.7), channel_id=1, source_target_pairs={{0,2},{1,3},{2,0},{3,1},{4,6},{5,7},{6,4},{7,5},{8,10},{9,11},{10,... | collective-permute-start | bytes 3538952 | tf_op jit(solution)/shard_map/ppermute | solution.py:729
  (21 other events, 113.1 us)
Sparse Core Ops, SparseCore 0:
  94.6 129.1 all-reduce.2

commit v6 on v5

--- a/solution.py
+++ b/solution.py
@@ -1094,11 +1094,11 @@
         chain_one.fly()
         chain_two.land()
         chain_two.fly()
+        y_given, unused = fence((y_given, chain_two.given))
         shares = [
             jnp.concatenate([y for (by, part), y in zip(calls, y_given) if by == step][::-1], axis=0)
             for step in steps
         ]
-        shares, unused = fence((shares, chain_two.given))
         returned = [rotated(y, "mlp", -step) for step, y in zip(steps, shares)]
         from_next = rotated(d_tail_rows, "mlp", -1)
         placed_bias = lax.dynamic_update_slice(

time: 273 us -> 267 us (0.978)
  waiting for transfers between devices: 31.9 us -> 29 us
    ppermute x9, waiting for transfers between devices: 14.9 us -> 4.35 us  [rotated(): lax.ppermute(value, axis, [(i, (i + by) % count) for i in range(count)])]
    ppermute x29, waiting for transfers between devices: 17 us -> 24.7 us  [flipped(): return lax.ppermute(value, GRID, [(i, i ^ mask) for i in range(count)])]
  transfers between devices with their start and end apart: 39 -> 39, of which waited for: 12 -> 11; matrix products, arithmetic and copies ran while one was open for 11% -> 11% of each run, Pallas kernels for 46% -> 47%
where the time goes in v6:
time: 267 us; the launch traced here: 263 us
  Pallas kernels  124 us (46%)
  starting transfers between devices  46 us (17%)
  waiting for transfers between devices  29 us (11%)
  other arithmetic  25.6 us (10%)
  matrix products  15.9 us (6%)
  between operations  14.8 us (6%)
  local copies, waits for them, and re-layouts  7.93 us (3%)
    ppermute x29, starting transfers between devices, flipped(): return lax.ppermute(value, GRID, [(i, i ^ mask) for i in range(count)])  34.1 us
    pallas_call x2, Pallas kernels, attention_backward(): pl.pallas_call(backward_kernel, grid=(pairs,), in_specs=[pl.BlockSpec(mem...  26.4 us
    ppermute x29, waiting for transfers between devices, flipped(): return lax.ppermute(value, GRID, [(i, i ^ mask) for i in range(count)])  24.7 us
    pallas_call x3, Pallas kernels, mlp_block(): pl.pallas_call(mlp_kernel, grid=(hidden // tile,), in_specs=[fixed, pl.Bl...  24.5 us
    pallas_call x2, Pallas kernels, weight_grads(): pl.pallas_call(kernel, grid=(steps,), in_specs=in_specs, out_specs=specs,...  13.6 us
    pallas_call x1, Pallas kernels, local_attention(): pl.pallas_call(local_kernel, grid=(PAIRS,), in_specs=[pl.BlockSpec(memory...  13.5 us
    pallas_call x1, Pallas kernels, memory_attention(): pl.pallas_call(memory_kernel, grid=(PAIRS,), in_specs=[pl.BlockSpec(memor...  12 us
    ppermute x9, starting transfers between devices, rotated(): lax.ppermute(value, axis, [(i, (i + by) % count) for i in range(count)])  11.9 us
  transfers between devices with their start and end apart: 39, of which 11 were waited for; matrix products, arithmetic and copies ran while one was open for 11% of the time, Pallas kernels for 47%

profile of v6, /device:TPU:0, one launch (start us, length us, event | category | flops | bytes accessed | tf_op | source)
XLA Modules:
  0.0 263.5 jit_solution(17322958809820506578)
XLA Ops:
  7.3 1.8 slice.83
  9.1 3.0 %collective-permute-start.26 = (bf16[256,768]{1,0:T(8,128)(2,1)}, bf16[256,768]{1,0:T(8,128)(2,1)}, u32[]{:S(2)}, u32[]{:S(2)}) collective-permute-start(bf16[256,768]{1,0:T(8,128)(2,1)} %slice.83), channel_id=1, source_target_pairs={{0,1},{1,0},{2,3},{3,2},{4,5},{5,4},{6,7},{7,6},{8,9},{9,8},{10,11... | collective-permute-start | bytes 1179656 | tf_op jit(solution)/shard_map/ppermute | solution.py:720
  12.1 2.0 collective-permute-start.25
  16.3 4.3 %fusion.3.q_ref.k_ref.v_ref = bf16[512,2304]{1,0:T(8,128)(2,1)S(1)} fusion(bf16[512,768]{1,0:T(8,128)(2,1)S(1)} %fusion.9, bf16[768,2304]{1,0:T(8,128)(2,1)} %w_ref.1, f32[2304]{0:T(1024)S(1)} %pad_maximum_fusion.9), kind=kOutput, calls=%fused_computation.37 | convolution fusion | flops 1814298624 | bytes 6693888 | tf_op jit(solution)/shard_map/dot_general | solution.py:27
  20.8 13.5 %local_attention.1 = (f32[256,768]{1,0:T(8,128)}, f32[6,8,512]{2,1,0:T(8,128)}, bf16[512,768]{1,0:T(8,128)(2,1)}, f32[512,768]{1,0:T(8,128)}, bf16[512,768]{1,0:T(8,128)(2,1)}, /*index=5*/bf16[256,768]{1,0:T(8,128)(2,1)}) custom-call(s32[1,3]{1,0:T(1,128)S(1)} %copy-done.25, bf16[512,2304]{1,0:T(8,128)(2,1)S(1)} %fusion.3.q_ref.k_ref.v_ref, ...), custom_call_target="tpu_custom_call" | custom-call | flops 2415919104 | bytes 3145728 | tf_op jit(solution)/shard_map/local_attention/pallas_call | solution.py:116
  34.5 4.7 %tail_projection.1 = (bf16[256,768]{1,0:T(8,128)(2,1)}, bf16[256,1536]{1,0:T(8,128)(2,1)}) custom-call(bf16[256,768]{1,0:T(8,128)(2,1)} %collective-permute-done.26.x_ref, f32[8,768]{1,0:T(8,128)S(1)} %concatenate.49.rows_ref.vb_ref, bf16[768,2304]{1,0:T(8,128)(2,1)} %w_ref.1), custom_call_target="tpu_custom_call" | custom-call | flops 603979776 | bytes 2359296 | tf_op jit(solution)/shard_map/tail_projection/pallas_call | solution.py:180
  39.7 12.0 %memory_attention.1 = (bf16[512,768]{1,0:T(8,128)(2,1)}, bf16[512,768]{1,0:T(8,128)(2,1)}, bf16[512,768]{1,0:T(8,128)(2,1)}, f32[6,8,256]{2,1,0:T(8,128)}, f32[5...) custom-call(s32[1,1]{1,0:T(1,128)S(6)} %select_n.313.reads, ...), custom_call_target="tpu_custom_call", output_to_operand_aliasing={{0}: (10, {}), {4}: (11, {}), {5}: (12, {})} | custom-call | flops 3221225472 | bytes 6291456 | tf_op jit(solution)/shard_map/memory_attention/pallas_call | solution.py:262
  51.7 2.1 collective-permute-start.28
  54.4 6.5 %mlp_block.3 = (bf16[1024,1536]{1,0:T(8,128)(2,1)}, bf16[1024,1536]{1,0:T(8,128)(2,1)}, f32[8,1536]{1,0:T(8,128)}, bf16[256,768]{1,0:T(8,128)(2,1)}, bf16[256,768]{1,0:T(8,128)(2,1)}) custom-call(bf16[256,768]{1,0:T(8,128)(2,1)} %collective-permute-done.29.x_ref, bf16[512,768]{1,0:T(8,128)(2,1)} %collective-permute-done.27.ct_ref, bf16[768,1536]{1,0:T(8,128)(2,1)} %wi_ref.5, ...), custom_call_target="tpu_custom_call" | custom-call | flops 2415919104 | bytes 7864320 | tf_op jit(solution)/shard_map/mlp_block/pallas_call | solution.py:372
  62.5 6.5 %mlp_block.4 = (bf16[1024,1536]{1,0:T(8,128)(2,1)}, bf16[1024,1536]{1,0:T(8,128)(2,1)}, f32[8,1536]{1,0:T(8,128)}, bf16[256,768]{1,0:T(8,128)(2,1)}, bf16[256,768]{1,0:T(8,128)(2,1)}) custom-call(bf16[256,768]{1,0:T(8,128)(2,1)} %collective-permute-done.28.x_ref, ...), custom_call_target="tpu_custom_call", output_to_operand_aliasing={{0}: (5, {}), {1}: (6, {})} | custom-call | flops 2415919104 | bytes 7864320 | tf_op jit(solution)/shard_map/mlp_block/pallas_call | solution.py:372
  69.1 2.6 collective-permute-start.31
  71.6 11.5 %mlp_block.5 = (bf16[1024,1536]{1,0:T(8,128)(2,1)}, bf16[1024,1536]{1,0:T(8,128)(2,1)}, f32[8,1536]{1,0:T(8,128)}, bf16[512,768]{1,0:T(8,128)(2,1)}, bf16[512,768]{1,0:T(8,128)(2,1)}) custom-call(bf16[512,768]{1,0:T(8,128)(2,1)} %get-tuple-element.258.x_ref, bf16[512,768]{1,0:T(8,128)(2,1)} %ct_ref.1, ...), custom_call_target="tpu_custom_call", output_to_operand_aliasing={{0}: (5, {}), {1}: (6, {})} | custom-call | flops 4831838208 | bytes 11010048 | tf_op jit(solution)/shard_map/mlp_block/pallas_call | solution.py:372
  83.1 6.5 %convolution_convert_fusion = bf16[1536,768]{1,0:T(8,128)(2,1)} fusion(bf16[1024,1536]{1,0:T(8,128)(2,1)} %get-tuple-element.294, bf16[512,768]{1,0:T(8,128)(2,1)} %collective-permute-done.27.ct_ref, bf16[512,768]{1,0:T(8,128)(2,1)} %ct_ref.1), kind=kOutput, calls=%fused_computation.38 | convolution fusion | flops 2420244480 | bytes 7077888 | tf_op jit(solution)/shard_map/dot_general | solution.py:1026
  89.7 5.1 %convolution_convert_fusion.1 = bf16[768,1536]{1,0:T(8,128)(2,1)} fusion(bf16[1024,1536]{1,0:T(8,128)(2,1)S(1)} %copy-done.2, bf16[256,768]{1,0:T(8,128)(2,1)} %collective-permute-done.29.x_ref, bf16[256,768]{1,0:T(8,128)(2,1)} %collective-permute-done.28.x_ref, bf16[512,768]{1,0:T(8,128)(2,1)S(1)} %copy-done.26), kind=kOutput, calls=%fused_computation.39 | convolution fusion | flops 2421817344 | bytes 7077888 | tf_op jit(solution)/shard_map/dot_general | solution.py:1026
  95.4 133.7 %conditional.1 = (bf16[384,1536]{1,0:T(8,128)(2,1)}, bf16[96,1536]{1,0:T(8,128)(2,1)}, f32[12,768]{1,0:T(8,128)}, bf16[512,768]{1,0:T(8,128)(2,1)}, bf16[512,768]{1,0:T(8,128)(2,1)}) conditional(s32[]{:T(128)} %bitcast.2, () %tuple.43, (bf16[512,768]{1,0:T(8,128)(2,1)}, bf16[512,768]{1,0:T(8,128)(2,1)}, f32[512,768]{1,0:T(8,128)}, ...), branch_computations={%region_2.3_spmd, %region_3.4_spmd} | conditional | flops 16139627520 | bytes 102844040 | solution.py:1152
  95.4 4.6 %middle_backward.1 = (f32[512,768]{1,0:T(8,128)}, bf16[512,768]{1,0:T(8,128)(2,1)}, f32[8,768]{1,0:T(8,128)}) custom-call(bf16[512,768]{1,0:T(8,128)(2,1)} %get-tuple-element.70.d_ref, bf16[512,768]{1,0:T(8,128)(2,1)} %get-tuple-element.71.ct_ref, f32[512,768]{1,0:T(8,128)} %get-tuple-element.72.middle_ref, f32[8,768]{1,0:T(8,128)S(1)} %get-tuple-element.73.rows_ref, ...), custom_call_target="tpu_custom_call" | custom-call | flops 7864320 | bytes 5505024 | tf_op jit(solution)/shard_map/cond/branch_1_fun/middle_backward/pallas_call | solution.py:595
  100.0 9.6 %attention_backward.2 = (bf16[3,512,256]{2,1,0:T(8,128)(2,1)}, bf16[2,256,256]{2,1,0:T(8,128)(2,1)}, f32[8,256]{1,0:T(8,128)}) custom-call(s32[1,3]{1,0:T(1,128)S(1)} %get-tuple-element.66.lens, bf16[512,2304]{1,0:T(8,128)(2,1)S(1)} %get-tuple-element.67.q_ref.k_ref.v_ref, bf16[512,2304]{1,0:T(8,128)(2,1)S(1)} %get-tuple-element.67.q_ref.k_ref.v_ref, ...), custom_call_target="tpu_custom_call" | custom-call | flops 3758096384 | bytes 2621440 | tf_op jit(solution)/shard_map/cond/branch_1_fun/attention_backward/pallas_call | solution.py:501
  109.7 8.0 %weight_grads.2 = (bf16[384,1536]{1,0:T(8,128)(2,1)}, bf16[384,1536]{1,0:T(8,128)(2,1)}, bf16[768,512]{1,0:T(8,128)(2,1)}, bf16[768,256]{1,0:T(8,128)(2,1)}) custom-call(s32[1]{0:T(128)} %bitcast.1.side_ref, bf16[512,768]{1,0:T(8,128)(2,1)} %get-tuple-element.64.n_ref, bf16[256,768]{1,0:T(8,128)(2,1)S(1)} %copy-done.6, ...), custom_call_target="tpu_custom_call" | custom-call | flops 805306368 | bytes 1572864 | tf_op jit(solution)/shard_map/cond/branch_1_fun/weight_grads/pallas_call | solution.py:896
  117.8 3.3 %collective-permute-done.got_ref = bf16[384,1536]{1,0:T(8,128)(2,1)} collective-permute-done((bf16[384,1536]{1,0:T(8,128)(2,1)}, bf16[384,1536]{1,0:T(8,128)(2,1)}, u32[]{:S(2)}, u32[]{:S(2)}) %collective-permute-start) | collective-permute-done | bytes 1179680 | tf_op jit(solution)/shard_map/cond/branch_1_fun/ppermute | solution.py:729
  121.1 2.9 %split_sum.2 = (bf16[96,1536]{1,0:T(8,128)(2,1)}, bf16[96,1536]{1,0:T(8,128)(2,1)}, bf16[96,1536]{1,0:T(8,128)(2,1)}, bf16[96,1536]{1,0:T(8,128)(2,1)}) custom-call(s32[1]{0:T(128)} %bitcast.number_ref, bf16[384,1536]{1,0:T(8,128)(2,1)} %get-tuple-element.84.kept_ref, bf16[384,1536]{1,0:T(8,128)(2,1)} %collective-permute-done.got_ref), custom_call_target="tpu_custom_call" | custom-call | flops 1000 | bytes 1000 | tf_op jit(solution)/shard_map/cond/branch_1_fun/split_sum/pallas_call | solution.py:923
  124.0 1.7 collective-permute-start.2
  125.7 1.8 collective-permute-start.3
  127.5 16.8 %attention_backward.3 = (bf16[3,512,512]{2,1,0:T(8,128)(2,1)}, bf16[2,256,512]{2,1,0:T(8,128)(2,1)}, f32[8,512]{1,0:T(8,128)}) custom-call(s32[1,3]{1,0:T(1,128)S(1)} %get-tuple-element.66.lens, bf16[512,2304]{1,0:T(8,128)(2,1)S(1)} %get-tuple-element.67.q_ref.k_ref.v_ref, bf16[512,2304]{1,0:T(8,128)(2,1)S(1)} %get-tuple-element.67.q_ref.k_ref.v_ref, ...), custom_call_target="tpu_custom_call" | custom-call | flops 7516192768 | bytes 5242880 | tf_op jit(solution)/shard_map/cond/branch_1_fun/attention_backward/pallas_call | solution.py:501
  145.7 5.6 %weight_grads.3 = (bf16[384,1536]{1,0:T(8,128)(2,1)}, bf16[384,1536]{1,0:T(8,128)(2,1)}) custom-call(s32[1]{0:T(128)} %bitcast.1.side_ref, bf16[768,512]{1,0:T(8,128)(2,1)} %get-tuple-element.112.n_ref, bf16[768,256]{1,0:T(8,128)(2,1)} %get-tuple-element.113.nt_ref, bf16[3,512,512]{2,1,0:T(8,128)(2,1)} %get-tuple-element.126.d_ref.two_ref, ...), custom_call_target="tpu_custom_call" | custom-call | flops 1610612736 | bytes 3145728 | tf_op jit(solution)/shard_map/cond/branch_1_fun/weight_grads/pallas_call | solution.py:896
  151.2 1.6 collective-permute-start.4
  155.4 2.8 %split_sum.3 = (bf16[96,1536]{1,0:T(8,128)(2,1)}, bf16[96,1536]{1,0:T(8,128)(2,1)}, bf16[96,1536]{1,0:T(8,128)(2,1)}, bf16[96,1536]{1,0:T(8,128)(2,1)}) custom-call(s32[1]{0:T(128)} %bitcast.number_ref, bf16[384,1536]{1,0:T(8,128)(2,1)} %get-tuple-element.114.kept_ref, bf16[384,1536]{1,0:T(8,128)(2,1)} %copy-done.4), custom_call_target="tpu_custom_call" | custom-call | flops 1000 | bytes 1000 | tf_op jit(solution)/shard_map/cond/branch_1_fun/split_sum/pallas_call | solution.py:923
  159.9 1.8 collective-permute-start.9
  161.8 2.6 %collective-permute-start.6 = (bf16[24,1536]{1,0:T(8,128)(2,1)S(1)}, bf16[24,1536]{1,0:T(8,128)(2,1)S(1)}, u32[]{:S(2)}, u32[]{:S(2)}) collective-permute-start(bf16[24,1536]{1,0:T(8,128)(2,1)S(1)} %constant_dynamic-slice_fusion.2), channel_id=1, source_target_pairs={{0,16},{1,17},{2,18},{3,19},{4,20},{5,21},{6,22},{7,23},{8,24},{9,... | collective-permute-start | bytes 221192 | tf_op jit(solution)/shard_map/cond/branch_1_fun/ppermute | solution.py:729
  164.4 8.4 %qkv_backward.1 = (f32[512,768]{1,0:T(8,128)}, bf16[256,768]{1,0:T(8,128)(2,1)}, f32[8,768]{1,0:T(8,128)}) custom-call(bf16[3,512,256]{2,1,0:T(8,128)(2,1)} %get-tuple-element.125.d_ref.one_ref, bf16[3,512,512]{2,1,0:T(8,128)(2,1)} %get-tuple-element.126.d_ref.two_ref, bf16[2,256,256]{2,1,0:T(8,128)(2,1)} %get-tuple-element.127.dt_ref.t_one_ref, ...), custom_call_target="tpu_custom_call" | custom-call | flops 2415919104 | bytes 7864320 | tf_op jit(solution)/shard_map/cond/branch_1_fun/qkv_backward/pallas_call | solution.py:641
  173.1 6.0 %collective-permute-done.9 = bf16[96,1536]{1,0:T(8,128)(2,1)S(1)} collective-permute-done((bf16[96,1536]{1,0:T(8,128)(2,1)}, bf16[96,1536]{1,0:T(8,128)(2,1)S(1)}, u32[]{:S(2)}, u32[]{:S(2)}) %collective-permute-start.9) | collective-permute-done | bytes 294944 | tf_op jit(solution)/shard_map/cond/branch_1_fun/ppermute | solution.py:729
  179.4 1.6 collective-permute-start.11
  183.1 2.7 %collective-permute-start.10 = (bf16[24,1536]{1,0:T(8,128)(2,1)S(1)}, bf16[24,1536]{1,0:T(8,128)(2,1)S(1)}, u32[]{:S(2)}, u32[]{:S(2)}) collective-permute-start(bf16[24,1536]{1,0:T(8,128)(2,1)S(1)} %add_convert_fusion.6), channel_id=1, source_target_pairs={{0,16},{1,17},{2,18},{3,19},{4,20},{5,21},{6,22},{7,23},{8,24},{9,... | collective-permute-start | bytes 221192 | tf_op jit(solution)/shard_map/cond/branch_1_fun/ppermute | solution.py:729
  185.8 1.7 collective-permute-start.24
  189.0 3.3 %collective-permute-done.10 = bf16[24,1536]{1,0:T(8,128)(2,1)S(1)} collective-permute-done((bf16[24,1536]{1,0:T(8,128)(2,1)S(1)}, bf16[24,1536]{1,0:T(8,128)(2,1)S(1)}, u32[]{:S(2)}, u32[]{:S(2)}) %collective-permute-start.10) | collective-permute-done | bytes 73760 | tf_op jit(solution)/shard_map/cond/branch_1_fun/ppermute | solution.py:729
  192.4 1.9 collective-permute-start.18
  194.3 2.2 collective-permute-done.13
  197.8 4.1 %collective-permute-done.12 = bf16[48,1536]{1,0:T(8,128)(2,1)S(1)} collective-permute-done((bf16[48,1536]{1,0:T(8,128)(2,1)S(1)}, bf16[48,1536]{1,0:T(8,128)(2,1)S(1)}, u32[]{:S(2)}, u32[]{:S(2)}) %collective-permute-start.12) | collective-permute-done | bytes 147488 | tf_op jit(solution)/shard_map/cond/branch_1_fun/ppermute | solution.py:729
  202.6 4.1 %collective-permute-start.15 = (bf16[96,1536]{1,0:T(8,128)(2,1)}, bf16[96,1536]{1,0:T(8,128)(2,1)S(1)}, u32[]{:S(2)}, u32[]{:S(2)}) collective-permute-start(bf16[96,1536]{1,0:T(8,128)(2,1)} %pad_maximum_fusion.2), channel_id=1, source_target_pairs={{0,1},{1,0},{2,3},{3,2},{4,5},{5,4},{6,7},{7,6},{8,9},{9,8},{10,11... | collective-permute-start | bytes 884744 | tf_op jit(solution)/shard_map/cond/branch_1_fun/ppermute | solution.py:729
  208.1 2.9 %collective-permute-done.24.next_ref = bf16[256,768]{1,0:T(8,128)(2,1)S(1)} collective-permute-done((bf16[256,768]{1,0:T(8,128)(2,1)S(1)}, bf16[256,768]{1,0:T(8,128)(2,1)S(1)}, u32[]{:S(2)}, u32[]{:S(2)}) %collective-permute-start.24) | collective-permute-done | bytes 393248 | tf_op jit(solution)/shard_map/cond/branch_1_fun/ppermute | solution.py:720
  212.0 3.5 %input_backward.1 = bf16[512,768]{1,0:T(8,128)(2,1)} custom-call(f32[512,768]{1,0:T(8,128)} %get-tuple-element.160.dn_ref, bf16[256,768]{1,0:T(8,128)(2,1)} %copy-done.7, bf16[512,768]{1,0:T(8,128)(2,1)S(1)} %get-tuple-element.130.x_ref, f32[512,768]{1,0:T(8,128)} %get-tuple-element.162.dm_ref, f32[8,768]{1,0:T(8,128)} %copy-done.5), custom_call_target="tpu_custom_call" | custom-call | flops 7864320 | bytes 4718592 | tf_op jit(solution)/shard_map/cond/branch_1_fun/input_backward/pallas_call | solution.py:675
  217.7 2.6 collective-permute-start.22
  220.4 2.6 add_convert_fusion
  222.9 3.0 %collective-permute-done.23 = bf16[48,1536]{1,0:T(8,128)(2,1)S(1)} collective-permute-done((bf16[48,1536]{1,0:T(8,128)(2,1)S(1)}, bf16[48,1536]{1,0:T(8,128)(2,1)S(1)}, u32[]{:S(2)}, u32[]{:S(2)}) %collective-permute-start.23) | collective-permute-done | bytes 147488 | tf_op jit(solution)/shard_map/cond/branch_1_fun/ppermute | solution.py:729
  234.1 6.8 %widened.1 = (f32[768,1536]{1,0:T(8,128)}, f32[1536,768]{1,0:T(8,128)}) custom-call(bf16[768,1536]{1,0:T(8,128)(2,1)} %get-tuple-element.324.a_ref, bf16[1536,768]{1,0:T(8,128)(2,1)} %get-tuple-element.325.b_ref), custom_call_target="tpu_custom_call" | custom-call | bytes 14155776 | tf_op jit(solution)/shard_map/widened/pallas_call | solution.py:705
  240.8 2.0 collective-permute-done.35
  249.2 1.6 fusion.18
  251.0 1.7 broadcast_select_fusion.8
  252.9 3.5 %convert_element_type.148 = f32[768,2304]{1,0:T(8,128)} convert(bf16[768,2304]{1,0:T(8,128)(2,1)S(1)} %fusion.23) | non-fusion elementwise | flops 1769472 | bytes 10616832 | tf_op jit(solution)/shard_map/convert_element_type | solution.py:1197
  (184 shorter events, 36.8 us)
Async XLA Ops:
  7.2 8.6 %copy-start.17 = (bf16[768]{0:T(1024)(128)(2,1)S(1)}, bf16[768]{0:T(1024)(128)(2,1)}, u32[]{:S(2)}) copy-start(bf16[768]{0:T(1024)(128)(2,1)} %param.19) | copy-start | bytes 4612
  7.2 8.6 %copy-start.18 = (bf16[768]{0:T(1024)(128)(2,1)S(1)}, bf16[768]{0:T(1024)(128)(2,1)}, u32[]{:S(2)}) copy-start(bf16[768]{0:T(1024)(128)(2,1)} %param.20) | copy-start | bytes 4612
  7.2 8.6 %copy-start.14 = (bf16[2,768]{1,0:T(2,128)(2,1)S(1)}, bf16[2,768]{1,0:T(2,128)(2,1)}, u32[]{:S(2)}) copy-start(bf16[2,768]{1,0:T(2,128)(2,1)} %param.22) | copy-start | bytes 9220
  7.2 226.9 %all-reduce.3.cloned.1.call-start = ((), (), s32[]{:S(2)}) async-start(), calls=%async_computation | async-start | bytes 9437184 | tf_op jit(solution)/shard_map/psum | solution.py:1043
  9.1 25.4 %collective-permute-start.26 = (bf16[256,768]{1,0:T(8,128)(2,1)}, bf16[256,768]{1,0:T(8,128)(2,1)}, u32[]{:S(2)}, u32[]{:S(2)}) collective-permute-start(bf16[256,768]{1,0:T(8,128)(2,1)} %slice.83), channel_id=1, source_target_pairs={{0,1},{1,0},{2,3},{3,2},{4,5},{5,4},{6,7},{7,6},{8,9},{9,8},{10,11... | collective-permute-start | bytes 1179656 | tf_op jit(solution)/shard_map/ppermute | solution.py:720
  12.1 27.1 %collective-permute-start.27 = (bf16[512,768]{1,0:T(8,128)(2,1)}, bf16[512,768]{1,0:T(8,128)(2,1)}, u32[]{:S(2)}, u32[]{:S(2)}) collective-permute-start(bf16[512,768]{1,0:T(8,128)(2,1)} %ct_ref.1), channel_id=1, source_target_pairs={{0,1},{1,0},{2,3},{3,2},{4,5},{5,4},{6,7},{7,6},{8,9},{9,8},{10,11... | collective-permute-start | bytes 2359304 | tf_op jit(solution)/shard_map/ppermute | solution.py:720
  12.1 27.1 %collective-permute-start.25 = (s32[1,3]{1,0:T(1,128)}, s32[1,3]{1,0:T(1,128)S(1)}, u32[]{:S(2)}, u32[]{:S(2)}) collective-permute-start(s32[1,3]{1,0:T(1,128)} %lens.1), channel_id=1, source_target_pairs={{0,1},{1,0},{2,3},{3,2},{4,5},{5,4},{6,7},{7,6},{8,9},{9,8},{10,11... | collective-permute-start | bytes 44 | tf_op jit(solution)/shard_map/ppermute | solution.py:720
  34.3 19.5 %collective-permute-start.29 = (bf16[256,768]{1,0:T(8,128)(2,1)}, bf16[256,768]{1,0:T(8,128)(2,1)}, u32[]{:S(2)}, u32[]{:S(2)}) collective-permute-start(bf16[256,768]{1,0:T(8,128)(2,1)} %get-tuple-element.262), channel_id=1, source_target_pairs={{0,1},{1,0},{2,3},{3,2},{4,5},{5,4},{6,7},{7,6},{8,9},{9,8},{10,11... | collective-permute-start | bytes 1179656 | tf_op jit(solution)/shard_map/ppermute | solution.py:720
  39.7 14.1 %copy-start.20 = (bf16[1536]{0:T(1024)(128)(2,1)S(1)}, bf16[1536]{0:T(1024)(128)(2,1)}, u32[]{:S(2)}) copy-start(bf16[1536]{0:T(1024)(128)(2,1)} %param.28) | copy-start | bytes 9220
  51.7 10.8 %collective-permute-start.28 = (bf16[256,768]{1,0:T(8,128)(2,1)}, bf16[256,768]{1,0:T(8,128)(2,1)}, u32[]{:S(2)}, u32[]{:S(2)}) collective-permute-start(bf16[256,768]{1,0:T(8,128)(2,1)} %get-tuple-element.259), channel_id=1, source_target_pairs={{0,1},{1,0},{2,3},{3,2},{4,5},{5,4},{6,7},{7,6},{8,9},{9,8},{10,11... | collective-permute-start | bytes 1179656 | tf_op jit(solution)/shard_map/ppermute | solution.py:720
  61.0 22.1 %collective-permute-start.30 = (bf16[256,768]{1,0:T(8,128)(2,1)}, bf16[256,768]{1,0:T(8,128)(2,1)}, u32[]{:S(2)}, u32[]{:S(2)}) collective-permute-start(bf16[256,768]{1,0:T(8,128)(2,1)} %get-tuple-element.272), channel_id=1, source_target_pairs={{0,1},{1,0},{2,3},{3,2},{4,5},{5,4},{6,7},{7,6},{8,9},{9,8},{10,11... | collective-permute-start | bytes 1179656 | tf_op jit(solution)/shard_map/ppermute | solution.py:720
  69.1 14.1 %collective-permute-start.31 = (bf16[256,768]{1,0:T(8,128)(2,1)}, bf16[256,768]{1,0:T(8,128)(2,1)}, u32[]{:S(2)}, u32[]{:S(2)}) collective-permute-start(bf16[256,768]{1,0:T(8,128)(2,1)} %get-tuple-element.273), channel_id=1, source_target_pairs={{0,1},{1,0},{2,3},{3,2},{4,5},{5,4},{6,7},{7,6},{8,9},{9,8},{10,11... | collective-permute-start | bytes 1179656 | tf_op jit(solution)/shard_map/ppermute | solution.py:720
  100.0 9.6 %copy-start.6 = (bf16[256,768]{1,0:T(8,128)(2,1)S(1)}, bf16[256,768]{1,0:T(8,128)(2,1)}, u32[]{:S(2)}) copy-start(bf16[256,768]{1,0:T(8,128)(2,1)} %get-tuple-element.65.nt_ref) | copy-start | bytes 1179652 | tf_op jit(solution)/shard_map/cond
  117.7 9.8 %copy-start.28 = (f32[6,8,512]{2,1,0:T(8,128)S(1)}, f32[6,8,512]{2,1,0:T(8,128)}, u32[]{:S(2)}) copy-start(f32[6,8,512]{2,1,0:T(8,128)} %get-tuple-element.78.ll_ref) | copy-start | bytes 294916 | tf_op jit(solution)/shard_map/cond
  117.7 3.4 %collective-permute-start = (bf16[384,1536]{1,0:T(8,128)(2,1)}, bf16[384,1536]{1,0:T(8,128)(2,1)}, u32[]{:S(2)}, u32[]{:S(2)}) collective-permute-start(bf16[384,1536]{1,0:T(8,128)(2,1)} %get-tuple-element.85), channel_id=1, source_target_pairs={{0,2},{1,3},{2,0},{3,1},{4,6},{5,7},{6,4},{7,5},{8,10},{9,11},{10,... | collective-permute-start | bytes 3538952 | tf_op jit(solution)/shard_map/cond/branch_1_fun/ppermute | solution.py:729
  124.0 20.3 %copy-start.12 = (bf16[96,1536]{1,0:T(8,128)(2,1)S(1)}, bf16[96,1536]{1,0:T(8,128)(2,1)}, u32[]{:S(2)}) copy-start(bf16[96,1536]{1,0:T(8,128)(2,1)} %get-tuple-element.86) | copy-start | bytes 884740 | tf_op jit(solution)/shard_map/cond
  124.0 20.3 %collective-permute-start.1 = (bf16[96,1536]{1,0:T(8,128)(2,1)}, bf16[96,1536]{1,0:T(8,128)(2,1)}, u32[]{:S(2)}, u32[]{:S(2)}) collective-permute-start(bf16[96,1536]{1,0:T(8,128)(2,1)} %get-tuple-element.93), channel_id=1, source_target_pairs={{0,1},{1,0},{2,3},{3,2},{4,5},{5,4},{6,7},{7,6},{8,9},{9,8},{10,11... | collective-permute-start | bytes 884744 | tf_op jit(solution)/shard_map/cond/branch_1_fun/ppermute | solution.py:729
  124.0 20.3 %collective-permute-start.2 = (bf16[96,1536]{1,0:T(8,128)(2,1)}, bf16[96,1536]{1,0:T(8,128)(2,1)}, u32[]{:S(2)}, u32[]{:S(2)}) collective-permute-start(bf16[96,1536]{1,0:T(8,128)(2,1)} %get-tuple-element.94), channel_id=1, source_target_pairs={{0,4},{1,5},{2,6},{3,7},{4,0},{5,1},{6,2},{7,3},{8,12},{9,13},{10,... | collective-permute-start | bytes 884744 | tf_op jit(solution)/shard_map/cond/branch_1_fun/ppermute | solution.py:729
  125.7 18.6 %collective-permute-start.3 = (bf16[96,1536]{1,0:T(8,128)(2,1)}, bf16[96,1536]{1,0:T(8,128)(2,1)}, u32[]{:S(2)}, u32[]{:S(2)}) collective-permute-start(bf16[96,1536]{1,0:T(8,128)(2,1)} %get-tuple-element.95), channel_id=1, source_target_pairs={{0,5},{1,4},{2,7},{3,6},{4,1},{5,0},{6,3},{7,2},{8,13},{9,12},{10,... | collective-permute-start | bytes 884744 | tf_op jit(solution)/shard_map/cond/branch_1_fun/ppermute | solution.py:729
  151.2 3.1 %collective-permute-start.5 = (bf16[384,1536]{1,0:T(8,128)(2,1)}, bf16[384,1536]{1,0:T(8,128)(2,1)S(1)}, u32[]{:S(2)}, u32[]{:S(2)}) collective-permute-start(bf16[384,1536]{1,0:T(8,128)(2,1)} %get-tuple-element.115), channel_id=1, source_target_pairs={{0,2},{1,3},{2,0},{3,1},{4,6},{5,7},{6,4},{7,5},{8,10},{9,11},{10,... | collective-permute-start | bytes 3538952 | tf_op jit(solution)/shard_map/cond/branch_1_fun/ppermute | solution.py:729
  151.2 10.4 %collective-permute-start.4 = (bf16[48,1536]{1,0:T(8,128)(2,1)S(1)}, bf16[48,1536]{1,0:T(8,128)(2,1)S(1)}, u32[]{:S(2)}, u32[]{:S(2)}) collective-permute-start(bf16[48,1536]{1,0:T(8,128)(2,1)S(1)} %constant_dynamic-slice_fusion.3), channel_id=1, source_target_pairs={{0,8},{1,9},{2,10},{3,11},{4,12},{5,13},{6,14},{7,15},{8,0},{9,1},... | collective-permute-start | bytes 442376 | tf_op jit(solution)/shard_map/cond/branch_1_fun/ppermute | solution.py:729
  158.2 14.9 %collective-permute-start.7 = (bf16[96,1536]{1,0:T(8,128)(2,1)}, bf16[96,1536]{1,0:T(8,128)(2,1)S(1)}, u32[]{:S(2)}, u32[]{:S(2)}) collective-permute-start(bf16[96,1536]{1,0:T(8,128)(2,1)} %get-tuple-element.119), channel_id=1, source_target_pairs={{0,1},{1,0},{2,3},{3,2},{4,5},{5,4},{6,7},{7,6},{8,9},{9,8},{10,11... | collective-permute-start | bytes 884744 | tf_op jit(solution)/shard_map/cond/branch_1_fun/ppermute | solution.py:729
  158.4 14.7 %collective-permute-start.8 = (bf16[96,1536]{1,0:T(8,128)(2,1)}, bf16[96,1536]{1,0:T(8,128)(2,1)S(1)}, u32[]{:S(2)}, u32[]{:S(2)}) collective-permute-start(bf16[96,1536]{1,0:T(8,128)(2,1)} %get-tuple-element.120), channel_id=1, source_target_pairs={{0,4},{1,5},{2,6},{3,7},{4,0},{5,1},{6,2},{7,3},{8,12},{9,13},{10,... | collective-permute-start | bytes 884744 | tf_op jit(solution)/shard_map/cond/branch_1_fun/ppermute | solution.py:729
  159.9 19.3 %collective-permute-start.9 = (bf16[96,1536]{1,0:T(8,128)(2,1)}, bf16[96,1536]{1,0:T(8,128)(2,1)S(1)}, u32[]{:S(2)}, u32[]{:S(2)}) collective-permute-start(bf16[96,1536]{1,0:T(8,128)(2,1)} %get-tuple-element.121), channel_id=1, source_target_pairs={{0,5},{1,4},{2,7},{3,6},{4,1},{5,0},{6,3},{7,2},{8,13},{9,12},{10,... | collective-permute-start | bytes 884744 | tf_op jit(solution)/shard_map/cond/branch_1_fun/ppermute | solution.py:729
  161.8 11.4 %collective-permute-start.6 = (bf16[24,1536]{1,0:T(8,128)(2,1)S(1)}, bf16[24,1536]{1,0:T(8,128)(2,1)S(1)}, u32[]{:S(2)}, u32[]{:S(2)}) collective-permute-start(bf16[24,1536]{1,0:T(8,128)(2,1)S(1)} %constant_dynamic-slice_fusion.2), channel_id=1, source_target_pairs={{0,16},{1,17},{2,18},{3,19},{4,20},{5,21},{6,22},{7,23},{8,24},{9,... | collective-permute-start | bytes 221192 | tf_op jit(solution)/shard_map/cond/branch_1_fun/ppermute | solution.py:729
  164.4 14.8 %copy-start.11 = (bf16[96,1536]{1,0:T(8,128)(2,1)S(1)}, bf16[96,1536]{1,0:T(8,128)(2,1)}, u32[]{:S(2)}) copy-start(bf16[96,1536]{1,0:T(8,128)(2,1)} %get-tuple-element.136) | copy-start | bytes 884740 | tf_op jit(solution)/shard_map/cond
  179.4 8.2 %collective-permute-start.11 = (bf16[48,1536]{1,0:T(8,128)(2,1)S(1)}, bf16[48,1536]{1,0:T(8,128)(2,1)S(1)}, u32[]{:S(2)}, u32[]{:S(2)}) collective-permute-start(bf16[48,1536]{1,0:T(8,128)(2,1)S(1)} %constant_dynamic-slice_fusion.1), channel_id=1, source_target_pairs={{0,8},{1,9},{2,10},{3,11},{4,12},{5,13},{6,14},{7,15},{8,0},{9,1},... | collective-permute-start | bytes 442376 | tf_op jit(solution)/shard_map/cond/branch_1_fun/ppermute | solution.py:729
  181.9 33.7 %collective-permute-start.21 = (bf16[512,768]{1,0:T(8,128)(2,1)}, bf16[512,768]{1,0:T(8,128)(2,1)}, u32[]{:S(2)}, u32[]{:S(2)}) collective-permute-start(bf16[512,768]{1,0:T(8,128)(2,1)} %pad_maximum_fusion.1), channel_id=1, source_target_pairs={{0,1},{1,0},{2,3},{3,2},{4,5},{5,4},{6,7},{7,6},{8,9},{9,8},{10,11... | collective-permute-start | bytes 2359304 | tf_op jit(solution)/shard_map/cond/branch_1_fun/ppermute | solution.py:720
  183.0 9.4 %collective-permute-start.14 = (f32[12,768]{1,0:T(8,128)S(1)}, f32[12,768]{1,0:T(8,128)S(1)}, u32[]{:S(2)}, u32[]{:S(2)}) collective-permute-start(f32[12,768]{1,0:T(8,128)S(1)} %fusion.1), channel_id=1, source_target_pairs={{0,2},{1,3},{2,0},{3,1},{4,6},{5,7},{6,4},{7,5},{8,10},{9,11},{10,... | collective-permute-start | bytes 110600 | tf_op jit(solution)/shard_map/cond/branch_1_fun/ppermute | solution.py:729
  183.1 9.2 %collective-permute-start.10 = (bf16[24,1536]{1,0:T(8,128)(2,1)S(1)}, bf16[24,1536]{1,0:T(8,128)(2,1)S(1)}, u32[]{:S(2)}, u32[]{:S(2)}) collective-permute-start(bf16[24,1536]{1,0:T(8,128)(2,1)S(1)} %add_convert_fusion.6), channel_id=1, source_target_pairs={{0,16},{1,17},{2,18},{3,19},{4,20},{5,21},{6,22},{7,23},{8,24},{9,... | collective-permute-start | bytes 221192 | tf_op jit(solution)/shard_map/cond/branch_1_fun/ppermute | solution.py:729
  185.8 25.2 %collective-permute-start.24 = (bf16[256,768]{1,0:T(8,128)(2,1)S(1)}, bf16[256,768]{1,0:T(8,128)(2,1)S(1)}, u32[]{:S(2)}, u32[]{:S(2)}) collective-permute-start(bf16[256,768]{1,0:T(8,128)(2,1)S(1)} %copy-done.27), channel_id=1, source_target_pairs={{0,1},{1,0},{2,3},{3,2},{4,5},{5,4},{6,7},{7,6},{8,9},{9,8},{10,11... | collective-permute-start | bytes 1179656 | tf_op jit(solution)/shard_map/cond/branch_1_fun/ppermute | solution.py:720
  187.6 8.9 %collective-permute-start.13 = (bf16[24,1536]{1,0:T(8,128)(2,1)S(1)}, bf16[24,1536]{1,0:T(8,128)(2,1)S(1)}, u32[]{:S(2)}, u32[]{:S(2)}) collective-permute-start(bf16[24,1536]{1,0:T(8,128)(2,1)S(1)} %constant_dynamic-slice_fusion), channel_id=1, source_target_pairs={{0,16},{1,17},{2,18},{3,19},{4,20},{5,21},{6,22},{7,23},{8,24},{9,... | collective-permute-start | bytes 221192 | tf_op jit(solution)/shard_map/cond/branch_1_fun/ppermute | solution.py:729
  192.3 9.5 %collective-permute-start.12 = (bf16[48,1536]{1,0:T(8,128)(2,1)S(1)}, bf16[48,1536]{1,0:T(8,128)(2,1)S(1)}, u32[]{:S(2)}, u32[]{:S(2)}) collective-permute-start(bf16[48,1536]{1,0:T(8,128)(2,1)S(1)} %pad_maximum_fusion.4), channel_id=1, source_target_pairs={{0,8},{1,9},{2,10},{3,11},{4,12},{5,13},{6,14},{7,15},{8,0},{9,1},... | collective-permute-start | bytes 442376 | tf_op jit(solution)/shard_map/cond/branch_1_fun/ppermute | solution.py:729
  192.4 14.3 %collective-permute-start.18 = (f32[12,768]{1,0:T(8,128)S(1)}, f32[12,768]{1,0:T(8,128)S(1)}, u32[]{:S(2)}, u32[]{:S(2)}) collective-permute-start(f32[12,768]{1,0:T(8,128)S(1)} %add.132), channel_id=1, source_target_pairs={{0,4},{1,5},{2,6},{3,7},{4,0},{5,1},{6,2},{7,3},{8,12},{9,13},{10,... | collective-permute-start | bytes 110600 | tf_op jit(solution)/shard_map/cond/branch_1_fun/ppermute | solution.py:729
  196.6 15.5 %copy-start.10 = (bf16[24,1536]{1,0:T(8,128)(2,1)}, bf16[24,1536]{1,0:T(8,128)(2,1)S(1)}, u32[]{:S(2)}) copy-start(bf16[24,1536]{1,0:T(8,128)(2,1)S(1)} %add_convert_fusion.5) | copy-start | bytes 221188 | tf_op jit(solution)/shard_map/cond
  196.6 11.5 %collective-permute-start.20 = (bf16[24,1536]{1,0:T(8,128)(2,1)S(1)}, bf16[24,1536]{1,0:T(8,128)(2,1)S(1)}, u32[]{:S(2)}, u32[]{:S(2)}) collective-permute-start(bf16[24,1536]{1,0:T(8,128)(2,1)S(1)} %add_convert_fusion.5), channel_id=1, source_target_pairs={{0,16},{1,17},{2,18},{3,19},{4,20},{5,21},{6,22},{7,23},{8,24},{9,... | collective-permute-start | bytes 221192 | tf_op jit(solution)/shard_map/cond/branch_1_fun/ppermute | solution.py:729
  202.6 24.7 %collective-permute-start.15 = (bf16[96,1536]{1,0:T(8,128)(2,1)}, bf16[96,1536]{1,0:T(8,128)(2,1)S(1)}, u32[]{:S(2)}, u32[]{:S(2)}) collective-permute-start(bf16[96,1536]{1,0:T(8,128)(2,1)} %pad_maximum_fusion.2), channel_id=1, source_target_pairs={{0,1},{1,0},{2,3},{3,2},{4,5},{5,4},{6,7},{7,6},{8,9},{9,8},{10,11... | collective-permute-start | bytes 884744 | tf_op jit(solution)/shard_map/cond/branch_1_fun/ppermute | solution.py:729
  206.8 20.6 %collective-permute-start.16 = (bf16[96,1536]{1,0:T(8,128)(2,1)}, bf16[96,1536]{1,0:T(8,128)(2,1)S(1)}, u32[]{:S(2)}, u32[]{:S(2)}) collective-permute-start(bf16[96,1536]{1,0:T(8,128)(2,1)} %pad_maximum_fusion.2), channel_id=1, source_target_pairs={{0,4},{1,5},{2,6},{3,7},{4,0},{5,1},{6,2},{7,3},{8,12},{9,13},{10,... | collective-permute-start | bytes 884744 | tf_op jit(solution)/shard_map/cond/branch_1_fun/ppermute | solution.py:729
  208.1 8.8 %collective-permute-start.19 = (f32[12,768]{1,0:T(8,128)}, f32[12,768]{1,0:T(8,128)}, u32[]{:S(2)}, u32[]{:S(2)}) collective-permute-start(f32[12,768]{1,0:T(8,128)} %add.134), channel_id=1, source_target_pairs={{0,8},{1,9},{2,10},{3,11},{4,12},{5,13},{6,14},{7,15},{8,0},{9,1},... | collective-permute-start | bytes 110600 | tf_op jit(solution)/shard_map/cond/branch_1_fun/ppermute | solution.py:729
  211.0 16.4 %collective-permute-start.17 = (bf16[96,1536]{1,0:T(8,128)(2,1)}, bf16[96,1536]{1,0:T(8,128)(2,1)S(1)}, u32[]{:S(2)}, u32[]{:S(2)}) collective-permute-start(bf16[96,1536]{1,0:T(8,128)(2,1)} %pad_maximum_fusion.2), channel_id=1, source_target_pairs={{0,5},{1,4},{2,7},{3,6},{4,1},{5,0},{6,3},{7,2},{8,13},{9,12},{10,... | collective-permute-start | bytes 884744 | tf_op jit(solution)/shard_map/cond/branch_1_fun/ppermute | solution.py:729
  216.5 9.4 %collective-permute-start.23 = (bf16[48,1536]{1,0:T(8,128)(2,1)S(1)}, bf16[48,1536]{1,0:T(8,128)(2,1)S(1)}, u32[]{:S(2)}, u32[]{:S(2)}) collective-permute-start(bf16[48,1536]{1,0:T(8,128)(2,1)S(1)} %pad_maximum_fusion.5), channel_id=1, source_target_pairs={{0,8},{1,9},{2,10},{3,11},{4,12},{5,13},{6,14},{7,15},{8,0},{9,1},... | collective-permute-start | bytes 442376 | tf_op jit(solution)/shard_map/cond/branch_1_fun/ppermute | solution.py:729
  217.7 9.0 %collective-permute-start.22 = (f32[12,768]{1,0:T(8,128)S(1)}, f32[12,768]{1,0:T(8,128)S(1)}, u32[]{:S(2)}, u32[]{:S(2)}) collective-permute-start(f32[12,768]{1,0:T(8,128)S(1)} %add.135), channel_id=1, source_target_pairs={{0,16},{1,17},{2,18},{3,19},{4,20},{5,21},{6,22},{7,23},{8,24},{9,... | collective-permute-start | bytes 110600 | tf_op jit(solution)/shard_map/cond/branch_1_fun/ppermute | solution.py:729
  229.2 16.4 %collective-permute-start.32 = (bf16[96,1536]{1,0:T(8,128)(2,1)}, bf16[96,1536]{1,0:T(8,128)(2,1)S(1)}, u32[]{:S(2)}, u32[]{:S(2)}) collective-permute-start(bf16[96,1536]{1,0:T(8,128)(2,1)} %get-tuple-element.291), channel_id=1, source_target_pairs={{0,1},{1,0},{2,3},{3,2},{4,5},{5,4},{6,7},{7,6},{8,9},{9,8},{10,11... | collective-permute-start | bytes 884744 | tf_op jit(solution)/shard_map/ppermute | solution.py:729
  230.6 15.0 %collective-permute-start.33 = (bf16[96,1536]{1,0:T(8,128)(2,1)}, bf16[96,1536]{1,0:T(8,128)(2,1)S(1)}, u32[]{:S(2)}, u32[]{:S(2)}) collective-permute-start(bf16[96,1536]{1,0:T(8,128)(2,1)} %get-tuple-element.291), channel_id=1, source_target_pairs={{0,4},{1,5},{2,6},{3,7},{4,0},{5,1},{6,2},{7,3},{8,12},{9,13},{10,... | collective-permute-start | bytes 884744 | tf_op jit(solution)/shard_map/ppermute | solution.py:729
  231.4 14.2 %collective-permute-start.34 = (bf16[96,1536]{1,0:T(8,128)(2,1)}, bf16[96,1536]{1,0:T(8,128)(2,1)S(1)}, u32[]{:S(2)}, u32[]{:S(2)}) collective-permute-start(bf16[96,1536]{1,0:T(8,128)(2,1)} %get-tuple-element.291), channel_id=1, source_target_pairs={{0,5},{1,4},{2,7},{3,6},{4,1},{5,0},{6,3},{7,2},{8,13},{9,12},{10,... | collective-permute-start | bytes 884744 | tf_op jit(solution)/shard_map/ppermute | solution.py:729
  232.7 10.1 %collective-permute-start.35 = (f32[12,768]{1,0:T(8,128)}, f32[12,768]{1,0:T(8,128)S(1)}, u32[]{:S(2)}, u32[]{:S(2)}) collective-permute-start(f32[12,768]{1,0:T(8,128)} %get-tuple-element.292), channel_id=1, source_target_pairs={{0,1},{1,0},{2,3},{3,2},{4,5},{5,4},{6,7},{7,6},{8,9},{9,8},{10,11... | collective-permute-start | bytes 110600 | tf_op jit(solution)/shard_map/ppermute | solution.py:729
  234.1 13.7 %collective-permute-start.36 = (bf16[384,1536]{1,0:T(8,128)(2,1)}, bf16[384,1536]{1,0:T(8,128)(2,1)S(1)}, u32[]{:S(2)}, u32[]{:S(2)}) collective-permute-start(bf16[384,1536]{1,0:T(8,128)(2,1)} %get-tuple-element.302), channel_id=1, source_target_pairs={{0,2},{1,3},{2,0},{3,1},{4,6},{5,7},{6,4},{7,5},{8,10},{9,11},{10,... | collective-permute-start | bytes 3538952 | tf_op jit(solution)/shard_map/ppermute | solution.py:729
  247.8 3.2 %collective-permute-start.37 = (bf16[384,1536]{1,0:T(8,128)(2,1)}, bf16[384,1536]{1,0:T(8,128)(2,1)}, u32[]{:S(2)}, u32[]{:S(2)}) collective-permute-start(bf16[384,1536]{1,0:T(8,128)(2,1)} %pad_maximum_fusion.7), channel_id=1, source_target_pairs={{0,2},{1,3},{2,0},{3,1},{4,6},{5,7},{6,4},{7,5},{8,10},{9,11},{10,... | collective-permute-start | bytes 3538952 | tf_op jit(solution)/shard_map/ppermute | solution.py:729
  (21 other events, 101.4 us)
Sparse Core Ops, SparseCore 0:
  94.9 134.4 all-reduce.2

commit v7 on v6

--- a/solution.py
+++ b/solution.py
@@ -1129,9 +1129,9 @@
                 chain = chains[name]
                 chain.got, token = fence((chain.got, token))
                 turns += 1
-                if turns == 7:
+                if turns == 9:
                     chain.got, returned = fence((chain.got, returned))
-                if turns == 9:
+                if turns == 10:
                     input_grad = input_backward(d_normed, from_next, inputs, d_middle, rows)
                     chain.got, input_grad = fence((chain.got, input_grad))
                 if turns == 11:

time: 267 us -> 274 us (1.026)
  waiting for transfers between devices: 29 us -> 33.8 us
    ppermute x29, waiting for transfers between devices: 24.7 us -> 32.3 us  [flipped(): return lax.ppermute(value, GRID, [(i, i ^ mask) for i in range(count)])]
    ppermute x9, waiting for transfers between devices: 4.35 us -> 1.49 us  [rotated(): lax.ppermute(value, axis, [(i, (i + by) % count) for i in range(count)])]
  transfers between devices with their start and end apart: 39 -> 39, of which waited for: 11 -> 14; matrix products, arithmetic and copies ran while one was open for 11% -> 11% of each run, Pallas kernels for 47% -> 46%
where the time goes in v7:
time: 274 us; the launch traced here: 268 us
  Pallas kernels  124 us (45%)
  starting transfers between devices  45.1 us (16%)
  waiting for transfers between devices  33.8 us (12%)
  other arithmetic  26.1 us (10%)
  matrix products  15.9 us (6%)
  between operations  14.8 us (5%)
  local copies, waits for them, and re-layouts  8.53 us (3%)
    ppermute x29, starting transfers between devices, flipped(): return lax.ppermute(value, GRID, [(i, i ^ mask) for i in range(count)])  33.2 us
    ppermute x29, waiting for transfers between devices, flipped(): return lax.ppermute(value, GRID, [(i, i ^ mask) for i in range(count)])  32.3 us
    pallas_call x2, Pallas kernels, attention_backward(): pl.pallas_call(backward_kernel, grid=(pairs,), in_specs=[pl.BlockSpec(mem...  26.4 us
    pallas_call x3, Pallas kernels, mlp_block(): pl.pallas_call(mlp_kernel, grid=(hidden // tile,), in_specs=[fixed, pl.Bl...  24.5 us
    pallas_call x2, Pallas kernels, weight_grads(): pl.pallas_call(kernel, grid=(steps,), in_specs=in_specs, out_specs=specs,...  13.6 us
    pallas_call x1, Pallas kernels, local_attention(): pl.pallas_call(local_kernel, grid=(PAIRS,), in_specs=[pl.BlockSpec(memory...  13.5 us
    pallas_call x1, Pallas kernels, memory_attention(): pl.pallas_call(memory_kernel, grid=(PAIRS,), in_specs=[pl.BlockSpec(memor...  12 us
    ppermute x9, starting transfers between devices, rotated(): lax.ppermute(value, axis, [(i, (i + by) % count) for i in range(count)])  11.9 us
  transfers between devices with their start and end apart: 39, of which 14 were waited for; matrix products, arithmetic and copies ran while one was open for 11% of the time, Pallas kernels for 46%

profile of v7, /device:TPU:0, one launch (start us, length us, event | category | flops | bytes accessed | tf_op | source)
XLA Modules:
  0.0 268.4 jit_solution(7862827156132900408)
XLA Ops:
  7.3 1.8 slice.83
  9.1 3.0 %collective-permute-start.26 = (bf16[256,768]{1,0:T(8,128)(2,1)}, bf16[256,768]{1,0:T(8,128)(2,1)}, u32[]{:S(2)}, u32[]{:S(2)}) collective-permute-start(bf16[256,768]{1,0:T(8,128)(2,1)} %slice.83), channel_id=1, source_target_pairs={{0,1},{1,0},{2,3},{3,2},{4,5},{5,4},{6,7},{7,6},{8,9},{9,8},{10,11... | collective-permute-start | bytes 1179656 | tf_op jit(solution)/shard_map/ppermute | solution.py:720
  12.1 2.0 collective-permute-start.25
  16.3 4.3 %fusion.3.q_ref.k_ref.v_ref = bf16[512,2304]{1,0:T(8,128)(2,1)S(1)} fusion(bf16[512,768]{1,0:T(8,128)(2,1)S(1)} %fusion.9, bf16[768,2304]{1,0:T(8,128)(2,1)} %w_ref.1, f32[2304]{0:T(1024)S(1)} %pad_maximum_fusion.9), kind=kOutput, calls=%fused_computation.37 | convolution fusion | flops 1814298624 | bytes 6693888 | tf_op jit(solution)/shard_map/dot_general | solution.py:27
  20.8 13.5 %local_attention.1 = (f32[256,768]{1,0:T(8,128)}, f32[6,8,512]{2,1,0:T(8,128)}, bf16[512,768]{1,0:T(8,128)(2,1)}, f32[512,768]{1,0:T(8,128)}, bf16[512,768]{1,0:T(8,128)(2,1)}, /*index=5*/bf16[256,768]{1,0:T(8,128)(2,1)}) custom-call(s32[1,3]{1,0:T(1,128)S(1)} %copy-done.26, bf16[512,2304]{1,0:T(8,128)(2,1)S(1)} %fusion.3.q_ref.k_ref.v_ref, ...), custom_call_target="tpu_custom_call" | custom-call | flops 2415919104 | bytes 3145728 | tf_op jit(solution)/shard_map/local_attention/pallas_call | solution.py:116
  34.5 4.7 %tail_projection.1 = (bf16[256,768]{1,0:T(8,128)(2,1)}, bf16[256,1536]{1,0:T(8,128)(2,1)}) custom-call(bf16[256,768]{1,0:T(8,128)(2,1)} %collective-permute-done.26.x_ref, f32[8,768]{1,0:T(8,128)S(1)} %concatenate.49.rows_ref.vb_ref, bf16[768,2304]{1,0:T(8,128)(2,1)} %w_ref.1), custom_call_target="tpu_custom_call" | custom-call | flops 603979776 | bytes 2359296 | tf_op jit(solution)/shard_map/tail_projection/pallas_call | solution.py:180
  39.7 12.0 %memory_attention.1 = (bf16[512,768]{1,0:T(8,128)(2,1)}, bf16[512,768]{1,0:T(8,128)(2,1)}, bf16[512,768]{1,0:T(8,128)(2,1)}, f32[6,8,256]{2,1,0:T(8,128)}, f32[5...) custom-call(s32[1,1]{1,0:T(1,128)S(6)} %select_n.313.reads, ...), custom_call_target="tpu_custom_call", output_to_operand_aliasing={{0}: (10, {}), {4}: (11, {}), {5}: (12, {})} | custom-call | flops 3221225472 | bytes 6291456 | tf_op jit(solution)/shard_map/memory_attention/pallas_call | solution.py:262
  51.7 2.1 collective-permute-start.28
  54.4 6.5 %mlp_block.3 = (bf16[1024,1536]{1,0:T(8,128)(2,1)}, bf16[1024,1536]{1,0:T(8,128)(2,1)}, f32[8,1536]{1,0:T(8,128)}, bf16[256,768]{1,0:T(8,128)(2,1)}, bf16[256,768]{1,0:T(8,128)(2,1)}) custom-call(bf16[256,768]{1,0:T(8,128)(2,1)} %collective-permute-done.29.x_ref, bf16[512,768]{1,0:T(8,128)(2,1)} %collective-permute-done.27.ct_ref, bf16[768,1536]{1,0:T(8,128)(2,1)} %wi_ref.5, ...), custom_call_target="tpu_custom_call" | custom-call | flops 2415919104 | bytes 7864320 | tf_op jit(solution)/shard_map/mlp_block/pallas_call | solution.py:372
  62.5 6.5 %mlp_block.4 = (bf16[1024,1536]{1,0:T(8,128)(2,1)}, bf16[1024,1536]{1,0:T(8,128)(2,1)}, f32[8,1536]{1,0:T(8,128)}, bf16[256,768]{1,0:T(8,128)(2,1)}, bf16[256,768]{1,0:T(8,128)(2,1)}) custom-call(bf16[256,768]{1,0:T(8,128)(2,1)} %collective-permute-done.28.x_ref, ...), custom_call_target="tpu_custom_call", output_to_operand_aliasing={{0}: (5, {}), {1}: (6, {})} | custom-call | flops 2415919104 | bytes 7864320 | tf_op jit(solution)/shard_map/mlp_block/pallas_call | solution.py:372
  69.1 2.6 collective-permute-start.31
  71.6 11.5 %mlp_block.5 = (bf16[1024,1536]{1,0:T(8,128)(2,1)}, bf16[1024,1536]{1,0:T(8,128)(2,1)}, f32[8,1536]{1,0:T(8,128)}, bf16[512,768]{1,0:T(8,128)(2,1)}, bf16[512,768]{1,0:T(8,128)(2,1)}) custom-call(bf16[512,768]{1,0:T(8,128)(2,1)} %get-tuple-element.258.x_ref, bf16[512,768]{1,0:T(8,128)(2,1)} %ct_ref.1, ...), custom_call_target="tpu_custom_call", output_to_operand_aliasing={{0}: (5, {}), {1}: (6, {})} | custom-call | flops 4831838208 | bytes 11010048 | tf_op jit(solution)/shard_map/mlp_block/pallas_call | solution.py:372
  83.1 6.5 %convolution_convert_fusion = bf16[1536,768]{1,0:T(8,128)(2,1)} fusion(bf16[1024,1536]{1,0:T(8,128)(2,1)} %get-tuple-element.294, bf16[512,768]{1,0:T(8,128)(2,1)} %collective-permute-done.27.ct_ref, bf16[512,768]{1,0:T(8,128)(2,1)} %ct_ref.1), kind=kOutput, calls=%fused_computation.38 | convolution fusion | flops 2420244480 | bytes 7077888 | tf_op jit(solution)/shard_map/dot_general | solution.py:1026
  89.7 5.1 %convolution_convert_fusion.1 = bf16[768,1536]{1,0:T(8,128)(2,1)} fusion(bf16[1024,1536]{1,0:T(8,128)(2,1)S(1)} %copy-done.2, bf16[256,768]{1,0:T(8,128)(2,1)} %collective-permute-done.29.x_ref, bf16[256,768]{1,0:T(8,128)(2,1)} %collective-permute-done.28.x_ref, bf16[512,768]{1,0:T(8,128)(2,1)S(1)} %copy-done.27), kind=kOutput, calls=%fused_computation.39 | convolution fusion | flops 2421817344 | bytes 7077888 | tf_op jit(solution)/shard_map/dot_general | solution.py:1026
  95.4 141.2 %conditional.1 = (bf16[384,1536]{1,0:T(8,128)(2,1)}, bf16[96,1536]{1,0:T(8,128)(2,1)}, f32[12,768]{1,0:T(8,128)}, bf16[512,768]{1,0:T(8,128)(2,1)}, bf16[512,768]{1,0:T(8,128)(2,1)}) conditional(s32[]{:T(128)} %bitcast.2, () %tuple.43, (bf16[512,768]{1,0:T(8,128)(2,1)}, bf16[512,768]{1,0:T(8,128)(2,1)}, f32[512,768]{1,0:T(8,128)}, ...), branch_computations={%region_2.3_spmd, %region_3.4_spmd} | conditional | flops 16139627520 | bytes 104416912 | solution.py:1152
  95.4 4.6 %middle_backward.1 = (f32[512,768]{1,0:T(8,128)}, bf16[512,768]{1,0:T(8,128)(2,1)}, f32[8,768]{1,0:T(8,128)}) custom-call(bf16[512,768]{1,0:T(8,128)(2,1)} %get-tuple-element.70.d_ref, bf16[512,768]{1,0:T(8,128)(2,1)} %get-tuple-element.71.ct_ref, f32[512,768]{1,0:T(8,128)} %get-tuple-element.72.middle_ref, f32[8,768]{1,0:T(8,128)S(1)} %get-tuple-element.73.rows_ref, ...), custom_call_target="tpu_custom_call" | custom-call | flops 7864320 | bytes 5505024 | tf_op jit(solution)/shard_map/cond/branch_1_fun/middle_backward/pallas_call | solution.py:595
  100.0 9.6 %attention_backward.2 = (bf16[3,512,256]{2,1,0:T(8,128)(2,1)}, bf16[2,256,256]{2,1,0:T(8,128)(2,1)}, f32[8,256]{1,0:T(8,128)}) custom-call(s32[1,3]{1,0:T(1,128)S(1)} %get-tuple-element.66.lens, bf16[512,2304]{1,0:T(8,128)(2,1)S(1)} %get-tuple-element.67.q_ref.k_ref.v_ref, bf16[512,2304]{1,0:T(8,128)(2,1)S(1)} %get-tuple-element.67.q_ref.k_ref.v_ref, ...), custom_call_target="tpu_custom_call" | custom-call | flops 3758096384 | bytes 2621440 | tf_op jit(solution)/shard_map/cond/branch_1_fun/attention_backward/pallas_call | solution.py:501
  109.7 8.0 %weight_grads.2 = (bf16[384,1536]{1,0:T(8,128)(2,1)}, bf16[384,1536]{1,0:T(8,128)(2,1)}, bf16[768,512]{1,0:T(8,128)(2,1)}, bf16[768,256]{1,0:T(8,128)(2,1)}) custom-call(s32[1]{0:T(128)} %bitcast.1.side_ref, bf16[512,768]{1,0:T(8,128)(2,1)} %get-tuple-element.64.n_ref, bf16[256,768]{1,0:T(8,128)(2,1)S(1)} %copy-done.9, ...), custom_call_target="tpu_custom_call" | custom-call | flops 805306368 | bytes 1572864 | tf_op jit(solution)/shard_map/cond/branch_1_fun/weight_grads/pallas_call | solution.py:896
  117.8 3.3 %collective-permute-done.got_ref = bf16[384,1536]{1,0:T(8,128)(2,1)} collective-permute-done((bf16[384,1536]{1,0:T(8,128)(2,1)}, bf16[384,1536]{1,0:T(8,128)(2,1)}, u32[]{:S(2)}, u32[]{:S(2)}) %collective-permute-start) | collective-permute-done | bytes 1179680 | tf_op jit(solution)/shard_map/cond/branch_1_fun/ppermute | solution.py:729
  121.1 2.9 %split_sum.2 = (bf16[96,1536]{1,0:T(8,128)(2,1)}, bf16[96,1536]{1,0:T(8,128)(2,1)}, bf16[96,1536]{1,0:T(8,128)(2,1)}, bf16[96,1536]{1,0:T(8,128)(2,1)}) custom-call(s32[1]{0:T(128)} %bitcast.number_ref, bf16[384,1536]{1,0:T(8,128)(2,1)} %get-tuple-element.84.kept_ref, bf16[384,1536]{1,0:T(8,128)(2,1)} %collective-permute-done.got_ref), custom_call_target="tpu_custom_call" | custom-call | flops 1000 | bytes 1000 | tf_op jit(solution)/shard_map/cond/branch_1_fun/split_sum/pallas_call | solution.py:923
  124.0 1.7 collective-permute-start.2
  125.7 1.8 collective-permute-start.3
  127.5 16.8 %attention_backward.3 = (bf16[3,512,512]{2,1,0:T(8,128)(2,1)}, bf16[2,256,512]{2,1,0:T(8,128)(2,1)}, f32[8,512]{1,0:T(8,128)}) custom-call(s32[1,3]{1,0:T(1,128)S(1)} %get-tuple-element.66.lens, bf16[512,2304]{1,0:T(8,128)(2,1)S(1)} %get-tuple-element.67.q_ref.k_ref.v_ref, bf16[512,2304]{1,0:T(8,128)(2,1)S(1)} %get-tuple-element.67.q_ref.k_ref.v_ref, ...), custom_call_target="tpu_custom_call" | custom-call | flops 7516192768 | bytes 5242880 | tf_op jit(solution)/shard_map/cond/branch_1_fun/attention_backward/pallas_call | solution.py:501
  145.7 5.6 %weight_grads.3 = (bf16[384,1536]{1,0:T(8,128)(2,1)}, bf16[384,1536]{1,0:T(8,128)(2,1)}) custom-call(s32[1]{0:T(128)} %bitcast.1.side_ref, bf16[768,512]{1,0:T(8,128)(2,1)} %get-tuple-element.112.n_ref, bf16[768,256]{1,0:T(8,128)(2,1)} %get-tuple-element.113.nt_ref, bf16[3,512,512]{2,1,0:T(8,128)(2,1)} %get-tuple-element.126.d_ref.two_ref, ...), custom_call_target="tpu_custom_call" | custom-call | flops 1610612736 | bytes 3145728 | tf_op jit(solution)/shard_map/cond/branch_1_fun/weight_grads/pallas_call | solution.py:896
  155.4 2.8 %split_sum.3 = (bf16[96,1536]{1,0:T(8,128)(2,1)}, bf16[96,1536]{1,0:T(8,128)(2,1)}, bf16[96,1536]{1,0:T(8,128)(2,1)}, bf16[96,1536]{1,0:T(8,128)(2,1)}) custom-call(s32[1]{0:T(128)} %bitcast.number_ref, bf16[384,1536]{1,0:T(8,128)(2,1)} %get-tuple-element.114.kept_ref, bf16[384,1536]{1,0:T(8,128)(2,1)} %copy-done.4), custom_call_target="tpu_custom_call" | custom-call | flops 1000 | bytes 1000 | tf_op jit(solution)/shard_map/cond/branch_1_fun/split_sum/pallas_call | solution.py:923
  159.9 1.8 collective-permute-start.9
  161.8 2.6 collective-permute-start.6
  164.4 8.4 %qkv_backward.1 = (f32[512,768]{1,0:T(8,128)}, bf16[256,768]{1,0:T(8,128)(2,1)}, f32[8,768]{1,0:T(8,128)}) custom-call(bf16[3,512,256]{2,1,0:T(8,128)(2,1)} %get-tuple-element.125.d_ref.one_ref, bf16[3,512,512]{2,1,0:T(8,128)(2,1)} %get-tuple-element.126.d_ref.two_ref, bf16[2,256,256]{2,1,0:T(8,128)(2,1)} %get-tuple-element.127.dt_ref.t_one_ref, ...), custom_call_target="tpu_custom_call" | custom-call | flops 2415919104 | bytes 7864320 | tf_op jit(solution)/shard_map/cond/branch_1_fun/qkv_backward/pallas_call | solution.py:641
  173.1 6.0 %collective-permute-done.9 = bf16[96,1536]{1,0:T(8,128)(2,1)S(1)} collective-permute-done((bf16[96,1536]{1,0:T(8,128)(2,1)}, bf16[96,1536]{1,0:T(8,128)(2,1)S(1)}, u32[]{:S(2)}, u32[]{:S(2)}) %collective-permute-start.9) | collective-permute-done | bytes 294944 | tf_op jit(solution)/shard_map/cond/branch_1_fun/ppermute | solution.py:729
  179.4 1.6 collective-permute-start.11
  183.1 2.7 %collective-permute-start.10 = (bf16[24,1536]{1,0:T(8,128)(2,1)S(1)}, bf16[24,1536]{1,0:T(8,128)(2,1)S(1)}, u32[]{:S(2)}, u32[]{:S(2)}) collective-permute-start(bf16[24,1536]{1,0:T(8,128)(2,1)S(1)} %add_convert_fusion.6), channel_id=1, source_target_pairs={{0,16},{1,17},{2,18},{3,19},{4,20},{5,21},{6,22},{7,23},{8,24},{9,... | collective-permute-start | bytes 221192 | tf_op jit(solution)/shard_map/cond/branch_1_fun/ppermute | solution.py:729
  185.8 1.7 collective-permute-start.24
  188.9 3.3 %collective-permute-done.10 = bf16[24,1536]{1,0:T(8,128)(2,1)S(1)} collective-permute-done((bf16[24,1536]{1,0:T(8,128)(2,1)S(1)}, bf16[24,1536]{1,0:T(8,128)(2,1)S(1)}, u32[]{:S(2)}, u32[]{:S(2)}) %collective-permute-start.10) | collective-permute-done | bytes 73760 | tf_op jit(solution)/shard_map/cond/branch_1_fun/ppermute | solution.py:729
  192.4 1.9 collective-permute-start.18
  194.3 2.2 collective-permute-done.13
  197.8 4.1 %collective-permute-done.12 = bf16[48,1536]{1,0:T(8,128)(2,1)S(1)} collective-permute-done((bf16[48,1536]{1,0:T(8,128)(2,1)S(1)}, bf16[48,1536]{1,0:T(8,128)(2,1)S(1)}, u32[]{:S(2)}, u32[]{:S(2)}) %collective-permute-start.12) | collective-permute-done | bytes 147488 | tf_op jit(solution)/shard_map/cond/branch_1_fun/ppermute | solution.py:729
  202.7 2.5 collective-permute-done.20
  206.5 1.7 collective-permute-start.22
  208.5 1.7 collective-permute-start.15
  210.3 7.5 %collective-permute-done.19 = f32[12,768]{1,0:T(8,128)S(1)} collective-permute-done((f32[12,768]{1,0:T(8,128)S(1)}, f32[12,768]{1,0:T(8,128)S(1)}, u32[]{:S(2)}, u32[]{:S(2)}) %collective-permute-start.19) | collective-permute-done | bytes 36896 | tf_op jit(solution)/shard_map/cond/branch_1_fun/ppermute | solution.py:729
  219.8 2.0 collective-permute-start.17
  221.8 3.5 %input_backward.1 = bf16[512,768]{1,0:T(8,128)(2,1)} custom-call(f32[512,768]{1,0:T(8,128)} %get-tuple-element.161.dn_ref, bf16[256,768]{1,0:T(8,128)(2,1)} %copy-done.10, bf16[512,768]{1,0:T(8,128)(2,1)S(1)} %get-tuple-element.130.x_ref, f32[512,768]{1,0:T(8,128)} %get-tuple-element.163.dm_ref, f32[8,768]{1,0:T(8,128)} %copy-done.8), custom_call_target="tpu_custom_call" | custom-call | flops 7864320 | bytes 4718592 | tf_op jit(solution)/shard_map/cond/branch_1_fun/input_backward/pallas_call | solution.py:675
  225.3 2.2 collective-permute-start.21
  232.6 2.3 add_convert_fusion
  238.1 2.1 collective-permute-start.34
  240.3 6.8 %widened.1 = (f32[768,1536]{1,0:T(8,128)}, f32[1536,768]{1,0:T(8,128)}) custom-call(bf16[768,1536]{1,0:T(8,128)(2,1)} %get-tuple-element.324.a_ref, bf16[1536,768]{1,0:T(8,128)(2,1)} %get-tuple-element.325.b_ref), custom_call_target="tpu_custom_call" | custom-call | bytes 14155776 | tf_op jit(solution)/shard_map/widened/pallas_call | solution.py:705
  255.9 1.7 broadcast_select_fusion.8
  257.9 3.5 %convert_element_type.148 = f32[768,2304]{1,0:T(8,128)} convert(bf16[768,2304]{1,0:T(8,128)(2,1)S(1)} %fusion.23) | non-fusion elementwise | flops 1769472 | bytes 10616832 | tf_op jit(solution)/shard_map/convert_element_type | solution.py:1197
  (184 shorter events, 39.9 us)
Async XLA Ops:
  7.2 8.6 %copy-start.18 = (bf16[768]{0:T(1024)(128)(2,1)S(1)}, bf16[768]{0:T(1024)(128)(2,1)}, u32[]{:S(2)}) copy-start(bf16[768]{0:T(1024)(128)(2,1)} %param.19) | copy-start | bytes 4612
  7.2 8.6 %copy-start.19 = (bf16[768]{0:T(1024)(128)(2,1)S(1)}, bf16[768]{0:T(1024)(128)(2,1)}, u32[]{:S(2)}) copy-start(bf16[768]{0:T(1024)(128)(2,1)} %param.20) | copy-start | bytes 4612
  7.2 8.6 %copy-start.15 = (bf16[2,768]{1,0:T(2,128)(2,1)S(1)}, bf16[2,768]{1,0:T(2,128)(2,1)}, u32[]{:S(2)}) copy-start(bf16[2,768]{1,0:T(2,128)(2,1)} %param.22) | copy-start | bytes 9220
  7.2 233.1 %all-reduce.3.cloned.1.call-start = ((), (), s32[]{:S(2)}) async-start(), calls=%async_computation | async-start | bytes 9437184 | tf_op jit(solution)/shard_map/psum | solution.py:1043
  9.1 25.4 %collective-permute-start.26 = (bf16[256,768]{1,0:T(8,128)(2,1)}, bf16[256,768]{1,0:T(8,128)(2,1)}, u32[]{:S(2)}, u32[]{:S(2)}) collective-permute-start(bf16[256,768]{1,0:T(8,128)(2,1)} %slice.83), channel_id=1, source_target_pairs={{0,1},{1,0},{2,3},{3,2},{4,5},{5,4},{6,7},{7,6},{8,9},{9,8},{10,11... | collective-permute-start | bytes 1179656 | tf_op jit(solution)/shard_map/ppermute | solution.py:720
  12.1 27.1 %collective-permute-start.27 = (bf16[512,768]{1,0:T(8,128)(2,1)}, bf16[512,768]{1,0:T(8,128)(2,1)}, u32[]{:S(2)}, u32[]{:S(2)}) collective-permute-start(bf16[512,768]{1,0:T(8,128)(2,1)} %ct_ref.1), channel_id=1, source_target_pairs={{0,1},{1,0},{2,3},{3,2},{4,5},{5,4},{6,7},{7,6},{8,9},{9,8},{10,11... | collective-permute-start | bytes 2359304 | tf_op jit(solution)/shard_map/ppermute | solution.py:720
  12.1 27.1 %collective-permute-start.25 = (s32[1,3]{1,0:T(1,128)}, s32[1,3]{1,0:T(1,128)S(1)}, u32[]{:S(2)}, u32[]{:S(2)}) collective-permute-start(s32[1,3]{1,0:T(1,128)} %lens.1), channel_id=1, source_target_pairs={{0,1},{1,0},{2,3},{3,2},{4,5},{5,4},{6,7},{7,6},{8,9},{9,8},{10,11... | collective-permute-start | bytes 44 | tf_op jit(solution)/shard_map/ppermute | solution.py:720
  34.3 19.5 %collective-permute-start.29 = (bf16[256,768]{1,0:T(8,128)(2,1)}, bf16[256,768]{1,0:T(8,128)(2,1)}, u32[]{:S(2)}, u32[]{:S(2)}) collective-permute-start(bf16[256,768]{1,0:T(8,128)(2,1)} %get-tuple-element.262), channel_id=1, source_target_pairs={{0,1},{1,0},{2,3},{3,2},{4,5},{5,4},{6,7},{7,6},{8,9},{9,8},{10,11... | collective-permute-start | bytes 1179656 | tf_op jit(solution)/shard_map/ppermute | solution.py:720
  39.7 14.1 %copy-start.21 = (bf16[1536]{0:T(1024)(128)(2,1)S(1)}, bf16[1536]{0:T(1024)(128)(2,1)}, u32[]{:S(2)}) copy-start(bf16[1536]{0:T(1024)(128)(2,1)} %param.28) | copy-start | bytes 9220
  51.7 10.8 %collective-permute-start.28 = (bf16[256,768]{1,0:T(8,128)(2,1)}, bf16[256,768]{1,0:T(8,128)(2,1)}, u32[]{:S(2)}, u32[]{:S(2)}) collective-permute-start(bf16[256,768]{1,0:T(8,128)(2,1)} %get-tuple-element.259), channel_id=1, source_target_pairs={{0,1},{1,0},{2,3},{3,2},{4,5},{5,4},{6,7},{7,6},{8,9},{9,8},{10,11... | collective-permute-start | bytes 1179656 | tf_op jit(solution)/shard_map/ppermute | solution.py:720
  61.0 22.1 %collective-permute-start.30 = (bf16[256,768]{1,0:T(8,128)(2,1)}, bf16[256,768]{1,0:T(8,128)(2,1)}, u32[]{:S(2)}, u32[]{:S(2)}) collective-permute-start(bf16[256,768]{1,0:T(8,128)(2,1)} %get-tuple-element.272), channel_id=1, source_target_pairs={{0,1},{1,0},{2,3},{3,2},{4,5},{5,4},{6,7},{7,6},{8,9},{9,8},{10,11... | collective-permute-start | bytes 1179656 | tf_op jit(solution)/shard_map/ppermute | solution.py:720
  69.1 14.1 %collective-permute-start.31 = (bf16[256,768]{1,0:T(8,128)(2,1)}, bf16[256,768]{1,0:T(8,128)(2,1)}, u32[]{:S(2)}, u32[]{:S(2)}) collective-permute-start(bf16[256,768]{1,0:T(8,128)(2,1)} %get-tuple-element.273), channel_id=1, source_target_pairs={{0,1},{1,0},{2,3},{3,2},{4,5},{5,4},{6,7},{7,6},{8,9},{9,8},{10,11... | collective-permute-start | bytes 1179656 | tf_op jit(solution)/shard_map/ppermute | solution.py:720
  100.0 9.6 %copy-start.9 = (bf16[256,768]{1,0:T(8,128)(2,1)S(1)}, bf16[256,768]{1,0:T(8,128)(2,1)}, u32[]{:S(2)}) copy-start(bf16[256,768]{1,0:T(8,128)(2,1)} %get-tuple-element.65.nt_ref) | copy-start | bytes 1179652 | tf_op jit(solution)/shard_map/cond
  117.7 9.8 %copy-start.28 = (f32[6,8,512]{2,1,0:T(8,128)S(1)}, f32[6,8,512]{2,1,0:T(8,128)}, u32[]{:S(2)}) copy-start(f32[6,8,512]{2,1,0:T(8,128)} %get-tuple-element.78.ll_ref) | copy-start | bytes 294916 | tf_op jit(solution)/shard_map/cond
  117.7 3.4 %collective-permute-start = (bf16[384,1536]{1,0:T(8,128)(2,1)}, bf16[384,1536]{1,0:T(8,128)(2,1)}, u32[]{:S(2)}, u32[]{:S(2)}) collective-permute-start(bf16[384,1536]{1,0:T(8,128)(2,1)} %get-tuple-element.85), channel_id=1, source_target_pairs={{0,2},{1,3},{2,0},{3,1},{4,6},{5,7},{6,4},{7,5},{8,10},{9,11},{10,... | collective-permute-start | bytes 3538952 | tf_op jit(solution)/shard_map/cond/branch_1_fun/ppermute | solution.py:729
  124.0 20.3 %copy-start.14 = (bf16[96,1536]{1,0:T(8,128)(2,1)S(1)}, bf16[96,1536]{1,0:T(8,128)(2,1)}, u32[]{:S(2)}) copy-start(bf16[96,1536]{1,0:T(8,128)(2,1)} %get-tuple-element.86) | copy-start | bytes 884740 | tf_op jit(solution)/shard_map/cond
  124.0 20.3 %collective-permute-start.1 = (bf16[96,1536]{1,0:T(8,128)(2,1)}, bf16[96,1536]{1,0:T(8,128)(2,1)}, u32[]{:S(2)}, u32[]{:S(2)}) collective-permute-start(bf16[96,1536]{1,0:T(8,128)(2,1)} %get-tuple-element.93), channel_id=1, source_target_pairs={{0,1},{1,0},{2,3},{3,2},{4,5},{5,4},{6,7},{7,6},{8,9},{9,8},{10,11... | collective-permute-start | bytes 884744 | tf_op jit(solution)/shard_map/cond/branch_1_fun/ppermute | solution.py:729
  124.0 20.3 %collective-permute-start.2 = (bf16[96,1536]{1,0:T(8,128)(2,1)}, bf16[96,1536]{1,0:T(8,128)(2,1)}, u32[]{:S(2)}, u32[]{:S(2)}) collective-permute-start(bf16[96,1536]{1,0:T(8,128)(2,1)} %get-tuple-element.94), channel_id=1, source_target_pairs={{0,4},{1,5},{2,6},{3,7},{4,0},{5,1},{6,2},{7,3},{8,12},{9,13},{10,... | collective-permute-start | bytes 884744 | tf_op jit(solution)/shard_map/cond/branch_1_fun/ppermute | solution.py:729
  125.7 18.6 %collective-permute-start.3 = (bf16[96,1536]{1,0:T(8,128)(2,1)}, bf16[96,1536]{1,0:T(8,128)(2,1)}, u32[]{:S(2)}, u32[]{:S(2)}) collective-permute-start(bf16[96,1536]{1,0:T(8,128)(2,1)} %get-tuple-element.95), channel_id=1, source_target_pairs={{0,5},{1,4},{2,7},{3,6},{4,1},{5,0},{6,3},{7,2},{8,13},{9,12},{10,... | collective-permute-start | bytes 884744 | tf_op jit(solution)/shard_map/cond/branch_1_fun/ppermute | solution.py:729
  151.2 3.1 %collective-permute-start.5 = (bf16[384,1536]{1,0:T(8,128)(2,1)}, bf16[384,1536]{1,0:T(8,128)(2,1)S(1)}, u32[]{:S(2)}, u32[]{:S(2)}) collective-permute-start(bf16[384,1536]{1,0:T(8,128)(2,1)} %get-tuple-element.115), channel_id=1, source_target_pairs={{0,2},{1,3},{2,0},{3,1},{4,6},{5,7},{6,4},{7,5},{8,10},{9,11},{10,... | collective-permute-start | bytes 3538952 | tf_op jit(solution)/shard_map/cond/branch_1_fun/ppermute | solution.py:729
  151.2 10.4 %collective-permute-start.4 = (bf16[48,1536]{1,0:T(8,128)(2,1)S(1)}, bf16[48,1536]{1,0:T(8,128)(2,1)S(1)}, u32[]{:S(2)}, u32[]{:S(2)}) collective-permute-start(bf16[48,1536]{1,0:T(8,128)(2,1)S(1)} %constant_dynamic-slice_fusion.3), channel_id=1, source_target_pairs={{0,8},{1,9},{2,10},{3,11},{4,12},{5,13},{6,14},{7,15},{8,0},{9,1},... | collective-permute-start | bytes 442376 | tf_op jit(solution)/shard_map/cond/branch_1_fun/ppermute | solution.py:729
  158.2 14.9 %collective-permute-start.7 = (bf16[96,1536]{1,0:T(8,128)(2,1)}, bf16[96,1536]{1,0:T(8,128)(2,1)S(1)}, u32[]{:S(2)}, u32[]{:S(2)}) collective-permute-start(bf16[96,1536]{1,0:T(8,128)(2,1)} %get-tuple-element.119), channel_id=1, source_target_pairs={{0,1},{1,0},{2,3},{3,2},{4,5},{5,4},{6,7},{7,6},{8,9},{9,8},{10,11... | collective-permute-start | bytes 884744 | tf_op jit(solution)/shard_map/cond/branch_1_fun/ppermute | solution.py:729
  158.4 14.7 %collective-permute-start.8 = (bf16[96,1536]{1,0:T(8,128)(2,1)}, bf16[96,1536]{1,0:T(8,128)(2,1)S(1)}, u32[]{:S(2)}, u32[]{:S(2)}) collective-permute-start(bf16[96,1536]{1,0:T(8,128)(2,1)} %get-tuple-element.120), channel_id=1, source_target_pairs={{0,4},{1,5},{2,6},{3,7},{4,0},{5,1},{6,2},{7,3},{8,12},{9,13},{10,... | collective-permute-start | bytes 884744 | tf_op jit(solution)/shard_map/cond/branch_1_fun/ppermute | solution.py:729
  159.9 19.3 %collective-permute-start.9 = (bf16[96,1536]{1,0:T(8,128)(2,1)}, bf16[96,1536]{1,0:T(8,128)(2,1)S(1)}, u32[]{:S(2)}, u32[]{:S(2)}) collective-permute-start(bf16[96,1536]{1,0:T(8,128)(2,1)} %get-tuple-element.121), channel_id=1, source_target_pairs={{0,5},{1,4},{2,7},{3,6},{4,1},{5,0},{6,3},{7,2},{8,13},{9,12},{10,... | collective-permute-start | bytes 884744 | tf_op jit(solution)/shard_map/cond/branch_1_fun/ppermute | solution.py:729
  161.8 11.4 %collective-permute-start.6 = (bf16[24,1536]{1,0:T(8,128)(2,1)S(1)}, bf16[24,1536]{1,0:T(8,128)(2,1)S(1)}, u32[]{:S(2)}, u32[]{:S(2)}) collective-permute-start(bf16[24,1536]{1,0:T(8,128)(2,1)S(1)} %constant_dynamic-slice_fusion.2), channel_id=1, source_target_pairs={{0,16},{1,17},{2,18},{3,19},{4,20},{5,21},{6,22},{7,23},{8,24},{9,... | collective-permute-start | bytes 221192 | tf_op jit(solution)/shard_map/cond/branch_1_fun/ppermute | solution.py:729
  164.4 14.8 %copy-start.13 = (bf16[96,1536]{1,0:T(8,128)(2,1)S(1)}, bf16[96,1536]{1,0:T(8,128)(2,1)}, u32[]{:S(2)}) copy-start(bf16[96,1536]{1,0:T(8,128)(2,1)} %get-tuple-element.136) | copy-start | bytes 884740 | tf_op jit(solution)/shard_map/cond
  179.4 8.2 %collective-permute-start.11 = (bf16[48,1536]{1,0:T(8,128)(2,1)S(1)}, bf16[48,1536]{1,0:T(8,128)(2,1)S(1)}, u32[]{:S(2)}, u32[]{:S(2)}) collective-permute-start(bf16[48,1536]{1,0:T(8,128)(2,1)S(1)} %constant_dynamic-slice_fusion.1), channel_id=1, source_target_pairs={{0,8},{1,9},{2,10},{3,11},{4,12},{5,13},{6,14},{7,15},{8,0},{9,1},... | collective-permute-start | bytes 442376 | tf_op jit(solution)/shard_map/cond/branch_1_fun/ppermute | solution.py:729
  181.9 45.7 %collective-permute-start.23 = (bf16[512,768]{1,0:T(8,128)(2,1)}, bf16[512,768]{1,0:T(8,128)(2,1)}, u32[]{:S(2)}, u32[]{:S(2)}) collective-permute-start(bf16[512,768]{1,0:T(8,128)(2,1)} %pad_maximum_fusion.1), channel_id=1, source_target_pairs={{0,1},{1,0},{2,3},{3,2},{4,5},{5,4},{6,7},{7,6},{8,9},{9,8},{10,11... | collective-permute-start | bytes 2359304 | tf_op jit(solution)/shard_map/cond/branch_1_fun/ppermute | solution.py:720
  182.9 9.4 %collective-permute-start.14 = (f32[12,768]{1,0:T(8,128)S(1)}, f32[12,768]{1,0:T(8,128)S(1)}, u32[]{:S(2)}, u32[]{:S(2)}) collective-permute-start(f32[12,768]{1,0:T(8,128)S(1)} %fusion.1), channel_id=1, source_target_pairs={{0,2},{1,3},{2,0},{3,1},{4,6},{5,7},{6,4},{7,5},{8,10},{9,11},{10,... | collective-permute-start | bytes 110600 | tf_op jit(solution)/shard_map/cond/branch_1_fun/ppermute | solution.py:729
  183.1 9.2 %collective-permute-start.10 = (bf16[24,1536]{1,0:T(8,128)(2,1)S(1)}, bf16[24,1536]{1,0:T(8,128)(2,1)S(1)}, u32[]{:S(2)}, u32[]{:S(2)}) collective-permute-start(bf16[24,1536]{1,0:T(8,128)(2,1)S(1)} %add_convert_fusion.6), channel_id=1, source_target_pairs={{0,16},{1,17},{2,18},{3,19},{4,20},{5,21},{6,22},{7,23},{8,24},{9,... | collective-permute-start | bytes 221192 | tf_op jit(solution)/shard_map/cond/branch_1_fun/ppermute | solution.py:729
  185.8 34.0 %collective-permute-start.24 = (bf16[256,768]{1,0:T(8,128)(2,1)}, bf16[256,768]{1,0:T(8,128)(2,1)S(1)}, u32[]{:S(2)}, u32[]{:S(2)}) collective-permute-start(bf16[256,768]{1,0:T(8,128)(2,1)} %get-tuple-element.162), channel_id=1, source_target_pairs={{0,1},{1,0},{2,3},{3,2},{4,5},{5,4},{6,7},{7,6},{8,9},{9,8},{10,11... | collective-permute-start | bytes 1179656 | tf_op jit(solution)/shard_map/cond/branch_1_fun/ppermute | solution.py:720
  187.6 9.0 %collective-permute-start.13 = (bf16[24,1536]{1,0:T(8,128)(2,1)S(1)}, bf16[24,1536]{1,0:T(8,128)(2,1)S(1)}, u32[]{:S(2)}, u32[]{:S(2)}) collective-permute-start(bf16[24,1536]{1,0:T(8,128)(2,1)S(1)} %constant_dynamic-slice_fusion), channel_id=1, source_target_pairs={{0,16},{1,17},{2,18},{3,19},{4,20},{5,21},{6,22},{7,23},{8,24},{9,... | collective-permute-start | bytes 221192 | tf_op jit(solution)/shard_map/cond/branch_1_fun/ppermute | solution.py:729
  192.3 9.5 %collective-permute-start.12 = (bf16[48,1536]{1,0:T(8,128)(2,1)S(1)}, bf16[48,1536]{1,0:T(8,128)(2,1)S(1)}, u32[]{:S(2)}, u32[]{:S(2)}) collective-permute-start(bf16[48,1536]{1,0:T(8,128)(2,1)S(1)} %pad_maximum_fusion.4), channel_id=1, source_target_pairs={{0,8},{1,9},{2,10},{3,11},{4,12},{5,13},{6,14},{7,15},{8,0},{9,1},... | collective-permute-start | bytes 442376 | tf_op jit(solution)/shard_map/cond/branch_1_fun/ppermute | solution.py:729
  192.4 10.2 %collective-permute-start.18 = (f32[12,768]{1,0:T(8,128)S(1)}, f32[12,768]{1,0:T(8,128)S(1)}, u32[]{:S(2)}, u32[]{:S(2)}) collective-permute-start(f32[12,768]{1,0:T(8,128)S(1)} %add.132), channel_id=1, source_target_pairs={{0,4},{1,5},{2,6},{3,7},{4,0},{5,1},{6,2},{7,3},{8,12},{9,13},{10,... | collective-permute-start | bytes 110600 | tf_op jit(solution)/shard_map/cond/branch_1_fun/ppermute | solution.py:729
  196.6 8.6 %collective-permute-start.20 = (bf16[24,1536]{1,0:T(8,128)(2,1)S(1)}, bf16[24,1536]{1,0:T(8,128)(2,1)S(1)}, u32[]{:S(2)}, u32[]{:S(2)}) collective-permute-start(bf16[24,1536]{1,0:T(8,128)(2,1)S(1)} %add_convert_fusion.5), channel_id=1, source_target_pairs={{0,16},{1,17},{2,18},{3,19},{4,20},{5,21},{6,22},{7,23},{8,24},{9,... | collective-permute-start | bytes 221192 | tf_op jit(solution)/shard_map/cond/branch_1_fun/ppermute | solution.py:729
  206.5 18.8 %collective-permute-start.22 = (bf16[48,1536]{1,0:T(8,128)(2,1)}, bf16[48,1536]{1,0:T(8,128)(2,1)}, u32[]{:S(2)}, u32[]{:S(2)}) collective-permute-start(bf16[48,1536]{1,0:T(8,128)(2,1)} %pad_maximum_fusion.5), channel_id=1, source_target_pairs={{0,8},{1,9},{2,10},{3,11},{4,12},{5,13},{6,14},{7,15},{8,0},{9,1},... | collective-permute-start | bytes 442376 | tf_op jit(solution)/shard_map/cond/branch_1_fun/ppermute | solution.py:729
  208.1 9.6 %collective-permute-start.19 = (f32[12,768]{1,0:T(8,128)S(1)}, f32[12,768]{1,0:T(8,128)S(1)}, u32[]{:S(2)}, u32[]{:S(2)}) collective-permute-start(f32[12,768]{1,0:T(8,128)S(1)} %add.134), channel_id=1, source_target_pairs={{0,8},{1,9},{2,10},{3,11},{4,12},{5,13},{6,14},{7,15},{8,0},{9,1},... | collective-permute-start | bytes 110600 | tf_op jit(solution)/shard_map/cond/branch_1_fun/ppermute | solution.py:729
  208.5 23.5 %collective-permute-start.15 = (bf16[96,1536]{1,0:T(8,128)(2,1)}, bf16[96,1536]{1,0:T(8,128)(2,1)S(1)}, u32[]{:S(2)}, u32[]{:S(2)}) collective-permute-start(bf16[96,1536]{1,0:T(8,128)(2,1)} %pad_maximum_fusion.2), channel_id=1, source_target_pairs={{0,1},{1,0},{2,3},{3,2},{4,5},{5,4},{6,7},{7,6},{8,9},{9,8},{10,11... | collective-permute-start | bytes 884744 | tf_op jit(solution)/shard_map/cond/branch_1_fun/ppermute | solution.py:729
  217.8 14.2 %collective-permute-start.16 = (bf16[96,1536]{1,0:T(8,128)(2,1)}, bf16[96,1536]{1,0:T(8,128)(2,1)S(1)}, u32[]{:S(2)}, u32[]{:S(2)}) collective-permute-start(bf16[96,1536]{1,0:T(8,128)(2,1)} %pad_maximum_fusion.2), channel_id=1, source_target_pairs={{0,4},{1,5},{2,6},{3,7},{4,0},{5,1},{6,2},{7,3},{8,12},{9,13},{10,... | collective-permute-start | bytes 884744 | tf_op jit(solution)/shard_map/cond/branch_1_fun/ppermute | solution.py:729
  219.8 12.8 %collective-permute-start.17 = (bf16[96,1536]{1,0:T(8,128)(2,1)}, bf16[96,1536]{1,0:T(8,128)(2,1)S(1)}, u32[]{:S(2)}, u32[]{:S(2)}) collective-permute-start(bf16[96,1536]{1,0:T(8,128)(2,1)} %pad_maximum_fusion.2), channel_id=1, source_target_pairs={{0,5},{1,4},{2,7},{3,6},{4,1},{5,0},{6,3},{7,2},{8,13},{9,12},{10,... | collective-permute-start | bytes 884744 | tf_op jit(solution)/shard_map/cond/branch_1_fun/ppermute | solution.py:729
  221.8 10.8 %copy-start.1 = (f32[512,768]{1,0:T(8,128)S(1)}, f32[512,768]{1,0:T(8,128)}, u32[]{:S(2)}) copy-start(f32[512,768]{1,0:T(8,128)} %get-tuple-element.72.middle_ref) | copy-start | bytes 4718596 | tf_op jit(solution)/shard_map/cond
  225.3 5.3 %collective-permute-start.21 = (f32[12,768]{1,0:T(8,128)}, f32[12,768]{1,0:T(8,128)S(1)}, u32[]{:S(2)}, u32[]{:S(2)}) collective-permute-start(f32[12,768]{1,0:T(8,128)} %add.135), channel_id=1, source_target_pairs={{0,16},{1,17},{2,18},{3,19},{4,20},{5,21},{6,22},{7,23},{8,24},{9,... | collective-permute-start | bytes 110600 | tf_op jit(solution)/shard_map/cond/branch_1_fun/ppermute | solution.py:729
  236.7 13.4 %collective-permute-start.32 = (bf16[96,1536]{1,0:T(8,128)(2,1)}, bf16[96,1536]{1,0:T(8,128)(2,1)S(1)}, u32[]{:S(2)}, u32[]{:S(2)}) collective-permute-start(bf16[96,1536]{1,0:T(8,128)(2,1)} %get-tuple-element.291), channel_id=1, source_target_pairs={{0,1},{1,0},{2,3},{3,2},{4,5},{5,4},{6,7},{7,6},{8,9},{9,8},{10,11... | collective-permute-start | bytes 884744 | tf_op jit(solution)/shard_map/ppermute | solution.py:729
  236.8 13.3 %collective-permute-start.33 = (bf16[96,1536]{1,0:T(8,128)(2,1)}, bf16[96,1536]{1,0:T(8,128)(2,1)S(1)}, u32[]{:S(2)}, u32[]{:S(2)}) collective-permute-start(bf16[96,1536]{1,0:T(8,128)(2,1)} %get-tuple-element.291), channel_id=1, source_target_pairs={{0,4},{1,5},{2,6},{3,7},{4,0},{5,1},{6,2},{7,3},{8,12},{9,13},{10,... | collective-permute-start | bytes 884744 | tf_op jit(solution)/shard_map/ppermute | solution.py:729
  238.1 12.4 %collective-permute-start.34 = (bf16[96,1536]{1,0:T(8,128)(2,1)}, bf16[96,1536]{1,0:T(8,128)(2,1)S(1)}, u32[]{:S(2)}, u32[]{:S(2)}) collective-permute-start(bf16[96,1536]{1,0:T(8,128)(2,1)} %get-tuple-element.291), channel_id=1, source_target_pairs={{0,5},{1,4},{2,7},{3,6},{4,1},{5,0},{6,3},{7,2},{8,13},{9,12},{10,... | collective-permute-start | bytes 884744 | tf_op jit(solution)/shard_map/ppermute | solution.py:729
  240.2 7.1 %collective-permute-start.35 = (f32[12,768]{1,0:T(8,128)}, f32[12,768]{1,0:T(8,128)S(1)}, u32[]{:S(2)}, u32[]{:S(2)}) collective-permute-start(f32[12,768]{1,0:T(8,128)} %get-tuple-element.292), channel_id=1, source_target_pairs={{0,1},{1,0},{2,3},{3,2},{4,5},{5,4},{6,7},{7,6},{8,9},{9,8},{10,11... | collective-permute-start | bytes 110600 | tf_op jit(solution)/shard_map/ppermute | solution.py:729
  240.3 12.4 %collective-permute-start.36 = (bf16[384,1536]{1,0:T(8,128)(2,1)}, bf16[384,1536]{1,0:T(8,128)(2,1)S(1)}, u32[]{:S(2)}, u32[]{:S(2)}) collective-permute-start(bf16[384,1536]{1,0:T(8,128)(2,1)} %get-tuple-element.302), channel_id=1, source_target_pairs={{0,2},{1,3},{2,0},{3,1},{4,6},{5,7},{6,4},{7,5},{8,10},{9,11},{10,... | collective-permute-start | bytes 3538952 | tf_op jit(solution)/shard_map/ppermute | solution.py:729
  252.7 3.2 %collective-permute-start.37 = (bf16[384,1536]{1,0:T(8,128)(2,1)}, bf16[384,1536]{1,0:T(8,128)(2,1)}, u32[]{:S(2)}, u32[]{:S(2)}) collective-permute-start(bf16[384,1536]{1,0:T(8,128)(2,1)} %pad_maximum_fusion.7), channel_id=1, source_target_pairs={{0,2},{1,3},{2,0},{3,1},{4,6},{5,7},{6,4},{7,5},{8,10},{9,11},{10,... | collective-permute-start | bytes 3538952 | tf_op jit(solution)/shard_map/ppermute | solution.py:729
  (21 other events, 92.6 us)
Sparse Core Ops, SparseCore 0:
  94.9 133.7 all-reduce.2
